TPU v7x, 32 devices: a whole 2x2x4 slice. The times are simulated.
32 devices in a mesh: row: 4 (over y, core), col: 8 (over z, x).
Axes of the slice: x: 2, y: 2, z: 4, core: 2. Of those that a mesh axis runs over, the one named last changes fastest.
Arguments:
- kernels: bfloat16 [6, 4096, 6144], P(None, 'col', 'row'), may hold values from -0.03125 to 0.03125
- history: bfloat16 [6, 6144, 256], P(None, ('row', 'col')), may hold values from -6 to 6
- incident: float32 [32, 128, 256], P(('row', 'col')), may hold values from -6 to 6
- owner: int32 [32], replicated, may hold values from 0 to 3, as said below
- tile_pairs: int32 [384, 2], P(('row', 'col')), may hold values from 0 to 31, as said below
- tile_values: bfloat16 [384, 128, 128], P(('row', 'col')), may hold values from -0.109375 to 0.109375
- tile_counts: int32 [32], P(('row', 'col')), may hold values from 1 to 12, as said below
Outputs:
- density: float32 [32, 128, 256], P(('row', 'col'))
Inputs may be any that keep to these rules, and one draw needn't show every extreme that they name: `owner`: within each block of 4 consecutive clusters starting at a multiple of 4, the owners are all different. tile_pairs[t, 0] is the cluster whose slot is t // 12; for a target cluster k the sources of its slot are distinct clusters whose block (cluster // 4) is k // 4 - 1, k // 4 or k // 4 + 1, modulo 8. `tile_counts`: some device has all 12 slots live.
All inputs are finite; a program needn't handle non-finite values.
Results may differ from a plain program's by a relative error of at most 0.0012.
Values may be sent and summed in bfloat16 or wider, within the bound.
No kernel may reach another device: no remote copies, remote signals or barrier semaphores. Data moves between devices by JAX's collectives and lax.ppermute only.
A program may use at most 128 MiB of HBM per device.

v0:
```python
import jax
import jax.numpy as jnp
from jax import lax
from jax.sharding import PartitionSpec as P

SWEEPS = 3


damping = 0.7


def with_halo(cells, sides, width):
    for axis, dim in sides:
        count = lax.axis_size(axis)
        head = lax.slice_in_dim(cells, 0, width, axis=dim)
        tail = lax.slice_in_dim(cells, cells.shape[dim] - width, cells.shape[dim], axis=dim)
        cells = jnp.concatenate(
            [
                lax.ppermute(tail, axis, [(i, (i + 1) % count) for i in range(count)]),
                cells,
                lax.ppermute(head, axis, [((i + 1) % count, i) for i in range(count)]),
            ],
            axis=dim,
        )
    return cells


def per_device(kernels, history, incident, owner, tile_pairs, tile_values, tile_counts):
    row_count = lax.axis_size("row")
    col_count = lax.axis_size("col")
    columns = history.shape[2]
    cluster = incident.shape[1]
    retarded = lax.dot_general(
        kernels,
        lax.all_gather(history, "col", axis=1, tiled=True),
        (((0, 2), (0, 1)), ((), ())),
        preferred_element_type=jnp.float32,
    )
    col_index = lax.axis_index("col")
    row_index = lax.axis_index("row")
    block_owner = lax.dynamic_slice_in_dim(owner, col_index * row_count, row_count)
    positions = jnp.arange(row_count, dtype=jnp.int32)
    blocks = retarded.reshape(row_count, cluster, columns)
    block_sum = lax.psum_scatter(blocks, "row", scatter_dimension=0, tiled=True)
    everyone = lax.all_gather(block_sum, "row", axis=0, tiled=True)
    chosen = jnp.sum(jnp.where(block_owner == row_index, positions, 0))
    owned_sum = lax.dynamic_index_in_dim(everyone, chosen, 0, keepdims=False)
    driven = incident[0] - owned_sum
    sources = tile_pairs[:, 1]
    clusters = jnp.arange(owner.shape[0], dtype=jnp.int32)
    src_owner = jnp.sum(jnp.where(sources[:, None] == clusters[None, :], owner[None, :], 0), axis=1)
    src_block = sources // row_count
    window_slot = (src_block - col_index + 1 + col_count) % col_count * row_count + src_owner
    active = jnp.arange(tile_values.shape[0], dtype=jnp.int32) < tile_counts[0]
    density = driven
    for sweep_step in range(SWEEPS):
        rounded = density.astype(jnp.bfloat16)
        block_part = lax.all_gather(rounded, "row", axis=0, tiled=True)
        window = with_halo(block_part, (("col", 0),), row_count * cluster)
        window = window.reshape(-1, cluster, columns)
        picked = jnp.take(window, window_slot, axis=0)
        picked = jnp.where(active[:, None, None], picked, jnp.zeros((), jnp.bfloat16))
        near_term = lax.dot_general(
            tile_values, picked, (((0, 2), (0, 1)), ((), ())), preferred_element_type=jnp.float32
        )
        density = density + damping * (driven - density - near_term)
    return density[None]


def solution(mesh):
    in_specs = (
        P(None, "col", "row"),
        P(None, ("row", "col"), None),
        P(("row", "col"), None, None),
        P(),
        P(("row", "col"), None),
        P(("row", "col"), None, None),
        P(("row", "col")),
    )
    out_specs = P(("row", "col"), None, None)
    return jax.shard_map(
        per_device, mesh=mesh, in_specs=in_specs, out_specs=out_specs, check_vma=False
    )
```

profile of v0, /device:TPU:0, one launch (start us, length us, event | category | flops | bytes accessed | tf_op | source)
XLA Modules:
  0.0 202.0 jit_solution(14236669765198058881)
XLA Ops:
  6.5 0.7 all-gather.2.cloned.1.call-update
  7.3 84.3 %all-gather.2.cloned.1.call-done = bf16[6,1536,256]{2,1,0:T(8,128)(2,1)} async-done(((bf16[6,192,256]{2,1,0:T(8,128)(2,1)}), bf16[6,1536,256]{2,1,0:T(8,128)(2,1)}) %all-gather.2.cloned.1.call-update) | async-done | bytes 4718608 | tf_op jit(solution)/shard_map/all_gather | solution.py:35
  91.6 8.4 %fusion.34 = f32[512,256,1]{1,0,2:T(8,128)} fusion(bf16[6,512,1536]{2,1,0:T(8,128)(2,1)} %param.9, bf16[6,1536,256]{2,1,0:T(8,128)(2,1)} %all-gather.2.cloned.1.call-done), kind=kOutput, calls=%fused_computation.66 | convolution fusion | flops 2415919104 | bytes 14680064 | tf_op jit(solution)/shard_map/dot_general | solution.py:33
  100.1 0.7 fusion.22
  102.1 0.1 copy.30
  103.5 0.2 select_reduce_fusion
  103.7 16.5 %reduce-scatter.2.cloned.1.call-done = f32[1,128,256]{2,1,0:T(8,128)} async-done(((f32[4,128,256]{2,1,0:T(8,128)}), f32[1,128,256]{2,1,0:T(8,128)}) %reduce-scatter.2.cloned.1.call-update) | async-done | bytes 131088 | tf_op jit(solution)/shard_map/reduce_scatter | solution.py:44
  120.2 6.8 %all_gather.16 = f32[4,128,256]{2,1,0:T(8,128)S(1)} all-gather(f32[1,128,256]{2,1,0:T(8,128)} %reduce-scatter.2.cloned.1.call-done), channel_id=1, replica_groups=mesh['row'=4,'col'=8] {'row'}, dimensions={0}, use_global_device_ids=true | all-gather | bytes 655360 | tf_op jit(solution)/shard_map/all_gather | solution.py:45
  127.2 5.9 %all_gather.17 = bf16[512,256]{0,1:T(8,128)(2,1)S(1)} all-gather(bf16[128,256]{0,1:T(8,128)(2,1)S(1)} %get-tuple-element.8), channel_id=1, replica_groups=mesh['row'=4,'col'=8] {'row'}, dimensions={0}, use_global_device_ids=true | all-gather | bytes 327680 | tf_op jit(solution)/shard_map/all_gather | solution.py:58
  133.1 1.5 collective-permute-start
  134.6 3.2 %collective-permute-start.1 = (bf16[512,256]{0,1:T(8,128)(2,1)S(1)}, bf16[512,256]{0,1:T(8,128)(2,1)S(1)}, u32[]{:S(2)}, u32[]{:S(2)}) collective-permute-start(bf16[512,256]{0,1:T(8,128)(2,1)S(1)} %all_gather.17), channel_id=1, source_target_pairs={{1,0},{2,1},{3,2},{4,3},{5,4},{6,5},{7,6},{0,7},{9,8},{10,9},{11,1... | collective-permute-start | bytes 786440 | tf_op jit(solution)/shard_map/ppermute | solution.py:21
  137.8 8.4 %collective-permute-done = bf16[512,256]{0,1:T(8,128)(2,1)S(1)} collective-permute-done((bf16[512,256]{0,1:T(8,128)(2,1)S(1)}, bf16[512,256]{0,1:T(8,128)(2,1)S(1)}, u32[]{:S(2)}, u32[]{:S(2)}) %collective-permute-start) | collective-permute-done | bytes 262176 | tf_op jit(solution)/shard_map/ppermute | solution.py:19
  146.2 2.2 %collective-permute-done.1 = bf16[512,256]{0,1:T(8,128)(2,1)S(1)} collective-permute-done((bf16[512,256]{0,1:T(8,128)(2,1)S(1)}, bf16[512,256]{0,1:T(8,128)(2,1)S(1)}, u32[]{:S(2)}, u32[]{:S(2)}) %collective-permute-start.1) | collective-permute-done | bytes 262176 | tf_op jit(solution)/shard_map/ppermute | solution.py:21
  148.5 0.3 copy.31
  148.8 0.6 gather_fusion
  149.4 0.5 fusion.32
  149.9 5.8 %all_gather.18 = bf16[512,256]{0,1:T(8,128)(2,1)S(1)} all-gather(bf16[128,256]{0,1:T(8,128)(2,1)S(1)} %get-tuple-element.10), channel_id=1, replica_groups=mesh['row'=4,'col'=8] {'row'}, dimensions={0}, use_global_device_ids=true | all-gather | bytes 327680 | tf_op jit(solution)/shard_map/all_gather | solution.py:58
  155.7 0.3 collective-permute-start.2
  156.0 4.4 %collective-permute-start.3 = (bf16[512,256]{0,1:T(8,128)(2,1)S(1)}, bf16[512,256]{0,1:T(8,128)(2,1)S(1)}, u32[]{:S(2)}, u32[]{:S(2)}) collective-permute-start(bf16[512,256]{0,1:T(8,128)(2,1)S(1)} %all_gather.18), channel_id=1, source_target_pairs={{1,0},{2,1},{3,2},{4,3},{5,4},{6,5},{7,6},{0,7},{9,8},{10,9},{11,1... | collective-permute-start | bytes 786440 | tf_op jit(solution)/shard_map/ppermute | solution.py:21
  160.5 7.3 %collective-permute-done.2 = bf16[512,256]{0,1:T(8,128)(2,1)S(1)} collective-permute-done((bf16[512,256]{0,1:T(8,128)(2,1)S(1)}, bf16[512,256]{0,1:T(8,128)(2,1)S(1)}, u32[]{:S(2)}, u32[]{:S(2)}) %collective-permute-start.2) | collective-permute-done | bytes 262176 | tf_op jit(solution)/shard_map/ppermute | solution.py:19
  167.7 2.8 %collective-permute-done.3 = bf16[512,256]{0,1:T(8,128)(2,1)S(1)} collective-permute-done((bf16[512,256]{0,1:T(8,128)(2,1)S(1)}, bf16[512,256]{0,1:T(8,128)(2,1)S(1)}, u32[]{:S(2)}, u32[]{:S(2)}) %collective-permute-start.3) | collective-permute-done | bytes 262176 | tf_op jit(solution)/shard_map/ppermute | solution.py:21
  170.6 0.3 copy.33
  170.9 0.6 gather_fusion.1
  171.5 0.5 fusion.33
  172.0 5.8 %all_gather.19 = bf16[512,256]{0,1:T(8,128)(2,1)S(1)} all-gather(bf16[128,256]{0,1:T(8,128)(2,1)S(1)} %get-tuple-element.12), channel_id=1, replica_groups=mesh['row'=4,'col'=8] {'row'}, dimensions={0}, use_global_device_ids=true | all-gather | bytes 327680 | tf_op jit(solution)/shard_map/all_gather | solution.py:58
  177.8 4.7 %collective-permute-start.5 = (bf16[512,256]{0,1:T(8,128)(2,1)S(1)}, bf16[512,256]{0,1:T(8,128)(2,1)S(1)}, u32[]{:S(2)}, u32[]{:S(2)}) collective-permute-start(bf16[512,256]{0,1:T(8,128)(2,1)S(1)} %all_gather.19), channel_id=1, source_target_pairs={{1,0},{2,1},{3,2},{4,3},{5,4},{6,5},{7,6},{0,7},{9,8},{10,9},{11,1... | collective-permute-start | bytes 786440 | tf_op jit(solution)/shard_map/ppermute | solution.py:21
  182.5 7.3 %collective-permute-done.4 = bf16[512,256]{0,1:T(8,128)(2,1)S(1)} collective-permute-done((bf16[512,256]{0,1:T(8,128)(2,1)S(1)}, bf16[512,256]{0,1:T(8,128)(2,1)S(1)}, u32[]{:S(2)}, u32[]{:S(2)}) %collective-permute-start.4) | collective-permute-done | bytes 262176 | tf_op jit(solution)/shard_map/ppermute | solution.py:19
  189.8 3.1 %collective-permute-done.5 = bf16[512,256]{0,1:T(8,128)(2,1)S(1)} collective-permute-done((bf16[512,256]{0,1:T(8,128)(2,1)S(1)}, bf16[512,256]{0,1:T(8,128)(2,1)S(1)}, u32[]{:S(2)}, u32[]{:S(2)}) %collective-permute-start.5) | collective-permute-done | bytes 262176 | tf_op jit(solution)/shard_map/ppermute | solution.py:21
  192.9 0.3 copy.35
  193.2 0.6 gather_fusion.2
  193.8 0.5 fusion.9
  194.4 0.8 copy.37
  (21 shorter events, 0.4 us)
Async XLA Ops:
  6.5 142.9 %copy-start = (bf16[12,128,128]{2,1,0:T(8,128)(2,1)S(1)}, bf16[12,128,128]{2,1,0:T(8,128)(2,1)}, u32[]{:S(2)}) copy-start(bf16[12,128,128]{2,1,0:T(8,128)(2,1)} %param.14) | copy-start | bytes 1179652
  6.5 85.1 %all-gather.2.cloned.1.call-start = ((), (), s32[]{:S(2)}) async-start(), calls=%async_computation.1 | async-start | bytes 5308416 | tf_op jit(solution)/shard_map/all_gather | solution.py:35
  7.3 92.8 %copy-start.2 = (s32[32]{0:T(128)S(1)}, s32[32]{0:T(128)}, u32[]{:S(2)}) copy-start(s32[32]{0:T(128)} %param.12) | copy-start | bytes 388
  7.3 94.8 %copy-start.1 = (f32[1,128,256]{2,1,0:T(8,128)S(1)}, f32[1,128,256]{2,1,0:T(8,128)}, u32[]{:S(2)}) copy-start(f32[1,128,256]{2,1,0:T(8,128)} %param.11) | copy-start | bytes 393220
  7.3 96.2 %copy-start.3 = (s32[12,2]{0,1:T(2,128)S(1)}, s32[12,2]{0,1:T(2,128)}, u32[]{:S(2)}) copy-start(s32[12,2]{0,1:T(2,128)} %param.13) | copy-start | bytes 292
  7.3 112.9 %reduce-scatter.2.cloned.1.call-start = ((), (), s32[]{:S(2)}) async-start(), calls=%async_computation.2 | async-start | bytes 655360 | tf_op jit(solution)/shard_map/reduce_scatter | solution.py:44
  133.1 13.2 %collective-permute-start = (bf16[512,256]{0,1:T(8,128)(2,1)S(1)}, bf16[512,256]{0,1:T(8,128)(2,1)S(1)}, u32[]{:S(2)}, u32[]{:S(2)}) collective-permute-start(bf16[512,256]{0,1:T(8,128)(2,1)S(1)} %all_gather.17), channel_id=1, source_target_pairs={{0,1},{1,2},{2,3},{3,4},{4,5},{5,6},{6,7},{7,0},{8,9},{9,10},{10,1... | collective-permute-start | bytes 786440 | tf_op jit(solution)/shard_map/ppermute | solution.py:19
  134.6 13.9 %collective-permute-start.1 = (bf16[512,256]{0,1:T(8,128)(2,1)S(1)}, bf16[512,256]{0,1:T(8,128)(2,1)S(1)}, u32[]{:S(2)}, u32[]{:S(2)}) collective-permute-start(bf16[512,256]{0,1:T(8,128)(2,1)S(1)} %all_gather.17), channel_id=1, source_target_pairs={{1,0},{2,1},{3,2},{4,3},{5,4},{6,5},{7,6},{0,7},{9,8},{10,9},{11,1... | collective-permute-start | bytes 786440 | tf_op jit(solution)/shard_map/ppermute | solution.py:21
  155.7 12.0 %collective-permute-start.2 = (bf16[512,256]{0,1:T(8,128)(2,1)S(1)}, bf16[512,256]{0,1:T(8,128)(2,1)S(1)}, u32[]{:S(2)}, u32[]{:S(2)}) collective-permute-start(bf16[512,256]{0,1:T(8,128)(2,1)S(1)} %all_gather.18), channel_id=1, source_target_pairs={{0,1},{1,2},{2,3},{3,4},{4,5},{5,6},{6,7},{7,0},{8,9},{9,10},{10,1... | collective-permute-start | bytes 786440 | tf_op jit(solution)/shard_map/ppermute | solution.py:19
  156.0 14.5 %collective-permute-start.3 = (bf16[512,256]{0,1:T(8,128)(2,1)S(1)}, bf16[512,256]{0,1:T(8,128)(2,1)S(1)}, u32[]{:S(2)}, u32[]{:S(2)}) collective-permute-start(bf16[512,256]{0,1:T(8,128)(2,1)S(1)} %all_gather.18), channel_id=1, source_target_pairs={{1,0},{2,1},{3,2},{4,3},{5,4},{6,5},{7,6},{0,7},{9,8},{10,9},{11,1... | collective-permute-start | bytes 786440 | tf_op jit(solution)/shard_map/ppermute | solution.py:21
  177.8 12.0 %collective-permute-start.4 = (bf16[512,256]{0,1:T(8,128)(2,1)S(1)}, bf16[512,256]{0,1:T(8,128)(2,1)S(1)}, u32[]{:S(2)}, u32[]{:S(2)}) collective-permute-start(bf16[512,256]{0,1:T(8,128)(2,1)S(1)} %all_gather.19), channel_id=1, source_target_pairs={{0,1},{1,2},{2,3},{3,4},{4,5},{5,6},{6,7},{7,0},{8,9},{9,10},{10,1... | collective-permute-start | bytes 786440 | tf_op jit(solution)/shard_map/ppermute | solution.py:19
  177.8 15.1 %collective-permute-start.5 = (bf16[512,256]{0,1:T(8,128)(2,1)S(1)}, bf16[512,256]{0,1:T(8,128)(2,1)S(1)}, u32[]{:S(2)}, u32[]{:S(2)}) collective-permute-start(bf16[512,256]{0,1:T(8,128)(2,1)S(1)} %all_gather.19), channel_id=1, source_target_pairs={{1,0},{2,1},{3,2},{4,3},{5,4},{6,5},{7,6},{0,7},{9,8},{10,9},{11,1... | collective-permute-start | bytes 786440 | tf_op jit(solution)/shard_map/ppermute | solution.py:21
Sparse Core Ops, SparseCore 0:
  9.5 82.0 all-gather.1
  100.2 20.0 reduce-scatter.1
where the time goes:
time: 202 us
  waiting for transfers between devices  133 us (66%)
  blocking collectives  24.3 us (12%)
  between operations  16.2 us (8%)
  starting transfers between devices  14.2 us (7%)
  matrix products  10 us (5%)
  local copies, waits for them, and re-layouts  3.57 us (2%)
    all_gather x1, waiting for transfers between devices, per_device(): lax.all_gather(history, 'col', axis=1, tiled=True)  84.3 us
    ppermute x3, waiting for transfers between devices, with_halo(): lax.ppermute(tail, axis, [(i, (i + 1) % count) for i in range(count)])  22.9 us
    all_gather x3, blocking collectives, per_device(): block_part = lax.all_gather(rounded, 'row', axis=0, tiled=True)  17.5 us
    reduce_scatter x1, waiting for transfers between devices, per_device(): block_sum = lax.psum_scatter(blocks, 'row', scatter_dimension=0, tiled=True)  16.5 us
    ppermute x3, starting transfers between devices, with_halo(): lax.ppermute(head, axis, [((i + 1) % count, i) for i in range(count)])  12.4 us
    dot_general x1, matrix products, per_device(): lax.dot_general(kernels, lax.all_gather(history, 'col', axis=1, tiled=Tru...  8.41 us
    ppermute x3, waiting for transfers between devices, with_halo(): lax.ppermute(head, axis, [((i + 1) % count, i) for i in range(count)])  8.1 us
    all_gather x1, blocking collectives, per_device(): everyone = lax.all_gather(block_sum, 'row', axis=0, tiled=True)  6.78 us
  transfers between devices with their start and end apart: 8, of which 8 were waited for; matrix products, arithmetic and copies ran while one was open for 1% of the time, Pallas kernels for 0%

commit v1 on v0

v1 whole, which is shorter than its diff:
```python
import functools

import jax
import jax.numpy as jnp
from jax import lax
from jax.experimental import pallas as pl
from jax.experimental.pallas import tpu as pltpu
from jax.sharding import PartitionSpec as P

SWEEPS = 3
CHUNKS = 1


damping = 0.7


def cost(flops, moved):
    return pl.CostEstimate(flops=flops, bytes_accessed=moved, transcendentals=0)


def dense_tiles(pick, live, tile_values):
    slots = pick.shape[0]
    _, rows, depth = tile_values.shape

    def body(pick_ref, live_ref, tile_ref, out_ref):
        keep = live_ref[pl.program_id(0)] > 0
        out_ref[...] = jnp.where(keep, tile_ref[0], jnp.zeros((), tile_ref.dtype))

    return pl.pallas_call(
        body,
        out_shape=jax.ShapeDtypeStruct((rows, slots * depth), tile_values.dtype),
        grid_spec=pltpu.PrefetchScalarGridSpec(
            num_scalar_prefetch=2,
            grid=(slots,),
            in_specs=[pl.BlockSpec((1, rows, depth), lambda q, pick, live: (pick[q], 0, 0))],
            out_specs=pl.BlockSpec((rows, depth), lambda q, pick, live: (0, q)),
        ),
        cost_estimate=cost(0, 4 * slots * rows * depth),
        name="dense_tiles",
    )(pick, live, tile_values)


def stack_rows(source, parts):
    count = len(parts)
    rows, width = parts[0].shape

    def body(source_ref, *refs):
        out_ref = refs[-1]
        wanted = source_ref[pl.program_id(0)]
        for m in range(count):

            @pl.when(wanted == m)
            def _(m=m):
                out_ref[...] = refs[m][...]

    return pl.pallas_call(
        body,
        out_shape=jax.ShapeDtypeStruct((count * rows, width), parts[0].dtype),
        grid_spec=pltpu.PrefetchScalarGridSpec(
            num_scalar_prefetch=1,
            grid=(count,),
            in_specs=[pl.BlockSpec((rows, width), lambda i, s: (0, 0))] * count,
            out_specs=pl.BlockSpec((rows, width), lambda i, s: (i, 0)),
        ),
        cost_estimate=cost(0, 4 * count * rows * width),
        name="stack_rows",
    )(source, *parts)


def multiply(where, kernels, sides, seed, inner, spread):
    lags, rows, _ = kernels.shape
    count = len(sides)
    _, depth, columns = sides[0][0].shape
    first = isinstance(seed, tuple)

    def body(where_ref, kernel_ref, seed_ref, *refs):
        blocks = refs[: 2 * count]
        if spread:
            outs, (total, pair, turned) = refs[2 * count : -3], refs[-3:]
        else:
            (total,), (pair,) = refs[2 * count : -1], refs[-1:]
        side, lag = pl.program_id(0), pl.program_id(1)

        @pl.when((side == 0) & (lag == 0))
        def _():
            if first:
                total[...] = jnp.zeros_like(total)
                height = seed_ref.shape[0]
                at = pl.multiple_of(where_ref[2] * height, height)
                total[pl.ds(at, height), :] = -seed_ref[...]
            else:
                total[...] = seed_ref[...]

        inside = where_ref[0]
        for s in range(count):

            @pl.when((side == s) & (where_ref[4 + 2 * s] > 0))
            def _(s=s):
                here = pl.multiple_of(inside * depth, depth)
                there = pl.multiple_of((1 - inside) * depth, depth)
                pair[pl.ds(here, depth), :] = blocks[2 * s][0]
                pair[pl.ds(there, depth), :] = blocks[2 * s + 1][0]
                total[...] += jnp.dot(kernel_ref[0], pair[...], preferred_element_type=jnp.float32)

        if spread:

            @pl.when((side == count - 1) & (lag == lags - 1))
            def _():
                turned[...] = total[...].T
                width = columns // spread
                for m in range(spread):
                    at = pl.multiple_of((where_ref[1] ^ m) * width, width)
                    outs[m][...] = turned[pl.ds(at, width), :]

    def block_map(s):
        return lambda p, j, w: (jnp.where(p == s, j * w[4 + 2 * s], 0 if s else (lags - 1) * w[4 + 2 * s]), 0, 0)

    block_specs = [pl.BlockSpec((1, depth, columns), block_map(s)) for s in range(count) for _ in range(2)]
    if first:
        seed, chunk = seed
        seed_spec = pl.BlockSpec((seed.shape[0], columns), lambda p, j, w: (0, chunk))
    else:
        seed_spec = pl.BlockSpec((rows, columns), lambda p, j, w: (0, 0))
    scratch = [pltpu.VMEM((2 * depth, columns), sides[0][0].dtype)]
    whole = (rows, columns)
    if spread:
        part = (columns // spread, rows)
        out_shape = [jax.ShapeDtypeStruct(part, jnp.float32)] * spread
        out_specs = [pl.BlockSpec(part, lambda p, j, w: (0, 0))] * spread
        scratch = [pltpu.VMEM(whole, jnp.float32)] + scratch + [pltpu.VMEM(whole[::-1], jnp.float32)]
    else:
        out_shape = jax.ShapeDtypeStruct(whole, jnp.float32)
        out_specs = pl.BlockSpec(whole, lambda p, j, w: (0, 0))

    return pl.pallas_call(
        body,
        out_shape=out_shape,
        grid_spec=pltpu.PrefetchScalarGridSpec(
            num_scalar_prefetch=1,
            grid=(count, lags),
            in_specs=[
                pl.BlockSpec((1, rows, 2 * depth), lambda p, j, w: (j * w[4 + 2 * p], 0, w[3 + 2 * p])),
                seed_spec,
                *block_specs,
            ],
            out_specs=out_specs,
            scratch_shapes=scratch,
        ),
        cost_estimate=cost(4 * count * lags * rows * depth * columns, 4 * count * lags * depth * (rows + columns)),
        name="multiply",
    )(where, kernels, seed, *[b for side in sides for b in side])


def multiply_plain(where, kernels, sides, seed, inner, spread):
    depth, columns = sides[0][0].shape[1:]
    rows = kernels.shape[1]
    if isinstance(seed, tuple):
        incident, chunk = seed
        total = jnp.zeros((rows, columns), jnp.float32)
        part = -lax.slice_in_dim(incident, chunk * columns, (chunk + 1) * columns, axis=1)
        total = lax.dynamic_update_slice_in_dim(total, part, where[2] * incident.shape[0], 0)
    else:
        total = seed
    for s, (own, other) in enumerate(sides):
        lower = jnp.where(where[0] == 0, own, other)
        upper = jnp.where(where[0] == 0, other, own)
        pair = jnp.concatenate([lower, upper], axis=1)
        piece = lax.dynamic_slice_in_dim(kernels, where[3 + 2 * s] * 2 * depth, 2 * depth, axis=2)
        product = lax.dot_general(piece, pair, (((0, 2), (0, 1)), ((), ())), preferred_element_type=jnp.float32)
        total = total + jnp.where(where[4 + 2 * s] > 0, product, jnp.zeros((), jnp.float32))
    if not spread:
        return total
    turned = total.T
    width = columns // spread
    return [lax.dynamic_slice_in_dim(turned, (where[1] ^ m) * width, width, 0) for m in range(spread)]


def sweep(chosen, dense, driven, density, rounded, left, right, last):
    width, rows = driven.shape
    count = chosen.shape[0]
    height = rows // count

    def body(chosen_ref, dense_ref, driven_ref, density_ref, rounded_ref, left_ref, right_ref, *outs):
        def term(ref, k):
            return lax.dot_general(
                ref[...],
                dense_ref[:, k * rows : (k + 1) * rows],
                (((1,), (1,)), ((), ())),
                preferred_element_type=jnp.float32,
            )

        near = term(rounded_ref, 1) + term(left_ref, 0) + term(right_ref, 2)
        old = density_ref[...]
        new = old + damping * (driven_ref[...] - old - near)
        if last:
            outs[-1][...] = new
            for m in range(count):
                at = pl.multiple_of(chosen_ref[m] * height, height)
                outs[m][...] = outs[-1][:, pl.ds(at, height)]
        else:
            outs[0][...] = new
            outs[1][...] = new.astype(outs[1].dtype)

    if last:
        out_shape = [jax.ShapeDtypeStruct((width, height), jnp.float32)] * count
        scratch = [pltpu.VMEM((width, rows), jnp.float32)]
    else:
        out_shape = [
            jax.ShapeDtypeStruct((width, rows), jnp.float32),
            jax.ShapeDtypeStruct((width, rows), rounded.dtype),
        ]
        scratch = []
    vmem = pl.BlockSpec(memory_space=pltpu.VMEM)
    return pl.pallas_call(
        body,
        out_shape=out_shape,
        in_specs=[pl.BlockSpec(memory_space=pltpu.SMEM)] + [vmem] * 6,
        out_specs=[vmem] * len(out_shape),
        scratch_shapes=scratch,
        cost_estimate=cost(6 * width * rows * rows, 6 * rows * rows + 20 * width * rows),
        name="sweep_last" if last else "sweep",
    )(chosen, dense, driven, density, rounded, left, right)


def assemble(place, groups):
    count = len(groups[0])
    width, height = groups[0][0].shape
    columns = len(groups) * count * width

    def body(place_ref, *refs):
        out_ref, turned = refs[-2:]
        for g in range(len(groups)):
            for m in range(count):
                at = pl.multiple_of((place_ref[1] ^ m) * width, width)
                turned[pl.ds(g * count * width + at, width), :] = refs[g * count + m][...]
        out_ref[0] = turned[...].T

    vmem = pl.BlockSpec(memory_space=pltpu.VMEM)
    flat = [piece for group in groups for piece in group]
    return pl.pallas_call(
        body,
        out_shape=jax.ShapeDtypeStruct((1, height, columns), jnp.float32),
        in_specs=[pl.BlockSpec(memory_space=pltpu.SMEM)] + [vmem] * len(flat),
        out_specs=vmem,
        scratch_shapes=[pltpu.VMEM((columns, height), jnp.float32)],
        cost_estimate=cost(0, 8 * columns * height),
        name="assemble",
    )(place, *flat)


def per_device(kernels, history, incident, owner, tile_pairs, tile_values, tile_counts):
    row_count = lax.axis_size("row")
    col_count = lax.axis_size("col")
    columns = history.shape[2]
    depth = history.shape[1]
    inner = 2
    outer = col_count // inner
    row_index = lax.axis_index("row")
    col_index = lax.axis_index("col")
    outer_at, inner_at = col_index // inner, col_index % inner

    def across_rows(x, m):
        return lax.ppermute(x, "row", [(i, i ^ m) for i in range(row_count)])

    def shifted(x, by):
        pairs = [(i, i + by * inner) for i in range(col_count) if 0 <= i + by * inner < col_count]
        return lax.ppermute(x, "col", pairs)

    def swapped(x, by):
        pairs = [(i ^ 1, i) for i in range(col_count) if 0 <= i // inner - by < outer]
        return lax.ppermute(x, "col", pairs)

    order = jnp.arange(row_count, dtype=jnp.int32)
    block_owner = lax.dynamic_slice_in_dim(owner, col_index * row_count, row_count)
    relative = order ^ row_index
    chosen = jnp.sum(jnp.where(block_owner[None, :] == relative[:, None], order[None, :], 0), axis=1)
    source_row = block_owner ^ row_index

    slots = jnp.arange(3 * row_count, dtype=jnp.int32)
    sources = tile_pairs[:, 1]
    window = (sources // row_count - col_index + 1 + col_count) % col_count * row_count + sources % row_count
    tiles = jnp.arange(tile_values.shape[0], dtype=jnp.int32)
    hit = (tiles < tile_counts[0])[None, :] & (window[None, :] == slots[:, None])
    pick = jnp.sum(jnp.where(hit, tiles[None, :], 0), axis=1)
    live = jnp.sum(hit.astype(jnp.int32), axis=1)
    own_tiles = dense_tiles(pick, live, tile_values)
    dense = stack_rows(source_row, [own_tiles] + [across_rows(own_tiles, m) for m in range(1, row_count)])

    product = multiply if (inner * depth) % 128 == 0 else multiply_plain

    def where_of(*sides):
        head = [inner_at, row_index, chosen[0]]
        for by in sides:
            at = outer_at - by
            there = (at >= 0) & (at < outer)
            head += [jnp.where(there, at, outer_at), there.astype(jnp.int32)]
        return jnp.stack([h.astype(jnp.int32) for h in head])

    place = where_of(0)
    width = columns // CHUNKS
    groups = []
    for chunk in range(CHUNKS):
        own = lax.slice_in_dim(history, chunk * width, (chunk + 1) * width, axis=2)
        low = high = own
        total = product(place, kernels, [(own, swapped(own, 0))], (incident[0], chunk), inner, 0)
        for step in range(1, outer):
            low, high = shifted(low, 1), shifted(high, -1)
            sides = [(low, swapped(low, step)), (high, swapped(high, -step))]
            spread = row_count if step == outer - 1 else 0
            total = product(where_of(step, -step), kernels, sides, total, inner, spread)
        summed = total[0]
        for m in range(1, row_count):
            summed = summed + across_rows(total[m], m)
        driven = -summed
        density = driven
        rounded = density.astype(jnp.bfloat16)
        for step in range(SWEEPS):
            left = lax.ppermute(rounded, "col", [(i, (i + 1) % col_count) for i in range(col_count)])
            right = lax.ppermute(rounded, "col", [((i + 1) % col_count, i) for i in range(col_count)])
            last = step == SWEEPS - 1
            result = sweep(chosen, dense, driven, density, rounded, left, right, last)
            if not last:
                density, rounded = result
        groups.append([result[0]] + [across_rows(result[m], m) for m in range(1, row_count)])
    return assemble(place, groups)


def solution(mesh):
    in_specs = (
        P(None, "col", "row"),
        P(None, ("row", "col"), None),
        P(("row", "col"), None, None),
        P(),
        P(("row", "col"), None),
        P(("row", "col"), None, None),
        P(("row", "col")),
    )
    out_specs = P(("row", "col"), None, None)
    return jax.shard_map(
        per_device, mesh=mesh, in_specs=in_specs, out_specs=out_specs, check_vma=False
    )
```

time: 202 us -> 160 us (0.79)
  waiting for transfers between devices: 133 us -> 43.4 us
  Pallas kernels: 0 us -> 50.7 us
  starting transfers between devices: 14.2 us -> 53.2 us
  blocking collectives: 24.3 us -> 0 us
  between operations: 16.2 us -> 0.97 us
  matrix products: 10 us -> 0 us
  other arithmetic: 1.1 us -> 4.39 us
  local copies, waits for them, and re-layouts: 3.57 us -> 5.97 us
    all_gather x1 -> x0, waiting for transfers between devices: 84.3 us -> none  [per_device(): lax.all_gather(history, 'col', axis=1, tiled=True)]
    pallas_call x0 -> x10, Pallas kernels: none -> 50.7 us  [the longest x4 30.6 us: multiply(): pl.pallas_call(body, out_shape=out_shape, grid_spec=pltpu.PrefetchScalarG...]
    ppermute x6 -> x28, starting transfers between devices: 14.2 us -> 53.2 us  [the longest x6 17.6 us: shifted(): return lax.ppermute(x, 'col', pairs)]
    all_gather x4 -> x0, blocking collectives: 24.3 us -> none  [the longest x3 17.5 us: per_device(): block_part = lax.all_gather(rounded, 'row', axis=0, tiled=True)]
    reduce_scatter x1 -> x0, waiting for transfers between devices: 16.5 us -> none  [per_device(): block_sum = lax.psum_scatter(blocks, 'row', scatter_dimension=0, tiled=True)]
    ppermute x6 -> x28, waiting for transfers between devices: 31 us -> 43.4 us  [the longest x6 21.8 us: shifted(): return lax.ppermute(x, 'col', pairs)]
    dot_general x4 -> x0, matrix products: 10 us -> none  [the longest x1 8.41 us: per_device(): lax.dot_general(kernels, lax.all_gather(history, 'col', axis=1, tiled=Tru...]
    unnamed x10 -> x40, local copies, waits for them, and re-layouts: 0.19 us -> 3.32 us
  transfers between devices with their start and end apart: 8 -> 28, of which waited for: 8 -> 12; matrix products, arithmetic and copies ran while one was open for 1% -> 4% of each run, Pallas kernels for 0% -> 20%
where the time goes in v1:
time: 160 us; the launch traced here: 159 us
  starting transfers between devices  53.2 us (33%)
  Pallas kernels  50.7 us (32%)
  waiting for transfers between devices  43.4 us (27%)
  local copies, waits for them, and re-layouts  5.97 us (4%)
  other arithmetic  4.39 us (3%)
    pallas_call x4, Pallas kernels, multiply(): pl.pallas_call(body, out_shape=out_shape, grid_spec=pltpu.PrefetchScalarG...  30.6 us
    ppermute x6, waiting for transfers between devices, shifted(): return lax.ppermute(x, 'col', pairs)  21.8 us
    ppermute x6, starting transfers between devices, shifted(): return lax.ppermute(x, 'col', pairs)  17.6 us
    ppermute x7, starting transfers between devices, swapped(): return lax.ppermute(x, 'col', pairs)  15.2 us
    ppermute x9, waiting for transfers between devices, across_rows(): return lax.ppermute(x, 'row', [(i, i ^ m) for i in range(row_count)])  14.5 us
    ppermute x3, starting transfers between devices, per_device(): lax.ppermute(rounded, 'col', [((i + 1) % col_count, i) for i in range(col...  11.4 us
    pallas_call x3, Pallas kernels, sweep(): pl.pallas_call(body, out_shape=out_shape, in_specs=[pl.BlockSpec(memory_s...  8.45 us
    pallas_call x1, Pallas kernels, dense_tiles(): pl.pallas_call(body, out_shape=jax.ShapeDtypeStruct((rows, slots * depth)...  6.27 us
  transfers between devices with their start and end apart: 28, of which 12 were waited for; matrix products, arithmetic and copies ran while one was open for 4% of the time, Pallas kernels for 20%

profile of v1, /device:TPU:0, one launch (start us, length us, event | category | flops | bytes accessed | tf_op | source)
XLA Modules:
  0.0 158.6 jit_solution(18127993034369821253)
XLA Ops:
  0.0 5.0 %collective-permute-start.4 = (bf16[6,192,256]{2,1,0:T(8,128)(2,1)}, bf16[6,192,256]{2,1,0:T(8,128)(2,1)S(1)}, u32[]{:S(2)}, u32[]{:S(2)}) collective-permute-start(bf16[6,192,256]{2,1,0:T(8,128)(2,1)} %refs_0_.1), channel_id=1, source_target_pairs={{0,2},{1,3},{2,4},{3,5},{4,6},{5,7},{8,10},{9,11},{10,12},{11,13},... | collective-permute-start | bytes 1769480 | tf_op jit(solution)/shard_map/ppermute | solution.py:267
  6.3 11.5 %collective-permute-done.4.refs_0_ = bf16[6,192,256]{2,1,0:T(8,128)(2,1)S(1)} collective-permute-done((bf16[6,192,256]{2,1,0:T(8,128)(2,1)}, bf16[6,192,256]{2,1,0:T(8,128)(2,1)S(1)}, u32[]{:S(2)}, u32[]{:S(2)}) %collective-permute-start.4) | collective-permute-done | bytes 589856 | tf_op jit(solution)/shard_map/ppermute | solution.py:267
  17.8 4.3 %collective-permute-start.8 = (bf16[6,192,256]{2,1,0:T(8,128)(2,1)S(1)}, bf16[6,192,256]{2,1,0:T(8,128)(2,1)S(1)}, u32[]{:S(2)}, u32[]{:S(2)}) collective-permute-start(bf16[6,192,256]{2,1,0:T(8,128)(2,1)S(1)} %collective-permute-done.4.refs_0_), channel_id=1, source_target_pairs={{0,2},{1,3},{2,4},{3,5},{4,6},{5,7},{8,10},{9,11},{10,12},{11,13},... | collective-permute-start | bytes 1769480 | tf_op jit(solution)/shard_map/ppermute | solution.py:267
  23.5 1.6 collective-permute-start.3
  26.5 7.3 %collective-permute-done.8.refs_0_ = bf16[6,192,256]{2,1,0:T(8,128)(2,1)S(1)} collective-permute-done((bf16[6,192,256]{2,1,0:T(8,128)(2,1)S(1)}, bf16[6,192,256]{2,1,0:T(8,128)(2,1)S(1)}, u32[]{:S(2)}, u32[]{:S(2)}) %collective-permute-start.8) | collective-permute-done | bytes 589856 | tf_op jit(solution)/shard_map/ppermute | solution.py:267
  33.8 4.4 %collective-permute-start.12 = (bf16[6,192,256]{2,1,0:T(8,128)(2,1)S(1)}, bf16[6,192,256]{2,1,0:T(8,128)(2,1)S(1)}, u32[]{:S(2)}, u32[]{:S(2)}) collective-permute-start(bf16[6,192,256]{2,1,0:T(8,128)(2,1)S(1)} %collective-permute-done.8.refs_0_), channel_id=1, source_target_pairs={{0,2},{1,3},{2,4},{3,5},{4,6},{5,7},{8,10},{9,11},{10,12},{11,13},... | collective-permute-start | bytes 1769480 | tf_op jit(solution)/shard_map/ppermute | solution.py:267
  39.6 3.4 %collective-permute-start.7 = (bf16[6,192,256]{2,1,0:T(8,128)(2,1)S(1)}, bf16[6,192,256]{2,1,0:T(8,128)(2,1)}, u32[]{:S(2)}, u32[]{:S(2)}) collective-permute-start(bf16[6,192,256]{2,1,0:T(8,128)(2,1)S(1)} %collective-permute-done.6.refs_2_), channel_id=1, source_target_pairs={{1,0},{0,1},{3,2},{2,3},{5,4},{4,5},{9,8},{8,9},{11,10},{10,11},{1... | collective-permute-start | bytes 1769480 | tf_op jit(solution)/shard_map/ppermute | solution.py:271
  43.7 2.4 %collective-permute-start.11 = (bf16[6,192,256]{2,1,0:T(8,128)(2,1)S(1)}, bf16[6,192,256]{2,1,0:T(8,128)(2,1)}, u32[]{:S(2)}, u32[]{:S(2)}) collective-permute-start(bf16[6,192,256]{2,1,0:T(8,128)(2,1)S(1)} %collective-permute-done.10.refs_2_), channel_id=1, source_target_pairs={{1,0},{0,1},{3,2},{2,3},{9,8},{8,9},{11,10},{10,11},{17,16},{16,17... | collective-permute-start | bytes 1769480 | tf_op jit(solution)/shard_map/ppermute | solution.py:271
  50.7 2.7 %collective-permute-done.14.refs_2_ = bf16[6,192,256]{2,1,0:T(8,128)(2,1)S(1)} collective-permute-done((bf16[6,192,256]{2,1,0:T(8,128)(2,1)S(1)}, bf16[6,192,256]{2,1,0:T(8,128)(2,1)S(1)}, u32[]{:S(2)}, u32[]{:S(2)}) %collective-permute-start.14) | collective-permute-done | bytes 589856 | tf_op jit(solution)/shard_map/ppermute | solution.py:267
  53.4 3.4 %collective-permute-start.15 = (bf16[6,192,256]{2,1,0:T(8,128)(2,1)S(1)}, bf16[6,192,256]{2,1,0:T(8,128)(2,1)}, u32[]{:S(2)}, u32[]{:S(2)}) collective-permute-start(bf16[6,192,256]{2,1,0:T(8,128)(2,1)S(1)} %collective-permute-done.14.refs_2_), channel_id=1, source_target_pairs={{1,0},{0,1},{9,8},{8,9},{17,16},{16,17},{25,24},{24,25}} | collective-permute-start | bytes 1769480 | tf_op jit(solution)/shard_map/ppermute | solution.py:271
  60.3 6.2 %multiply.4.seed_ref = f32[512,256]{1,0:T(8,128)} custom-call(s32[5]{0:T(128)} %stack.92.where_ref.place_ref, bf16[6,512,1536]{2,1,0:T(8,128)(2,1)} %kernel_ref.7, f32[128,256]{1,0:T(8,128)} %bitcast.33, bf16[6,192,256]{2,1,0:T(8,128)(2,1)} %refs_0_.1, bf16[6,192,256]{2,1,0:T(8,128)(2,1)} %collective-permute-done.3.refs_1_), custom_call_target="tpu_custom_call" | custom-call | flops 603979776 | bytes 3538944 | tf_op jit(solution)/shard_map/multiply/pallas_call | solution.py:135
  66.6 8.0 %multiply.5.seed_ref = f32[512,256]{1,0:T(8,128)} custom-call(s32[7]{0:T(128)} %stack.113.where_ref, bf16[6,512,1536]{2,1,0:T(8,128)(2,1)} %kernel_ref.7, f32[512,256]{1,0:T(8,128)} %multiply.4.seed_ref, bf16[6,192,256]{2,1,0:T(8,128)(2,1)} %copy-done.1, bf16[6,192,256]{2,1,0:T(8,128)(2,1)} %collective-permute-done.5.refs_1_, ...), custom_call_target="tpu_custom_call" | custom-call | flops 1207959552 | bytes 7077888 | tf_op jit(solution)/shard_map/multiply/pallas_call | solution.py:135
  74.6 8.0 %multiply.6.seed_ref = f32[512,256]{1,0:T(8,128)} custom-call(s32[7]{0:T(128)} %stack.106.where_ref, bf16[6,512,1536]{2,1,0:T(8,128)(2,1)} %kernel_ref.7, f32[512,256]{1,0:T(8,128)} %multiply.5.seed_ref, bf16[6,192,256]{2,1,0:T(8,128)(2,1)} %copy-done, bf16[6,192,256]{2,1,0:T(8,128)(2,1)} %collective-permute-done.9.refs_1_, bf16[6,192,256]{2,1,0:T(8,128)(2,1)} %copy-done.4, ...), custom_call_target="tpu_custom_call" | custom-call | flops 1207959552 | bytes 7077888 | tf_op jit(solution)/shard_map/multiply/pallas_call | solution.py:135
  82.7 8.4 %multiply.7 = (f32[64,512]{1,0:T(8,128)}, f32[64,512]{1,0:T(8,128)}, f32[64,512]{1,0:T(8,128)}, f32[64,512]{1,0:T(8,128)}) custom-call(s32[7]{0:T(128)} %stack.99.where_ref, bf16[6,512,1536]{2,1,0:T(8,128)(2,1)} %kernel_ref.7, f32[512,256]{1,0:T(8,128)} %multiply.6.seed_ref, bf16[6,192,256]{2,1,0:T(8,128)(2,1)} %copy-done.3, ...), custom_call_target="tpu_custom_call" | custom-call | flops 1207959552 | bytes 7077888 | tf_op jit(solution)/shard_map/multiply/pallas_call | solution.py:135
  91.0 1.6 collective-permute-start.17
  93.6 6.3 %dense_tiles.1.refs_0_ = bf16[128,1536]{1,0:T(8,128)(2,1)} custom-call(s32[12]{0:T(128)} %get-tuple-element.30.pick_ref, s32[12]{0:T(128)} %get-tuple-element.29.live_ref, bf16[12,128,128]{2,1,0:T(8,128)(2,1)} %tile_ref.1), custom_call_target="tpu_custom_call" | custom-call | bytes 786432 | tf_op jit(solution)/shard_map/dense_tiles/pallas_call | solution.py:29
  102.3 1.6 %fusion.4 = (bf16[64,512]{1,0:T(8,128)(2,1)S(1)}, f32[64,512]{1,0:T(8,128)}) fusion(f32[64,512]{1,0:T(8,128)S(1)} %collective-permute-done.18, f32[64,512]{1,0:T(8,128)S(1)} %collective-permute-done.17, f32[64,512]{1,0:T(8,128)} %get-tuple-element.17, f32[64,512]{1,0:T(8,128)S(1)} %collective-permute-done.16), kind=kLoop, calls=%fused_computation.21 | loop fusion | flops 163840 | bytes 720896 | tf_op jit(solution)/shard_map/convert_element_type | solution.py:316
  104.5 4.2 %collective-permute-start.20 = (bf16[64,512]{1,0:T(8,128)(2,1)S(1)}, bf16[64,512]{1,0:T(8,128)(2,1)S(1)}, u32[]{:S(2)}, u32[]{:S(2)}) collective-permute-start(bf16[64,512]{1,0:T(8,128)(2,1)S(1)} %get-tuple-element.31.rounded_ref), channel_id=1, source_target_pairs={{1,0},{2,1},{3,2},{4,3},{5,4},{6,5},{7,6},{0,7},{9,8},{10,9},{11,1... | collective-permute-start | bytes 196616 | tf_op jit(solution)/shard_map/ppermute | solution.py:319
  108.7 4.5 %collective-permute-done.1.refs_2_ = bf16[128,1536]{1,0:T(8,128)(2,1)S(1)} collective-permute-done((bf16[128,1536]{1,0:T(8,128)(2,1)}, bf16[128,1536]{1,0:T(8,128)(2,1)S(1)}, u32[]{:S(2)}, u32[]{:S(2)}) %collective-permute-start.1) | collective-permute-done | bytes 393248 | tf_op jit(solution)/shard_map/ppermute | solution.py:263
  113.2 6.8 %collective-permute-done.2.refs_3_ = bf16[128,1536]{1,0:T(8,128)(2,1)S(1)} collective-permute-done((bf16[128,1536]{1,0:T(8,128)(2,1)}, bf16[128,1536]{1,0:T(8,128)(2,1)S(1)}, u32[]{:S(2)}, u32[]{:S(2)}) %collective-permute-start.2) | collective-permute-done | bytes 393248 | tf_op jit(solution)/shard_map/ppermute | solution.py:263
  120.7 3.8 %stack_rows.1.dense_ref = bf16[512,1536]{1,0:T(8,128)(2,1)} custom-call(s32[4]{0:T(128)} %get-tuple-element.33.source_ref, bf16[128,1536]{1,0:T(8,128)(2,1)} %dense_tiles.1.refs_0_, bf16[128,1536]{1,0:T(8,128)(2,1)} %copy-done.6, bf16[128,1536]{1,0:T(8,128)(2,1)} %copy-done.7, bf16[128,1536]{1,0:T(8,128)(2,1)} %copy-done.8), custom_call_target="tpu_custom_call" | custom-call | bytes 3145728 | tf_op jit(solution)/shard_map/stack_rows/pallas_call | solution.py:56
  125.1 2.8 %sweep.2 = (f32[64,512]{1,0:T(8,128)}, bf16[64,512]{1,0:T(8,128)(2,1)}) custom-call(s32[4]{0:T(128)} %copy-done.19, bf16[512,1536]{1,0:T(8,128)(2,1)} %stack_rows.1.dense_ref, f32[64,512]{1,0:T(8,128)} %get-tuple-element.32.driven_ref.density_ref, f32[64,512]{1,0:T(8,128)} %get-tuple-element.32.driven_ref.density_ref, bf16[64,512]{1,0:T(8,128)(2,1)} %copy-done.9, ...), custom_call_target="tpu_custom_call" | custom-call | flops 100663296 | bytes 2228224 | tf_op jit(solution)/shard_map/sweep/pallas_call | solution.py:214
  128.5 4.2 %collective-permute-start.22 = (bf16[64,512]{1,0:T(8,128)(2,1)}, bf16[64,512]{1,0:T(8,128)(2,1)S(1)}, u32[]{:S(2)}, u32[]{:S(2)}) collective-permute-start(bf16[64,512]{1,0:T(8,128)(2,1)} %get-tuple-element.22.rounded_ref), channel_id=1, source_target_pairs={{1,0},{2,1},{3,2},{4,3},{5,4},{6,5},{7,6},{0,7},{9,8},{10,9},{11,1... | collective-permute-start | bytes 196616 | tf_op jit(solution)/shard_map/ppermute | solution.py:319
  132.7 2.9 %collective-permute-done.21.left_ref = bf16[64,512]{1,0:T(8,128)(2,1)S(1)} collective-permute-done((bf16[64,512]{1,0:T(8,128)(2,1)}, bf16[64,512]{1,0:T(8,128)(2,1)S(1)}, u32[]{:S(2)}, u32[]{:S(2)}) %collective-permute-start.21) | collective-permute-done | bytes 65568 | tf_op jit(solution)/shard_map/ppermute | solution.py:318
  137.5 2.8 %sweep.3 = (f32[64,512]{1,0:T(8,128)}, bf16[64,512]{1,0:T(8,128)(2,1)}) custom-call(s32[4]{0:T(128)} %copy-done.19, bf16[512,1536]{1,0:T(8,128)(2,1)} %stack_rows.1.dense_ref, f32[64,512]{1,0:T(8,128)} %get-tuple-element.32.driven_ref.density_ref, f32[64,512]{1,0:T(8,128)} %get-tuple-element.21.density_ref, bf16[64,512]{1,0:T(8,128)(2,1)} %get-tuple-element.22.rounded_ref, ...), custom_call_target="tpu_custom_call" | custom-call | flops 100663296 | bytes 2228224 | tf_op jit(solution)/shard_map/sweep/pallas_call | solution.py:214
  140.3 1.7 %collective-permute-start.23 = (bf16[64,512]{1,0:T(8,128)(2,1)}, bf16[64,512]{1,0:T(8,128)(2,1)S(1)}, u32[]{:S(2)}, u32[]{:S(2)}) collective-permute-start(bf16[64,512]{1,0:T(8,128)(2,1)} %get-tuple-element.24.rounded_ref), channel_id=1, source_target_pairs={{0,1},{1,2},{2,3},{3,4},{4,5},{5,6},{6,7},{7,0},{8,9},{9,10},{10,1... | collective-permute-start | bytes 196616 | tf_op jit(solution)/shard_map/ppermute | solution.py:318
  142.0 3.0 %collective-permute-start.24 = (bf16[64,512]{1,0:T(8,128)(2,1)}, bf16[64,512]{1,0:T(8,128)(2,1)S(1)}, u32[]{:S(2)}, u32[]{:S(2)}) collective-permute-start(bf16[64,512]{1,0:T(8,128)(2,1)} %get-tuple-element.24.rounded_ref), channel_id=1, source_target_pairs={{1,0},{2,1},{3,2},{4,3},{5,4},{6,5},{7,6},{0,7},{9,8},{10,9},{11,1... | collective-permute-start | bytes 196616 | tf_op jit(solution)/shard_map/ppermute | solution.py:319
  145.0 2.5 %collective-permute-done.23.left_ref = bf16[64,512]{1,0:T(8,128)(2,1)S(1)} collective-permute-done((bf16[64,512]{1,0:T(8,128)(2,1)}, bf16[64,512]{1,0:T(8,128)(2,1)S(1)}, u32[]{:S(2)}, u32[]{:S(2)}) %collective-permute-start.23) | collective-permute-done | bytes 65568 | tf_op jit(solution)/shard_map/ppermute | solution.py:318
  148.5 2.8 %sweep_last.1 = (f32[64,128]{1,0:T(8,128)}, f32[64,128]{1,0:T(8,128)}, f32[64,128]{1,0:T(8,128)}, f32[64,128]{1,0:T(8,128)}) custom-call(s32[4]{0:T(128)} %copy-done.19, bf16[512,1536]{1,0:T(8,128)(2,1)} %stack_rows.1.dense_ref, f32[64,512]{1,0:T(8,128)} %get-tuple-element.32.driven_ref.density_ref, f32[64,512]{1,0:T(8,128)} %get-tuple-element.23.density_ref, ...), custom_call_target="tpu_custom_call" | custom-call | flops 100663296 | bytes 2228224 | tf_op jit(solution)/shard_map/sweep_last/pallas_call | solution.py:214
  151.3 1.5 collective-permute-start.26
  153.2 2.3 %collective-permute-done.26.refs_2_ = f32[64,128]{1,0:T(8,128)S(1)} collective-permute-done((f32[64,128]{1,0:T(8,128)}, f32[64,128]{1,0:T(8,128)S(1)}, u32[]{:S(2)}, u32[]{:S(2)}) %collective-permute-start.26) | collective-permute-done | bytes 32800 | tf_op jit(solution)/shard_map/ppermute | solution.py:263
  157.0 1.6 assemble.1
  (84 shorter events, 24.2 us)
Async XLA Ops:
  0.0 17.8 %collective-permute-start.4 = (bf16[6,192,256]{2,1,0:T(8,128)(2,1)}, bf16[6,192,256]{2,1,0:T(8,128)(2,1)S(1)}, u32[]{:S(2)}, u32[]{:S(2)}) collective-permute-start(bf16[6,192,256]{2,1,0:T(8,128)(2,1)} %refs_0_.1), channel_id=1, source_target_pairs={{0,2},{1,3},{2,4},{3,5},{4,6},{5,7},{8,10},{9,11},{10,12},{11,13},... | collective-permute-start | bytes 1769480 | tf_op jit(solution)/shard_map/ppermute | solution.py:267
  5.0 17.2 %collective-permute-start.6 = (bf16[6,192,256]{2,1,0:T(8,128)(2,1)}, bf16[6,192,256]{2,1,0:T(8,128)(2,1)S(1)}, u32[]{:S(2)}, u32[]{:S(2)}) collective-permute-start(bf16[6,192,256]{2,1,0:T(8,128)(2,1)} %refs_0_.1), channel_id=1, source_target_pairs={{2,0},{3,1},{4,2},{5,3},{6,4},{7,5},{10,8},{11,9},{12,10},{13,11},... | collective-permute-start | bytes 1769480 | tf_op jit(solution)/shard_map/ppermute | solution.py:267
  17.8 48.7 %copy-start.1 = (bf16[6,192,256]{2,1,0:T(8,128)(2,1)}, bf16[6,192,256]{2,1,0:T(8,128)(2,1)S(1)}, u32[]{:S(2)}) copy-start(bf16[6,192,256]{2,1,0:T(8,128)(2,1)S(1)} %collective-permute-done.4.refs_0_) | copy-start | bytes 1769476
  17.8 16.0 %collective-permute-start.8 = (bf16[6,192,256]{2,1,0:T(8,128)(2,1)S(1)}, bf16[6,192,256]{2,1,0:T(8,128)(2,1)S(1)}, u32[]{:S(2)}, u32[]{:S(2)}) collective-permute-start(bf16[6,192,256]{2,1,0:T(8,128)(2,1)S(1)} %collective-permute-done.4.refs_0_), channel_id=1, source_target_pairs={{0,2},{1,3},{2,4},{3,5},{4,6},{5,7},{8,10},{9,11},{10,12},{11,13},... | collective-permute-start | bytes 1769480 | tf_op jit(solution)/shard_map/ppermute | solution.py:267
  22.2 44.4 %copy-start.2 = (bf16[6,192,256]{2,1,0:T(8,128)(2,1)}, bf16[6,192,256]{2,1,0:T(8,128)(2,1)S(1)}, u32[]{:S(2)}) copy-start(bf16[6,192,256]{2,1,0:T(8,128)(2,1)S(1)} %collective-permute-done.6.refs_2_) | copy-start | bytes 1769476
  22.2 16.1 %collective-permute-start.10 = (bf16[6,192,256]{2,1,0:T(8,128)(2,1)S(1)}, bf16[6,192,256]{2,1,0:T(8,128)(2,1)S(1)}, u32[]{:S(2)}, u32[]{:S(2)}) collective-permute-start(bf16[6,192,256]{2,1,0:T(8,128)(2,1)S(1)} %collective-permute-done.6.refs_2_), channel_id=1, source_target_pairs={{2,0},{3,1},{4,2},{5,3},{6,4},{7,5},{10,8},{11,9},{12,10},{13,11},... | collective-permute-start | bytes 1769480 | tf_op jit(solution)/shard_map/ppermute | solution.py:267
  23.5 20.2 %collective-permute-start.3 = (bf16[6,192,256]{2,1,0:T(8,128)(2,1)}, bf16[6,192,256]{2,1,0:T(8,128)(2,1)}, u32[]{:S(2)}, u32[]{:S(2)}) collective-permute-start(bf16[6,192,256]{2,1,0:T(8,128)(2,1)} %refs_0_.1), channel_id=1, source_target_pairs={{1,0},{0,1},{3,2},{2,3},{5,4},{4,5},{7,6},{6,7},{9,8},{8,9},{11,10... | collective-permute-start | bytes 1769480 | tf_op jit(solution)/shard_map/ppermute | solution.py:271
  25.0 21.1 %collective-permute-start.5 = (bf16[6,192,256]{2,1,0:T(8,128)(2,1)S(1)}, bf16[6,192,256]{2,1,0:T(8,128)(2,1)}, u32[]{:S(2)}, u32[]{:S(2)}) collective-permute-start(bf16[6,192,256]{2,1,0:T(8,128)(2,1)S(1)} %collective-permute-done.4.refs_0_), channel_id=1, source_target_pairs={{3,2},{2,3},{5,4},{4,5},{7,6},{6,7},{11,10},{10,11},{13,12},{12,13... | collective-permute-start | bytes 1769480 | tf_op jit(solution)/shard_map/ppermute | solution.py:271
  33.8 40.7 %copy-start = (bf16[6,192,256]{2,1,0:T(8,128)(2,1)}, bf16[6,192,256]{2,1,0:T(8,128)(2,1)S(1)}, u32[]{:S(2)}) copy-start(bf16[6,192,256]{2,1,0:T(8,128)(2,1)S(1)} %collective-permute-done.8.refs_0_) | copy-start | bytes 1769476
  33.8 15.3 %collective-permute-start.12 = (bf16[6,192,256]{2,1,0:T(8,128)(2,1)S(1)}, bf16[6,192,256]{2,1,0:T(8,128)(2,1)S(1)}, u32[]{:S(2)}, u32[]{:S(2)}) collective-permute-start(bf16[6,192,256]{2,1,0:T(8,128)(2,1)S(1)} %collective-permute-done.8.refs_0_), channel_id=1, source_target_pairs={{0,2},{1,3},{2,4},{3,5},{4,6},{5,7},{8,10},{9,11},{10,12},{11,13},... | collective-permute-start | bytes 1769480 | tf_op jit(solution)/shard_map/ppermute | solution.py:267
  38.3 36.3 %copy-start.4 = (bf16[6,192,256]{2,1,0:T(8,128)(2,1)}, bf16[6,192,256]{2,1,0:T(8,128)(2,1)S(1)}, u32[]{:S(2)}) copy-start(bf16[6,192,256]{2,1,0:T(8,128)(2,1)S(1)} %collective-permute-done.10.refs_2_) | copy-start | bytes 1769476
  38.3 15.1 %collective-permute-start.14 = (bf16[6,192,256]{2,1,0:T(8,128)(2,1)S(1)}, bf16[6,192,256]{2,1,0:T(8,128)(2,1)S(1)}, u32[]{:S(2)}, u32[]{:S(2)}) collective-permute-start(bf16[6,192,256]{2,1,0:T(8,128)(2,1)S(1)} %collective-permute-done.10.refs_2_), channel_id=1, source_target_pairs={{2,0},{3,1},{4,2},{5,3},{6,4},{7,5},{10,8},{11,9},{12,10},{13,11},... | collective-permute-start | bytes 1769480 | tf_op jit(solution)/shard_map/ppermute | solution.py:267
  39.6 27.0 %collective-permute-start.7 = (bf16[6,192,256]{2,1,0:T(8,128)(2,1)S(1)}, bf16[6,192,256]{2,1,0:T(8,128)(2,1)}, u32[]{:S(2)}, u32[]{:S(2)}) collective-permute-start(bf16[6,192,256]{2,1,0:T(8,128)(2,1)S(1)} %collective-permute-done.6.refs_2_), channel_id=1, source_target_pairs={{1,0},{0,1},{3,2},{2,3},{5,4},{4,5},{9,8},{8,9},{11,10},{10,11},{1... | collective-permute-start | bytes 1769480 | tf_op jit(solution)/shard_map/ppermute | solution.py:271
  43.7 30.9 %collective-permute-start.11 = (bf16[6,192,256]{2,1,0:T(8,128)(2,1)S(1)}, bf16[6,192,256]{2,1,0:T(8,128)(2,1)}, u32[]{:S(2)}, u32[]{:S(2)}) collective-permute-start(bf16[6,192,256]{2,1,0:T(8,128)(2,1)S(1)} %collective-permute-done.10.refs_2_), channel_id=1, source_target_pairs={{1,0},{0,1},{3,2},{2,3},{9,8},{8,9},{11,10},{10,11},{17,16},{16,17... | collective-permute-start | bytes 1769480 | tf_op jit(solution)/shard_map/ppermute | solution.py:271
  46.2 28.4 %collective-permute-start.9 = (bf16[6,192,256]{2,1,0:T(8,128)(2,1)S(1)}, bf16[6,192,256]{2,1,0:T(8,128)(2,1)}, u32[]{:S(2)}, u32[]{:S(2)}) collective-permute-start(bf16[6,192,256]{2,1,0:T(8,128)(2,1)S(1)} %collective-permute-done.8.refs_0_), channel_id=1, source_target_pairs={{5,4},{4,5},{7,6},{6,7},{13,12},{12,13},{15,14},{14,15},{21,20},{2... | collective-permute-start | bytes 1769480 | tf_op jit(solution)/shard_map/ppermute | solution.py:271
  49.2 33.5 %collective-permute-start.13 = (bf16[6,192,256]{2,1,0:T(8,128)(2,1)S(1)}, bf16[6,192,256]{2,1,0:T(8,128)(2,1)}, u32[]{:S(2)}, u32[]{:S(2)}) collective-permute-start(bf16[6,192,256]{2,1,0:T(8,128)(2,1)S(1)} %collective-permute-done.12.refs_0_), channel_id=1, source_target_pairs={{7,6},{6,7},{15,14},{14,15},{23,22},{22,23},{31,30},{30,31}} | collective-permute-start | bytes 1769480 | tf_op jit(solution)/shard_map/ppermute | solution.py:271
  53.4 29.3 %collective-permute-start.15 = (bf16[6,192,256]{2,1,0:T(8,128)(2,1)S(1)}, bf16[6,192,256]{2,1,0:T(8,128)(2,1)}, u32[]{:S(2)}, u32[]{:S(2)}) collective-permute-start(bf16[6,192,256]{2,1,0:T(8,128)(2,1)S(1)} %collective-permute-done.14.refs_2_), channel_id=1, source_target_pairs={{1,0},{0,1},{9,8},{8,9},{17,16},{16,17},{25,24},{24,25}} | collective-permute-start | bytes 1769480 | tf_op jit(solution)/shard_map/ppermute | solution.py:271
  91.0 11.1 %collective-permute-start.16 = (f32[64,512]{1,0:T(8,128)}, f32[64,512]{1,0:T(8,128)S(1)}, u32[]{:S(2)}, u32[]{:S(2)}) collective-permute-start(f32[64,512]{1,0:T(8,128)} %get-tuple-element.18), channel_id=1, source_target_pairs={{0,8},{8,0},{16,24},{24,16},{1,9},{9,1},{17,25},{25,17},{2,10},{10... | collective-permute-start | bytes 393224 | tf_op jit(solution)/shard_map/ppermute | solution.py:263
  91.0 11.3 %collective-permute-start.17 = (f32[64,512]{1,0:T(8,128)}, f32[64,512]{1,0:T(8,128)S(1)}, u32[]{:S(2)}, u32[]{:S(2)}) collective-permute-start(f32[64,512]{1,0:T(8,128)} %get-tuple-element.19), channel_id=1, source_target_pairs={{0,16},{8,24},{16,0},{24,8},{1,17},{9,25},{17,1},{25,9},{2,18},{10... | collective-permute-start | bytes 393224 | tf_op jit(solution)/shard_map/ppermute | solution.py:263
  92.6 9.7 %collective-permute-start.18 = (f32[64,512]{1,0:T(8,128)}, f32[64,512]{1,0:T(8,128)S(1)}, u32[]{:S(2)}, u32[]{:S(2)}) collective-permute-start(f32[64,512]{1,0:T(8,128)} %get-tuple-element.20), channel_id=1, source_target_pairs={{0,24},{8,16},{16,8},{24,0},{1,25},{9,17},{17,9},{25,1},{2,26},{10... | collective-permute-start | bytes 393224 | tf_op jit(solution)/shard_map/ppermute | solution.py:263
  99.9 8.8 %collective-permute-start = (bf16[128,1536]{1,0:T(8,128)(2,1)}, bf16[128,1536]{1,0:T(8,128)(2,1)S(1)}, u32[]{:S(2)}, u32[]{:S(2)}) collective-permute-start(bf16[128,1536]{1,0:T(8,128)(2,1)} %dense_tiles.1.refs_0_), channel_id=1, source_target_pairs={{0,8},{8,0},{16,24},{24,16},{1,9},{9,1},{17,25},{25,17},{2,10},{10... | collective-permute-start | bytes 1179656 | tf_op jit(solution)/shard_map/ppermute | solution.py:263
  101.0 12.2 %collective-permute-start.1 = (bf16[128,1536]{1,0:T(8,128)(2,1)}, bf16[128,1536]{1,0:T(8,128)(2,1)S(1)}, u32[]{:S(2)}, u32[]{:S(2)}) collective-permute-start(bf16[128,1536]{1,0:T(8,128)(2,1)} %dense_tiles.1.refs_0_), channel_id=1, source_target_pairs={{0,16},{8,24},{16,0},{24,8},{1,17},{9,25},{17,1},{25,9},{2,18},{10... | collective-permute-start | bytes 1179656 | tf_op jit(solution)/shard_map/ppermute | solution.py:263
  102.1 17.8 %collective-permute-start.2 = (bf16[128,1536]{1,0:T(8,128)(2,1)}, bf16[128,1536]{1,0:T(8,128)(2,1)S(1)}, u32[]{:S(2)}, u32[]{:S(2)}) collective-permute-start(bf16[128,1536]{1,0:T(8,128)(2,1)} %dense_tiles.1.refs_0_), channel_id=1, source_target_pairs={{0,24},{8,16},{16,8},{24,0},{1,25},{9,17},{17,9},{25,1},{2,26},{10... | collective-permute-start | bytes 1179656 | tf_op jit(solution)/shard_map/ppermute | solution.py:263
  103.9 20.5 %collective-permute-start.19 = (bf16[64,512]{1,0:T(8,128)(2,1)S(1)}, bf16[64,512]{1,0:T(8,128)(2,1)S(1)}, u32[]{:S(2)}, u32[]{:S(2)}) collective-permute-start(bf16[64,512]{1,0:T(8,128)(2,1)S(1)} %get-tuple-element.31.rounded_ref), channel_id=1, source_target_pairs={{0,1},{1,2},{2,3},{3,4},{4,5},{5,6},{6,7},{7,0},{8,9},{9,10},{10,1... | collective-permute-start | bytes 196616 | tf_op jit(solution)/shard_map/ppermute | solution.py:318
  104.5 20.0 %collective-permute-start.20 = (bf16[64,512]{1,0:T(8,128)(2,1)S(1)}, bf16[64,512]{1,0:T(8,128)(2,1)S(1)}, u32[]{:S(2)}, u32[]{:S(2)}) collective-permute-start(bf16[64,512]{1,0:T(8,128)(2,1)S(1)} %get-tuple-element.31.rounded_ref), channel_id=1, source_target_pairs={{1,0},{2,1},{3,2},{4,3},{5,4},{6,5},{7,6},{0,7},{9,8},{10,9},{11,1... | collective-permute-start | bytes 196616 | tf_op jit(solution)/shard_map/ppermute | solution.py:319
  127.9 7.6 %collective-permute-start.21 = (bf16[64,512]{1,0:T(8,128)(2,1)}, bf16[64,512]{1,0:T(8,128)(2,1)S(1)}, u32[]{:S(2)}, u32[]{:S(2)}) collective-permute-start(bf16[64,512]{1,0:T(8,128)(2,1)} %get-tuple-element.22.rounded_ref), channel_id=1, source_target_pairs={{0,1},{1,2},{2,3},{3,4},{4,5},{5,6},{6,7},{7,0},{8,9},{9,10},{10,1... | collective-permute-start | bytes 196616 | tf_op jit(solution)/shard_map/ppermute | solution.py:318
  128.5 8.4 %collective-permute-start.22 = (bf16[64,512]{1,0:T(8,128)(2,1)}, bf16[64,512]{1,0:T(8,128)(2,1)S(1)}, u32[]{:S(2)}, u32[]{:S(2)}) collective-permute-start(bf16[64,512]{1,0:T(8,128)(2,1)} %get-tuple-element.22.rounded_ref), channel_id=1, source_target_pairs={{1,0},{2,1},{3,2},{4,3},{5,4},{6,5},{7,6},{0,7},{9,8},{10,9},{11,1... | collective-permute-start | bytes 196616 | tf_op jit(solution)/shard_map/ppermute | solution.py:319
  140.3 7.2 %collective-permute-start.23 = (bf16[64,512]{1,0:T(8,128)(2,1)}, bf16[64,512]{1,0:T(8,128)(2,1)S(1)}, u32[]{:S(2)}, u32[]{:S(2)}) collective-permute-start(bf16[64,512]{1,0:T(8,128)(2,1)} %get-tuple-element.24.rounded_ref), channel_id=1, source_target_pairs={{0,1},{1,2},{2,3},{3,4},{4,5},{5,6},{6,7},{7,0},{8,9},{9,10},{10,1... | collective-permute-start | bytes 196616 | tf_op jit(solution)/shard_map/ppermute | solution.py:318
  142.0 5.9 %collective-permute-start.24 = (bf16[64,512]{1,0:T(8,128)(2,1)}, bf16[64,512]{1,0:T(8,128)(2,1)S(1)}, u32[]{:S(2)}, u32[]{:S(2)}) collective-permute-start(bf16[64,512]{1,0:T(8,128)(2,1)} %get-tuple-element.24.rounded_ref), channel_id=1, source_target_pairs={{1,0},{2,1},{3,2},{4,3},{5,4},{6,5},{7,6},{0,7},{9,8},{10,9},{11,1... | collective-permute-start | bytes 196616 | tf_op jit(solution)/shard_map/ppermute | solution.py:319
  151.3 1.9 %collective-permute-start.25 = (f32[64,128]{1,0:T(8,128)}, f32[64,128]{1,0:T(8,128)S(1)}, u32[]{:S(2)}, u32[]{:S(2)}) collective-permute-start(f32[64,128]{1,0:T(8,128)} %get-tuple-element.26), channel_id=1, source_target_pairs={{0,8},{8,0},{16,24},{24,16},{1,9},{9,1},{17,25},{25,17},{2,10},{10... | collective-permute-start | bytes 98312 | tf_op jit(solution)/shard_map/ppermute | solution.py:263
  151.3 4.2 %collective-permute-start.26 = (f32[64,128]{1,0:T(8,128)}, f32[64,128]{1,0:T(8,128)S(1)}, u32[]{:S(2)}, u32[]{:S(2)}) collective-permute-start(f32[64,128]{1,0:T(8,128)} %get-tuple-element.27), channel_id=1, source_target_pairs={{0,16},{8,24},{16,0},{24,8},{1,17},{9,25},{17,1},{25,9},{2,18},{10... | collective-permute-start | bytes 98312 | tf_op jit(solution)/shard_map/ppermute | solution.py:263
  152.8 3.6 %collective-permute-start.27 = (f32[64,128]{1,0:T(8,128)}, f32[64,128]{1,0:T(8,128)S(1)}, u32[]{:S(2)}, u32[]{:S(2)}) collective-permute-start(f32[64,128]{1,0:T(8,128)} %get-tuple-element.28), channel_id=1, source_target_pairs={{0,24},{8,16},{16,8},{24,0},{1,25},{9,17},{17,9},{25,1},{2,26},{10... | collective-permute-start | bytes 98312 | tf_op jit(solution)/shard_map/ppermute | solution.py:263
  (16 other events, 112.8 us)

commit v2 on v0

v2 whole, which is shorter than its diff:
```python
import jax
import jax.numpy as jnp
from jax import lax
from jax.experimental import pallas as pl
from jax.experimental.pallas import tpu as pltpu
from jax.sharding import PartitionSpec as P

SWEEPS = 3
PARTS = 2
LANES = 128


damping = 0.7


def cost(flops, moved):
    return pl.CostEstimate(flops=flops, bytes_accessed=moved, transcendentals=0)


def params(limit):
    return pltpu.CompilerParams(vmem_limit_bytes=limit * 2**20)


VMEM = pl.BlockSpec(memory_space=pltpu.VMEM)
SMEM = pl.BlockSpec(memory_space=pltpu.SMEM)


def dense_tiles(pick, live, tile_values):
    slots = pick.shape[0]
    _, rows, depth = tile_values.shape

    def body(pick_ref, live_ref, tile_ref, out_ref):
        for q in range(slots):
            tile = tile_ref[pick_ref[q]]
            out_ref[:, q * depth : (q + 1) * depth] = jnp.where(live_ref[q] > 0, tile, jnp.zeros_like(tile))

    return pl.pallas_call(
        body,
        out_shape=jax.ShapeDtypeStruct((rows, slots * depth), tile_values.dtype),
        in_specs=[SMEM, SMEM, VMEM],
        out_specs=VMEM,
        compiler_params=params(8),
        cost_estimate=cost(0, 4 * slots * rows * depth),
        name="dense_tiles",
    )(pick, live, tile_values)


def stack_rows(chosen, parts):
    count = len(parts)
    rows, width = parts[0].shape

    def body(chosen_ref, *refs):
        for m in range(count):
            at = pl.multiple_of(chosen_ref[m] * rows, rows)
            refs[-1][pl.ds(at, rows), :] = refs[m][...]

    return pl.pallas_call(
        body,
        out_shape=jax.ShapeDtypeStruct((count * rows, width), parts[0].dtype),
        in_specs=[SMEM] + [VMEM] * count,
        out_specs=VMEM,
        compiler_params=params(16),
        cost_estimate=cost(0, 4 * count * rows * width),
        name="stack_rows",
    )(chosen, *parts)


def multiply(table, base, kernels, blocks, seed, spread):
    lags, rows, _ = kernels.shape
    lags //= PARTS
    count = len(blocks)
    places = (table.shape[0] - 2) // 2
    depth, columns = blocks[0][2].shape[1:]
    window = -(-(depth + LANES - 1) // LANES)
    tall = window * LANES
    first = seed.ndim == 2 and seed.shape[0] != rows
    order = [b[0] for b in blocks]
    part = [b[1] for b in blocks]
    whole_own = blocks[0][2].shape[0] != lags

    def body(table_ref, *refs):
        lanes, seed_ref = refs[:window], refs[window]
        given = refs[window + 1 : window + 1 + len(arrays)]
        rest = refs[window + 1 + len(arrays) :]
        if spread:
            keep, give, total, padded, turned = rest
        else:
            total, padded = rest
        step = pl.program_id(0)

        @pl.when(step == 0)
        def _():
            if first:
                total[...] = jnp.zeros_like(total)
                height = seed_ref.shape[0]
                at = pl.multiple_of(table_ref[2 * places + 1] * height, height)
                total[pl.ds(at, height), :] = -seed_ref[...]
            else:
                total[...] = seed_ref[...]

        padded[...] = jnp.zeros_like(padded)
        for s in range(count):

            @pl.when(step == s)
            def _(s=s):
                shift = table_ref[places + order[s]]
                source = given[0 if whole_own else s]
                for lag in range(lags):
                    at = pl.multiple_of(lag * tall + shift, 32)
                    padded[pl.ds(at, depth), :] = source[lag]

        left = jnp.concatenate([lanes[w][lag] for lag in range(lags) for w in range(window)], axis=1)
        total[...] += jnp.dot(left, padded[...], preferred_element_type=jnp.float32)

        if spread:

            @pl.when(step == count - 1)
            def _():
                turned[...] = total[...].T
                width = columns // spread
                for m in range(spread):
                    at = pl.multiple_of((table_ref[2 * places] ^ m) * width, width)
                    (give if m % 2 else keep)[m // 2] = turned[pl.ds(at, width), :]

    def static_pick(values, p):
        out = values[0]
        for s in range(1, len(values)):
            out = jnp.where(p == s, values[s], out)
        return out

    def lane_map(w):
        return lambda p, t: (static_pick(part, p), 0, t[static_pick(order, p)] + w)

    if whole_own:
        arrays = [blocks[0][2]]
        block_specs = [pl.BlockSpec((lags, depth, columns), lambda p, t: (p, 0, 0))]
    else:
        arrays = [b[2] for b in blocks]
        block_specs = [pl.BlockSpec((lags, depth, columns), lambda p, t: (0, 0, 0))] * count
    whole = (rows, columns)
    scratch = [pltpu.VMEM((lags * tall, columns), kernels.dtype)]
    if spread:
        piece = (spread // 2, columns // spread, rows)
        out_shape = [jax.ShapeDtypeStruct(piece, jnp.float32)] * 2
        out_specs = [pl.BlockSpec(piece, lambda p, t: (0, 0, 0))] * 2
        scratch = [pltpu.VMEM(whole, jnp.float32)] + scratch + [pltpu.VMEM(whole[::-1], jnp.float32)]
    else:
        out_shape = jax.ShapeDtypeStruct(whole, jnp.float32)
        out_specs = pl.BlockSpec(whole, lambda p, t: (0, 0))

    return pl.pallas_call(
        body,
        out_shape=out_shape,
        grid_spec=pltpu.PrefetchScalarGridSpec(
            num_scalar_prefetch=1,
            grid=(count,),
            in_specs=[pl.BlockSpec((lags, rows, LANES), lane_map(w)) for w in range(window)]
            + [pl.BlockSpec(seed.shape, lambda p, t: (0, 0))]
            + block_specs,
            out_specs=out_specs,
            scratch_shapes=scratch,
        ),
        compiler_params=params(24 if rows <= 512 else 56),
        cost_estimate=cost(2 * count * lags * rows * tall * columns, 2 * count * lags * tall * (rows + columns)),
        name="multiply",
    )(table, *[kernels] * window, seed, *arrays)


def sweep(chosen, dense, driven, density, rounded, left, right, last):
    width, rows = driven.shape
    count = chosen.shape[0]
    height = rows // count

    def body(chosen_ref, dense_ref, driven_ref, density_ref, rounded_ref, left_ref, right_ref, *outs):
        def term(ref, k):
            return lax.dot_general(
                ref[...],
                dense_ref[:, k * rows : (k + 1) * rows],
                (((1,), (1,)), ((), ())),
                preferred_element_type=jnp.float32,
            )

        near = term(rounded_ref, 1) + term(left_ref, 0) + term(right_ref, 2)
        old = density_ref[...]
        new = old + damping * (driven_ref[...] - old - near)
        if last:
            away, home, whole = outs
            whole[...] = new
            for m in range(count):
                at = pl.multiple_of(chosen_ref[m] * height, height)
                (away if m >= count // 2 else home)[m % (count // 2)] = whole[:, pl.ds(at, height)]
        else:
            outs[0][...] = new
            outs[1][...] = new.astype(outs[1].dtype)

    if last:
        out_shape = [jax.ShapeDtypeStruct((count // 2, width, height), jnp.float32)] * 2
        scratch = [pltpu.VMEM((width, rows), jnp.float32)]
    else:
        out_shape = [
            jax.ShapeDtypeStruct((width, rows), jnp.float32),
            jax.ShapeDtypeStruct((width, rows), rounded.dtype),
        ]
        scratch = []
    return pl.pallas_call(
        body,
        out_shape=out_shape,
        in_specs=[SMEM] + [VMEM] * 6,
        out_specs=[VMEM] * len(out_shape),
        scratch_shapes=scratch,
        compiler_params=params(24),
        cost_estimate=cost(6 * width * rows * rows, 6 * rows * rows + 20 * width * rows),
        name="sweep_last" if last else "sweep",
    )(chosen, dense, driven, density, rounded, left, right)


def assemble(table, pieces):
    arrays = [piece for _, piece in pieces]
    width, height = arrays[0].shape[1:]
    columns = width * sum(piece.shape[0] for piece in arrays)
    where = table.shape[0] - 2

    def body(table_ref, *refs):
        out_ref, turned = refs[-2:]
        for (offsets, _), ref in zip(pieces, refs):
            for t, m in enumerate(offsets):
                at = pl.multiple_of((table_ref[where] ^ m) * width, width)
                turned[pl.ds(at, width), :] = ref[t]
        out_ref[0] = turned[...].T

    return pl.pallas_call(
        body,
        out_shape=jax.ShapeDtypeStruct((1, height, columns), jnp.float32),
        in_specs=[SMEM] + [VMEM] * len(arrays),
        out_specs=VMEM,
        scratch_shapes=[pltpu.VMEM((columns, height), jnp.float32)],
        compiler_params=params(8),
        cost_estimate=cost(0, 8 * columns * height),
        name="assemble",
    )(table, *arrays)


def per_device(kernels, history, incident, owner, tile_pairs, tile_values, tile_counts):
    row_count = lax.axis_size("row")
    col_count = lax.axis_size("col")
    lags, depth, columns = history.shape
    half = lags // PARTS
    row_index = lax.axis_index("row")
    col_index = lax.axis_index("col")

    def across_rows(x, m):
        return lax.ppermute(x, "row", [(i, i ^ m) for i in range(row_count)])

    walk = list(range(0, col_count, 2)) + list(range(col_count - 1, 0, -2))

    def around(x, by):
        pairs = [(walk[p], walk[(p + by) % col_count]) for p in range(col_count)]
        return lax.ppermute(x, "col", pairs)

    places = [0] + [by for k in range(1, (col_count + 1) // 2) for by in (k, -k)] + [col_count // 2]
    spot = {by: k for k, by in enumerate(places)}
    count = len(places)
    own_spot = jnp.where(col_index % 2 == 0, col_index // 2, col_count - 1 - col_index // 2)
    index = jnp.arange(2 * count + 2, dtype=jnp.int32)
    k = index % count
    by = jnp.where(k % 2 == 1, (k + 1) // 2, -(k // 2))
    p = (own_spot - by + 2 * col_count) % col_count
    source = jnp.where(p < col_count // 2, 2 * p, 2 * (col_count - 1 - p) + 1)
    tall = -(-(depth + LANES - 1) // LANES)
    group = jnp.minimum(source * depth // LANES, kernels.shape[2] // LANES - tall)
    order = jnp.arange(row_count, dtype=jnp.int32)
    block_owner = lax.dynamic_slice_in_dim(owner, col_index * row_count, row_count)
    chosen = jnp.sum(
        jnp.where(block_owner[None, :] == (order ^ row_index)[:, None], order[None, :], 0), axis=1
    )
    table = jnp.where(index < count, group, source * depth - group * LANES)
    table = jnp.where(index == 2 * count, row_index, table)
    table = jnp.where(index == 2 * count + 1, jnp.sum(jnp.where(block_owner == row_index, order, 0)), table)

    slots = jnp.arange(3 * row_count, dtype=jnp.int32)
    sources = tile_pairs[:, 1]
    place = (sources // row_count - col_index + 1 + col_count) % col_count * row_count + sources % row_count
    tiles = jnp.arange(tile_values.shape[0], dtype=jnp.int32)
    hit = (tiles < tile_counts[0])[None, :] & (place[None, :] == slots[:, None])
    pick = jnp.sum(jnp.where(hit, tiles[None, :], 0), axis=1)
    live = jnp.sum(hit.astype(jnp.int32), axis=1)
    own_tiles = dense_tiles(pick, live, tile_values)
    dense = stack_rows(chosen, [own_tiles] + [across_rows(own_tiles, m) for m in range(1, row_count)])

    halves = [history[i * half : (i + 1) * half] for i in range(PARTS)]
    moving = {(way, i): halves[i] for i in range(PARTS) for way in (1, -1)}
    total = multiply(table, 0, kernels, [(0, i, history) for i in range(PARTS)], incident[0], 0)
    for step in range(1, (col_count + 1) // 2):
        moving = {key: around(x, key[0]) for key, x in moving.items()}
        blocks = [(spot[way * step], i, moving[way, i]) for i in range(PARTS) for way in (1, -1)]
        total = multiply(table, step, kernels, blocks, total, 0)
    far = spot[col_count // 2]
    blocks = [(far, i, around(moving[way, i], way)) for i, way in ((0, 1), (1, -1))]
    keep, give = multiply(table, far, kernels, blocks, total, row_count)

    bit = 1
    got = across_rows(give, bit)
    summed = [keep[t] + got[t] for t in range(row_count // 2)]
    while len(summed) > 1:
        bit *= 2
        odd = summed[1::2]
        got = across_rows(odd[0] if len(odd) == 1 else jnp.stack(odd), bit)
        got = [got] if len(odd) == 1 else [got[t] for t in range(len(odd))]
        summed = [a + b for a, b in zip(summed[0::2], got)]
    driven = -summed[0]

    density = driven
    rounded = density.astype(jnp.bfloat16)
    for step in range(SWEEPS):
        left = lax.ppermute(rounded, "col", [(i, (i + 1) % col_count) for i in range(col_count)])
        right = lax.ppermute(rounded, "col", [((i + 1) % col_count, i) for i in range(col_count)])
        result = sweep(chosen, dense, driven, density, rounded, left, right, step == SWEEPS - 1)
        if step < SWEEPS - 1:
            density, rounded = result

    away, home = result
    bit = row_count // 2
    got = across_rows(away, bit)
    sets = [((0,), home), ((bit,), got)]
    while bit > 1:
        bit //= 2
        pieces_next = []
        for offsets, array in sets:
            pieces_next.append((offsets, array[:bit]))
            sent = across_rows(array[bit : 2 * bit], bit)
            pieces_next.append((tuple(o ^ bit for o in offsets), sent))
        sets = pieces_next
    return assemble(table, [(offsets, array) for offsets, array in sets])


def solution(mesh):
    in_specs = (
        P(None, "col", "row"),
        P(None, ("row", "col"), None),
        P(("row", "col"), None, None),
        P(),
        P(("row", "col"), None),
        P(("row", "col"), None, None),
        P(("row", "col")),
    )
    out_specs = P(("row", "col"), None, None)
    return jax.shard_map(
        per_device, mesh=mesh, in_specs=in_specs, out_specs=out_specs, check_vma=False
    )
```

time: 202 us -> 110 us (0.54)
  waiting for transfers between devices: 133 us -> 41.8 us
  blocking collectives: 24.3 us -> 0 us
  Pallas kernels: 0 us -> 22.9 us
  starting transfers between devices: 14.2 us -> 35 us
  between operations: 16.2 us -> 0.89 us
  matrix products: 10 us -> 0 us
  local copies, waits for them, and re-layouts: 3.57 us -> 6.75 us
    all_gather x1 -> x0, waiting for transfers between devices: 84.3 us -> none  [per_device(): lax.all_gather(history, 'col', axis=1, tiled=True)]
    all_gather x4 -> x0, blocking collectives: 24.3 us -> none  [the longest x3 17.5 us: per_device(): block_part = lax.all_gather(rounded, 'row', axis=0, tiled=True)]
    pallas_call x0 -> x11, Pallas kernels: none -> 22.9 us  [the longest x5 16.8 us: multiply(): pl.pallas_call(body, out_shape=out_shape, grid_spec=pltpu.PrefetchScalarG...]
    ppermute x6 -> x28, starting transfers between devices: 14.2 us -> 35 us  [the longest x14 15.5 us: around(): return lax.ppermute(x, 'col', pairs)]
    reduce_scatter x1 -> x0, waiting for transfers between devices: 16.5 us -> none  [per_device(): block_sum = lax.psum_scatter(blocks, 'row', scatter_dimension=0, tiled=True)]
    ppermute x6 -> x28, waiting for transfers between devices: 31 us -> 41.8 us  [the longest x14 19.2 us: around(): return lax.ppermute(x, 'col', pairs)]
    dot_general x4 -> x0, matrix products: 10 us -> none  [the longest x1 8.41 us: per_device(): lax.dot_general(kernels, lax.all_gather(history, 'col', axis=1, tiled=Tru...]
    unnamed x10, local copies, waits for them, and re-layouts: 0.19 us -> 5.66 us
  transfers between devices with their start and end apart: 8 -> 28, of which waited for: 8 -> 12; matrix products, arithmetic and copies ran while one was open for 1% -> 2% of each run, Pallas kernels for 0% -> 14%
where the time goes in v2:
time: 110 us
  waiting for transfers between devices  41.8 us (38%)
  starting transfers between devices  35 us (32%)
  Pallas kernels  22.9 us (21%)
  local copies, waits for them, and re-layouts  6.75 us (6%)
  other arithmetic  2.43 us (2%)
    ppermute x14, waiting for transfers between devices, around(): return lax.ppermute(x, 'col', pairs)  19.2 us
    ppermute x8, waiting for transfers between devices, across_rows(): return lax.ppermute(x, 'row', [(i, i ^ m) for i in range(row_count)])  18.1 us
    pallas_call x5, Pallas kernels, multiply(): pl.pallas_call(body, out_shape=out_shape, grid_spec=pltpu.PrefetchScalarG...  16.8 us
    ppermute x14, starting transfers between devices, around(): return lax.ppermute(x, 'col', pairs)  15.5 us
    ppermute x3, starting transfers between devices, per_device(): lax.ppermute(rounded, 'col', [((i + 1) % col_count, i) for i in range(col...  12.4 us
    unnamed x10, local copies, waits for them, and re-layouts  5.66 us
    ppermute x8, starting transfers between devices, across_rows(): return lax.ppermute(x, 'row', [(i, i ^ m) for i in range(row_count)])  5.17 us
    ppermute x3, waiting for transfers between devices, per_device(): lax.ppermute(rounded, 'col', [(i, (i + 1) % col_count) for i in range(col...  4.46 us
  transfers between devices with their start and end apart: 28, of which 12 were waited for; matrix products, arithmetic and copies ran while one was open for 2% of the time, Pallas kernels for 14%

profile of v2, /device:TPU:0, one launch (start us, length us, event | category | flops | bytes accessed | tf_op | source)
XLA Modules:
  0.0 109.7 jit_solution(10670481551748915669)
XLA Ops:
  1.1 3.1 %collective-permute-start.3 = (bf16[3,192,256]{2,1,0:T(8,128)(2,1)S(1)}, bf16[3,192,256]{2,1,0:T(8,128)(2,1)S(1)}, u32[]{:S(2)}, u32[]{:S(2)}) collective-permute-start(bf16[3,192,256]{2,1,0:T(8,128)(2,1)S(1)} %get-tuple-element.28), channel_id=1, source_target_pairs={{0,2},{2,4},{4,6},{6,7},{7,5},{5,3},{3,1},{1,0},{8,10},{10,12},{12... | collective-permute-start | bytes 884744 | tf_op jit(solution)/shard_map/ppermute | solution.py:258
  4.2 1.9 %collective-permute-start.4 = (bf16[3,192,256]{2,1,0:T(8,128)(2,1)S(1)}, bf16[3,192,256]{2,1,0:T(8,128)(2,1)S(1)}, u32[]{:S(2)}, u32[]{:S(2)}) collective-permute-start(bf16[3,192,256]{2,1,0:T(8,128)(2,1)S(1)} %get-tuple-element.28), channel_id=1, source_target_pairs={{0,1},{2,0},{4,2},{6,4},{7,6},{5,7},{3,5},{1,3},{8,9},{10,8},{12,1... | collective-permute-start | bytes 884744 | tf_op jit(solution)/shard_map/ppermute | solution.py:258
  6.2 5.7 %collective-permute-done.3.refs_4_ = bf16[3,192,256]{2,1,0:T(8,128)(2,1)S(1)} collective-permute-done((bf16[3,192,256]{2,1,0:T(8,128)(2,1)S(1)}, bf16[3,192,256]{2,1,0:T(8,128)(2,1)S(1)}, u32[]{:S(2)}, u32[]{:S(2)}) %collective-permute-start.3) | collective-permute-done | bytes 294944 | tf_op jit(solution)/shard_map/ppermute | solution.py:258
  12.0 2.1 %collective-permute-start.7 = (bf16[3,192,256]{2,1,0:T(8,128)(2,1)S(1)}, bf16[3,192,256]{2,1,0:T(8,128)(2,1)S(1)}, u32[]{:S(2)}, u32[]{:S(2)}) collective-permute-start(bf16[3,192,256]{2,1,0:T(8,128)(2,1)S(1)} %collective-permute-done.3.refs_4_), channel_id=1, source_target_pairs={{0,2},{2,4},{4,6},{6,7},{7,5},{5,3},{3,1},{1,0},{8,10},{10,12},{12... | collective-permute-start | bytes 884744 | tf_op jit(solution)/shard_map/ppermute | solution.py:258
  14.1 6.3 %collective-permute-done.4.refs_5_ = bf16[3,192,256]{2,1,0:T(8,128)(2,1)S(1)} collective-permute-done((bf16[3,192,256]{2,1,0:T(8,128)(2,1)S(1)}, bf16[3,192,256]{2,1,0:T(8,128)(2,1)S(1)}, u32[]{:S(2)}, u32[]{:S(2)}) %collective-permute-start.4) | collective-permute-done | bytes 294944 | tf_op jit(solution)/shard_map/ppermute | solution.py:258
  20.4 2.0 %collective-permute-start.9 = (bf16[3,192,256]{2,1,0:T(8,128)(2,1)S(1)}, bf16[3,192,256]{2,1,0:T(8,128)(2,1)S(1)}, u32[]{:S(2)}, u32[]{:S(2)}) collective-permute-start(bf16[3,192,256]{2,1,0:T(8,128)(2,1)S(1)} %collective-permute-done.5.refs_6_), channel_id=1, source_target_pairs={{0,2},{2,4},{4,6},{6,7},{7,5},{5,3},{3,1},{1,0},{8,10},{10,12},{12... | collective-permute-start | bytes 884744 | tf_op jit(solution)/shard_map/ppermute | solution.py:258
  22.4 2.2 %collective-permute-done.7.refs_4_ = bf16[3,192,256]{2,1,0:T(8,128)(2,1)S(1)} collective-permute-done((bf16[3,192,256]{2,1,0:T(8,128)(2,1)S(1)}, bf16[3,192,256]{2,1,0:T(8,128)(2,1)S(1)}, u32[]{:S(2)}, u32[]{:S(2)}) %collective-permute-start.7) | collective-permute-done | bytes 294944 | tf_op jit(solution)/shard_map/ppermute | solution.py:258
  24.6 2.1 %collective-permute-start.11 = (bf16[3,192,256]{2,1,0:T(8,128)(2,1)S(1)}, bf16[3,192,256]{2,1,0:T(8,128)(2,1)S(1)}, u32[]{:S(2)}, u32[]{:S(2)}) collective-permute-start(bf16[3,192,256]{2,1,0:T(8,128)(2,1)S(1)} %collective-permute-done.7.refs_4_), channel_id=1, source_target_pairs={{0,2},{2,4},{4,6},{6,7},{7,5},{5,3},{3,1},{1,0},{8,10},{10,12},{12... | collective-permute-start | bytes 884744 | tf_op jit(solution)/shard_map/ppermute | solution.py:258
  26.7 1.4 %fusion.6 = (s32[]{:T(128)}, s32[4]{0:T(128)S(1)}) fusion(s32[]{:T(128)S(6)} %axis_index.25, s32[32]{0:T(128)} %param.10, s32[]{:T(128)S(6)} %select_n.98), kind=kLoop, calls=%fused_computation.43 | loop fusion | flops 11 | bytes 44 | tf_op jit(solution)/shard_map/reduce_sum | solution.py:278
  28.1 4.9 %collective-permute-done.8.refs_5_ = bf16[3,192,256]{2,1,0:T(8,128)(2,1)S(1)} collective-permute-done((bf16[3,192,256]{2,1,0:T(8,128)(2,1)S(1)}, bf16[3,192,256]{2,1,0:T(8,128)(2,1)S(1)}, u32[]{:S(2)}, u32[]{:S(2)}) %collective-permute-start.8) | collective-permute-done | bytes 294944 | tf_op jit(solution)/shard_map/ppermute | solution.py:258
  33.0 2.0 %collective-permute-start.13 = (bf16[3,192,256]{2,1,0:T(8,128)(2,1)S(1)}, bf16[3,192,256]{2,1,0:T(8,128)(2,1)S(1)}, u32[]{:S(2)}, u32[]{:S(2)}) collective-permute-start(bf16[3,192,256]{2,1,0:T(8,128)(2,1)S(1)} %collective-permute-done.9.refs_6_), channel_id=1, source_target_pairs={{0,2},{2,4},{4,6},{6,7},{7,5},{5,3},{3,1},{1,0},{8,10},{10,12},{12... | collective-permute-start | bytes 884744 | tf_op jit(solution)/shard_map/ppermute | solution.py:258
  36.4 3.7 %copy-done = bf16[6,512,1536]{2,1,0:T(8,128)(2,1)S(1)} copy-done((bf16[6,512,1536]{2,1,0:T(8,128)(2,1)S(1)}, bf16[6,512,1536]{2,1,0:T(8,128)(2,1)}, u32[]{:S(2)}) %copy-start) | copy-done | bytes 9437208
  42.0 2.3 %multiply.5.refs_3_ = f32[512,256]{1,0:T(8,128)S(1)} custom-call(s32[18]{0:T(128)S(1)} %compare_select_fusion.9.table_ref, bf16[6,512,1536]{2,1,0:T(8,128)(2,1)S(1)} %copy-done, bf16[6,512,1536]{2,1,0:T(8,128)(2,1)S(1)} %copy-done, bf16[6,512,1536]{2,1,0:T(8,128)(2,1)S(1)} %copy-done, f32[128,256]{1,0:T(8,128)S(1)} %bitcast.25, ...), custom_call_target="tpu_custom_call" | custom-call | flops 603979776 | bytes 3538944 | tf_op jit(solution)/shard_map/multiply/pallas_call | solution.py:151
  44.3 1.6 %collective-permute-start.15 = (bf16[3,192,256]{2,1,0:T(8,128)(2,1)S(1)}, bf16[3,192,256]{2,1,0:T(8,128)(2,1)S(1)}, u32[]{:S(2)}, u32[]{:S(2)}) collective-permute-start(bf16[3,192,256]{2,1,0:T(8,128)(2,1)S(1)} %collective-permute-done.11.refs_4_), channel_id=1, source_target_pairs={{0,2},{2,4},{4,6},{6,7},{7,5},{5,3},{3,1},{1,0},{8,10},{10,12},{12... | collective-permute-start | bytes 884744 | tf_op jit(solution)/shard_map/ppermute | solution.py:258
  46.4 4.0 %multiply.6.refs_3_ = f32[512,256]{1,0:T(8,128)S(1)} custom-call(s32[18]{0:T(128)S(1)} %compare_select_fusion.9.table_ref, bf16[6,512,1536]{2,1,0:T(8,128)(2,1)S(1)} %copy-done, bf16[6,512,1536]{2,1,0:T(8,128)(2,1)S(1)} %copy-done, bf16[6,512,1536]{2,1,0:T(8,128)(2,1)S(1)} %copy-done, f32[512,256]{1,0:T(8,128)S(1)} %multiply.5.refs_3_, ...), custom_call_target="tpu_custom_call" | custom-call | flops 1207959552 | bytes 7077888 | tf_op jit(solution)/shard_map/multiply/pallas_call | solution.py:151
  50.4 4.0 %multiply.7.refs_3_ = f32[512,256]{1,0:T(8,128)S(1)} custom-call(s32[18]{0:T(128)S(1)} %compare_select_fusion.9.table_ref, bf16[6,512,1536]{2,1,0:T(8,128)(2,1)S(1)} %copy-done, bf16[6,512,1536]{2,1,0:T(8,128)(2,1)S(1)} %copy-done, bf16[6,512,1536]{2,1,0:T(8,128)(2,1)S(1)} %copy-done, f32[512,256]{1,0:T(8,128)S(1)} %multiply.6.refs_3_, ...), custom_call_target="tpu_custom_call" | custom-call | flops 1207959552 | bytes 7077888 | tf_op jit(solution)/shard_map/multiply/pallas_call | solution.py:151
  54.5 4.0 %multiply.8.refs_3_ = f32[512,256]{1,0:T(8,128)S(1)} custom-call(s32[18]{0:T(128)S(1)} %compare_select_fusion.9.table_ref, bf16[6,512,1536]{2,1,0:T(8,128)(2,1)S(1)} %copy-done, bf16[6,512,1536]{2,1,0:T(8,128)(2,1)S(1)} %copy-done, bf16[6,512,1536]{2,1,0:T(8,128)(2,1)S(1)} %copy-done, f32[512,256]{1,0:T(8,128)S(1)} %multiply.7.refs_3_, ...), custom_call_target="tpu_custom_call" | custom-call | flops 1207959552 | bytes 7077888 | tf_op jit(solution)/shard_map/multiply/pallas_call | solution.py:151
  58.6 2.5 %multiply.9 = (f32[2,64,512]{2,1,0:T(8,128)S(1)}, f32[2,64,512]{2,1,0:T(8,128)S(1)}) custom-call(s32[18]{0:T(128)S(1)} %compare_select_fusion.9.table_ref, bf16[6,512,1536]{2,1,0:T(8,128)(2,1)S(1)} %copy-done, bf16[6,512,1536]{2,1,0:T(8,128)(2,1)S(1)} %copy-done, bf16[6,512,1536]{2,1,0:T(8,128)(2,1)S(1)} %copy-done, f32[512,256]{1,0:T(8,128)S(1)} %multiply.8.refs_3_, ...), custom_call_target="tpu_custom_call" | custom-call | flops 603979776 | bytes 3538944 | tf_op jit(solution)/shard_map/multiply/pallas_call | solution.py:151
  61.2 1.5 %collective-permute-done.17 = f32[2,64,512]{2,1,0:T(8,128)S(1)} collective-permute-done((f32[2,64,512]{2,1,0:T(8,128)S(1)}, f32[2,64,512]{2,1,0:T(8,128)S(1)}, u32[]{:S(2)}, u32[]{:S(2)}) %collective-permute-start.17) | collective-permute-done | bytes 262176 | tf_op jit(solution)/shard_map/ppermute | solution.py:252
  62.7 1.6 %collective-permute-start.18 = (f32[64,512]{1,0:T(8,128)S(1)}, f32[64,512]{1,0:T(8,128)S(1)}, u32[]{:S(2)}, u32[]{:S(2)}) collective-permute-start(f32[64,512]{1,0:T(8,128)S(1)} %fusion), channel_id=1, source_target_pairs={{0,16},{8,24},{16,0},{24,8},{1,17},{9,25},{17,1},{25,9},{2,18},{10... | collective-permute-start | bytes 393224 | tf_op jit(solution)/shard_map/ppermute | solution.py:252
  65.7 1.3 %collective-permute-start.2 = (bf16[128,1536]{1,0:T(8,128)(2,1)S(1)}, bf16[128,1536]{1,0:T(8,128)(2,1)S(1)}, u32[]{:S(2)}, u32[]{:S(2)}) collective-permute-start(bf16[128,1536]{1,0:T(8,128)(2,1)S(1)} %dense_tiles.1.refs_0_), channel_id=1, source_target_pairs={{0,24},{8,16},{16,8},{24,0},{1,25},{9,17},{17,9},{25,1},{2,26},{10... | collective-permute-start | bytes 1179656 | tf_op jit(solution)/shard_map/ppermute | solution.py:252
  67.0 1.4 %collective-permute-done.18 = f32[64,512]{1,0:T(8,128)S(1)} collective-permute-done((f32[64,512]{1,0:T(8,128)S(1)}, f32[64,512]{1,0:T(8,128)S(1)}, u32[]{:S(2)}, u32[]{:S(2)}) %collective-permute-start.18) | collective-permute-done | bytes 131104 | tf_op jit(solution)/shard_map/ppermute | solution.py:252
  68.7 4.5 %collective-permute-start.20 = (bf16[64,512]{1,0:T(8,128)(2,1)S(1)}, bf16[64,512]{1,0:T(8,128)(2,1)S(1)}, u32[]{:S(2)}, u32[]{:S(2)}) collective-permute-start(bf16[64,512]{1,0:T(8,128)(2,1)S(1)} %get-tuple-element.23.rounded_ref), channel_id=1, source_target_pairs={{1,0},{2,1},{3,2},{4,3},{5,4},{6,5},{7,6},{0,7},{9,8},{10,9},{11,1... | collective-permute-start | bytes 196616 | tf_op jit(solution)/shard_map/ppermute | solution.py:316
  73.4 3.8 %collective-permute-done.1.refs_2_ = bf16[128,1536]{1,0:T(8,128)(2,1)S(1)} collective-permute-done((bf16[128,1536]{1,0:T(8,128)(2,1)S(1)}, bf16[128,1536]{1,0:T(8,128)(2,1)S(1)}, u32[]{:S(2)}, u32[]{:S(2)}) %collective-permute-start.1) | collective-permute-done | bytes 393248 | tf_op jit(solution)/shard_map/ppermute | solution.py:252
  77.2 7.5 %collective-permute-done.2.refs_3_ = bf16[128,1536]{1,0:T(8,128)(2,1)S(1)} collective-permute-done((bf16[128,1536]{1,0:T(8,128)(2,1)S(1)}, bf16[128,1536]{1,0:T(8,128)(2,1)S(1)}, u32[]{:S(2)}, u32[]{:S(2)}) %collective-permute-start.2) | collective-permute-done | bytes 393248 | tf_op jit(solution)/shard_map/ppermute | solution.py:252
  86.9 4.4 %collective-permute-start.22 = (bf16[64,512]{1,0:T(8,128)(2,1)S(1)}, bf16[64,512]{1,0:T(8,128)(2,1)S(1)}, u32[]{:S(2)}, u32[]{:S(2)}) collective-permute-start(bf16[64,512]{1,0:T(8,128)(2,1)S(1)} %get-tuple-element.16.rounded_ref), channel_id=1, source_target_pairs={{1,0},{2,1},{3,2},{4,3},{5,4},{6,5},{7,6},{0,7},{9,8},{10,9},{11,1... | collective-permute-start | bytes 196616 | tf_op jit(solution)/shard_map/ppermute | solution.py:316
  91.3 2.3 %collective-permute-done.21.left_ref = bf16[64,512]{1,0:T(8,128)(2,1)S(1)} collective-permute-done((bf16[64,512]{1,0:T(8,128)(2,1)S(1)}, bf16[64,512]{1,0:T(8,128)(2,1)S(1)}, u32[]{:S(2)}, u32[]{:S(2)}) %collective-permute-start.21) | collective-permute-done | bytes 65568 | tf_op jit(solution)/shard_map/ppermute | solution.py:315
  96.0 3.5 %collective-permute-start.24 = (bf16[64,512]{1,0:T(8,128)(2,1)S(1)}, bf16[64,512]{1,0:T(8,128)(2,1)S(1)}, u32[]{:S(2)}, u32[]{:S(2)}) collective-permute-start(bf16[64,512]{1,0:T(8,128)(2,1)S(1)} %get-tuple-element.18.rounded_ref), channel_id=1, source_target_pairs={{1,0},{2,1},{3,2},{4,3},{5,4},{6,5},{7,6},{0,7},{9,8},{10,9},{11,1... | collective-permute-start | bytes 196616 | tf_op jit(solution)/shard_map/ppermute | solution.py:316
  99.5 2.2 %collective-permute-done.23.left_ref = bf16[64,512]{1,0:T(8,128)(2,1)S(1)} collective-permute-done((bf16[64,512]{1,0:T(8,128)(2,1)S(1)}, bf16[64,512]{1,0:T(8,128)(2,1)S(1)}, u32[]{:S(2)}, u32[]{:S(2)}) %collective-permute-start.23) | collective-permute-done | bytes 65568 | tf_op jit(solution)/shard_map/ppermute | solution.py:315
  102.9 1.6 %collective-permute-start.26 = (f32[2,64,128]{2,1,0:T(8,128)S(1)}, f32[2,64,128]{2,1,0:T(8,128)S(1)}, u32[]{:S(2)}, u32[]{:S(2)}) collective-permute-start(f32[2,64,128]{2,1,0:T(8,128)S(1)} %get-tuple-element.20), channel_id=1, source_target_pairs={{0,16},{8,24},{16,0},{24,8},{1,17},{9,25},{17,1},{25,9},{2,18},{10... | collective-permute-start | bytes 196616 | tf_op jit(solution)/shard_map/ppermute | solution.py:252
  104.5 2.7 %collective-permute-done.26 = f32[2,64,128]{2,1,0:T(8,128)S(1)} collective-permute-done((f32[2,64,128]{2,1,0:T(8,128)S(1)}, f32[2,64,128]{2,1,0:T(8,128)S(1)}, u32[]{:S(2)}, u32[]{:S(2)}) %collective-permute-start.26) | collective-permute-done | bytes 65568 | tf_op jit(solution)/shard_map/ppermute | solution.py:252
  108.4 1.3 %assemble.1 = f32[1,128,256]{2,1,0:T(8,128)} custom-call(s32[18]{0:T(128)S(1)} %compare_select_fusion.9.table_ref, f32[1,64,128]{2,1,0:T(8,128)S(1)} %get-tuple-element.32.refs_0_, f32[1,64,128]{2,1,0:T(8,128)S(1)} %collective-permute-done.25.refs_1_, f32[1,64,128]{2,1,0:T(8,128)S(1)} %get-tuple-element.30.refs_2_, ...), custom_call_target="tpu_custom_call" | custom-call | bytes 262144 | tf_op jit(solution)/shard_map/assemble/pallas_call | solution.py:231
  (57 shorter events, 13.3 us)
Async XLA Ops:
  1.1 10.9 %collective-permute-start.3 = (bf16[3,192,256]{2,1,0:T(8,128)(2,1)S(1)}, bf16[3,192,256]{2,1,0:T(8,128)(2,1)S(1)}, u32[]{:S(2)}, u32[]{:S(2)}) collective-permute-start(bf16[3,192,256]{2,1,0:T(8,128)(2,1)S(1)} %get-tuple-element.28), channel_id=1, source_target_pairs={{0,2},{2,4},{4,6},{6,7},{7,5},{5,3},{3,1},{1,0},{8,10},{10,12},{12... | collective-permute-start | bytes 884744 | tf_op jit(solution)/shard_map/ppermute | solution.py:258
  4.2 9.9 %collective-permute-start.6 = (bf16[3,192,256]{2,1,0:T(8,128)(2,1)S(1)}, bf16[3,192,256]{2,1,0:T(8,128)(2,1)S(1)}, u32[]{:S(2)}, u32[]{:S(2)}) collective-permute-start(bf16[3,192,256]{2,1,0:T(8,128)(2,1)S(1)} %get-tuple-element.27), channel_id=1, source_target_pairs={{0,1},{2,0},{4,2},{6,4},{7,6},{5,7},{3,5},{1,3},{8,9},{10,8},{12,1... | collective-permute-start | bytes 884744 | tf_op jit(solution)/shard_map/ppermute | solution.py:258
  4.2 16.2 %collective-permute-start.4 = (bf16[3,192,256]{2,1,0:T(8,128)(2,1)S(1)}, bf16[3,192,256]{2,1,0:T(8,128)(2,1)S(1)}, u32[]{:S(2)}, u32[]{:S(2)}) collective-permute-start(bf16[3,192,256]{2,1,0:T(8,128)(2,1)S(1)} %get-tuple-element.28), channel_id=1, source_target_pairs={{0,1},{2,0},{4,2},{6,4},{7,6},{5,7},{3,5},{1,3},{8,9},{10,8},{12,1... | collective-permute-start | bytes 884744 | tf_op jit(solution)/shard_map/ppermute | solution.py:258
  6.1 14.3 %collective-permute-start.5 = (bf16[3,192,256]{2,1,0:T(8,128)(2,1)S(1)}, bf16[3,192,256]{2,1,0:T(8,128)(2,1)S(1)}, u32[]{:S(2)}, u32[]{:S(2)}) collective-permute-start(bf16[3,192,256]{2,1,0:T(8,128)(2,1)S(1)} %get-tuple-element.27), channel_id=1, source_target_pairs={{0,2},{2,4},{4,6},{6,7},{7,5},{5,3},{3,1},{1,0},{8,10},{10,12},{12... | collective-permute-start | bytes 884744 | tf_op jit(solution)/shard_map/ppermute | solution.py:258
  12.0 12.6 %collective-permute-start.7 = (bf16[3,192,256]{2,1,0:T(8,128)(2,1)S(1)}, bf16[3,192,256]{2,1,0:T(8,128)(2,1)S(1)}, u32[]{:S(2)}, u32[]{:S(2)}) collective-permute-start(bf16[3,192,256]{2,1,0:T(8,128)(2,1)S(1)} %collective-permute-done.3.refs_4_), channel_id=1, source_target_pairs={{0,2},{2,4},{4,6},{6,7},{7,5},{5,3},{3,1},{1,0},{8,10},{10,12},{12... | collective-permute-start | bytes 884744 | tf_op jit(solution)/shard_map/ppermute | solution.py:258
  14.1 12.6 %collective-permute-start.10 = (bf16[3,192,256]{2,1,0:T(8,128)(2,1)S(1)}, bf16[3,192,256]{2,1,0:T(8,128)(2,1)S(1)}, u32[]{:S(2)}, u32[]{:S(2)}) collective-permute-start(bf16[3,192,256]{2,1,0:T(8,128)(2,1)S(1)} %collective-permute-done.6.refs_7_), channel_id=1, source_target_pairs={{0,1},{2,0},{4,2},{6,4},{7,6},{5,7},{3,5},{1,3},{8,9},{10,8},{12,1... | collective-permute-start | bytes 884744 | tf_op jit(solution)/shard_map/ppermute | solution.py:258
  20.4 12.6 %collective-permute-start.8 = (bf16[3,192,256]{2,1,0:T(8,128)(2,1)S(1)}, bf16[3,192,256]{2,1,0:T(8,128)(2,1)S(1)}, u32[]{:S(2)}, u32[]{:S(2)}) collective-permute-start(bf16[3,192,256]{2,1,0:T(8,128)(2,1)S(1)} %collective-permute-done.4.refs_5_), channel_id=1, source_target_pairs={{0,1},{2,0},{4,2},{6,4},{7,6},{5,7},{3,5},{1,3},{8,9},{10,8},{12,1... | collective-permute-start | bytes 884744 | tf_op jit(solution)/shard_map/ppermute | solution.py:258
  20.4 12.6 %collective-permute-start.9 = (bf16[3,192,256]{2,1,0:T(8,128)(2,1)S(1)}, bf16[3,192,256]{2,1,0:T(8,128)(2,1)S(1)}, u32[]{:S(2)}, u32[]{:S(2)}) collective-permute-start(bf16[3,192,256]{2,1,0:T(8,128)(2,1)S(1)} %collective-permute-done.5.refs_6_), channel_id=1, source_target_pairs={{0,2},{2,4},{4,6},{6,7},{7,5},{5,3},{3,1},{1,0},{8,10},{10,12},{12... | collective-permute-start | bytes 884744 | tf_op jit(solution)/shard_map/ppermute | solution.py:258
  24.6 19.7 %collective-permute-start.11 = (bf16[3,192,256]{2,1,0:T(8,128)(2,1)S(1)}, bf16[3,192,256]{2,1,0:T(8,128)(2,1)S(1)}, u32[]{:S(2)}, u32[]{:S(2)}) collective-permute-start(bf16[3,192,256]{2,1,0:T(8,128)(2,1)S(1)} %collective-permute-done.7.refs_4_), channel_id=1, source_target_pairs={{0,2},{2,4},{4,6},{6,7},{7,5},{5,3},{3,1},{1,0},{8,10},{10,12},{12... | collective-permute-start | bytes 884744 | tf_op jit(solution)/shard_map/ppermute | solution.py:258
  26.7 19.2 %collective-permute-start.14 = (bf16[3,192,256]{2,1,0:T(8,128)(2,1)S(1)}, bf16[3,192,256]{2,1,0:T(8,128)(2,1)S(1)}, u32[]{:S(2)}, u32[]{:S(2)}) collective-permute-start(bf16[3,192,256]{2,1,0:T(8,128)(2,1)S(1)} %collective-permute-done.10.refs_7_), channel_id=1, source_target_pairs={{0,1},{2,0},{4,2},{6,4},{7,6},{5,7},{3,5},{1,3},{8,9},{10,8},{12,1... | collective-permute-start | bytes 884744 | tf_op jit(solution)/shard_map/ppermute | solution.py:258
  33.0 21.5 %collective-permute-start.12 = (bf16[3,192,256]{2,1,0:T(8,128)(2,1)S(1)}, bf16[3,192,256]{2,1,0:T(8,128)(2,1)S(1)}, u32[]{:S(2)}, u32[]{:S(2)}) collective-permute-start(bf16[3,192,256]{2,1,0:T(8,128)(2,1)S(1)} %collective-permute-done.8.refs_5_), channel_id=1, source_target_pairs={{0,1},{2,0},{4,2},{6,4},{7,6},{5,7},{3,5},{1,3},{8,9},{10,8},{12,1... | collective-permute-start | bytes 884744 | tf_op jit(solution)/shard_map/ppermute | solution.py:258
  33.0 21.5 %collective-permute-start.13 = (bf16[3,192,256]{2,1,0:T(8,128)(2,1)S(1)}, bf16[3,192,256]{2,1,0:T(8,128)(2,1)S(1)}, u32[]{:S(2)}, u32[]{:S(2)}) collective-permute-start(bf16[3,192,256]{2,1,0:T(8,128)(2,1)S(1)} %collective-permute-done.9.refs_6_), channel_id=1, source_target_pairs={{0,2},{2,4},{4,6},{6,7},{7,5},{5,3},{3,1},{1,0},{8,10},{10,12},{12... | collective-permute-start | bytes 884744 | tf_op jit(solution)/shard_map/ppermute | solution.py:258
  36.4 3.7 %copy-start = (bf16[6,512,1536]{2,1,0:T(8,128)(2,1)S(1)}, bf16[6,512,1536]{2,1,0:T(8,128)(2,1)}, u32[]{:S(2)}) copy-start(bf16[6,512,1536]{2,1,0:T(8,128)(2,1)} %refs_2_.9) | copy-start | bytes 28311556
  40.1 1.1 copy-start.1
  44.3 14.3 %collective-permute-start.15 = (bf16[3,192,256]{2,1,0:T(8,128)(2,1)S(1)}, bf16[3,192,256]{2,1,0:T(8,128)(2,1)S(1)}, u32[]{:S(2)}, u32[]{:S(2)}) collective-permute-start(bf16[3,192,256]{2,1,0:T(8,128)(2,1)S(1)} %collective-permute-done.11.refs_4_), channel_id=1, source_target_pairs={{0,2},{2,4},{4,6},{6,7},{7,5},{5,3},{3,1},{1,0},{8,10},{10,12},{12... | collective-permute-start | bytes 884744 | tf_op jit(solution)/shard_map/ppermute | solution.py:258
  46.0 12.7 %collective-permute-start.16 = (bf16[3,192,256]{2,1,0:T(8,128)(2,1)S(1)}, bf16[3,192,256]{2,1,0:T(8,128)(2,1)S(1)}, u32[]{:S(2)}, u32[]{:S(2)}) collective-permute-start(bf16[3,192,256]{2,1,0:T(8,128)(2,1)S(1)} %collective-permute-done.14.refs_7_), channel_id=1, source_target_pairs={{0,1},{2,0},{4,2},{6,4},{7,6},{5,7},{3,5},{1,3},{8,9},{10,8},{12,1... | collective-permute-start | bytes 884744 | tf_op jit(solution)/shard_map/ppermute | solution.py:258
  58.6 2.6 %copy-start.4 = (s32[12,2]{0,1:T(2,128)S(1)}, s32[12,2]{0,1:T(2,128)}, u32[]{:S(2)}) copy-start(s32[12,2]{0,1:T(2,128)} %param.11) | copy-start | bytes 292
  58.6 5.8 %copy-start.2 = (bf16[12,128,128]{2,1,0:T(8,128)(2,1)S(1)}, bf16[12,128,128]{2,1,0:T(8,128)(2,1)}, u32[]{:S(2)}) copy-start(bf16[12,128,128]{2,1,0:T(8,128)(2,1)} %tile_ref.1) | copy-start | bytes 1179652
  61.1 1.6 %collective-permute-start.17 = (f32[2,64,512]{2,1,0:T(8,128)S(1)}, f32[2,64,512]{2,1,0:T(8,128)S(1)}, u32[]{:S(2)}, u32[]{:S(2)}) collective-permute-start(f32[2,64,512]{2,1,0:T(8,128)S(1)} %get-tuple-element.14), channel_id=1, source_target_pairs={{0,8},{8,0},{16,24},{24,16},{1,9},{9,1},{17,25},{25,17},{2,10},{10... | collective-permute-start | bytes 786440 | tf_op jit(solution)/shard_map/ppermute | solution.py:252
  62.7 5.7 %collective-permute-start.18 = (f32[64,512]{1,0:T(8,128)S(1)}, f32[64,512]{1,0:T(8,128)S(1)}, u32[]{:S(2)}, u32[]{:S(2)}) collective-permute-start(f32[64,512]{1,0:T(8,128)S(1)} %fusion), channel_id=1, source_target_pairs={{0,16},{8,24},{16,0},{24,8},{1,17},{9,25},{17,1},{25,9},{2,18},{10... | collective-permute-start | bytes 393224 | tf_op jit(solution)/shard_map/ppermute | solution.py:252
  65.1 8.3 %collective-permute-start = (bf16[128,1536]{1,0:T(8,128)(2,1)S(1)}, bf16[128,1536]{1,0:T(8,128)(2,1)S(1)}, u32[]{:S(2)}, u32[]{:S(2)}) collective-permute-start(bf16[128,1536]{1,0:T(8,128)(2,1)S(1)} %dense_tiles.1.refs_0_), channel_id=1, source_target_pairs={{0,8},{8,0},{16,24},{24,16},{1,9},{9,1},{17,25},{25,17},{2,10},{10... | collective-permute-start | bytes 1179656 | tf_op jit(solution)/shard_map/ppermute | solution.py:252
  65.2 12.1 %collective-permute-start.1 = (bf16[128,1536]{1,0:T(8,128)(2,1)S(1)}, bf16[128,1536]{1,0:T(8,128)(2,1)S(1)}, u32[]{:S(2)}, u32[]{:S(2)}) collective-permute-start(bf16[128,1536]{1,0:T(8,128)(2,1)S(1)} %dense_tiles.1.refs_0_), channel_id=1, source_target_pairs={{0,16},{8,24},{16,0},{24,8},{1,17},{9,25},{17,1},{25,9},{2,18},{10... | collective-permute-start | bytes 1179656 | tf_op jit(solution)/shard_map/ppermute | solution.py:252
  65.7 19.0 %collective-permute-start.2 = (bf16[128,1536]{1,0:T(8,128)(2,1)S(1)}, bf16[128,1536]{1,0:T(8,128)(2,1)S(1)}, u32[]{:S(2)}, u32[]{:S(2)}) collective-permute-start(bf16[128,1536]{1,0:T(8,128)(2,1)S(1)} %dense_tiles.1.refs_0_), channel_id=1, source_target_pairs={{0,24},{8,16},{16,8},{24,0},{1,25},{9,17},{17,9},{25,1},{2,26},{10... | collective-permute-start | bytes 1179656 | tf_op jit(solution)/shard_map/ppermute | solution.py:252
  68.4 16.9 %collective-permute-start.19 = (bf16[64,512]{1,0:T(8,128)(2,1)S(1)}, bf16[64,512]{1,0:T(8,128)(2,1)S(1)}, u32[]{:S(2)}, u32[]{:S(2)}) collective-permute-start(bf16[64,512]{1,0:T(8,128)(2,1)S(1)} %get-tuple-element.23.rounded_ref), channel_id=1, source_target_pairs={{0,1},{1,2},{2,3},{3,4},{4,5},{5,6},{6,7},{7,0},{8,9},{9,10},{10,1... | collective-permute-start | bytes 196616 | tf_op jit(solution)/shard_map/ppermute | solution.py:315
  68.7 16.6 %collective-permute-start.20 = (bf16[64,512]{1,0:T(8,128)(2,1)S(1)}, bf16[64,512]{1,0:T(8,128)(2,1)S(1)}, u32[]{:S(2)}, u32[]{:S(2)}) collective-permute-start(bf16[64,512]{1,0:T(8,128)(2,1)S(1)} %get-tuple-element.23.rounded_ref), channel_id=1, source_target_pairs={{1,0},{2,1},{3,2},{4,3},{5,4},{6,5},{7,6},{0,7},{9,8},{10,9},{11,1... | collective-permute-start | bytes 196616 | tf_op jit(solution)/shard_map/ppermute | solution.py:316
  86.5 7.0 %collective-permute-start.21 = (bf16[64,512]{1,0:T(8,128)(2,1)S(1)}, bf16[64,512]{1,0:T(8,128)(2,1)S(1)}, u32[]{:S(2)}, u32[]{:S(2)}) collective-permute-start(bf16[64,512]{1,0:T(8,128)(2,1)S(1)} %get-tuple-element.16.rounded_ref), channel_id=1, source_target_pairs={{0,1},{1,2},{2,3},{3,4},{4,5},{5,6},{6,7},{7,0},{8,9},{9,10},{10,1... | collective-permute-start | bytes 196616 | tf_op jit(solution)/shard_map/ppermute | solution.py:315
  86.9 6.7 %collective-permute-start.22 = (bf16[64,512]{1,0:T(8,128)(2,1)S(1)}, bf16[64,512]{1,0:T(8,128)(2,1)S(1)}, u32[]{:S(2)}, u32[]{:S(2)}) collective-permute-start(bf16[64,512]{1,0:T(8,128)(2,1)S(1)} %get-tuple-element.16.rounded_ref), channel_id=1, source_target_pairs={{1,0},{2,1},{3,2},{4,3},{5,4},{6,5},{7,6},{0,7},{9,8},{10,9},{11,1... | collective-permute-start | bytes 196616 | tf_op jit(solution)/shard_map/ppermute | solution.py:316
  94.7 7.0 %collective-permute-start.23 = (bf16[64,512]{1,0:T(8,128)(2,1)S(1)}, bf16[64,512]{1,0:T(8,128)(2,1)S(1)}, u32[]{:S(2)}, u32[]{:S(2)}) collective-permute-start(bf16[64,512]{1,0:T(8,128)(2,1)S(1)} %get-tuple-element.18.rounded_ref), channel_id=1, source_target_pairs={{0,1},{1,2},{2,3},{3,4},{4,5},{5,6},{6,7},{7,0},{8,9},{9,10},{10,1... | collective-permute-start | bytes 196616 | tf_op jit(solution)/shard_map/ppermute | solution.py:315
  96.0 5.7 %collective-permute-start.24 = (bf16[64,512]{1,0:T(8,128)(2,1)S(1)}, bf16[64,512]{1,0:T(8,128)(2,1)S(1)}, u32[]{:S(2)}, u32[]{:S(2)}) collective-permute-start(bf16[64,512]{1,0:T(8,128)(2,1)S(1)} %get-tuple-element.18.rounded_ref), channel_id=1, source_target_pairs={{1,0},{2,1},{3,2},{4,3},{5,4},{6,5},{7,6},{0,7},{9,8},{10,9},{11,1... | collective-permute-start | bytes 196616 | tf_op jit(solution)/shard_map/ppermute | solution.py:316
  102.9 4.3 %collective-permute-start.26 = (f32[2,64,128]{2,1,0:T(8,128)S(1)}, f32[2,64,128]{2,1,0:T(8,128)S(1)}, u32[]{:S(2)}, u32[]{:S(2)}) collective-permute-start(f32[2,64,128]{2,1,0:T(8,128)S(1)} %get-tuple-element.20), channel_id=1, source_target_pairs={{0,16},{8,24},{16,0},{24,8},{1,17},{9,25},{17,1},{25,9},{2,18},{10... | collective-permute-start | bytes 196616 | tf_op jit(solution)/shard_map/ppermute | solution.py:252
  104.5 2.8 %collective-permute-start.25 = (f32[1,64,128]{2,1,0:T(8,128)S(1)}, f32[1,64,128]{2,1,0:T(8,128)S(1)}, u32[]{:S(2)}, u32[]{:S(2)}) collective-permute-start(f32[1,64,128]{2,1,0:T(8,128)S(1)} %get-tuple-element.31), channel_id=1, source_target_pairs={{0,8},{8,0},{16,24},{24,16},{1,9},{9,1},{17,25},{25,17},{2,10},{10... | collective-permute-start | bytes 98312 | tf_op jit(solution)/shard_map/ppermute | solution.py:252
  107.2 1.2 %collective-permute-start.27 = (f32[1,64,128]{2,1,0:T(8,128)S(1)}, f32[1,64,128]{2,1,0:T(8,128)S(1)}, u32[]{:S(2)}, u32[]{:S(2)}) collective-permute-start(f32[1,64,128]{2,1,0:T(8,128)S(1)} %get-tuple-element.29), channel_id=1, source_target_pairs={{0,8},{8,0},{16,24},{24,16},{1,9},{9,1},{17,25},{25,17},{2,10},{10... | collective-permute-start | bytes 98312 | tf_op jit(solution)/shard_map/ppermute | solution.py:252
  (1 other events, 0.9 us)

commit v3 on v0

v3 whole, which is shorter than its diff:
```python
import jax
import jax.numpy as jnp
from jax import lax
from jax.experimental import pallas as pl
from jax.experimental.pallas import tpu as pltpu
from jax.sharding import PartitionSpec as P


SWEEPS = 3
PARTS = 2
LANES = 128


damping = 0.7


def cost(flops, moved):
    return pl.CostEstimate(flops=flops, bytes_accessed=moved, transcendentals=0)


def params(limit):
    return pltpu.CompilerParams(vmem_limit_bytes=limit * 2**20)


VMEM = pl.BlockSpec(memory_space=pltpu.VMEM)
SMEM = pl.BlockSpec(memory_space=pltpu.SMEM)


def mate(p, side, count):
    return p ^ 1 if side == 1 else (p + (1 if p % 2 else -1)) % count


def early_side(step, part, final):
    return 1 if (final - step + part) % 2 == 0 else 2


def prepare(owner, pairs, counts, tile_values):
    rows = lax.axis_size("row")
    cols = lax.axis_size("col")
    tiles, height, deep = tile_values.shape
    slots = 3 * rows

    def body(owner_ref, pairs_ref, counts_ref, tile_ref, chosen_ref, out_ref, pick, live):
        row, col = lax.axis_index("row"), lax.axis_index("col")
        for i in range(rows):
            chosen_ref[owner_ref[col * rows + i] ^ row] = i
        for q in range(slots):
            pick[q] = 0
            live[q] = 0
        ahead = jnp.where(lax.rem(col, 2) == 0, 1, cols - 1)
        for t in range(tiles):

            @pl.when(t < counts_ref[0])
            def _(t=t):
                source = pairs_ref[1, t]
                apart = lax.rem(source // rows - col + cols, cols)
                block = jnp.where(apart == 0, 1, jnp.where(apart == ahead, 2, 0))
                slot = block * rows + lax.rem(source, rows)
                pick[slot] = t
                live[slot] = 1

        for q in range(slots):
            tile = tile_ref[pick[q]]
            out_ref[:, q * deep : (q + 1) * deep] = jnp.where(live[q] > 0, tile, jnp.zeros_like(tile))

    return pl.pallas_call(
        body,
        out_shape=[
            jax.ShapeDtypeStruct((rows,), jnp.int32),
            jax.ShapeDtypeStruct((height, slots * deep), tile_values.dtype),
        ],
        in_specs=[SMEM] * 3 + [VMEM],
        out_specs=[SMEM, VMEM],
        scratch_shapes=[pltpu.SMEM((slots,), jnp.int32), pltpu.SMEM((slots,), jnp.int32)],
        compiler_params=params(4),
        cost_estimate=cost(0, 4 * slots * height * deep),
        name="prepare",
    )(owner, pairs, counts, tile_values)


def stack_rows(chosen, parts):
    count = len(parts)
    rows, width = parts[0].shape

    def body(chosen_ref, *refs):
        for m in range(count):
            at = pl.multiple_of(chosen_ref[m] * rows, rows)
            refs[-1][pl.ds(at, rows), :] = refs[m][...]

    return pl.pallas_call(
        body,
        out_shape=jax.ShapeDtypeStruct((count * rows, width), parts[0].dtype),
        in_specs=[SMEM] + [VMEM] * count,
        out_specs=VMEM,
        compiler_params=params(4 if rows * count <= 512 else 24),
        cost_estimate=cost(0, 4 * count * rows * width),
        name="stack_rows",
    )(chosen, *parts)


def multiply(kernels, blocks, seed, incident, chosen, spread):
    rows = kernels.shape[1]
    cols = lax.axis_size("col")
    count = len(blocks)
    lags, depth, columns = blocks[0][3].shape
    tall = -(-(depth + LANES - 1) // LANES) * LANES
    extra = ([] if seed is None else [seed]) + ([] if incident is None else [incident, chosen])

    def body(kernel_ref, *refs):
        given, refs = refs[:count], refs[count:]
        seed_ref, refs = (None, refs) if seed is None else (refs[0], refs[1:])
        if incident is not None:
            (incident_ref, chosen_ref), refs = refs[:2], refs[2:]
        if spread:
            keep, give, (padded, total, turned) = refs[0], refs[1:-3], refs[-3:]
        else:
            total, padded = refs
        row, col = lax.axis_index("row"), lax.axis_index("col")
        stop = jnp.where(lax.rem(col, 2) == 0, col // 2, cols - 1 - col // 2)
        sign = jnp.where(lax.rem(stop, 2) == 1, 1, -1)
        padded[...] = jnp.zeros_like(padded)
        for s, (step, side, part, _) in enumerate(blocks):
            back = sign * (step if side == 1 else -step)
            at = lax.rem(stop - back + cols, cols)
            source = jnp.where(at < cols // 2, 2 * at, 2 * (cols - 1 - at) + 1)
            group = jnp.minimum(source * depth // LANES, (kernels.shape[2] - tall) // LANES)
            shift = source * depth - group * LANES
            for lag in range(lags):
                place = pl.multiple_of(lag * tall + shift, 32)
                padded[s, pl.ds(place, depth), :] = given[s][lag]
            lane = pl.multiple_of(group * LANES, LANES)
            left = jnp.concatenate([kernel_ref[part * lags + lag, :, pl.ds(lane, tall)] for lag in range(lags)], axis=1)
            product = jnp.dot(left, padded[s], preferred_element_type=jnp.float32)
            if s or seed is not None:
                product = (total if s else seed_ref)[...] + product
            total[...] = product
        if incident is not None:
            height = incident.shape[0]
            mine = pl.ds(pl.multiple_of(chosen_ref[0] * height, height), height)
            total[mine, :] = total[mine, :] - incident_ref[...]
        if spread:
            turned[...] = total[...].T
            width = columns // spread
            for m in range(spread):
                at = pl.multiple_of((row ^ m) * width, width)
                value = turned[pl.ds(at, width), :]
                if m % 2:
                    give[m // 2][...] = value
                else:
                    keep[m // 2] = value

    whole = (rows, columns)
    scratch = [pltpu.VMEM((count, lags * tall, columns), kernels.dtype)]
    if spread:
        piece = (columns // spread, rows)
        out_shape = [jax.ShapeDtypeStruct((spread // 2, *piece), jnp.float32)]
        out_shape += [jax.ShapeDtypeStruct(piece, jnp.float32)] * (spread // 2)
        scratch += [pltpu.VMEM(whole, jnp.float32), pltpu.VMEM(whole[::-1], jnp.float32)]
    else:
        out_shape = jax.ShapeDtypeStruct(whole, jnp.float32)
    in_specs = [VMEM] * (1 + count + len(extra))
    if incident is not None:
        in_specs[-1] = SMEM

    return pl.pallas_call(
        body,
        out_shape=out_shape,
        in_specs=in_specs,
        out_specs=[VMEM] * len(out_shape) if spread else VMEM,
        scratch_shapes=scratch,
        compiler_params=params(16 if rows <= 512 else 40),
        cost_estimate=cost(2 * count * lags * rows * tall * columns, 2 * count * lags * tall * (rows + columns)),
        name="multiply",
    )(kernels, *[block[3] for block in blocks], *extra)


def steady(dense, driven, density, rounded, near_side):
    width, rows = driven.shape

    def body(dense_ref, driven_ref, density_ref, rounded_ref, side_ref, out_ref):
        def term(ref, k):
            return lax.dot_general(
                ref[...],
                dense_ref[:, k * rows : (k + 1) * rows],
                (((1,), (1,)), ((), ())),
                preferred_element_type=jnp.float32,
            )

        near = term(rounded_ref, 1) + term(side_ref, 2)
        old = density_ref[...]
        out_ref[...] = old + damping * (driven_ref[...] - old - near)

    return pl.pallas_call(
        body,
        out_shape=jax.ShapeDtypeStruct((width, rows), jnp.float32),
        in_specs=[VMEM] * 5,
        out_specs=VMEM,
        compiler_params=params(8 if rows <= 512 else 24),
        cost_estimate=cost(4 * width * rows * rows, 4 * rows * rows + 16 * width * rows),
        name="steady",
    )(dense, driven, density, rounded, near_side)


def sweep(dense, base, far_side, chosen):
    width, rows = base.shape

    def update(dense_ref, base_ref, side_ref):
        near = lax.dot_general(
            side_ref[...], dense_ref[:, :rows], (((1,), (1,)), ((), ())), preferred_element_type=jnp.float32
        )
        return base_ref[...] - damping * near

    def body(dense_ref, base_ref, side_ref, density_ref, rounded_ref):
        new = update(dense_ref, base_ref, side_ref)
        density_ref[...] = new
        rounded_ref[...] = new.astype(rounded_ref.dtype)

    def body_last(chosen_ref, dense_ref, base_ref, side_ref, away, home, whole):
        whole[...] = update(dense_ref, base_ref, side_ref)
        for m in range(count):
            at = pl.multiple_of(chosen_ref[m] * height, height)
            (away if m >= count // 2 else home)[m % (count // 2)] = whole[:, pl.ds(at, height)]

    same = dict(
        out_specs=[VMEM] * 2,
        compiler_params=params(8 if rows <= 512 else 24),
        cost_estimate=cost(2 * width * rows * rows, 2 * rows * rows + 12 * width * rows),
    )
    if chosen is None:
        out_shape = [
            jax.ShapeDtypeStruct((width, rows), jnp.float32),
            jax.ShapeDtypeStruct((width, rows), far_side.dtype),
        ]
        return pl.pallas_call(body, out_shape=out_shape, in_specs=[VMEM] * 3, name="sweep", **same)(
            dense, base, far_side
        )
    count = chosen.shape[0]
    height = rows // count
    return pl.pallas_call(
        body_last,
        out_shape=[jax.ShapeDtypeStruct((count // 2, width, height), jnp.float32)] * 2,
        in_specs=[SMEM] + [VMEM] * 3,
        scratch_shapes=[pltpu.VMEM((width, rows), jnp.float32)],
        name="sweep_last",
        **same,
    )(chosen, dense, base, far_side)


def assemble(pieces):
    arrays = [piece for _, piece in pieces]
    width, height = arrays[0].shape[1:]
    columns = width * sum(piece.shape[0] for piece in arrays)

    def body(*refs):
        row = lax.axis_index("row")
        out_ref, turned = refs[-2:]
        for (offsets, _), ref in zip(pieces, refs):
            for t, m in enumerate(offsets):
                at = pl.multiple_of((row ^ m) * width, width)
                turned[pl.ds(at, width), :] = ref[t]
        out_ref[0] = turned[...].T

    return pl.pallas_call(
        body,
        out_shape=jax.ShapeDtypeStruct((1, height, columns), jnp.float32),
        in_specs=[VMEM] * len(arrays),
        out_specs=VMEM,
        scratch_shapes=[pltpu.VMEM((columns, height), jnp.float32)],
        compiler_params=params(8),
        cost_estimate=cost(0, 8 * columns * height),
        name="assemble",
    )(*arrays)


def per_device(kernels, history, incident, owner, tile_pairs, tile_values, tile_counts):
    row_count = lax.axis_size("row")
    col_count = lax.axis_size("col")
    lags, _, _ = history.shape
    half = lags // PARTS

    def across_rows(x, m):
        return lax.ppermute(x, "row", [(i, i ^ m) for i in range(row_count)])

    walk = list(range(0, col_count, 2)) + list(range(col_count - 1, 0, -2))

    def swap_walk(x, side):
        return lax.ppermute(x, "col", [(walk[p], walk[mate(p, side, col_count)]) for p in range(col_count)])

    def swap_cols(x, side):
        return lax.ppermute(x, "col", [(c, mate(c, side, col_count)) for c in range(col_count)])

    chosen, own_tiles = prepare(owner, tile_pairs.T, tile_counts, tile_values)
    parts = [own_tiles]
    for m in range(1, row_count):
        parts.append(across_rows(own_tiles, m))
    dense = stack_rows(chosen, parts)

    halves = [history[i * half : (i + 1) * half] for i in range(PARTS)]
    moving = {(side, i): halves[i] for i in range(PARTS) for side in (1, 2)}
    final = col_count // 2

    def turn(step, rank):
        out = {}
        for i in range(PARTS):
            side = early_side(step, i, final) if rank == 0 else 3 - early_side(step, i, final)
            out[side, i] = swap_walk(moving[3 - side, i], side)
        return out

    total = multiply(kernels, [(0, 1, i, x) for i, x in enumerate(halves)], None, None, None, 0)
    for step in range(1, final):
        turns = [turn(step, rank) for rank in range(2)]
        moving = turns[0] | turns[1]
        for rank in range(2):
            blocks = [(step, side, i, x) for (side, i), x in turns[rank].items()]
            field = (incident[0], chosen) if (step, rank) == (final - 1, 1) else (None, None)
            total = multiply(kernels, blocks, total, *field, 0)
    blocks = [(final, 1, i, x) for (_, i), x in turn(final, 0).items()]
    keep, *give = multiply(kernels, blocks, total, None, None, row_count)

    bit = 1
    summed = [keep[t] + across_rows(give[t], bit) for t in range(row_count // 2)]
    while len(summed) > 1:
        bit *= 2
        summed = [summed[t] + across_rows(summed[t + 1], bit) for t in range(0, len(summed), 2)]
    driven = -summed[0]

    density = driven
    rounded = density.astype(jnp.bfloat16)
    for step in range(SWEEPS):
        far_side, near_side = swap_cols(rounded, 2), swap_cols(rounded, 1)
        base = steady(dense, driven, density, rounded, near_side)
        result = sweep(dense, base, far_side, chosen if step == SWEEPS - 1 else None)
        if step < SWEEPS - 1:
            density, rounded = result

    away, home = result
    bit = row_count // 2
    got = across_rows(away, bit)
    sets = [((0,), home), ((bit,), got)]
    while bit > 1:
        bit //= 2
        pieces_next = []
        for offsets, array in sets:
            pieces_next.append((offsets, array[:bit]))
            sent = across_rows(array[bit : 2 * bit], bit)
            pieces_next.append((tuple(o ^ bit for o in offsets), sent))
        sets = pieces_next
    return assemble([(offsets, array) for offsets, array in sets])


def solution(mesh):
    in_specs = (
        P(None, "col", "row"),
        P(None, ("row", "col"), None),
        P(("row", "col"), None, None),
        P(),
        P(("row", "col"), None),
        P(("row", "col"), None, None),
        P(("row", "col")),
    )
    out_specs = P(("row", "col"), None, None)
    return jax.shard_map(
        per_device, mesh=mesh, in_specs=in_specs, out_specs=out_specs, check_vma=False
    )
```

time: 202 us -> 101 us (0.50)
  waiting for transfers between devices: 133 us -> 41.7 us
  blocking collectives: 24.3 us -> 0 us
  starting transfers between devices: 14.2 us -> 37.8 us
  between operations: 16.2 us -> 0.93 us
  Pallas kernels: 0 us -> 13.9 us
  matrix products: 10 us -> 0 us
  local copies, waits for them, and re-layouts: 3.57 us -> 6.79 us
    all_gather x1 -> x0, waiting for transfers between devices: 84.3 us -> none  [per_device(): lax.all_gather(history, 'col', axis=1, tiled=True)]
    all_gather x4 -> x0, blocking collectives: 24.3 us -> none  [the longest x3 17.5 us: per_device(): block_part = lax.all_gather(rounded, 'row', axis=0, tiled=True)]
    ppermute x6 -> x29, starting transfers between devices: 14.2 us -> 37.8 us  [the longest x14 21.5 us: swap_walk(): lax.ppermute(x, 'col', [(walk[p], walk[mate(p, side, col_count)]) for p i...]
    reduce_scatter x1 -> x0, waiting for transfers between devices: 16.5 us -> none  [per_device(): block_sum = lax.psum_scatter(blocks, 'row', scatter_dimension=0, tiled=True)]
    pallas_call x0 -> x17, Pallas kernels: none -> 13.9 us  [the longest x8 8.41 us: multiply(): pl.pallas_call(body, out_shape=out_shape, in_specs=in_specs, out_specs=[V...]
    ppermute x6 -> x29, waiting for transfers between devices: 31 us -> 41.7 us  [the longest x9 18.9 us: across_rows(): return lax.ppermute(x, 'row', [(i, i ^ m) for i in range(row_count)])]
    dot_general x4 -> x0, matrix products: 10 us -> none  [the longest x1 8.41 us: per_device(): lax.dot_general(kernels, lax.all_gather(history, 'col', axis=1, tiled=Tru...]
    unnamed x10 -> x16, local copies, waits for them, and re-layouts: 0.19 us -> 5.64 us
  transfers between devices with their start and end apart: 8 -> 29, of which waited for: 8 -> 16; matrix products, arithmetic and copies ran while one was open for 1% -> 0% of each run, Pallas kernels for 0% -> 10%
where the time goes in v3:
time: 101 us
  waiting for transfers between devices  41.7 us (41%)
  starting transfers between devices  37.8 us (37%)
  Pallas kernels  13.9 us (14%)
  local copies, waits for them, and re-layouts  6.79 us (7%)
    ppermute x14, starting transfers between devices, swap_walk(): lax.ppermute(x, 'col', [(walk[p], walk[mate(p, side, col_count)]) for p i...  21.5 us
    ppermute x9, waiting for transfers between devices, across_rows(): return lax.ppermute(x, 'row', [(i, i ^ m) for i in range(row_count)])  18.9 us
    ppermute x14, waiting for transfers between devices, swap_walk(): lax.ppermute(x, 'col', [(walk[p], walk[mate(p, side, col_count)]) for p i...  14.6 us
    ppermute x6, starting transfers between devices, swap_cols(): lax.ppermute(x, 'col', [(c, mate(c, side, col_count)) for c in range(col_...  10.6 us
    pallas_call x8, Pallas kernels, multiply(): pl.pallas_call(body, out_shape=out_shape, in_specs=in_specs, out_specs=[V...  8.41 us
    ppermute x6, waiting for transfers between devices, swap_cols(): lax.ppermute(x, 'col', [(c, mate(c, side, col_count)) for c in range(col_...  8.23 us
    unnamed x16, local copies, waits for them, and re-layouts  5.64 us
    ppermute x9, starting transfers between devices, across_rows(): return lax.ppermute(x, 'row', [(i, i ^ m) for i in range(row_count)])  5.61 us
  transfers between devices with their start and end apart: 29, of which 16 were waited for; matrix products, arithmetic and copies ran while one was open for 0% of the time, Pallas kernels for 10%

profile of v3, /device:TPU:0, one launch (start us, length us, event | category | flops | bytes accessed | tf_op | source)
XLA Modules:
  0.0 101.1 jit_solution(7174012708849040097)
XLA Ops:
  1.2 3.1 %collective-permute-start.7 = (bf16[3,192,256]{2,1,0:T(8,128)(2,1)S(1)}, bf16[3,192,256]{2,1,0:T(8,128)(2,1)S(1)}, u32[]{:S(2)}, u32[]{:S(2)}) collective-permute-start(bf16[3,192,256]{2,1,0:T(8,128)(2,1)S(1)} %get-tuple-element.29.refs_1_), channel_id=1, source_target_pairs={{0,2},{2,0},{4,6},{6,4},{7,5},{5,7},{3,1},{1,3},{8,10},{10,8},{12,... | collective-permute-start | bytes 884744 | tf_op jit(solution)/shard_map/ppermute | solution.py:287
  4.3 1.5 %collective-permute-start.3 = (bf16[3,192,256]{2,1,0:T(8,128)(2,1)S(1)}, bf16[3,192,256]{2,1,0:T(8,128)(2,1)S(1)}, u32[]{:S(2)}, u32[]{:S(2)}) collective-permute-start(bf16[3,192,256]{2,1,0:T(8,128)(2,1)S(1)} %get-tuple-element.30.refs_0_), channel_id=1, source_target_pairs={{0,1},{2,4},{4,2},{6,7},{7,6},{5,3},{3,5},{1,0},{8,9},{10,12},{12,... | collective-permute-start | bytes 884744 | tf_op jit(solution)/shard_map/ppermute | solution.py:287
  5.8 1.7 %collective-permute-start.11 = (bf16[3,192,256]{2,1,0:T(8,128)(2,1)S(1)}, bf16[3,192,256]{2,1,0:T(8,128)(2,1)S(1)}, u32[]{:S(2)}, u32[]{:S(2)}) collective-permute-start(bf16[3,192,256]{2,1,0:T(8,128)(2,1)S(1)} %get-tuple-element.30.refs_0_), channel_id=1, source_target_pairs={{0,2},{2,0},{4,6},{6,4},{7,5},{5,7},{3,1},{1,3},{8,10},{10,8},{12,... | collective-permute-start | bytes 884744 | tf_op jit(solution)/shard_map/ppermute | solution.py:287
  7.4 1.5 %collective-permute-start.14 = (bf16[3,192,256]{2,1,0:T(8,128)(2,1)S(1)}, bf16[3,192,256]{2,1,0:T(8,128)(2,1)S(1)}, u32[]{:S(2)}, u32[]{:S(2)}) collective-permute-start(bf16[3,192,256]{2,1,0:T(8,128)(2,1)S(1)} %get-tuple-element.29.refs_1_), channel_id=1, source_target_pairs={{0,1},{2,4},{4,2},{6,7},{7,6},{5,3},{3,5},{1,0},{8,9},{10,12},{12,... | collective-permute-start | bytes 884744 | tf_op jit(solution)/shard_map/ppermute | solution.py:287
  8.9 3.2 %collective-permute-done.7.refs_1_ = bf16[3,192,256]{2,1,0:T(8,128)(2,1)S(1)} collective-permute-done((bf16[3,192,256]{2,1,0:T(8,128)(2,1)S(1)}, bf16[3,192,256]{2,1,0:T(8,128)(2,1)S(1)}, u32[]{:S(2)}, u32[]{:S(2)}) %collective-permute-start.7) | collective-permute-done | bytes 294944 | tf_op jit(solution)/shard_map/ppermute | solution.py:287
  12.1 1.9 %collective-permute-start.8 = (bf16[3,192,256]{2,1,0:T(8,128)(2,1)S(1)}, bf16[3,192,256]{2,1,0:T(8,128)(2,1)S(1)}, u32[]{:S(2)}, u32[]{:S(2)}) collective-permute-start(bf16[3,192,256]{2,1,0:T(8,128)(2,1)S(1)} %collective-permute-done.7.refs_1_), channel_id=1, source_target_pairs={{0,1},{2,4},{4,2},{6,7},{7,6},{5,3},{3,5},{1,0},{8,9},{10,12},{12,... | collective-permute-start | bytes 884744 | tf_op jit(solution)/shard_map/ppermute | solution.py:287
  14.2 1.6 %collective-permute-start.4 = (bf16[3,192,256]{2,1,0:T(8,128)(2,1)S(1)}, bf16[3,192,256]{2,1,0:T(8,128)(2,1)S(1)}, u32[]{:S(2)}, u32[]{:S(2)}) collective-permute-start(bf16[3,192,256]{2,1,0:T(8,128)(2,1)S(1)} %collective-permute-done.3.refs_0_), channel_id=1, source_target_pairs={{0,2},{2,0},{4,6},{6,4},{7,5},{5,7},{3,1},{1,3},{8,10},{10,8},{12,... | collective-permute-start | bytes 884744 | tf_op jit(solution)/shard_map/ppermute | solution.py:287
  15.7 2.7 %collective-permute-done.11.refs_0_ = bf16[3,192,256]{2,1,0:T(8,128)(2,1)S(1)} collective-permute-done((bf16[3,192,256]{2,1,0:T(8,128)(2,1)S(1)}, bf16[3,192,256]{2,1,0:T(8,128)(2,1)S(1)}, u32[]{:S(2)}, u32[]{:S(2)}) %collective-permute-start.11) | collective-permute-done | bytes 294944 | tf_op jit(solution)/shard_map/ppermute | solution.py:287
  18.5 1.9 %collective-permute-start.12 = (bf16[3,192,256]{2,1,0:T(8,128)(2,1)S(1)}, bf16[3,192,256]{2,1,0:T(8,128)(2,1)S(1)}, u32[]{:S(2)}, u32[]{:S(2)}) collective-permute-start(bf16[3,192,256]{2,1,0:T(8,128)(2,1)S(1)} %collective-permute-done.11.refs_0_), channel_id=1, source_target_pairs={{0,1},{2,4},{4,2},{6,7},{7,6},{5,3},{3,5},{1,0},{8,9},{10,12},{12,... | collective-permute-start | bytes 884744 | tf_op jit(solution)/shard_map/ppermute | solution.py:287
  20.5 1.6 %collective-permute-start.15 = (bf16[3,192,256]{2,1,0:T(8,128)(2,1)S(1)}, bf16[3,192,256]{2,1,0:T(8,128)(2,1)S(1)}, u32[]{:S(2)}, u32[]{:S(2)}) collective-permute-start(bf16[3,192,256]{2,1,0:T(8,128)(2,1)S(1)} %collective-permute-done.14.refs_1_), channel_id=1, source_target_pairs={{0,2},{2,0},{4,6},{6,4},{7,5},{5,7},{3,1},{1,3},{8,10},{10,8},{12,... | collective-permute-start | bytes 884744 | tf_op jit(solution)/shard_map/ppermute | solution.py:287
  22.1 4.7 %collective-permute-done.8.refs_1_ = bf16[3,192,256]{2,1,0:T(8,128)(2,1)S(1)} collective-permute-done((bf16[3,192,256]{2,1,0:T(8,128)(2,1)S(1)}, bf16[3,192,256]{2,1,0:T(8,128)(2,1)S(1)}, u32[]{:S(2)}, u32[]{:S(2)}) %collective-permute-start.8) | collective-permute-done | bytes 294944 | tf_op jit(solution)/shard_map/ppermute | solution.py:287
  27.9 1.5 %collective-permute-start.5 = (bf16[3,192,256]{2,1,0:T(8,128)(2,1)S(1)}, bf16[3,192,256]{2,1,0:T(8,128)(2,1)S(1)}, u32[]{:S(2)}, u32[]{:S(2)}) collective-permute-start(bf16[3,192,256]{2,1,0:T(8,128)(2,1)S(1)} %collective-permute-done.4.refs_0_), channel_id=1, source_target_pairs={{0,1},{2,4},{4,2},{6,7},{7,6},{5,3},{3,5},{1,0},{8,9},{10,12},{12,... | collective-permute-start | bytes 884744 | tf_op jit(solution)/shard_map/ppermute | solution.py:287
  29.4 3.7 %collective-permute-done.12.refs_0_ = bf16[3,192,256]{2,1,0:T(8,128)(2,1)S(1)} collective-permute-done((bf16[3,192,256]{2,1,0:T(8,128)(2,1)S(1)}, bf16[3,192,256]{2,1,0:T(8,128)(2,1)S(1)}, u32[]{:S(2)}, u32[]{:S(2)}) %collective-permute-start.12) | collective-permute-done | bytes 294944 | tf_op jit(solution)/shard_map/ppermute | solution.py:287
  34.2 1.5 %collective-permute-start.16 = (bf16[3,192,256]{2,1,0:T(8,128)(2,1)S(1)}, bf16[3,192,256]{2,1,0:T(8,128)(2,1)S(1)}, u32[]{:S(2)}, u32[]{:S(2)}) collective-permute-start(bf16[3,192,256]{2,1,0:T(8,128)(2,1)S(1)} %collective-permute-done.15.refs_1_), channel_id=1, source_target_pairs={{0,1},{2,4},{4,2},{6,7},{7,6},{5,3},{3,5},{1,0},{8,9},{10,12},{12,... | collective-permute-start | bytes 884744 | tf_op jit(solution)/shard_map/ppermute | solution.py:287
  35.7 3.7 %copy-done = bf16[6,512,1536]{2,1,0:T(8,128)(2,1)S(1)} copy-done((bf16[6,512,1536]{2,1,0:T(8,128)(2,1)S(1)}, bf16[6,512,1536]{2,1,0:T(8,128)(2,1)}, u32[]{:S(2)}) %copy-start) | copy-done | bytes 9437208
  41.0 1.4 %prepare.1 = (s32[4]{0:T(128)S(1)}, bf16[128,1536]{1,0:T(8,128)(2,1)S(1)}) custom-call(s32[32]{0:T(128)S(1)} %copy-done.4, s32[2,12]{1,0:T(2,128)S(1)} %bitcast.14, s32[1]{0:T(128)S(6)} %copy.8.counts_ref, bf16[12,128,128]{2,1,0:T(8,128)(2,1)S(1)} %copy-done.1), custom_call_target="tpu_custom_call" | custom-call | bytes 786432 | tf_op jit(solution)/shard_map/prepare/pallas_call | solution.py:66
  50.8 1.5 %multiply.14.refs_2_ = f32[512,256]{1,0:T(8,128)S(1)} custom-call(bf16[6,512,1536]{2,1,0:T(8,128)(2,1)S(1)} %bitcast.12, bf16[3,192,256]{2,1,0:T(8,128)(2,1)S(1)} %collective-permute-done.13.refs_0_, bf16[3,192,256]{2,1,0:T(8,128)(2,1)S(1)} %collective-permute-done.16.refs_1_, f32[512,256]{1,0:T(8,128)S(1)} %multiply.13.refs_2_, f32[128,256]{1,0:T(8,128)S(1)} %bitcast.13, ...), custom_call_target="tpu_custom_call" | custom-call | flops 603979776 | bytes 3538944 | tf_op jit(solution)/shard_map/multiply/pallas_call | solution.py:165
  54.9 1.6 %collective-permute-start.19 = (f32[64,512]{1,0:T(8,128)S(1)}, f32[64,512]{1,0:T(8,128)S(1)}, u32[]{:S(2)}, u32[]{:S(2)}) collective-permute-start(f32[64,512]{1,0:T(8,128)S(1)} %bitcast_add_fusion), channel_id=1, source_target_pairs={{0,16},{8,24},{16,0},{24,8},{1,17},{9,25},{17,1},{25,9},{2,18},{10... | collective-permute-start | bytes 393224 | tf_op jit(solution)/shard_map/ppermute | solution.py:282
  57.0 1.4 %collective-permute-start.2 = (bf16[128,1536]{1,0:T(8,128)(2,1)S(1)}, bf16[128,1536]{1,0:T(8,128)(2,1)S(1)}, u32[]{:S(2)}, u32[]{:S(2)}) collective-permute-start(bf16[128,1536]{1,0:T(8,128)(2,1)S(1)} %get-tuple-element.17.refs_0_), channel_id=1, source_target_pairs={{0,24},{8,16},{16,8},{24,0},{1,25},{9,17},{17,9},{25,1},{2,26},{10... | collective-permute-start | bytes 1179656 | tf_op jit(solution)/shard_map/ppermute | solution.py:282
  58.4 3.0 %collective-permute-done.19 = f32[64,512]{1,0:T(8,128)S(1)} collective-permute-done((f32[64,512]{1,0:T(8,128)S(1)}, f32[64,512]{1,0:T(8,128)S(1)}, u32[]{:S(2)}, u32[]{:S(2)}) %collective-permute-start.19) | collective-permute-done | bytes 131104 | tf_op jit(solution)/shard_map/ppermute | solution.py:282
  61.4 1.5 %collective-permute-start.20 = (bf16[64,512]{1,0:T(8,128)(2,1)S(1)}, bf16[64,512]{1,0:T(8,128)(2,1)S(1)}, u32[]{:S(2)}, u32[]{:S(2)}) collective-permute-start(bf16[64,512]{1,0:T(8,128)(2,1)S(1)} %get-tuple-element.27.rounded_ref), channel_id=1, source_target_pairs={{0,1},{1,0},{2,3},{3,2},{4,5},{5,4},{6,7},{7,6},{8,9},{9,8},{10,11... | collective-permute-start | bytes 196616 | tf_op jit(solution)/shard_map/ppermute | solution.py:290
  62.9 2.5 %collective-permute-start.21 = (bf16[64,512]{1,0:T(8,128)(2,1)S(1)}, bf16[64,512]{1,0:T(8,128)(2,1)S(1)}, u32[]{:S(2)}, u32[]{:S(2)}) collective-permute-start(bf16[64,512]{1,0:T(8,128)(2,1)S(1)} %get-tuple-element.27.rounded_ref), channel_id=1, source_target_pairs={{0,7},{1,2},{2,1},{3,4},{4,3},{5,6},{6,5},{7,0},{8,15},{9,10},{10,... | collective-permute-start | bytes 196616 | tf_op jit(solution)/shard_map/ppermute | solution.py:290
  65.4 4.4 %collective-permute-done.1.refs_2_ = bf16[128,1536]{1,0:T(8,128)(2,1)S(1)} collective-permute-done((bf16[128,1536]{1,0:T(8,128)(2,1)S(1)}, bf16[128,1536]{1,0:T(8,128)(2,1)S(1)}, u32[]{:S(2)}, u32[]{:S(2)}) %collective-permute-start.1) | collective-permute-done | bytes 393248 | tf_op jit(solution)/shard_map/ppermute | solution.py:282
  69.8 6.8 %collective-permute-done.2.refs_3_ = bf16[128,1536]{1,0:T(8,128)(2,1)S(1)} collective-permute-done((bf16[128,1536]{1,0:T(8,128)(2,1)S(1)}, bf16[128,1536]{1,0:T(8,128)(2,1)S(1)}, u32[]{:S(2)}, u32[]{:S(2)}) %collective-permute-start.2) | collective-permute-done | bytes 393248 | tf_op jit(solution)/shard_map/ppermute | solution.py:282
  78.0 1.5 %collective-permute-start.22 = (bf16[64,512]{1,0:T(8,128)(2,1)S(1)}, bf16[64,512]{1,0:T(8,128)(2,1)S(1)}, u32[]{:S(2)}, u32[]{:S(2)}) collective-permute-start(bf16[64,512]{1,0:T(8,128)(2,1)S(1)} %get-tuple-element.22.rounded_ref), channel_id=1, source_target_pairs={{0,1},{1,0},{2,3},{3,2},{4,5},{5,4},{6,7},{7,6},{8,9},{9,8},{10,11... | collective-permute-start | bytes 196616 | tf_op jit(solution)/shard_map/ppermute | solution.py:290
  79.5 2.5 %collective-permute-start.23 = (bf16[64,512]{1,0:T(8,128)(2,1)S(1)}, bf16[64,512]{1,0:T(8,128)(2,1)S(1)}, u32[]{:S(2)}, u32[]{:S(2)}) collective-permute-start(bf16[64,512]{1,0:T(8,128)(2,1)S(1)} %get-tuple-element.22.rounded_ref), channel_id=1, source_target_pairs={{0,7},{1,2},{2,1},{3,4},{4,3},{5,6},{6,5},{7,0},{8,15},{9,10},{10,... | collective-permute-start | bytes 196616 | tf_op jit(solution)/shard_map/ppermute | solution.py:290
  83.1 3.5 %collective-permute-done.23.side_ref = bf16[64,512]{1,0:T(8,128)(2,1)S(1)} collective-permute-done((bf16[64,512]{1,0:T(8,128)(2,1)S(1)}, bf16[64,512]{1,0:T(8,128)(2,1)S(1)}, u32[]{:S(2)}, u32[]{:S(2)}) %collective-permute-start.23) | collective-permute-done | bytes 65568 | tf_op jit(solution)/shard_map/ppermute | solution.py:290
  86.9 2.5 %collective-permute-start.25 = (bf16[64,512]{1,0:T(8,128)(2,1)S(1)}, bf16[64,512]{1,0:T(8,128)(2,1)S(1)}, u32[]{:S(2)}, u32[]{:S(2)}) collective-permute-start(bf16[64,512]{1,0:T(8,128)(2,1)S(1)} %get-tuple-element.24.rounded_ref), channel_id=1, source_target_pairs={{0,7},{1,2},{2,1},{3,4},{4,3},{5,6},{6,5},{7,0},{8,15},{9,10},{10,... | collective-permute-start | bytes 196616 | tf_op jit(solution)/shard_map/ppermute | solution.py:290
  89.5 1.7 %collective-permute-done.24.side_ref = bf16[64,512]{1,0:T(8,128)(2,1)S(1)} collective-permute-done((bf16[64,512]{1,0:T(8,128)(2,1)S(1)}, bf16[64,512]{1,0:T(8,128)(2,1)S(1)}, u32[]{:S(2)}, u32[]{:S(2)}) %collective-permute-start.24) | collective-permute-done | bytes 65568 | tf_op jit(solution)/shard_map/ppermute | solution.py:290
  91.6 2.3 %collective-permute-done.25.side_ref = bf16[64,512]{1,0:T(8,128)(2,1)S(1)} collective-permute-done((bf16[64,512]{1,0:T(8,128)(2,1)S(1)}, bf16[64,512]{1,0:T(8,128)(2,1)S(1)}, u32[]{:S(2)}, u32[]{:S(2)}) %collective-permute-start.25) | collective-permute-done | bytes 65568 | tf_op jit(solution)/shard_map/ppermute | solution.py:290
  94.8 1.6 %collective-permute-start.27 = (f32[2,64,128]{2,1,0:T(8,128)S(1)}, f32[2,64,128]{2,1,0:T(8,128)S(1)}, u32[]{:S(2)}, u32[]{:S(2)}) collective-permute-start(f32[2,64,128]{2,1,0:T(8,128)S(1)} %get-tuple-element.26), channel_id=1, source_target_pairs={{0,16},{8,24},{16,0},{24,8},{1,17},{9,25},{17,1},{25,9},{2,18},{10... | collective-permute-start | bytes 196616 | tf_op jit(solution)/shard_map/ppermute | solution.py:282
  96.4 2.7 %collective-permute-done.27 = f32[2,64,128]{2,1,0:T(8,128)S(1)} collective-permute-done((f32[2,64,128]{2,1,0:T(8,128)S(1)}, f32[2,64,128]{2,1,0:T(8,128)S(1)}, u32[]{:S(2)}, u32[]{:S(2)}) %collective-permute-start.27) | collective-permute-done | bytes 65568 | tf_op jit(solution)/shard_map/ppermute | solution.py:282
  (65 shorter events, 22.0 us)
Async XLA Ops:
  0.0 41.0 %copy-start.3 = (s32[12,2]{0,1:T(2,128)S(1)}, s32[12,2]{0,1:T(2,128)}, u32[]{:S(2)}) copy-start(s32[12,2]{0,1:T(2,128)} %param.11) | copy-start | bytes 292
  0.0 41.0 %copy-start.4 = (s32[32]{0:T(128)S(1)}, s32[32]{0:T(128)}, u32[]{:S(2)}) copy-start(s32[32]{0:T(128)} %owner_ref.1) | copy-start | bytes 388
  0.0 41.0 %copy-start.1 = (bf16[12,128,128]{2,1,0:T(8,128)(2,1)S(1)}, bf16[12,128,128]{2,1,0:T(8,128)(2,1)}, u32[]{:S(2)}) copy-start(bf16[12,128,128]{2,1,0:T(8,128)(2,1)} %tile_ref.1) | copy-start | bytes 1179652
  1.2 11.0 %collective-permute-start.7 = (bf16[3,192,256]{2,1,0:T(8,128)(2,1)S(1)}, bf16[3,192,256]{2,1,0:T(8,128)(2,1)S(1)}, u32[]{:S(2)}, u32[]{:S(2)}) collective-permute-start(bf16[3,192,256]{2,1,0:T(8,128)(2,1)S(1)} %get-tuple-element.29.refs_1_), channel_id=1, source_target_pairs={{0,2},{2,0},{4,6},{6,4},{7,5},{5,7},{3,1},{1,3},{8,10},{10,8},{12,... | collective-permute-start | bytes 884744 | tf_op jit(solution)/shard_map/ppermute | solution.py:287
  4.3 9.9 %collective-permute-start.3 = (bf16[3,192,256]{2,1,0:T(8,128)(2,1)S(1)}, bf16[3,192,256]{2,1,0:T(8,128)(2,1)S(1)}, u32[]{:S(2)}, u32[]{:S(2)}) collective-permute-start(bf16[3,192,256]{2,1,0:T(8,128)(2,1)S(1)} %get-tuple-element.30.refs_0_), channel_id=1, source_target_pairs={{0,1},{2,4},{4,2},{6,7},{7,6},{5,3},{3,5},{1,0},{8,9},{10,12},{12,... | collective-permute-start | bytes 884744 | tf_op jit(solution)/shard_map/ppermute | solution.py:287
  5.8 12.7 %collective-permute-start.11 = (bf16[3,192,256]{2,1,0:T(8,128)(2,1)S(1)}, bf16[3,192,256]{2,1,0:T(8,128)(2,1)S(1)}, u32[]{:S(2)}, u32[]{:S(2)}) collective-permute-start(bf16[3,192,256]{2,1,0:T(8,128)(2,1)S(1)} %get-tuple-element.30.refs_0_), channel_id=1, source_target_pairs={{0,2},{2,0},{4,6},{6,4},{7,5},{5,7},{3,1},{1,3},{8,10},{10,8},{12,... | collective-permute-start | bytes 884744 | tf_op jit(solution)/shard_map/ppermute | solution.py:287
  7.4 13.0 %collective-permute-start.14 = (bf16[3,192,256]{2,1,0:T(8,128)(2,1)S(1)}, bf16[3,192,256]{2,1,0:T(8,128)(2,1)S(1)}, u32[]{:S(2)}, u32[]{:S(2)}) collective-permute-start(bf16[3,192,256]{2,1,0:T(8,128)(2,1)S(1)} %get-tuple-element.29.refs_1_), channel_id=1, source_target_pairs={{0,1},{2,4},{4,2},{6,7},{7,6},{5,3},{3,5},{1,0},{8,9},{10,12},{12,... | collective-permute-start | bytes 884744 | tf_op jit(solution)/shard_map/ppermute | solution.py:287
  12.1 14.7 %collective-permute-start.8 = (bf16[3,192,256]{2,1,0:T(8,128)(2,1)S(1)}, bf16[3,192,256]{2,1,0:T(8,128)(2,1)S(1)}, u32[]{:S(2)}, u32[]{:S(2)}) collective-permute-start(bf16[3,192,256]{2,1,0:T(8,128)(2,1)S(1)} %collective-permute-done.7.refs_1_), channel_id=1, source_target_pairs={{0,1},{2,4},{4,2},{6,7},{7,6},{5,3},{3,5},{1,0},{8,9},{10,12},{12,... | collective-permute-start | bytes 884744 | tf_op jit(solution)/shard_map/ppermute | solution.py:287
  14.2 13.8 %collective-permute-start.4 = (bf16[3,192,256]{2,1,0:T(8,128)(2,1)S(1)}, bf16[3,192,256]{2,1,0:T(8,128)(2,1)S(1)}, u32[]{:S(2)}, u32[]{:S(2)}) collective-permute-start(bf16[3,192,256]{2,1,0:T(8,128)(2,1)S(1)} %collective-permute-done.3.refs_0_), channel_id=1, source_target_pairs={{0,2},{2,0},{4,6},{6,4},{7,5},{5,7},{3,1},{1,3},{8,10},{10,8},{12,... | collective-permute-start | bytes 884744 | tf_op jit(solution)/shard_map/ppermute | solution.py:287
  18.5 14.7 %collective-permute-start.12 = (bf16[3,192,256]{2,1,0:T(8,128)(2,1)S(1)}, bf16[3,192,256]{2,1,0:T(8,128)(2,1)S(1)}, u32[]{:S(2)}, u32[]{:S(2)}) collective-permute-start(bf16[3,192,256]{2,1,0:T(8,128)(2,1)S(1)} %collective-permute-done.11.refs_0_), channel_id=1, source_target_pairs={{0,1},{2,4},{4,2},{6,7},{7,6},{5,3},{3,5},{1,0},{8,9},{10,12},{12,... | collective-permute-start | bytes 884744 | tf_op jit(solution)/shard_map/ppermute | solution.py:287
  20.5 13.8 %collective-permute-start.15 = (bf16[3,192,256]{2,1,0:T(8,128)(2,1)S(1)}, bf16[3,192,256]{2,1,0:T(8,128)(2,1)S(1)}, u32[]{:S(2)}, u32[]{:S(2)}) collective-permute-start(bf16[3,192,256]{2,1,0:T(8,128)(2,1)S(1)} %collective-permute-done.14.refs_1_), channel_id=1, source_target_pairs={{0,2},{2,0},{4,6},{6,4},{7,5},{5,7},{3,1},{1,3},{8,10},{10,8},{12,... | collective-permute-start | bytes 884744 | tf_op jit(solution)/shard_map/ppermute | solution.py:287
  26.8 15.6 %collective-permute-start.9 = (bf16[3,192,256]{2,1,0:T(8,128)(2,1)S(1)}, bf16[3,192,256]{2,1,0:T(8,128)(2,1)S(1)}, u32[]{:S(2)}, u32[]{:S(2)}) collective-permute-start(bf16[3,192,256]{2,1,0:T(8,128)(2,1)S(1)} %collective-permute-done.8.refs_1_), channel_id=1, source_target_pairs={{0,2},{2,0},{4,6},{6,4},{7,5},{5,7},{3,1},{1,3},{8,10},{10,8},{12,... | collective-permute-start | bytes 884744 | tf_op jit(solution)/shard_map/ppermute | solution.py:287
  27.9 15.1 %collective-permute-start.5 = (bf16[3,192,256]{2,1,0:T(8,128)(2,1)S(1)}, bf16[3,192,256]{2,1,0:T(8,128)(2,1)S(1)}, u32[]{:S(2)}, u32[]{:S(2)}) collective-permute-start(bf16[3,192,256]{2,1,0:T(8,128)(2,1)S(1)} %collective-permute-done.4.refs_0_), channel_id=1, source_target_pairs={{0,1},{2,4},{4,2},{6,7},{7,6},{5,3},{3,5},{1,0},{8,9},{10,12},{12,... | collective-permute-start | bytes 884744 | tf_op jit(solution)/shard_map/ppermute | solution.py:287
  33.1 15.7 %collective-permute-start.13 = (bf16[3,192,256]{2,1,0:T(8,128)(2,1)S(1)}, bf16[3,192,256]{2,1,0:T(8,128)(2,1)S(1)}, u32[]{:S(2)}, u32[]{:S(2)}) collective-permute-start(bf16[3,192,256]{2,1,0:T(8,128)(2,1)S(1)} %collective-permute-done.12.refs_0_), channel_id=1, source_target_pairs={{0,2},{2,0},{4,6},{6,4},{7,5},{5,7},{3,1},{1,3},{8,10},{10,8},{12,... | collective-permute-start | bytes 884744 | tf_op jit(solution)/shard_map/ppermute | solution.py:287
  34.2 14.6 %collective-permute-start.16 = (bf16[3,192,256]{2,1,0:T(8,128)(2,1)S(1)}, bf16[3,192,256]{2,1,0:T(8,128)(2,1)S(1)}, u32[]{:S(2)}, u32[]{:S(2)}) collective-permute-start(bf16[3,192,256]{2,1,0:T(8,128)(2,1)S(1)} %collective-permute-done.15.refs_1_), channel_id=1, source_target_pairs={{0,1},{2,4},{4,2},{6,7},{7,6},{5,3},{3,5},{1,0},{8,9},{10,12},{12,... | collective-permute-start | bytes 884744 | tf_op jit(solution)/shard_map/ppermute | solution.py:287
  42.4 9.9 %collective-permute-start.10 = (bf16[3,192,256]{2,1,0:T(8,128)(2,1)S(1)}, bf16[3,192,256]{2,1,0:T(8,128)(2,1)S(1)}, u32[]{:S(2)}, u32[]{:S(2)}) collective-permute-start(bf16[3,192,256]{2,1,0:T(8,128)(2,1)S(1)} %collective-permute-done.9.refs_1_), channel_id=1, source_target_pairs={{0,1},{2,4},{4,2},{6,7},{7,6},{5,3},{3,5},{1,0},{8,9},{10,12},{12,... | collective-permute-start | bytes 884744 | tf_op jit(solution)/shard_map/ppermute | solution.py:287
  43.1 9.3 %collective-permute-start.6 = (bf16[3,192,256]{2,1,0:T(8,128)(2,1)S(1)}, bf16[3,192,256]{2,1,0:T(8,128)(2,1)S(1)}, u32[]{:S(2)}, u32[]{:S(2)}) collective-permute-start(bf16[3,192,256]{2,1,0:T(8,128)(2,1)S(1)} %collective-permute-done.5.refs_0_), channel_id=1, source_target_pairs={{0,2},{2,0},{4,6},{6,4},{7,5},{5,7},{3,1},{1,3},{8,10},{10,8},{12,... | collective-permute-start | bytes 884744 | tf_op jit(solution)/shard_map/ppermute | solution.py:287
  53.5 1.4 %collective-permute-start.18 = (f32[64,512]{1,0:T(8,128)S(1)}, f32[64,512]{1,0:T(8,128)S(1)}, u32[]{:S(2)}, u32[]{:S(2)}) collective-permute-start(f32[64,512]{1,0:T(8,128)S(1)} %get-tuple-element.20), channel_id=1, source_target_pairs={{0,8},{8,0},{16,24},{24,16},{1,9},{9,1},{17,25},{25,17},{2,10},{10... | collective-permute-start | bytes 393224 | tf_op jit(solution)/shard_map/ppermute | solution.py:282
  53.6 4.8 %collective-permute-start.17 = (f32[64,512]{1,0:T(8,128)S(1)}, f32[64,512]{1,0:T(8,128)S(1)}, u32[]{:S(2)}, u32[]{:S(2)}) collective-permute-start(f32[64,512]{1,0:T(8,128)S(1)} %get-tuple-element.19), channel_id=1, source_target_pairs={{0,8},{8,0},{16,24},{24,16},{1,9},{9,1},{17,25},{25,17},{2,10},{10... | collective-permute-start | bytes 393224 | tf_op jit(solution)/shard_map/ppermute | solution.py:282
  54.9 6.4 %collective-permute-start.19 = (f32[64,512]{1,0:T(8,128)S(1)}, f32[64,512]{1,0:T(8,128)S(1)}, u32[]{:S(2)}, u32[]{:S(2)}) collective-permute-start(f32[64,512]{1,0:T(8,128)S(1)} %bitcast_add_fusion), channel_id=1, source_target_pairs={{0,16},{8,24},{16,0},{24,8},{1,17},{9,25},{17,1},{25,9},{2,18},{10... | collective-permute-start | bytes 393224 | tf_op jit(solution)/shard_map/ppermute | solution.py:282
  56.5 8.9 %collective-permute-start = (bf16[128,1536]{1,0:T(8,128)(2,1)S(1)}, bf16[128,1536]{1,0:T(8,128)(2,1)S(1)}, u32[]{:S(2)}, u32[]{:S(2)}) collective-permute-start(bf16[128,1536]{1,0:T(8,128)(2,1)S(1)} %get-tuple-element.17.refs_0_), channel_id=1, source_target_pairs={{0,8},{8,0},{16,24},{24,16},{1,9},{9,1},{17,25},{25,17},{2,10},{10... | collective-permute-start | bytes 1179656 | tf_op jit(solution)/shard_map/ppermute | solution.py:282
  56.5 13.3 %collective-permute-start.1 = (bf16[128,1536]{1,0:T(8,128)(2,1)S(1)}, bf16[128,1536]{1,0:T(8,128)(2,1)S(1)}, u32[]{:S(2)}, u32[]{:S(2)}) collective-permute-start(bf16[128,1536]{1,0:T(8,128)(2,1)S(1)} %get-tuple-element.17.refs_0_), channel_id=1, source_target_pairs={{0,16},{8,24},{16,0},{24,8},{1,17},{9,25},{17,1},{25,9},{2,18},{10... | collective-permute-start | bytes 1179656 | tf_op jit(solution)/shard_map/ppermute | solution.py:282
  57.0 19.6 %collective-permute-start.2 = (bf16[128,1536]{1,0:T(8,128)(2,1)S(1)}, bf16[128,1536]{1,0:T(8,128)(2,1)S(1)}, u32[]{:S(2)}, u32[]{:S(2)}) collective-permute-start(bf16[128,1536]{1,0:T(8,128)(2,1)S(1)} %get-tuple-element.17.refs_0_), channel_id=1, source_target_pairs={{0,24},{8,16},{16,8},{24,0},{1,25},{9,17},{17,9},{25,1},{2,26},{10... | collective-permute-start | bytes 1179656 | tf_op jit(solution)/shard_map/ppermute | solution.py:282
  61.4 15.8 %collective-permute-start.20 = (bf16[64,512]{1,0:T(8,128)(2,1)S(1)}, bf16[64,512]{1,0:T(8,128)(2,1)S(1)}, u32[]{:S(2)}, u32[]{:S(2)}) collective-permute-start(bf16[64,512]{1,0:T(8,128)(2,1)S(1)} %get-tuple-element.27.rounded_ref), channel_id=1, source_target_pairs={{0,1},{1,0},{2,3},{3,2},{4,5},{5,4},{6,7},{7,6},{8,9},{9,8},{10,11... | collective-permute-start | bytes 196616 | tf_op jit(solution)/shard_map/ppermute | solution.py:290
  62.9 14.7 %collective-permute-start.21 = (bf16[64,512]{1,0:T(8,128)(2,1)S(1)}, bf16[64,512]{1,0:T(8,128)(2,1)S(1)}, u32[]{:S(2)}, u32[]{:S(2)}) collective-permute-start(bf16[64,512]{1,0:T(8,128)(2,1)S(1)} %get-tuple-element.27.rounded_ref), channel_id=1, source_target_pairs={{0,7},{1,2},{2,1},{3,4},{4,3},{5,6},{6,5},{7,0},{8,15},{9,10},{10,... | collective-permute-start | bytes 196616 | tf_op jit(solution)/shard_map/ppermute | solution.py:290
  78.0 4.7 %collective-permute-start.22 = (bf16[64,512]{1,0:T(8,128)(2,1)S(1)}, bf16[64,512]{1,0:T(8,128)(2,1)S(1)}, u32[]{:S(2)}, u32[]{:S(2)}) collective-permute-start(bf16[64,512]{1,0:T(8,128)(2,1)S(1)} %get-tuple-element.22.rounded_ref), channel_id=1, source_target_pairs={{0,1},{1,0},{2,3},{3,2},{4,5},{5,4},{6,7},{7,6},{8,9},{9,8},{10,11... | collective-permute-start | bytes 196616 | tf_op jit(solution)/shard_map/ppermute | solution.py:290
  79.5 7.1 %collective-permute-start.23 = (bf16[64,512]{1,0:T(8,128)(2,1)S(1)}, bf16[64,512]{1,0:T(8,128)(2,1)S(1)}, u32[]{:S(2)}, u32[]{:S(2)}) collective-permute-start(bf16[64,512]{1,0:T(8,128)(2,1)S(1)} %get-tuple-element.22.rounded_ref), channel_id=1, source_target_pairs={{0,7},{1,2},{2,1},{3,4},{4,3},{5,6},{6,5},{7,0},{8,15},{9,10},{10,... | collective-permute-start | bytes 196616 | tf_op jit(solution)/shard_map/ppermute | solution.py:290
  86.9 4.3 %collective-permute-start.24 = (bf16[64,512]{1,0:T(8,128)(2,1)S(1)}, bf16[64,512]{1,0:T(8,128)(2,1)S(1)}, u32[]{:S(2)}, u32[]{:S(2)}) collective-permute-start(bf16[64,512]{1,0:T(8,128)(2,1)S(1)} %get-tuple-element.24.rounded_ref), channel_id=1, source_target_pairs={{0,1},{1,0},{2,3},{3,2},{4,5},{5,4},{6,7},{7,6},{8,9},{9,8},{10,11... | collective-permute-start | bytes 196616 | tf_op jit(solution)/shard_map/ppermute | solution.py:290
  86.9 7.0 %collective-permute-start.25 = (bf16[64,512]{1,0:T(8,128)(2,1)S(1)}, bf16[64,512]{1,0:T(8,128)(2,1)S(1)}, u32[]{:S(2)}, u32[]{:S(2)}) collective-permute-start(bf16[64,512]{1,0:T(8,128)(2,1)S(1)} %get-tuple-element.24.rounded_ref), channel_id=1, source_target_pairs={{0,7},{1,2},{2,1},{3,4},{4,3},{5,6},{6,5},{7,0},{8,15},{9,10},{10,... | collective-permute-start | bytes 196616 | tf_op jit(solution)/shard_map/ppermute | solution.py:290
  94.8 4.3 %collective-permute-start.27 = (f32[2,64,128]{2,1,0:T(8,128)S(1)}, f32[2,64,128]{2,1,0:T(8,128)S(1)}, u32[]{:S(2)}, u32[]{:S(2)}) collective-permute-start(f32[2,64,128]{2,1,0:T(8,128)S(1)} %get-tuple-element.26), channel_id=1, source_target_pairs={{0,16},{8,24},{16,0},{24,8},{1,17},{9,25},{17,1},{25,9},{2,18},{10... | collective-permute-start | bytes 196616 | tf_op jit(solution)/shard_map/ppermute | solution.py:282
  96.4 2.8 %collective-permute-start.26 = (f32[1,64,128]{2,1,0:T(8,128)S(1)}, f32[1,64,128]{2,1,0:T(8,128)S(1)}, u32[]{:S(2)}, u32[]{:S(2)}) collective-permute-start(f32[1,64,128]{2,1,0:T(8,128)S(1)} %get-tuple-element.33), channel_id=1, source_target_pairs={{0,8},{8,0},{16,24},{24,16},{1,9},{9,1},{17,25},{25,17},{2,10},{10... | collective-permute-start | bytes 98312 | tf_op jit(solution)/shard_map/ppermute | solution.py:282
  99.2 1.2 %collective-permute-start.28 = (f32[1,64,128]{2,1,0:T(8,128)S(1)}, f32[1,64,128]{2,1,0:T(8,128)S(1)}, u32[]{:S(2)}, u32[]{:S(2)}) collective-permute-start(f32[1,64,128]{2,1,0:T(8,128)S(1)} %get-tuple-element.31), channel_id=1, source_target_pairs={{0,8},{8,0},{16,24},{24,16},{1,9},{9,1},{17,25},{25,17},{2,10},{10... | collective-permute-start | bytes 98312 | tf_op jit(solution)/shard_map/ppermute | solution.py:282
  (5 other events, 15.7 us)

commit v4 on v3

--- a/solution.py
+++ b/solution.py
@@ -81,17 +81,22 @@
 def stack_rows(chosen, parts):
     count = len(parts)
     rows, width = parts[0].shape
+    side = width // 3
 
     def body(chosen_ref, *refs):
         for m in range(count):
             at = pl.multiple_of(chosen_ref[m] * rows, rows)
-            refs[-1][pl.ds(at, rows), :] = refs[m][...]
-
-    return pl.pallas_call(
-        body,
-        out_shape=jax.ShapeDtypeStruct((count * rows, width), parts[0].dtype),
+            refs[-2][pl.ds(at, rows), :] = refs[m][...]
+            refs[-1][m * rows : (m + 1) * rows, :] = refs[m][:, :side]
+
+    return pl.pallas_call(
+        body,
+        out_shape=[
+            jax.ShapeDtypeStruct((count * rows, width), parts[0].dtype),
+            jax.ShapeDtypeStruct((count * rows, side), parts[0].dtype),
+        ],
         in_specs=[SMEM] + [VMEM] * count,
-        out_specs=VMEM,
+        out_specs=[VMEM] * 2,
         compiler_params=params(4 if rows * count <= 512 else 24),
         cost_estimate=cost(0, 4 * count * rows * width),
         name="stack_rows",
@@ -174,10 +179,12 @@
     )(kernels, *[block[3] for block in blocks], *extra)
 
 
-def steady(dense, driven, density, rounded, near_side):
+def steady(dense, driven, density, rounded, near_side, chosen):
     width, rows = driven.shape
 
-    def body(dense_ref, driven_ref, density_ref, rounded_ref, side_ref, out_ref):
+    def body(*refs):
+        dense_ref, driven_ref, density_ref, rounded_ref, side_ref, out_ref = refs[:5] + refs[-1 if last else 5 :][:1]
+
         def term(ref, k):
             return lax.dot_general(
                 ref[...],
@@ -189,87 +196,80 @@
         near = term(rounded_ref, 1) + term(side_ref, 2)
         old = density_ref[...]
         out_ref[...] = old + damping * (driven_ref[...] - old - near)
-
-    return pl.pallas_call(
-        body,
-        out_shape=jax.ShapeDtypeStruct((width, rows), jnp.float32),
-        in_specs=[VMEM] * 5,
+        if last:
+            count = chosen.shape[0]
+            height = rows // count
+            for m in range(count):
+                at = pl.multiple_of(refs[5][m] * height, height)
+                refs[6][:, m * height : (m + 1) * height] = out_ref[:, pl.ds(at, height)]
+
+    last = chosen is not None
+    whole = (width, rows)
+    return pl.pallas_call(
+        body,
+        out_shape=jax.ShapeDtypeStruct(whole, jnp.float32),
+        in_specs=[VMEM] * 5 + [SMEM] * last,
         out_specs=VMEM,
+        scratch_shapes=[pltpu.VMEM(whole, jnp.float32)] * last,
         compiler_params=params(8 if rows <= 512 else 24),
         cost_estimate=cost(4 * width * rows * rows, 4 * rows * rows + 16 * width * rows),
         name="steady",
-    )(dense, driven, density, rounded, near_side)
-
-
-def sweep(dense, base, far_side, chosen):
+    )(dense, driven, density, rounded, near_side, *([chosen] if last else []))
+
+
+def sweep(dense, base, far_side, pieces):
     width, rows = base.shape
 
-    def update(dense_ref, base_ref, side_ref):
+    def body(dense_ref, base_ref, side_ref, *outs):
         near = lax.dot_general(
             side_ref[...], dense_ref[:, :rows], (((1,), (1,)), ((), ())), preferred_element_type=jnp.float32
         )
-        return base_ref[...] - damping * near
-
-    def body(dense_ref, base_ref, side_ref, density_ref, rounded_ref):
-        new = update(dense_ref, base_ref, side_ref)
-        density_ref[...] = new
-        rounded_ref[...] = new.astype(rounded_ref.dtype)
-
-    def body_last(chosen_ref, dense_ref, base_ref, side_ref, away, home, whole):
-        whole[...] = update(dense_ref, base_ref, side_ref)
-        for m in range(count):
-            at = pl.multiple_of(chosen_ref[m] * height, height)
-            (away if m >= count // 2 else home)[m % (count // 2)] = whole[:, pl.ds(at, height)]
-
-    same = dict(
-        out_specs=[VMEM] * 2,
+        new = base_ref[...] - damping * near
+        if pieces:
+            height = rows // pieces
+            for m in range(pieces):
+                outs[m][...] = new[:, m * height : (m + 1) * height]
+        else:
+            outs[0][...] = new
+            outs[1][...] = new.astype(far_side.dtype)
+
+    if pieces:
+        out_shape = [jax.ShapeDtypeStruct((width, rows // pieces), jnp.float32)] * pieces
+    else:
+        out_shape = [jax.ShapeDtypeStruct((width, rows), kind) for kind in (jnp.float32, far_side.dtype)]
+    return pl.pallas_call(
+        body,
+        out_shape=out_shape,
+        in_specs=[VMEM] * 3,
+        out_specs=[VMEM] * len(out_shape),
         compiler_params=params(8 if rows <= 512 else 24),
         cost_estimate=cost(2 * width * rows * rows, 2 * rows * rows + 12 * width * rows),
-    )
-    if chosen is None:
-        out_shape = [
-            jax.ShapeDtypeStruct((width, rows), jnp.float32),
-            jax.ShapeDtypeStruct((width, rows), far_side.dtype),
-        ]
-        return pl.pallas_call(body, out_shape=out_shape, in_specs=[VMEM] * 3, name="sweep", **same)(
-            dense, base, far_side
-        )
-    count = chosen.shape[0]
-    height = rows // count
-    return pl.pallas_call(
-        body_last,
-        out_shape=[jax.ShapeDtypeStruct((count // 2, width, height), jnp.float32)] * 2,
-        in_specs=[SMEM] + [VMEM] * 3,
-        scratch_shapes=[pltpu.VMEM((width, rows), jnp.float32)],
-        name="sweep_last",
-        **same,
-    )(chosen, dense, base, far_side)
+        name="sweep",
+    )(dense, base, far_side)
 
 
 def assemble(pieces):
-    arrays = [piece for _, piece in pieces]
-    width, height = arrays[0].shape[1:]
-    columns = width * sum(piece.shape[0] for piece in arrays)
+    width, height = pieces[0].shape
+    columns = width * len(pieces)
 
     def body(*refs):
         row = lax.axis_index("row")
         out_ref, turned = refs[-2:]
-        for (offsets, _), ref in zip(pieces, refs):
-            for t, m in enumerate(offsets):
-                at = pl.multiple_of((row ^ m) * width, width)
-                turned[pl.ds(at, width), :] = ref[t]
+        for m in range(len(pieces)):
+            at = pl.multiple_of((row ^ m) * width, width)
+            turned[pl.ds(at, width), :] = refs[m][...]
         out_ref[0] = turned[...].T
 
     return pl.pallas_call(
         body,
         out_shape=jax.ShapeDtypeStruct((1, height, columns), jnp.float32),
-        in_specs=[VMEM] * len(arrays),
+        in_specs=[VMEM] * len(pieces),
         out_specs=VMEM,
         scratch_shapes=[pltpu.VMEM((columns, height), jnp.float32)],
         compiler_params=params(8),
         cost_estimate=cost(0, 8 * columns * height),
         name="assemble",
-    )(*arrays)
+    )(*pieces)
 
 
 def per_device(kernels, history, incident, owner, tile_pairs, tile_values, tile_counts):
@@ -293,7 +293,7 @@
     parts = [own_tiles]
     for m in range(1, row_count):
         parts.append(across_rows(own_tiles, m))
-    dense = stack_rows(chosen, parts)
+    dense, dense_last = stack_rows(chosen, parts)
 
     halves = [history[i * half : (i + 1) * half] for i in range(PARTS)]
     moving = {(side, i): halves[i] for i in range(PARTS) for side in (1, 2)}
@@ -306,46 +306,50 @@
             out[side, i] = swap_walk(moving[3 - side, i], side)
         return out
 
+    def over_rows(keep, give, kind):
+        bit = 1
+        odd = list(give)
+        even = [keep[t] for t in range(row_count // 2)]
+        while True:
+            got = []
+            for x in odd:
+                got.append(across_rows(x, bit).astype(jnp.float32))
+            summed = [x + y for x, y in zip(even, got)]
+            if len(summed) == 1:
+                return summed[0]
+            bit *= 2
+            even, odd = summed[0::2], [x.astype(kind) for x in summed[1::2]]
+
     total = multiply(kernels, [(0, 1, i, x) for i, x in enumerate(halves)], None, None, None, 0)
     for step in range(1, final):
         turns = [turn(step, rank) for rank in range(2)]
         moving = turns[0] | turns[1]
         for rank in range(2):
             blocks = [(step, side, i, x) for (side, i), x in turns[rank].items()]
-            field = (incident[0], chosen) if (step, rank) == (final - 1, 1) else (None, None)
-            total = multiply(kernels, blocks, total, *field, 0)
-    blocks = [(final, 1, i, x) for (_, i), x in turn(final, 0).items()]
-    keep, *give = multiply(kernels, blocks, total, None, None, row_count)
-
-    bit = 1
-    summed = [keep[t] + across_rows(give[t], bit) for t in range(row_count // 2)]
-    while len(summed) > 1:
-        bit *= 2
-        summed = [summed[t] + across_rows(summed[t + 1], bit) for t in range(0, len(summed), 2)]
-    driven = -summed[0]
+            early = (step, rank) == (final - 1, 0)
+            field = (incident[0], chosen) if early else (None, None)
+            total = multiply(kernels, blocks, total, *field, row_count if early else 0)
+            if early:
+                early_sum = over_rows(total[0], total[1:], jnp.float32)
+                total = None
+    for i, ((_, part), x) in enumerate(reversed(turn(final, 0).items())):
+        total = multiply(kernels, [(final, 1, part, x)], total, None, None, i * row_count)
+    driven = -(over_rows(total[0], total[1:], jnp.bfloat16) + early_sum)
 
     density = driven
     rounded = density.astype(jnp.bfloat16)
     for step in range(SWEEPS):
         far_side, near_side = swap_cols(rounded, 2), swap_cols(rounded, 1)
-        base = steady(dense, driven, density, rounded, near_side)
-        result = sweep(dense, base, far_side, chosen if step == SWEEPS - 1 else None)
+        last = step == SWEEPS - 1
+        base = steady(dense, driven, density, rounded, near_side, chosen if last else None)
+        result = sweep(dense_last if last else dense, base, far_side, row_count if last else 0)
         if step < SWEEPS - 1:
             density, rounded = result
 
-    away, home = result
-    bit = row_count // 2
-    got = across_rows(away, bit)
-    sets = [((0,), home), ((bit,), got)]
-    while bit > 1:
-        bit //= 2
-        pieces_next = []
-        for offsets, array in sets:
-            pieces_next.append((offsets, array[:bit]))
-            sent = across_rows(array[bit : 2 * bit], bit)
-            pieces_next.append((tuple(o ^ bit for o in offsets), sent))
-        sets = pieces_next
-    return assemble([(offsets, array) for offsets, array in sets])
+    pieces = [result[0]]
+    for m in range(1, row_count):
+        pieces.append(across_rows(result[m], m))
+    return assemble(pieces)
 
 
 def solution(mesh):

time: 101 us -> 106 us (1.050)
  starting transfers between devices: 37.8 us -> 41.9 us
  local copies, waits for them, and re-layouts: 6.79 us -> 9.06 us
  waiting for transfers between devices: 41.7 us -> 39.8 us
    ppermute x14, waiting for transfers between devices: 14.6 us -> 10.9 us  [swap_walk(): lax.ppermute(x, 'col', [(walk[p], walk[mate(p, side, col_count)]) for p i...]
    ppermute x9 -> x12, waiting for transfers between devices: 18.9 us -> 21.8 us  [across_rows(): return lax.ppermute(x, 'row', [(i, i ^ m) for i in range(row_count)])]
    ppermute x9 -> x12, starting transfers between devices: 5.61 us -> 7.99 us  [across_rows(): return lax.ppermute(x, 'row', [(i, i ^ m) for i in range(row_count)])]
    unnamed x16, local copies, waits for them, and re-layouts: 5.64 us -> 7.97 us
    ppermute x6, starting transfers between devices: 10.6 us -> 12.2 us  [swap_cols(): lax.ppermute(x, 'col', [(c, mate(c, side, col_count)) for c in range(col_...]
    ppermute x6, waiting for transfers between devices: 8.23 us -> 7.1 us  [swap_cols(): lax.ppermute(x, 'col', [(c, mate(c, side, col_count)) for c in range(col_...]
    pallas_call x8 -> x9, Pallas kernels: 8.41 us -> 8.82 us  [multiply(): pl.pallas_call(body, out_shape=out_shape, in_specs=in_specs, out_specs=[V...]
  transfers between devices with their start and end apart: 29 -> 32, of which waited for: 16 -> 15; matrix products, arithmetic and copies ran while one was open for 0% -> 0% of each run, Pallas kernels for 10% -> 12%
where the time goes in v4:
time: 106 us
  starting transfers between devices  41.9 us (40%)
  waiting for transfers between devices  39.8 us (38%)
  Pallas kernels  14.4 us (14%)
  local copies, waits for them, and re-layouts  9.06 us (9%)
    ppermute x12, waiting for transfers between devices, across_rows(): return lax.ppermute(x, 'row', [(i, i ^ m) for i in range(row_count)])  21.8 us
    ppermute x14, starting transfers between devices, swap_walk(): lax.ppermute(x, 'col', [(walk[p], walk[mate(p, side, col_count)]) for p i...  21.7 us
    ppermute x6, starting transfers between devices, swap_cols(): lax.ppermute(x, 'col', [(c, mate(c, side, col_count)) for c in range(col_...  12.2 us
    ppermute x14, waiting for transfers between devices, swap_walk(): lax.ppermute(x, 'col', [(walk[p], walk[mate(p, side, col_count)]) for p i...  10.9 us
    pallas_call x9, Pallas kernels, multiply(): pl.pallas_call(body, out_shape=out_shape, in_specs=in_specs, out_specs=[V...  8.82 us
    ppermute x12, starting transfers between devices, across_rows(): return lax.ppermute(x, 'row', [(i, i ^ m) for i in range(row_count)])  7.99 us
    unnamed x16, local copies, waits for them, and re-layouts  7.97 us
    ppermute x6, waiting for transfers between devices, swap_cols(): lax.ppermute(x, 'col', [(c, mate(c, side, col_count)) for c in range(col_...  7.1 us
  transfers between devices with their start and end apart: 32, of which 15 were waited for; matrix products, arithmetic and copies ran while one was open for 0% of the time, Pallas kernels for 12%

profile of v4, /device:TPU:0, one launch (start us, length us, event | category | flops | bytes accessed | tf_op | source)
XLA Modules:
  0.0 106.1 jit_solution(9440679482081811766)
XLA Ops:
  1.1 3.1 %collective-permute-start.7 = (bf16[3,192,256]{2,1,0:T(8,128)(2,1)S(1)}, bf16[3,192,256]{2,1,0:T(8,128)(2,1)S(1)}, u32[]{:S(2)}, u32[]{:S(2)}) collective-permute-start(bf16[3,192,256]{2,1,0:T(8,128)(2,1)S(1)} %get-tuple-element.43.refs_1_), channel_id=1, source_target_pairs={{0,2},{2,0},{4,6},{6,4},{7,5},{5,7},{3,1},{1,3},{8,10},{10,8},{12,... | collective-permute-start | bytes 884744 | tf_op jit(solution)/shard_map/ppermute | solution.py:287
  4.2 1.5 %collective-permute-start.3 = (bf16[3,192,256]{2,1,0:T(8,128)(2,1)S(1)}, bf16[3,192,256]{2,1,0:T(8,128)(2,1)S(1)}, u32[]{:S(2)}, u32[]{:S(2)}) collective-permute-start(bf16[3,192,256]{2,1,0:T(8,128)(2,1)S(1)} %get-tuple-element.44.refs_0_), channel_id=1, source_target_pairs={{0,1},{2,4},{4,2},{6,7},{7,6},{5,3},{3,5},{1,0},{8,9},{10,12},{12,... | collective-permute-start | bytes 884744 | tf_op jit(solution)/shard_map/ppermute | solution.py:287
  5.7 1.7 %collective-permute-start.11 = (bf16[3,192,256]{2,1,0:T(8,128)(2,1)S(1)}, bf16[3,192,256]{2,1,0:T(8,128)(2,1)S(1)}, u32[]{:S(2)}, u32[]{:S(2)}) collective-permute-start(bf16[3,192,256]{2,1,0:T(8,128)(2,1)S(1)} %get-tuple-element.44.refs_0_), channel_id=1, source_target_pairs={{0,2},{2,0},{4,6},{6,4},{7,5},{5,7},{3,1},{1,3},{8,10},{10,8},{12,... | collective-permute-start | bytes 884744 | tf_op jit(solution)/shard_map/ppermute | solution.py:287
  7.4 1.5 %collective-permute-start.14 = (bf16[3,192,256]{2,1,0:T(8,128)(2,1)S(1)}, bf16[3,192,256]{2,1,0:T(8,128)(2,1)S(1)}, u32[]{:S(2)}, u32[]{:S(2)}) collective-permute-start(bf16[3,192,256]{2,1,0:T(8,128)(2,1)S(1)} %get-tuple-element.43.refs_1_), channel_id=1, source_target_pairs={{0,1},{2,4},{4,2},{6,7},{7,6},{5,3},{3,5},{1,0},{8,9},{10,12},{12,... | collective-permute-start | bytes 884744 | tf_op jit(solution)/shard_map/ppermute | solution.py:287
  8.9 3.2 %collective-permute-done.7.refs_1_ = bf16[3,192,256]{2,1,0:T(8,128)(2,1)S(1)} collective-permute-done((bf16[3,192,256]{2,1,0:T(8,128)(2,1)S(1)}, bf16[3,192,256]{2,1,0:T(8,128)(2,1)S(1)}, u32[]{:S(2)}, u32[]{:S(2)}) %collective-permute-start.7) | collective-permute-done | bytes 294944 | tf_op jit(solution)/shard_map/ppermute | solution.py:287
  12.1 1.9 %collective-permute-start.8 = (bf16[3,192,256]{2,1,0:T(8,128)(2,1)S(1)}, bf16[3,192,256]{2,1,0:T(8,128)(2,1)S(1)}, u32[]{:S(2)}, u32[]{:S(2)}) collective-permute-start(bf16[3,192,256]{2,1,0:T(8,128)(2,1)S(1)} %collective-permute-done.7.refs_1_), channel_id=1, source_target_pairs={{0,1},{2,4},{4,2},{6,7},{7,6},{5,3},{3,5},{1,0},{8,9},{10,12},{12,... | collective-permute-start | bytes 884744 | tf_op jit(solution)/shard_map/ppermute | solution.py:287
  14.1 1.6 %collective-permute-start.4 = (bf16[3,192,256]{2,1,0:T(8,128)(2,1)S(1)}, bf16[3,192,256]{2,1,0:T(8,128)(2,1)S(1)}, u32[]{:S(2)}, u32[]{:S(2)}) collective-permute-start(bf16[3,192,256]{2,1,0:T(8,128)(2,1)S(1)} %collective-permute-done.3.refs_0_), channel_id=1, source_target_pairs={{0,2},{2,0},{4,6},{6,4},{7,5},{5,7},{3,1},{1,3},{8,10},{10,8},{12,... | collective-permute-start | bytes 884744 | tf_op jit(solution)/shard_map/ppermute | solution.py:287
  15.7 2.7 %collective-permute-done.11.refs_0_ = bf16[3,192,256]{2,1,0:T(8,128)(2,1)S(1)} collective-permute-done((bf16[3,192,256]{2,1,0:T(8,128)(2,1)S(1)}, bf16[3,192,256]{2,1,0:T(8,128)(2,1)S(1)}, u32[]{:S(2)}, u32[]{:S(2)}) %collective-permute-start.11) | collective-permute-done | bytes 294944 | tf_op jit(solution)/shard_map/ppermute | solution.py:287
  18.4 1.9 %collective-permute-start.12 = (bf16[3,192,256]{2,1,0:T(8,128)(2,1)S(1)}, bf16[3,192,256]{2,1,0:T(8,128)(2,1)S(1)}, u32[]{:S(2)}, u32[]{:S(2)}) collective-permute-start(bf16[3,192,256]{2,1,0:T(8,128)(2,1)S(1)} %collective-permute-done.11.refs_0_), channel_id=1, source_target_pairs={{0,1},{2,4},{4,2},{6,7},{7,6},{5,3},{3,5},{1,0},{8,9},{10,12},{12,... | collective-permute-start | bytes 884744 | tf_op jit(solution)/shard_map/ppermute | solution.py:287
  20.4 1.6 %collective-permute-start.15 = (bf16[3,192,256]{2,1,0:T(8,128)(2,1)S(1)}, bf16[3,192,256]{2,1,0:T(8,128)(2,1)S(1)}, u32[]{:S(2)}, u32[]{:S(2)}) collective-permute-start(bf16[3,192,256]{2,1,0:T(8,128)(2,1)S(1)} %collective-permute-done.14.refs_1_), channel_id=1, source_target_pairs={{0,2},{2,0},{4,6},{6,4},{7,5},{5,7},{3,1},{1,3},{8,10},{10,8},{12,... | collective-permute-start | bytes 884744 | tf_op jit(solution)/shard_map/ppermute | solution.py:287
  22.0 4.7 %collective-permute-done.8.refs_1_ = bf16[3,192,256]{2,1,0:T(8,128)(2,1)S(1)} collective-permute-done((bf16[3,192,256]{2,1,0:T(8,128)(2,1)S(1)}, bf16[3,192,256]{2,1,0:T(8,128)(2,1)S(1)}, u32[]{:S(2)}, u32[]{:S(2)}) %collective-permute-start.8) | collective-permute-done | bytes 294944 | tf_op jit(solution)/shard_map/ppermute | solution.py:287
  26.7 1.1 %collective-permute-start.9 = (bf16[3,192,256]{2,1,0:T(8,128)(2,1)S(1)}, bf16[3,192,256]{2,1,0:T(8,128)(2,1)S(1)}, u32[]{:S(2)}, u32[]{:S(2)}) collective-permute-start(bf16[3,192,256]{2,1,0:T(8,128)(2,1)S(1)} %collective-permute-done.8.refs_1_), channel_id=1, source_target_pairs={{0,2},{2,0},{4,6},{6,4},{7,5},{5,7},{3,1},{1,3},{8,10},{10,8},{12,... | collective-permute-start | bytes 884744 | tf_op jit(solution)/shard_map/ppermute | solution.py:287
  27.9 1.5 %collective-permute-start.5 = (bf16[3,192,256]{2,1,0:T(8,128)(2,1)S(1)}, bf16[3,192,256]{2,1,0:T(8,128)(2,1)S(1)}, u32[]{:S(2)}, u32[]{:S(2)}) collective-permute-start(bf16[3,192,256]{2,1,0:T(8,128)(2,1)S(1)} %collective-permute-done.4.refs_0_), channel_id=1, source_target_pairs={{0,1},{2,4},{4,2},{6,7},{7,6},{5,3},{3,5},{1,0},{8,9},{10,12},{12,... | collective-permute-start | bytes 884744 | tf_op jit(solution)/shard_map/ppermute | solution.py:287
  32.3 1.4 %prepare.1 = (s32[4]{0:T(128)S(1)}, bf16[128,1536]{1,0:T(8,128)(2,1)S(1)}) custom-call(s32[32]{0:T(128)S(1)} %copy-done.4, s32[2,12]{1,0:T(2,128)S(1)} %bitcast.27, s32[1]{0:T(128)S(6)} %copy.8.counts_ref, bf16[12,128,128]{2,1,0:T(8,128)(2,1)S(1)} %copy-done.1), custom_call_target="tpu_custom_call" | custom-call | bytes 786432 | tf_op jit(solution)/shard_map/prepare/pallas_call | solution.py:66
  33.7 3.7 %copy-done = bf16[6,512,1536]{2,1,0:T(8,128)(2,1)S(1)} copy-done((bf16[6,512,1536]{2,1,0:T(8,128)(2,1)S(1)}, bf16[6,512,1536]{2,1,0:T(8,128)(2,1)}, u32[]{:S(2)}) %copy-start) | copy-done | bytes 9437208
  39.4 1.5 %collective-permute-start.16 = (bf16[3,192,256]{2,1,0:T(8,128)(2,1)S(1)}, bf16[3,192,256]{2,1,0:T(8,128)(2,1)S(1)}, u32[]{:S(2)}, u32[]{:S(2)}) collective-permute-start(bf16[3,192,256]{2,1,0:T(8,128)(2,1)S(1)} %collective-permute-done.15.refs_1_), channel_id=1, source_target_pairs={{0,1},{2,4},{4,2},{6,7},{7,6},{5,3},{3,5},{1,0},{8,9},{10,12},{12,... | collective-permute-start | bytes 884744 | tf_op jit(solution)/shard_map/ppermute | solution.py:287
  42.5 1.1 %collective-permute-start.6 = (bf16[3,192,256]{2,1,0:T(8,128)(2,1)S(1)}, bf16[3,192,256]{2,1,0:T(8,128)(2,1)S(1)}, u32[]{:S(2)}, u32[]{:S(2)}) collective-permute-start(bf16[3,192,256]{2,1,0:T(8,128)(2,1)S(1)} %collective-permute-done.5.refs_0_), channel_id=1, source_target_pairs={{0,2},{2,0},{4,6},{6,4},{7,5},{5,7},{3,1},{1,3},{8,10},{10,8},{12,... | collective-permute-start | bytes 884744 | tf_op jit(solution)/shard_map/ppermute | solution.py:287
  46.8 1.3 %slice-done.1 = s8[4194304]{0:T(1024)(128)(4,1)S(1)} async-done(((s8[9437184]{0:T(1024)(128)(4,1)}), s8[4194304]{0:T(1024)(128)(4,1)S(1)}, s32[]{:S(2)}) %slice-start.1) | async-done | bytes 4194328
  48.5 1.8 %multiply.17 = (f32[2,64,512]{2,1,0:T(8,128)S(1)}, f32[64,512]{1,0:T(8,128)S(1)}, f32[64,512]{1,0:T(8,128)S(1)}) custom-call(bf16[6,512,1536]{2,1,0:T(8,128)(2,1)S(1)} %bitcast.25, bf16[3,192,256]{2,1,0:T(8,128)(2,1)S(1)} %collective-permute-done.5.refs_0_, bf16[3,192,256]{2,1,0:T(8,128)(2,1)S(1)} %collective-permute-done.9.refs_1_, ...), custom_call_target="tpu_custom_call" | custom-call | flops 603979776 | bytes 3538944 | tf_op jit(solution)/shard_map/multiply/pallas_call | solution.py:170
  50.9 1.5 %collective-permute-start.1 = (bf16[128,1536]{1,0:T(8,128)(2,1)S(1)}, bf16[128,1536]{1,0:T(8,128)(2,1)S(1)}, u32[]{:S(2)}, u32[]{:S(2)}) collective-permute-start(bf16[128,1536]{1,0:T(8,128)(2,1)S(1)} %get-tuple-element.24.refs_0_), channel_id=1, source_target_pairs={{0,16},{8,24},{16,0},{24,8},{1,17},{9,25},{17,1},{25,9},{2,18},{10... | collective-permute-start | bytes 1179656 | tf_op jit(solution)/shard_map/ppermute | solution.py:282
  55.7 1.5 %collective-permute-start.22 = (f32[64,512]{1,0:T(8,128)S(1)}, f32[64,512]{1,0:T(8,128)S(1)}, u32[]{:S(2)}, u32[]{:S(2)}) collective-permute-start(f32[64,512]{1,0:T(8,128)S(1)} %bitcast_add_fusion), channel_id=1, source_target_pairs={{0,16},{8,24},{16,0},{24,8},{1,17},{9,25},{17,1},{25,9},{2,18},{10... | collective-permute-start | bytes 393224 | tf_op jit(solution)/shard_map/ppermute | solution.py:282
  57.4 15.8 %collective-permute-done.22 = f32[64,512]{1,0:T(8,128)S(1)} collective-permute-done((f32[64,512]{1,0:T(8,128)S(1)}, f32[64,512]{1,0:T(8,128)S(1)}, u32[]{:S(2)}, u32[]{:S(2)}) %collective-permute-start.22) | collective-permute-done | bytes 131104 | tf_op jit(solution)/shard_map/ppermute | solution.py:282
  73.2 1.5 %collective-permute-start.19 = (bf16[64,512]{1,0:T(8,128)(2,1)S(1)}, bf16[64,512]{1,0:T(8,128)(2,1)S(1)}, u32[]{:S(2)}, u32[]{:S(2)}) collective-permute-start(bf16[64,512]{1,0:T(8,128)(2,1)S(1)} %fusion.3), channel_id=1, source_target_pairs={{0,16},{8,24},{16,0},{24,8},{1,17},{9,25},{17,1},{25,9},{2,18},{10... | collective-permute-start | bytes 196616 | tf_op jit(solution)/shard_map/ppermute | solution.py:282
  74.8 2.7 %collective-permute-done.19 = bf16[64,512]{1,0:T(8,128)(2,1)S(1)} collective-permute-done((bf16[64,512]{1,0:T(8,128)(2,1)S(1)}, bf16[64,512]{1,0:T(8,128)(2,1)S(1)}, u32[]{:S(2)}, u32[]{:S(2)}) %collective-permute-start.19) | collective-permute-done | bytes 65568 | tf_op jit(solution)/shard_map/ppermute | solution.py:282
  78.2 3.7 %collective-permute-start.24 = (bf16[64,512]{1,0:T(8,128)(2,1)S(1)}, bf16[64,512]{1,0:T(8,128)(2,1)S(1)}, u32[]{:S(2)}, u32[]{:S(2)}) collective-permute-start(bf16[64,512]{1,0:T(8,128)(2,1)S(1)} %get-tuple-element.41.refs_3_), channel_id=1, source_target_pairs={{0,7},{1,2},{2,1},{3,4},{4,3},{5,6},{6,5},{7,0},{8,15},{9,10},{10,... | collective-permute-start | bytes 196616 | tf_op jit(solution)/shard_map/ppermute | solution.py:290
  83.1 2.1 %collective-permute-done.24.side_ref = bf16[64,512]{1,0:T(8,128)(2,1)S(1)} collective-permute-done((bf16[64,512]{1,0:T(8,128)(2,1)S(1)}, bf16[64,512]{1,0:T(8,128)(2,1)S(1)}, u32[]{:S(2)}, u32[]{:S(2)}) %collective-permute-start.24) | collective-permute-done | bytes 65568 | tf_op jit(solution)/shard_map/ppermute | solution.py:290
  85.5 3.8 %collective-permute-start.26 = (bf16[64,512]{1,0:T(8,128)(2,1)S(1)}, bf16[64,512]{1,0:T(8,128)(2,1)S(1)}, u32[]{:S(2)}, u32[]{:S(2)}) collective-permute-start(bf16[64,512]{1,0:T(8,128)(2,1)S(1)} %get-tuple-element.34.refs_3_), channel_id=1, source_target_pairs={{0,7},{1,2},{2,1},{3,4},{4,3},{5,6},{6,5},{7,0},{8,15},{9,10},{10,... | collective-permute-start | bytes 196616 | tf_op jit(solution)/shard_map/ppermute | solution.py:290
  90.2 2.3 %collective-permute-done.26.side_ref = bf16[64,512]{1,0:T(8,128)(2,1)S(1)} collective-permute-done((bf16[64,512]{1,0:T(8,128)(2,1)S(1)}, bf16[64,512]{1,0:T(8,128)(2,1)S(1)}, u32[]{:S(2)}, u32[]{:S(2)}) %collective-permute-start.26) | collective-permute-done | bytes 65568 | tf_op jit(solution)/shard_map/ppermute | solution.py:290
  93.1 3.7 %collective-permute-start.28 = (bf16[64,512]{1,0:T(8,128)(2,1)S(1)}, bf16[64,512]{1,0:T(8,128)(2,1)S(1)}, u32[]{:S(2)}, u32[]{:S(2)}) collective-permute-start(bf16[64,512]{1,0:T(8,128)(2,1)S(1)} %get-tuple-element.36.refs_3_), channel_id=1, source_target_pairs={{0,7},{1,2},{2,1},{3,4},{4,3},{5,6},{6,5},{7,0},{8,15},{9,10},{10,... | collective-permute-start | bytes 196616 | tf_op jit(solution)/shard_map/ppermute | solution.py:290
  98.2 1.9 %collective-permute-done.28.side_ref = bf16[64,512]{1,0:T(8,128)(2,1)S(1)} collective-permute-done((bf16[64,512]{1,0:T(8,128)(2,1)S(1)}, bf16[64,512]{1,0:T(8,128)(2,1)S(1)}, u32[]{:S(2)}, u32[]{:S(2)}) %collective-permute-start.28) | collective-permute-done | bytes 65568 | tf_op jit(solution)/shard_map/ppermute | solution.py:290
  100.4 1.6 %collective-permute-start.30 = (f32[64,128]{1,0:T(8,128)S(1)}, f32[64,128]{1,0:T(8,128)S(1)}, u32[]{:S(2)}, u32[]{:S(2)}) collective-permute-start(f32[64,128]{1,0:T(8,128)S(1)} %get-tuple-element.39), channel_id=1, source_target_pairs={{0,16},{8,24},{16,0},{24,8},{1,17},{9,25},{17,1},{25,9},{2,18},{10... | collective-permute-start | bytes 98312 | tf_op jit(solution)/shard_map/ppermute | solution.py:282
  102.3 2.1 %collective-permute-done.30.refs_2_ = f32[64,128]{1,0:T(8,128)S(1)} collective-permute-done((f32[64,128]{1,0:T(8,128)S(1)}, f32[64,128]{1,0:T(8,128)S(1)}, u32[]{:S(2)}, u32[]{:S(2)}) %collective-permute-start.30) | collective-permute-done | bytes 32800 | tf_op jit(solution)/shard_map/ppermute | solution.py:282
  (71 shorter events, 22.0 us)
Async XLA Ops:
  1.1 11.0 %collective-permute-start.7 = (bf16[3,192,256]{2,1,0:T(8,128)(2,1)S(1)}, bf16[3,192,256]{2,1,0:T(8,128)(2,1)S(1)}, u32[]{:S(2)}, u32[]{:S(2)}) collective-permute-start(bf16[3,192,256]{2,1,0:T(8,128)(2,1)S(1)} %get-tuple-element.43.refs_1_), channel_id=1, source_target_pairs={{0,2},{2,0},{4,6},{6,4},{7,5},{5,7},{3,1},{1,3},{8,10},{10,8},{12,... | collective-permute-start | bytes 884744 | tf_op jit(solution)/shard_map/ppermute | solution.py:287
  4.2 9.9 %collective-permute-start.3 = (bf16[3,192,256]{2,1,0:T(8,128)(2,1)S(1)}, bf16[3,192,256]{2,1,0:T(8,128)(2,1)S(1)}, u32[]{:S(2)}, u32[]{:S(2)}) collective-permute-start(bf16[3,192,256]{2,1,0:T(8,128)(2,1)S(1)} %get-tuple-element.44.refs_0_), channel_id=1, source_target_pairs={{0,1},{2,4},{4,2},{6,7},{7,6},{5,3},{3,5},{1,0},{8,9},{10,12},{12,... | collective-permute-start | bytes 884744 | tf_op jit(solution)/shard_map/ppermute | solution.py:287
  5.7 12.7 %collective-permute-start.11 = (bf16[3,192,256]{2,1,0:T(8,128)(2,1)S(1)}, bf16[3,192,256]{2,1,0:T(8,128)(2,1)S(1)}, u32[]{:S(2)}, u32[]{:S(2)}) collective-permute-start(bf16[3,192,256]{2,1,0:T(8,128)(2,1)S(1)} %get-tuple-element.44.refs_0_), channel_id=1, source_target_pairs={{0,2},{2,0},{4,6},{6,4},{7,5},{5,7},{3,1},{1,3},{8,10},{10,8},{12,... | collective-permute-start | bytes 884744 | tf_op jit(solution)/shard_map/ppermute | solution.py:287
  7.4 13.0 %collective-permute-start.14 = (bf16[3,192,256]{2,1,0:T(8,128)(2,1)S(1)}, bf16[3,192,256]{2,1,0:T(8,128)(2,1)S(1)}, u32[]{:S(2)}, u32[]{:S(2)}) collective-permute-start(bf16[3,192,256]{2,1,0:T(8,128)(2,1)S(1)} %get-tuple-element.43.refs_1_), channel_id=1, source_target_pairs={{0,1},{2,4},{4,2},{6,7},{7,6},{5,3},{3,5},{1,0},{8,9},{10,12},{12,... | collective-permute-start | bytes 884744 | tf_op jit(solution)/shard_map/ppermute | solution.py:287
  12.1 14.7 %collective-permute-start.8 = (bf16[3,192,256]{2,1,0:T(8,128)(2,1)S(1)}, bf16[3,192,256]{2,1,0:T(8,128)(2,1)S(1)}, u32[]{:S(2)}, u32[]{:S(2)}) collective-permute-start(bf16[3,192,256]{2,1,0:T(8,128)(2,1)S(1)} %collective-permute-done.7.refs_1_), channel_id=1, source_target_pairs={{0,1},{2,4},{4,2},{6,7},{7,6},{5,3},{3,5},{1,0},{8,9},{10,12},{12,... | collective-permute-start | bytes 884744 | tf_op jit(solution)/shard_map/ppermute | solution.py:287
  14.1 13.8 %collective-permute-start.4 = (bf16[3,192,256]{2,1,0:T(8,128)(2,1)S(1)}, bf16[3,192,256]{2,1,0:T(8,128)(2,1)S(1)}, u32[]{:S(2)}, u32[]{:S(2)}) collective-permute-start(bf16[3,192,256]{2,1,0:T(8,128)(2,1)S(1)} %collective-permute-done.3.refs_0_), channel_id=1, source_target_pairs={{0,2},{2,0},{4,6},{6,4},{7,5},{5,7},{3,1},{1,3},{8,10},{10,8},{12,... | collective-permute-start | bytes 884744 | tf_op jit(solution)/shard_map/ppermute | solution.py:287
  18.4 20.0 %collective-permute-start.12 = (bf16[3,192,256]{2,1,0:T(8,128)(2,1)S(1)}, bf16[3,192,256]{2,1,0:T(8,128)(2,1)S(1)}, u32[]{:S(2)}, u32[]{:S(2)}) collective-permute-start(bf16[3,192,256]{2,1,0:T(8,128)(2,1)S(1)} %collective-permute-done.11.refs_0_), channel_id=1, source_target_pairs={{0,1},{2,4},{4,2},{6,7},{7,6},{5,3},{3,5},{1,0},{8,9},{10,12},{12,... | collective-permute-start | bytes 884744 | tf_op jit(solution)/shard_map/ppermute | solution.py:287
  20.4 19.0 %collective-permute-start.15 = (bf16[3,192,256]{2,1,0:T(8,128)(2,1)S(1)}, bf16[3,192,256]{2,1,0:T(8,128)(2,1)S(1)}, u32[]{:S(2)}, u32[]{:S(2)}) collective-permute-start(bf16[3,192,256]{2,1,0:T(8,128)(2,1)S(1)} %collective-permute-done.14.refs_1_), channel_id=1, source_target_pairs={{0,2},{2,0},{4,6},{6,4},{7,5},{5,7},{3,1},{1,3},{8,10},{10,8},{12,... | collective-permute-start | bytes 884744 | tf_op jit(solution)/shard_map/ppermute | solution.py:287
  26.7 15.2 %collective-permute-start.9 = (bf16[3,192,256]{2,1,0:T(8,128)(2,1)S(1)}, bf16[3,192,256]{2,1,0:T(8,128)(2,1)S(1)}, u32[]{:S(2)}, u32[]{:S(2)}) collective-permute-start(bf16[3,192,256]{2,1,0:T(8,128)(2,1)S(1)} %collective-permute-done.8.refs_1_), channel_id=1, source_target_pairs={{0,2},{2,0},{4,6},{6,4},{7,5},{5,7},{3,1},{1,3},{8,10},{10,8},{12,... | collective-permute-start | bytes 884744 | tf_op jit(solution)/shard_map/ppermute | solution.py:287
  27.9 14.6 %collective-permute-start.5 = (bf16[3,192,256]{2,1,0:T(8,128)(2,1)S(1)}, bf16[3,192,256]{2,1,0:T(8,128)(2,1)S(1)}, u32[]{:S(2)}, u32[]{:S(2)}) collective-permute-start(bf16[3,192,256]{2,1,0:T(8,128)(2,1)S(1)} %collective-permute-done.4.refs_0_), channel_id=1, source_target_pairs={{0,1},{2,4},{4,2},{6,7},{7,6},{5,3},{3,5},{1,0},{8,9},{10,12},{12,... | collective-permute-start | bytes 884744 | tf_op jit(solution)/shard_map/ppermute | solution.py:287
  38.4 12.0 %collective-permute-start.13 = (bf16[3,192,256]{2,1,0:T(8,128)(2,1)S(1)}, bf16[3,192,256]{2,1,0:T(8,128)(2,1)S(1)}, u32[]{:S(2)}, u32[]{:S(2)}) collective-permute-start(bf16[3,192,256]{2,1,0:T(8,128)(2,1)S(1)} %collective-permute-done.12.refs_0_), channel_id=1, source_target_pairs={{0,2},{2,0},{4,6},{6,4},{7,5},{5,7},{3,1},{1,3},{8,10},{10,8},{12,... | collective-permute-start | bytes 884744 | tf_op jit(solution)/shard_map/ppermute | solution.py:287
  39.4 11.5 %collective-permute-start.16 = (bf16[3,192,256]{2,1,0:T(8,128)(2,1)S(1)}, bf16[3,192,256]{2,1,0:T(8,128)(2,1)S(1)}, u32[]{:S(2)}, u32[]{:S(2)}) collective-permute-start(bf16[3,192,256]{2,1,0:T(8,128)(2,1)S(1)} %collective-permute-done.15.refs_1_), channel_id=1, source_target_pairs={{0,1},{2,4},{4,2},{6,7},{7,6},{5,3},{3,5},{1,0},{8,9},{10,12},{12,... | collective-permute-start | bytes 884744 | tf_op jit(solution)/shard_map/ppermute | solution.py:287
  41.9 11.5 %collective-permute-start.10 = (bf16[3,192,256]{2,1,0:T(8,128)(2,1)S(1)}, bf16[3,192,256]{2,1,0:T(8,128)(2,1)S(1)}, u32[]{:S(2)}, u32[]{:S(2)}) collective-permute-start(bf16[3,192,256]{2,1,0:T(8,128)(2,1)S(1)} %collective-permute-done.9.refs_1_), channel_id=1, source_target_pairs={{0,1},{2,4},{4,2},{6,7},{7,6},{5,3},{3,5},{1,0},{8,9},{10,12},{12,... | collective-permute-start | bytes 884744 | tf_op jit(solution)/shard_map/ppermute | solution.py:287
  42.5 11.6 %collective-permute-start.6 = (bf16[3,192,256]{2,1,0:T(8,128)(2,1)S(1)}, bf16[3,192,256]{2,1,0:T(8,128)(2,1)S(1)}, u32[]{:S(2)}, u32[]{:S(2)}) collective-permute-start(bf16[3,192,256]{2,1,0:T(8,128)(2,1)S(1)} %collective-permute-done.5.refs_0_), channel_id=1, source_target_pairs={{0,2},{2,0},{4,6},{6,4},{7,5},{5,7},{3,1},{1,3},{8,10},{10,8},{12,... | collective-permute-start | bytes 884744 | tf_op jit(solution)/shard_map/ppermute | solution.py:287
  50.3 5.1 %collective-permute-start.21 = (f32[64,512]{1,0:T(8,128)S(1)}, f32[64,512]{1,0:T(8,128)S(1)}, u32[]{:S(2)}, u32[]{:S(2)}) collective-permute-start(f32[64,512]{1,0:T(8,128)S(1)} %get-tuple-element.32), channel_id=1, source_target_pairs={{0,8},{8,0},{16,24},{24,16},{1,9},{9,1},{17,25},{25,17},{2,10},{10... | collective-permute-start | bytes 393224 | tf_op jit(solution)/shard_map/ppermute | solution.py:282
  50.4 31.5 %collective-permute-start = (bf16[128,1536]{1,0:T(8,128)(2,1)S(1)}, bf16[128,1536]{1,0:T(8,128)(2,1)S(1)}, u32[]{:S(2)}, u32[]{:S(2)}) collective-permute-start(bf16[128,1536]{1,0:T(8,128)(2,1)S(1)} %get-tuple-element.24.refs_0_), channel_id=1, source_target_pairs={{0,8},{8,0},{16,24},{24,16},{1,9},{9,1},{17,25},{25,17},{2,10},{10... | collective-permute-start | bytes 1179656 | tf_op jit(solution)/shard_map/ppermute | solution.py:282
  50.9 31.0 %collective-permute-start.1 = (bf16[128,1536]{1,0:T(8,128)(2,1)S(1)}, bf16[128,1536]{1,0:T(8,128)(2,1)S(1)}, u32[]{:S(2)}, u32[]{:S(2)}) collective-permute-start(bf16[128,1536]{1,0:T(8,128)(2,1)S(1)} %get-tuple-element.24.refs_0_), channel_id=1, source_target_pairs={{0,16},{8,24},{16,0},{24,8},{1,17},{9,25},{17,1},{25,9},{2,18},{10... | collective-permute-start | bytes 1179656 | tf_op jit(solution)/shard_map/ppermute | solution.py:282
  53.4 28.5 %collective-permute-start.2 = (bf16[128,1536]{1,0:T(8,128)(2,1)S(1)}, bf16[128,1536]{1,0:T(8,128)(2,1)S(1)}, u32[]{:S(2)}, u32[]{:S(2)}) collective-permute-start(bf16[128,1536]{1,0:T(8,128)(2,1)S(1)} %get-tuple-element.24.refs_0_), channel_id=1, source_target_pairs={{0,24},{8,16},{16,8},{24,0},{1,25},{9,17},{17,9},{25,1},{2,26},{10... | collective-permute-start | bytes 1179656 | tf_op jit(solution)/shard_map/ppermute | solution.py:282
  54.1 1.6 %collective-permute-start.20 = (f32[64,512]{1,0:T(8,128)S(1)}, f32[64,512]{1,0:T(8,128)S(1)}, u32[]{:S(2)}, u32[]{:S(2)}) collective-permute-start(f32[64,512]{1,0:T(8,128)S(1)} %get-tuple-element.31), channel_id=1, source_target_pairs={{0,8},{8,0},{16,24},{24,16},{1,9},{9,1},{17,25},{25,17},{2,10},{10... | collective-permute-start | bytes 393224 | tf_op jit(solution)/shard_map/ppermute | solution.py:282
  55.5 1.8 %collective-permute-start.18 = (f32[64,512]{1,0:T(8,128)S(1)}, f32[64,512]{1,0:T(8,128)S(1)}, u32[]{:S(2)}, u32[]{:S(2)}) collective-permute-start(f32[64,512]{1,0:T(8,128)S(1)} %get-tuple-element.29), channel_id=1, source_target_pairs={{0,8},{8,0},{16,24},{24,16},{1,9},{9,1},{17,25},{25,17},{2,10},{10... | collective-permute-start | bytes 393224 | tf_op jit(solution)/shard_map/ppermute | solution.py:282
  55.7 17.5 %collective-permute-start.22 = (f32[64,512]{1,0:T(8,128)S(1)}, f32[64,512]{1,0:T(8,128)S(1)}, u32[]{:S(2)}, u32[]{:S(2)}) collective-permute-start(f32[64,512]{1,0:T(8,128)S(1)} %bitcast_add_fusion), channel_id=1, source_target_pairs={{0,16},{8,24},{16,0},{24,8},{1,17},{9,25},{17,1},{25,9},{2,18},{10... | collective-permute-start | bytes 393224 | tf_op jit(solution)/shard_map/ppermute | solution.py:282
  57.3 17.5 %collective-permute-start.17 = (f32[64,512]{1,0:T(8,128)S(1)}, f32[64,512]{1,0:T(8,128)S(1)}, u32[]{:S(2)}, u32[]{:S(2)}) collective-permute-start(f32[64,512]{1,0:T(8,128)S(1)} %get-tuple-element.28), channel_id=1, source_target_pairs={{0,8},{8,0},{16,24},{24,16},{1,9},{9,1},{17,25},{25,17},{2,10},{10... | collective-permute-start | bytes 393224 | tf_op jit(solution)/shard_map/ppermute | solution.py:282
  73.2 4.3 %collective-permute-start.19 = (bf16[64,512]{1,0:T(8,128)(2,1)S(1)}, bf16[64,512]{1,0:T(8,128)(2,1)S(1)}, u32[]{:S(2)}, u32[]{:S(2)}) collective-permute-start(bf16[64,512]{1,0:T(8,128)(2,1)S(1)} %fusion.3), channel_id=1, source_target_pairs={{0,16},{8,24},{16,0},{24,8},{1,17},{9,25},{17,1},{25,9},{2,18},{10... | collective-permute-start | bytes 196616 | tf_op jit(solution)/shard_map/ppermute | solution.py:282
  77.6 5.0 %collective-permute-start.23 = (bf16[64,512]{1,0:T(8,128)(2,1)S(1)}, bf16[64,512]{1,0:T(8,128)(2,1)S(1)}, u32[]{:S(2)}, u32[]{:S(2)}) collective-permute-start(bf16[64,512]{1,0:T(8,128)(2,1)S(1)} %get-tuple-element.41.refs_3_), channel_id=1, source_target_pairs={{0,1},{1,0},{2,3},{3,2},{4,5},{5,4},{6,7},{7,6},{8,9},{9,8},{10,11... | collective-permute-start | bytes 196616 | tf_op jit(solution)/shard_map/ppermute | solution.py:290
  78.2 7.0 %collective-permute-start.24 = (bf16[64,512]{1,0:T(8,128)(2,1)S(1)}, bf16[64,512]{1,0:T(8,128)(2,1)S(1)}, u32[]{:S(2)}, u32[]{:S(2)}) collective-permute-start(bf16[64,512]{1,0:T(8,128)(2,1)S(1)} %get-tuple-element.41.refs_3_), channel_id=1, source_target_pairs={{0,7},{1,2},{2,1},{3,4},{4,3},{5,6},{6,5},{7,0},{8,15},{9,10},{10,... | collective-permute-start | bytes 196616 | tf_op jit(solution)/shard_map/ppermute | solution.py:290
  85.5 4.3 %collective-permute-start.25 = (bf16[64,512]{1,0:T(8,128)(2,1)S(1)}, bf16[64,512]{1,0:T(8,128)(2,1)S(1)}, u32[]{:S(2)}, u32[]{:S(2)}) collective-permute-start(bf16[64,512]{1,0:T(8,128)(2,1)S(1)} %get-tuple-element.34.refs_3_), channel_id=1, source_target_pairs={{0,1},{1,0},{2,3},{3,2},{4,5},{5,4},{6,7},{7,6},{8,9},{9,8},{10,11... | collective-permute-start | bytes 196616 | tf_op jit(solution)/shard_map/ppermute | solution.py:290
  85.5 7.0 %collective-permute-start.26 = (bf16[64,512]{1,0:T(8,128)(2,1)S(1)}, bf16[64,512]{1,0:T(8,128)(2,1)S(1)}, u32[]{:S(2)}, u32[]{:S(2)}) collective-permute-start(bf16[64,512]{1,0:T(8,128)(2,1)S(1)} %get-tuple-element.34.refs_3_), channel_id=1, source_target_pairs={{0,7},{1,2},{2,1},{3,4},{4,3},{5,6},{6,5},{7,0},{8,15},{9,10},{10,... | collective-permute-start | bytes 196616 | tf_op jit(solution)/shard_map/ppermute | solution.py:290
  92.8 4.3 %collective-permute-start.27 = (bf16[64,512]{1,0:T(8,128)(2,1)S(1)}, bf16[64,512]{1,0:T(8,128)(2,1)S(1)}, u32[]{:S(2)}, u32[]{:S(2)}) collective-permute-start(bf16[64,512]{1,0:T(8,128)(2,1)S(1)} %get-tuple-element.36.refs_3_), channel_id=1, source_target_pairs={{0,1},{1,0},{2,3},{3,2},{4,5},{5,4},{6,7},{7,6},{8,9},{9,8},{10,11... | collective-permute-start | bytes 196616 | tf_op jit(solution)/shard_map/ppermute | solution.py:290
  93.1 7.0 %collective-permute-start.28 = (bf16[64,512]{1,0:T(8,128)(2,1)S(1)}, bf16[64,512]{1,0:T(8,128)(2,1)S(1)}, u32[]{:S(2)}, u32[]{:S(2)}) collective-permute-start(bf16[64,512]{1,0:T(8,128)(2,1)S(1)} %get-tuple-element.36.refs_3_), channel_id=1, source_target_pairs={{0,7},{1,2},{2,1},{3,4},{4,3},{5,6},{6,5},{7,0},{8,15},{9,10},{10,... | collective-permute-start | bytes 196616 | tf_op jit(solution)/shard_map/ppermute | solution.py:290
  100.4 1.9 %collective-permute-start.29 = (f32[64,128]{1,0:T(8,128)S(1)}, f32[64,128]{1,0:T(8,128)S(1)}, u32[]{:S(2)}, u32[]{:S(2)}) collective-permute-start(f32[64,128]{1,0:T(8,128)S(1)} %get-tuple-element.38), channel_id=1, source_target_pairs={{0,8},{8,0},{16,24},{24,16},{1,9},{9,1},{17,25},{25,17},{2,10},{10... | collective-permute-start | bytes 98312 | tf_op jit(solution)/shard_map/ppermute | solution.py:282
  100.4 4.0 %collective-permute-start.30 = (f32[64,128]{1,0:T(8,128)S(1)}, f32[64,128]{1,0:T(8,128)S(1)}, u32[]{:S(2)}, u32[]{:S(2)}) collective-permute-start(f32[64,128]{1,0:T(8,128)S(1)} %get-tuple-element.39), channel_id=1, source_target_pairs={{0,16},{8,24},{16,0},{24,8},{1,17},{9,25},{17,1},{25,9},{2,18},{10... | collective-permute-start | bytes 98312 | tf_op jit(solution)/shard_map/ppermute | solution.py:282
  102.0 3.4 %collective-permute-start.31 = (f32[64,128]{1,0:T(8,128)S(1)}, f32[64,128]{1,0:T(8,128)S(1)}, u32[]{:S(2)}, u32[]{:S(2)}) collective-permute-start(f32[64,128]{1,0:T(8,128)S(1)} %get-tuple-element.40), channel_id=1, source_target_pairs={{0,24},{8,16},{16,8},{24,0},{1,25},{9,17},{17,9},{25,1},{2,26},{10... | collective-permute-start | bytes 98312 | tf_op jit(solution)/shard_map/ppermute | solution.py:282
  (8 other events, 18.1 us)

commit v5 on v4

--- a/solution.py
+++ b/solution.py
@@ -310,15 +310,20 @@
         bit = 1
         odd = list(give)
         even = [keep[t] for t in range(row_count // 2)]
+        lost = []
         while True:
             got = []
-            for x in odd:
-                got.append(across_rows(x, bit).astype(jnp.float32))
+            for t, x in enumerate(odd):
+                near = x
+                if bit > 1 and kind != x.dtype:
+                    near = lax.reduce_precision(x, jnp.finfo(kind).nexp, jnp.finfo(kind).nmant)
+                    lost.append(((2 * t + 1) * bit, (x - near).astype(kind)))
+                got.append(across_rows(near.astype(kind if bit > 1 else x.dtype), bit).astype(x.dtype))
             summed = [x + y for x, y in zip(even, got)]
             if len(summed) == 1:
-                return summed[0]
+                return summed[0], lost
             bit *= 2
-            even, odd = summed[0::2], [x.astype(kind) for x in summed[1::2]]
+            even, odd = summed[0::2], summed[1::2]
 
     total = multiply(kernels, [(0, 1, i, x) for i, x in enumerate(halves)], None, None, None, 0)
     for step in range(1, final):
@@ -326,21 +331,22 @@
         moving = turns[0] | turns[1]
         for rank in range(2):
             blocks = [(step, side, i, x) for (side, i), x in turns[rank].items()]
-            early = (step, rank) == (final - 1, 0)
-            field = (incident[0], chosen) if early else (None, None)
-            total = multiply(kernels, blocks, total, *field, row_count if early else 0)
-            if early:
-                early_sum = over_rows(total[0], total[1:], jnp.float32)
-                total = None
+            field = (incident[0], chosen) if (step, rank) == (final - 1, 0) else (None, None)
+            total = multiply(kernels, blocks, total, *field, 0)
     for i, ((_, part), x) in enumerate(reversed(turn(final, 0).items())):
         total = multiply(kernels, [(final, 1, part, x)], total, None, None, i * row_count)
-    driven = -(over_rows(total[0], total[1:], jnp.bfloat16) + early_sum)
+    summed, lost = over_rows(total[0], total[1:], jnp.bfloat16)
+    driven = -summed
 
     density = driven
     rounded = density.astype(jnp.bfloat16)
     for step in range(SWEEPS):
         far_side, near_side = swap_cols(rounded, 2), swap_cols(rounded, 1)
         last = step == SWEEPS - 1
+        if step == 0:
+            rest = sum(across_rows(x, m).astype(jnp.float32) for m, x in lost)
+        if step == 1:
+            driven, density = driven - rest, density - rest
         base = steady(dense, driven, density, rounded, near_side, chosen if last else None)
         result = sweep(dense_last if last else dense, base, far_side, row_count if last else 0)
         if step < SWEEPS - 1:

time: 106 us -> 105 us (level)
  waiting for transfers between devices: 39.8 us -> 44.4 us
  starting transfers between devices: 41.9 us -> 38.4 us
  local copies, waits for them, and re-layouts: 9.06 us -> 6.8 us
    ppermute x14, waiting for transfers between devices: 10.9 us -> 14.6 us  [swap_walk(): lax.ppermute(x, 'col', [(walk[p], walk[mate(p, side, col_count)]) for p i...]
    ppermute x6, starting transfers between devices: 12.2 us -> 9.11 us  [swap_cols(): lax.ppermute(x, 'col', [(c, mate(c, side, col_count)) for c in range(col_...]
    ppermute x6, waiting for transfers between devices: 7.1 us -> 9.59 us  [swap_cols(): lax.ppermute(x, 'col', [(c, mate(c, side, col_count)) for c in range(col_...]
    unnamed x16, local copies, waits for them, and re-layouts: 7.97 us -> 5.66 us
    ppermute x12 -> x10, waiting for transfers between devices: 21.8 us -> 20.3 us  [across_rows(): return lax.ppermute(x, 'row', [(i, i ^ m) for i in range(row_count)])]
    ppermute x12 -> x10, starting transfers between devices: 7.99 us -> 7.73 us  [across_rows(): return lax.ppermute(x, 'row', [(i, i ^ m) for i in range(row_count)])]
  transfers between devices with their start and end apart: 32 -> 30, of which waited for: 15 -> 14; matrix products, arithmetic and copies ran while one was open for 0% -> 0% of each run, Pallas kernels for 12% -> 12%
where the time goes in v5:
time: 105 us
  waiting for transfers between devices  44.4 us (42%)
  starting transfers between devices  38.4 us (37%)
  Pallas kernels  14.1 us (13%)
  local copies, waits for them, and re-layouts  6.8 us (6%)
    ppermute x14, starting transfers between devices, swap_walk(): lax.ppermute(x, 'col', [(walk[p], walk[mate(p, side, col_count)]) for p i...  21.6 us
    ppermute x10, waiting for transfers between devices, across_rows(): return lax.ppermute(x, 'row', [(i, i ^ m) for i in range(row_count)])  20.3 us
    ppermute x14, waiting for transfers between devices, swap_walk(): lax.ppermute(x, 'col', [(walk[p], walk[mate(p, side, col_count)]) for p i...  14.6 us
    ppermute x6, waiting for transfers between devices, swap_cols(): lax.ppermute(x, 'col', [(c, mate(c, side, col_count)) for c in range(col_...  9.59 us
    ppermute x6, starting transfers between devices, swap_cols(): lax.ppermute(x, 'col', [(c, mate(c, side, col_count)) for c in range(col_...  9.11 us
    pallas_call x9, Pallas kernels, multiply(): pl.pallas_call(body, out_shape=out_shape, in_specs=in_specs, out_specs=[V...  8.57 us
    ppermute x10, starting transfers between devices, across_rows(): return lax.ppermute(x, 'row', [(i, i ^ m) for i in range(row_count)])  7.73 us
    unnamed x16, local copies, waits for them, and re-layouts  5.66 us
  transfers between devices with their start and end apart: 30, of which 14 were waited for; matrix products, arithmetic and copies ran while one was open for 0% of the time, Pallas kernels for 12%

profile of v5, /device:TPU:0, one launch (start us, length us, event | category | flops | bytes accessed | tf_op | source)
XLA Modules:
  0.0 104.8 jit_solution(5698979763401294968)
XLA Ops:
  1.2 3.1 %collective-permute-start.7 = (bf16[3,192,256]{2,1,0:T(8,128)(2,1)S(1)}, bf16[3,192,256]{2,1,0:T(8,128)(2,1)S(1)}, u32[]{:S(2)}, u32[]{:S(2)}) collective-permute-start(bf16[3,192,256]{2,1,0:T(8,128)(2,1)S(1)} %get-tuple-element.37.refs_1_), channel_id=1, source_target_pairs={{0,2},{2,0},{4,6},{6,4},{7,5},{5,7},{3,1},{1,3},{8,10},{10,8},{12,... | collective-permute-start | bytes 884744 | tf_op jit(solution)/shard_map/ppermute | solution.py:287
  4.3 1.5 %collective-permute-start.3 = (bf16[3,192,256]{2,1,0:T(8,128)(2,1)S(1)}, bf16[3,192,256]{2,1,0:T(8,128)(2,1)S(1)}, u32[]{:S(2)}, u32[]{:S(2)}) collective-permute-start(bf16[3,192,256]{2,1,0:T(8,128)(2,1)S(1)} %get-tuple-element.38.refs_0_), channel_id=1, source_target_pairs={{0,1},{2,4},{4,2},{6,7},{7,6},{5,3},{3,5},{1,0},{8,9},{10,12},{12,... | collective-permute-start | bytes 884744 | tf_op jit(solution)/shard_map/ppermute | solution.py:287
  5.8 1.7 %collective-permute-start.11 = (bf16[3,192,256]{2,1,0:T(8,128)(2,1)S(1)}, bf16[3,192,256]{2,1,0:T(8,128)(2,1)S(1)}, u32[]{:S(2)}, u32[]{:S(2)}) collective-permute-start(bf16[3,192,256]{2,1,0:T(8,128)(2,1)S(1)} %get-tuple-element.38.refs_0_), channel_id=1, source_target_pairs={{0,2},{2,0},{4,6},{6,4},{7,5},{5,7},{3,1},{1,3},{8,10},{10,8},{12,... | collective-permute-start | bytes 884744 | tf_op jit(solution)/shard_map/ppermute | solution.py:287
  7.4 1.5 %collective-permute-start.14 = (bf16[3,192,256]{2,1,0:T(8,128)(2,1)S(1)}, bf16[3,192,256]{2,1,0:T(8,128)(2,1)S(1)}, u32[]{:S(2)}, u32[]{:S(2)}) collective-permute-start(bf16[3,192,256]{2,1,0:T(8,128)(2,1)S(1)} %get-tuple-element.37.refs_1_), channel_id=1, source_target_pairs={{0,1},{2,4},{4,2},{6,7},{7,6},{5,3},{3,5},{1,0},{8,9},{10,12},{12,... | collective-permute-start | bytes 884744 | tf_op jit(solution)/shard_map/ppermute | solution.py:287
  8.9 3.2 %collective-permute-done.7.refs_1_ = bf16[3,192,256]{2,1,0:T(8,128)(2,1)S(1)} collective-permute-done((bf16[3,192,256]{2,1,0:T(8,128)(2,1)S(1)}, bf16[3,192,256]{2,1,0:T(8,128)(2,1)S(1)}, u32[]{:S(2)}, u32[]{:S(2)}) %collective-permute-start.7) | collective-permute-done | bytes 294944 | tf_op jit(solution)/shard_map/ppermute | solution.py:287
  12.1 1.9 %collective-permute-start.8 = (bf16[3,192,256]{2,1,0:T(8,128)(2,1)S(1)}, bf16[3,192,256]{2,1,0:T(8,128)(2,1)S(1)}, u32[]{:S(2)}, u32[]{:S(2)}) collective-permute-start(bf16[3,192,256]{2,1,0:T(8,128)(2,1)S(1)} %collective-permute-done.7.refs_1_), channel_id=1, source_target_pairs={{0,1},{2,4},{4,2},{6,7},{7,6},{5,3},{3,5},{1,0},{8,9},{10,12},{12,... | collective-permute-start | bytes 884744 | tf_op jit(solution)/shard_map/ppermute | solution.py:287
  14.2 1.6 %collective-permute-start.4 = (bf16[3,192,256]{2,1,0:T(8,128)(2,1)S(1)}, bf16[3,192,256]{2,1,0:T(8,128)(2,1)S(1)}, u32[]{:S(2)}, u32[]{:S(2)}) collective-permute-start(bf16[3,192,256]{2,1,0:T(8,128)(2,1)S(1)} %collective-permute-done.3.refs_0_), channel_id=1, source_target_pairs={{0,2},{2,0},{4,6},{6,4},{7,5},{5,7},{3,1},{1,3},{8,10},{10,8},{12,... | collective-permute-start | bytes 884744 | tf_op jit(solution)/shard_map/ppermute | solution.py:287
  15.7 2.7 %collective-permute-done.11.refs_0_ = bf16[3,192,256]{2,1,0:T(8,128)(2,1)S(1)} collective-permute-done((bf16[3,192,256]{2,1,0:T(8,128)(2,1)S(1)}, bf16[3,192,256]{2,1,0:T(8,128)(2,1)S(1)}, u32[]{:S(2)}, u32[]{:S(2)}) %collective-permute-start.11) | collective-permute-done | bytes 294944 | tf_op jit(solution)/shard_map/ppermute | solution.py:287
  18.5 1.9 %collective-permute-start.12 = (bf16[3,192,256]{2,1,0:T(8,128)(2,1)S(1)}, bf16[3,192,256]{2,1,0:T(8,128)(2,1)S(1)}, u32[]{:S(2)}, u32[]{:S(2)}) collective-permute-start(bf16[3,192,256]{2,1,0:T(8,128)(2,1)S(1)} %collective-permute-done.11.refs_0_), channel_id=1, source_target_pairs={{0,1},{2,4},{4,2},{6,7},{7,6},{5,3},{3,5},{1,0},{8,9},{10,12},{12,... | collective-permute-start | bytes 884744 | tf_op jit(solution)/shard_map/ppermute | solution.py:287
  20.5 1.6 %collective-permute-start.15 = (bf16[3,192,256]{2,1,0:T(8,128)(2,1)S(1)}, bf16[3,192,256]{2,1,0:T(8,128)(2,1)S(1)}, u32[]{:S(2)}, u32[]{:S(2)}) collective-permute-start(bf16[3,192,256]{2,1,0:T(8,128)(2,1)S(1)} %collective-permute-done.14.refs_1_), channel_id=1, source_target_pairs={{0,2},{2,0},{4,6},{6,4},{7,5},{5,7},{3,1},{1,3},{8,10},{10,8},{12,... | collective-permute-start | bytes 884744 | tf_op jit(solution)/shard_map/ppermute | solution.py:287
  22.1 4.7 %collective-permute-done.8.refs_1_ = bf16[3,192,256]{2,1,0:T(8,128)(2,1)S(1)} collective-permute-done((bf16[3,192,256]{2,1,0:T(8,128)(2,1)S(1)}, bf16[3,192,256]{2,1,0:T(8,128)(2,1)S(1)}, u32[]{:S(2)}, u32[]{:S(2)}) %collective-permute-start.8) | collective-permute-done | bytes 294944 | tf_op jit(solution)/shard_map/ppermute | solution.py:287
  27.9 1.5 %collective-permute-start.5 = (bf16[3,192,256]{2,1,0:T(8,128)(2,1)S(1)}, bf16[3,192,256]{2,1,0:T(8,128)(2,1)S(1)}, u32[]{:S(2)}, u32[]{:S(2)}) collective-permute-start(bf16[3,192,256]{2,1,0:T(8,128)(2,1)S(1)} %collective-permute-done.4.refs_0_), channel_id=1, source_target_pairs={{0,1},{2,4},{4,2},{6,7},{7,6},{5,3},{3,5},{1,0},{8,9},{10,12},{12,... | collective-permute-start | bytes 884744 | tf_op jit(solution)/shard_map/ppermute | solution.py:287
  29.4 3.7 %collective-permute-done.12.refs_0_ = bf16[3,192,256]{2,1,0:T(8,128)(2,1)S(1)} collective-permute-done((bf16[3,192,256]{2,1,0:T(8,128)(2,1)S(1)}, bf16[3,192,256]{2,1,0:T(8,128)(2,1)S(1)}, u32[]{:S(2)}, u32[]{:S(2)}) %collective-permute-start.12) | collective-permute-done | bytes 294944 | tf_op jit(solution)/shard_map/ppermute | solution.py:287
  34.2 1.5 %collective-permute-start.16 = (bf16[3,192,256]{2,1,0:T(8,128)(2,1)S(1)}, bf16[3,192,256]{2,1,0:T(8,128)(2,1)S(1)}, u32[]{:S(2)}, u32[]{:S(2)}) collective-permute-start(bf16[3,192,256]{2,1,0:T(8,128)(2,1)S(1)} %collective-permute-done.15.refs_1_), channel_id=1, source_target_pairs={{0,1},{2,4},{4,2},{6,7},{7,6},{5,3},{3,5},{1,0},{8,9},{10,12},{12,... | collective-permute-start | bytes 884744 | tf_op jit(solution)/shard_map/ppermute | solution.py:287
  35.7 3.7 %copy-done = bf16[6,512,1536]{2,1,0:T(8,128)(2,1)S(1)} copy-done((bf16[6,512,1536]{2,1,0:T(8,128)(2,1)S(1)}, bf16[6,512,1536]{2,1,0:T(8,128)(2,1)}, u32[]{:S(2)}) %copy-start) | copy-done | bytes 9437208
  41.0 1.4 %prepare.1 = (s32[4]{0:T(128)S(1)}, bf16[128,1536]{1,0:T(8,128)(2,1)S(1)}) custom-call(s32[32]{0:T(128)S(1)} %copy-done.4, s32[2,12]{1,0:T(2,128)S(1)} %bitcast.18, s32[1]{0:T(128)S(6)} %copy.8.counts_ref, bf16[12,128,128]{2,1,0:T(8,128)(2,1)S(1)} %copy-done.1), custom_call_target="tpu_custom_call" | custom-call | bytes 786432 | tf_op jit(solution)/shard_map/prepare/pallas_call | solution.py:66
  49.9 1.5 %multiply.14.refs_2_ = f32[512,256]{1,0:T(8,128)S(1)} custom-call(bf16[6,512,1536]{2,1,0:T(8,128)(2,1)S(1)} %bitcast.16, bf16[3,192,256]{2,1,0:T(8,128)(2,1)S(1)} %collective-permute-done.5.refs_0_, bf16[3,192,256]{2,1,0:T(8,128)(2,1)S(1)} %collective-permute-done.9.refs_1_, f32[512,256]{1,0:T(8,128)S(1)} %multiply.13.refs_2_, f32[128,256]{1,0:T(8,128)S(1)} %bitcast.17, ...), custom_call_target="tpu_custom_call" | custom-call | flops 603979776 | bytes 3538944 | tf_op jit(solution)/shard_map/multiply/pallas_call | solution.py:170
  54.3 1.5 %collective-permute-start.1 = (bf16[128,1536]{1,0:T(8,128)(2,1)S(1)}, bf16[128,1536]{1,0:T(8,128)(2,1)S(1)}, u32[]{:S(2)}, u32[]{:S(2)}) collective-permute-start(bf16[128,1536]{1,0:T(8,128)(2,1)S(1)} %get-tuple-element.21.refs_0_), channel_id=1, source_target_pairs={{0,16},{8,24},{16,0},{24,8},{1,17},{9,25},{17,1},{25,9},{2,18},{10... | collective-permute-start | bytes 1179656 | tf_op jit(solution)/shard_map/ppermute | solution.py:282
  56.5 1.6 %collective-permute-start.19 = (bf16[64,512]{1,0:T(8,128)(2,1)S(1)}, bf16[64,512]{1,0:T(8,128)(2,1)S(1)}, u32[]{:S(2)}, u32[]{:S(2)}) collective-permute-start(bf16[64,512]{1,0:T(8,128)(2,1)S(1)} %get-tuple-element.40), channel_id=1, source_target_pairs={{0,16},{8,24},{16,0},{24,8},{1,17},{9,25},{17,1},{25,9},{2,18},{10... | collective-permute-start | bytes 196616 | tf_op jit(solution)/shard_map/ppermute | solution.py:282
  58.1 17.2 %collective-permute-done.19 = bf16[64,512]{1,0:T(8,128)(2,1)S(1)} collective-permute-done((bf16[64,512]{1,0:T(8,128)(2,1)S(1)}, bf16[64,512]{1,0:T(8,128)(2,1)S(1)}, u32[]{:S(2)}, u32[]{:S(2)}) %collective-permute-start.19) | collective-permute-done | bytes 65568 | tf_op jit(solution)/shard_map/ppermute | solution.py:282
  75.3 1.6 %collective-permute-start.21 = (bf16[64,512]{1,0:T(8,128)(2,1)S(1)}, bf16[64,512]{1,0:T(8,128)(2,1)S(1)}, u32[]{:S(2)}, u32[]{:S(2)}) collective-permute-start(bf16[64,512]{1,0:T(8,128)(2,1)S(1)} %get-tuple-element.35.refs_3_), channel_id=1, source_target_pairs={{0,1},{1,0},{2,3},{3,2},{4,5},{5,4},{6,7},{7,6},{8,9},{9,8},{10,11... | collective-permute-start | bytes 196616 | tf_op jit(solution)/shard_map/ppermute | solution.py:290
  76.8 2.4 %collective-permute-start.22 = (bf16[64,512]{1,0:T(8,128)(2,1)S(1)}, bf16[64,512]{1,0:T(8,128)(2,1)S(1)}, u32[]{:S(2)}, u32[]{:S(2)}) collective-permute-start(bf16[64,512]{1,0:T(8,128)(2,1)S(1)} %get-tuple-element.35.refs_3_), channel_id=1, source_target_pairs={{0,7},{1,2},{2,1},{3,4},{4,3},{5,6},{6,5},{7,0},{8,15},{9,10},{10,... | collective-permute-start | bytes 196616 | tf_op jit(solution)/shard_map/ppermute | solution.py:290
  79.3 1.5 %collective-permute-start.20 = (bf16[64,512]{1,0:T(8,128)(2,1)S(1)}, bf16[64,512]{1,0:T(8,128)(2,1)S(1)}, u32[]{:S(2)}, u32[]{:S(2)}) collective-permute-start(bf16[64,512]{1,0:T(8,128)(2,1)S(1)} %get-tuple-element.39), channel_id=1, source_target_pairs={{0,16},{8,24},{16,0},{24,8},{1,17},{9,25},{17,1},{25,9},{2,18},{10... | collective-permute-start | bytes 196616 | tf_op jit(solution)/shard_map/ppermute | solution.py:282
  81.9 1.9 %collective-permute-done.22.side_ref = bf16[64,512]{1,0:T(8,128)(2,1)S(1)} collective-permute-done((bf16[64,512]{1,0:T(8,128)(2,1)S(1)}, bf16[64,512]{1,0:T(8,128)(2,1)S(1)}, u32[]{:S(2)}, u32[]{:S(2)}) %collective-permute-start.22) | collective-permute-done | bytes 65568 | tf_op jit(solution)/shard_map/ppermute | solution.py:290
  84.2 2.5 %collective-permute-start.24 = (bf16[64,512]{1,0:T(8,128)(2,1)S(1)}, bf16[64,512]{1,0:T(8,128)(2,1)S(1)}, u32[]{:S(2)}, u32[]{:S(2)}) collective-permute-start(bf16[64,512]{1,0:T(8,128)(2,1)S(1)} %get-tuple-element.28.refs_3_), channel_id=1, source_target_pairs={{0,7},{1,2},{2,1},{3,4},{4,3},{5,6},{6,5},{7,0},{8,15},{9,10},{10,... | collective-permute-start | bytes 196616 | tf_op jit(solution)/shard_map/ppermute | solution.py:290
  86.7 1.7 %collective-permute-done.23.refs_4_ = bf16[64,512]{1,0:T(8,128)(2,1)S(1)} collective-permute-done((bf16[64,512]{1,0:T(8,128)(2,1)S(1)}, bf16[64,512]{1,0:T(8,128)(2,1)S(1)}, u32[]{:S(2)}, u32[]{:S(2)}) %collective-permute-start.23) | collective-permute-done | bytes 65568 | tf_op jit(solution)/shard_map/ppermute | solution.py:290
  88.9 2.4 %collective-permute-done.24.side_ref = bf16[64,512]{1,0:T(8,128)(2,1)S(1)} collective-permute-done((bf16[64,512]{1,0:T(8,128)(2,1)S(1)}, bf16[64,512]{1,0:T(8,128)(2,1)S(1)}, u32[]{:S(2)}, u32[]{:S(2)}) %collective-permute-start.24) | collective-permute-done | bytes 65568 | tf_op jit(solution)/shard_map/ppermute | solution.py:290
  91.7 2.4 %collective-permute-start.26 = (bf16[64,512]{1,0:T(8,128)(2,1)S(1)}, bf16[64,512]{1,0:T(8,128)(2,1)S(1)}, u32[]{:S(2)}, u32[]{:S(2)}) collective-permute-start(bf16[64,512]{1,0:T(8,128)(2,1)S(1)} %get-tuple-element.30.refs_3_), channel_id=1, source_target_pairs={{0,7},{1,2},{2,1},{3,4},{4,3},{5,6},{6,5},{7,0},{8,15},{9,10},{10,... | collective-permute-start | bytes 196616 | tf_op jit(solution)/shard_map/ppermute | solution.py:290
  94.2 1.7 %collective-permute-done.25.refs_4_ = bf16[64,512]{1,0:T(8,128)(2,1)S(1)} collective-permute-done((bf16[64,512]{1,0:T(8,128)(2,1)S(1)}, bf16[64,512]{1,0:T(8,128)(2,1)S(1)}, u32[]{:S(2)}, u32[]{:S(2)}) %collective-permute-start.25) | collective-permute-done | bytes 65568 | tf_op jit(solution)/shard_map/ppermute | solution.py:290
  96.9 1.8 %collective-permute-done.26.side_ref = bf16[64,512]{1,0:T(8,128)(2,1)S(1)} collective-permute-done((bf16[64,512]{1,0:T(8,128)(2,1)S(1)}, bf16[64,512]{1,0:T(8,128)(2,1)S(1)}, u32[]{:S(2)}, u32[]{:S(2)}) %collective-permute-start.26) | collective-permute-done | bytes 65568 | tf_op jit(solution)/shard_map/ppermute | solution.py:290
  99.1 1.6 %collective-permute-start.28 = (f32[64,128]{1,0:T(8,128)S(1)}, f32[64,128]{1,0:T(8,128)S(1)}, u32[]{:S(2)}, u32[]{:S(2)}) collective-permute-start(f32[64,128]{1,0:T(8,128)S(1)} %get-tuple-element.33), channel_id=1, source_target_pairs={{0,16},{8,24},{16,0},{24,8},{1,17},{9,25},{17,1},{25,9},{2,18},{10... | collective-permute-start | bytes 98312 | tf_op jit(solution)/shard_map/ppermute | solution.py:282
  100.9 2.1 %collective-permute-done.28.refs_2_ = f32[64,128]{1,0:T(8,128)S(1)} collective-permute-done((f32[64,128]{1,0:T(8,128)S(1)}, f32[64,128]{1,0:T(8,128)S(1)}, u32[]{:S(2)}, u32[]{:S(2)}) %collective-permute-start.28) | collective-permute-done | bytes 32800 | tf_op jit(solution)/shard_map/ppermute | solution.py:282
  (67 shorter events, 21.2 us)
Async XLA Ops:
  0.0 41.0 %copy-start.4 = (s32[32]{0:T(128)S(1)}, s32[32]{0:T(128)}, u32[]{:S(2)}) copy-start(s32[32]{0:T(128)} %owner_ref.1) | copy-start | bytes 388
  0.0 41.0 %copy-start.1 = (bf16[12,128,128]{2,1,0:T(8,128)(2,1)S(1)}, bf16[12,128,128]{2,1,0:T(8,128)(2,1)}, u32[]{:S(2)}) copy-start(bf16[12,128,128]{2,1,0:T(8,128)(2,1)} %tile_ref.1) | copy-start | bytes 1179652
  1.2 11.0 %collective-permute-start.7 = (bf16[3,192,256]{2,1,0:T(8,128)(2,1)S(1)}, bf16[3,192,256]{2,1,0:T(8,128)(2,1)S(1)}, u32[]{:S(2)}, u32[]{:S(2)}) collective-permute-start(bf16[3,192,256]{2,1,0:T(8,128)(2,1)S(1)} %get-tuple-element.37.refs_1_), channel_id=1, source_target_pairs={{0,2},{2,0},{4,6},{6,4},{7,5},{5,7},{3,1},{1,3},{8,10},{10,8},{12,... | collective-permute-start | bytes 884744 | tf_op jit(solution)/shard_map/ppermute | solution.py:287
  4.3 9.9 %collective-permute-start.3 = (bf16[3,192,256]{2,1,0:T(8,128)(2,1)S(1)}, bf16[3,192,256]{2,1,0:T(8,128)(2,1)S(1)}, u32[]{:S(2)}, u32[]{:S(2)}) collective-permute-start(bf16[3,192,256]{2,1,0:T(8,128)(2,1)S(1)} %get-tuple-element.38.refs_0_), channel_id=1, source_target_pairs={{0,1},{2,4},{4,2},{6,7},{7,6},{5,3},{3,5},{1,0},{8,9},{10,12},{12,... | collective-permute-start | bytes 884744 | tf_op jit(solution)/shard_map/ppermute | solution.py:287
  5.8 12.7 %collective-permute-start.11 = (bf16[3,192,256]{2,1,0:T(8,128)(2,1)S(1)}, bf16[3,192,256]{2,1,0:T(8,128)(2,1)S(1)}, u32[]{:S(2)}, u32[]{:S(2)}) collective-permute-start(bf16[3,192,256]{2,1,0:T(8,128)(2,1)S(1)} %get-tuple-element.38.refs_0_), channel_id=1, source_target_pairs={{0,2},{2,0},{4,6},{6,4},{7,5},{5,7},{3,1},{1,3},{8,10},{10,8},{12,... | collective-permute-start | bytes 884744 | tf_op jit(solution)/shard_map/ppermute | solution.py:287
  7.4 13.0 %collective-permute-start.14 = (bf16[3,192,256]{2,1,0:T(8,128)(2,1)S(1)}, bf16[3,192,256]{2,1,0:T(8,128)(2,1)S(1)}, u32[]{:S(2)}, u32[]{:S(2)}) collective-permute-start(bf16[3,192,256]{2,1,0:T(8,128)(2,1)S(1)} %get-tuple-element.37.refs_1_), channel_id=1, source_target_pairs={{0,1},{2,4},{4,2},{6,7},{7,6},{5,3},{3,5},{1,0},{8,9},{10,12},{12,... | collective-permute-start | bytes 884744 | tf_op jit(solution)/shard_map/ppermute | solution.py:287
  12.1 14.7 %collective-permute-start.8 = (bf16[3,192,256]{2,1,0:T(8,128)(2,1)S(1)}, bf16[3,192,256]{2,1,0:T(8,128)(2,1)S(1)}, u32[]{:S(2)}, u32[]{:S(2)}) collective-permute-start(bf16[3,192,256]{2,1,0:T(8,128)(2,1)S(1)} %collective-permute-done.7.refs_1_), channel_id=1, source_target_pairs={{0,1},{2,4},{4,2},{6,7},{7,6},{5,3},{3,5},{1,0},{8,9},{10,12},{12,... | collective-permute-start | bytes 884744 | tf_op jit(solution)/shard_map/ppermute | solution.py:287
  14.2 13.8 %collective-permute-start.4 = (bf16[3,192,256]{2,1,0:T(8,128)(2,1)S(1)}, bf16[3,192,256]{2,1,0:T(8,128)(2,1)S(1)}, u32[]{:S(2)}, u32[]{:S(2)}) collective-permute-start(bf16[3,192,256]{2,1,0:T(8,128)(2,1)S(1)} %collective-permute-done.3.refs_0_), channel_id=1, source_target_pairs={{0,2},{2,0},{4,6},{6,4},{7,5},{5,7},{3,1},{1,3},{8,10},{10,8},{12,... | collective-permute-start | bytes 884744 | tf_op jit(solution)/shard_map/ppermute | solution.py:287
  18.5 14.7 %collective-permute-start.12 = (bf16[3,192,256]{2,1,0:T(8,128)(2,1)S(1)}, bf16[3,192,256]{2,1,0:T(8,128)(2,1)S(1)}, u32[]{:S(2)}, u32[]{:S(2)}) collective-permute-start(bf16[3,192,256]{2,1,0:T(8,128)(2,1)S(1)} %collective-permute-done.11.refs_0_), channel_id=1, source_target_pairs={{0,1},{2,4},{4,2},{6,7},{7,6},{5,3},{3,5},{1,0},{8,9},{10,12},{12,... | collective-permute-start | bytes 884744 | tf_op jit(solution)/shard_map/ppermute | solution.py:287
  20.5 13.8 %collective-permute-start.15 = (bf16[3,192,256]{2,1,0:T(8,128)(2,1)S(1)}, bf16[3,192,256]{2,1,0:T(8,128)(2,1)S(1)}, u32[]{:S(2)}, u32[]{:S(2)}) collective-permute-start(bf16[3,192,256]{2,1,0:T(8,128)(2,1)S(1)} %collective-permute-done.14.refs_1_), channel_id=1, source_target_pairs={{0,2},{2,0},{4,6},{6,4},{7,5},{5,7},{3,1},{1,3},{8,10},{10,8},{12,... | collective-permute-start | bytes 884744 | tf_op jit(solution)/shard_map/ppermute | solution.py:287
  26.8 15.6 %collective-permute-start.9 = (bf16[3,192,256]{2,1,0:T(8,128)(2,1)S(1)}, bf16[3,192,256]{2,1,0:T(8,128)(2,1)S(1)}, u32[]{:S(2)}, u32[]{:S(2)}) collective-permute-start(bf16[3,192,256]{2,1,0:T(8,128)(2,1)S(1)} %collective-permute-done.8.refs_1_), channel_id=1, source_target_pairs={{0,2},{2,0},{4,6},{6,4},{7,5},{5,7},{3,1},{1,3},{8,10},{10,8},{12,... | collective-permute-start | bytes 884744 | tf_op jit(solution)/shard_map/ppermute | solution.py:287
  27.9 16.1 %collective-permute-start.5 = (bf16[3,192,256]{2,1,0:T(8,128)(2,1)S(1)}, bf16[3,192,256]{2,1,0:T(8,128)(2,1)S(1)}, u32[]{:S(2)}, u32[]{:S(2)}) collective-permute-start(bf16[3,192,256]{2,1,0:T(8,128)(2,1)S(1)} %collective-permute-done.4.refs_0_), channel_id=1, source_target_pairs={{0,1},{2,4},{4,2},{6,7},{7,6},{5,3},{3,5},{1,0},{8,9},{10,12},{12,... | collective-permute-start | bytes 884744 | tf_op jit(solution)/shard_map/ppermute | solution.py:287
  33.1 18.3 %collective-permute-start.13 = (bf16[3,192,256]{2,1,0:T(8,128)(2,1)S(1)}, bf16[3,192,256]{2,1,0:T(8,128)(2,1)S(1)}, u32[]{:S(2)}, u32[]{:S(2)}) collective-permute-start(bf16[3,192,256]{2,1,0:T(8,128)(2,1)S(1)} %collective-permute-done.12.refs_0_), channel_id=1, source_target_pairs={{0,2},{2,0},{4,6},{6,4},{7,5},{5,7},{3,1},{1,3},{8,10},{10,8},{12,... | collective-permute-start | bytes 884744 | tf_op jit(solution)/shard_map/ppermute | solution.py:287
  34.2 17.2 %collective-permute-start.16 = (bf16[3,192,256]{2,1,0:T(8,128)(2,1)S(1)}, bf16[3,192,256]{2,1,0:T(8,128)(2,1)S(1)}, u32[]{:S(2)}, u32[]{:S(2)}) collective-permute-start(bf16[3,192,256]{2,1,0:T(8,128)(2,1)S(1)} %collective-permute-done.15.refs_1_), channel_id=1, source_target_pairs={{0,1},{2,4},{4,2},{6,7},{7,6},{5,3},{3,5},{1,0},{8,9},{10,12},{12,... | collective-permute-start | bytes 884744 | tf_op jit(solution)/shard_map/ppermute | solution.py:287
  42.4 10.0 %collective-permute-start.10 = (bf16[3,192,256]{2,1,0:T(8,128)(2,1)S(1)}, bf16[3,192,256]{2,1,0:T(8,128)(2,1)S(1)}, u32[]{:S(2)}, u32[]{:S(2)}) collective-permute-start(bf16[3,192,256]{2,1,0:T(8,128)(2,1)S(1)} %collective-permute-done.9.refs_1_), channel_id=1, source_target_pairs={{0,1},{2,4},{4,2},{6,7},{7,6},{5,3},{3,5},{1,0},{8,9},{10,12},{12,... | collective-permute-start | bytes 884744 | tf_op jit(solution)/shard_map/ppermute | solution.py:287
  44.0 9.0 %collective-permute-start.6 = (bf16[3,192,256]{2,1,0:T(8,128)(2,1)S(1)}, bf16[3,192,256]{2,1,0:T(8,128)(2,1)S(1)}, u32[]{:S(2)}, u32[]{:S(2)}) collective-permute-start(bf16[3,192,256]{2,1,0:T(8,128)(2,1)S(1)} %collective-permute-done.5.refs_0_), channel_id=1, source_target_pairs={{0,2},{2,0},{4,6},{6,4},{7,5},{5,7},{3,1},{1,3},{8,10},{10,8},{12,... | collective-permute-start | bytes 884744 | tf_op jit(solution)/shard_map/ppermute | solution.py:287
  53.7 2.7 %collective-permute-start.18 = (f32[64,512]{1,0:T(8,128)S(1)}, f32[64,512]{1,0:T(8,128)S(1)}, u32[]{:S(2)}, u32[]{:S(2)}) collective-permute-start(f32[64,512]{1,0:T(8,128)S(1)} %get-tuple-element.26), channel_id=1, source_target_pairs={{0,8},{8,0},{16,24},{24,16},{1,9},{9,1},{17,25},{25,17},{2,10},{10... | collective-permute-start | bytes 393224 | tf_op jit(solution)/shard_map/ppermute | solution.py:282
  53.8 25.4 %collective-permute-start = (bf16[128,1536]{1,0:T(8,128)(2,1)S(1)}, bf16[128,1536]{1,0:T(8,128)(2,1)S(1)}, u32[]{:S(2)}, u32[]{:S(2)}) collective-permute-start(bf16[128,1536]{1,0:T(8,128)(2,1)S(1)} %get-tuple-element.21.refs_0_), channel_id=1, source_target_pairs={{0,8},{8,0},{16,24},{24,16},{1,9},{9,1},{17,25},{25,17},{2,10},{10... | collective-permute-start | bytes 1179656 | tf_op jit(solution)/shard_map/ppermute | solution.py:282
  54.3 26.5 %collective-permute-start.1 = (bf16[128,1536]{1,0:T(8,128)(2,1)S(1)}, bf16[128,1536]{1,0:T(8,128)(2,1)S(1)}, u32[]{:S(2)}, u32[]{:S(2)}) collective-permute-start(bf16[128,1536]{1,0:T(8,128)(2,1)S(1)} %get-tuple-element.21.refs_0_), channel_id=1, source_target_pairs={{0,16},{8,24},{16,0},{24,8},{1,17},{9,25},{17,1},{25,9},{2,18},{10... | collective-permute-start | bytes 1179656 | tf_op jit(solution)/shard_map/ppermute | solution.py:282
  55.8 25.0 %collective-permute-start.2 = (bf16[128,1536]{1,0:T(8,128)(2,1)S(1)}, bf16[128,1536]{1,0:T(8,128)(2,1)S(1)}, u32[]{:S(2)}, u32[]{:S(2)}) collective-permute-start(bf16[128,1536]{1,0:T(8,128)(2,1)S(1)} %get-tuple-element.21.refs_0_), channel_id=1, source_target_pairs={{0,24},{8,16},{16,8},{24,0},{1,25},{9,17},{17,9},{25,1},{2,26},{10... | collective-permute-start | bytes 1179656 | tf_op jit(solution)/shard_map/ppermute | solution.py:282
  55.8 2.2 %collective-permute-start.17 = (f32[64,512]{1,0:T(8,128)S(1)}, f32[64,512]{1,0:T(8,128)S(1)}, u32[]{:S(2)}, u32[]{:S(2)}) collective-permute-start(f32[64,512]{1,0:T(8,128)S(1)} %get-tuple-element.25), channel_id=1, source_target_pairs={{0,8},{8,0},{16,24},{24,16},{1,9},{9,1},{17,25},{25,17},{2,10},{10... | collective-permute-start | bytes 393224 | tf_op jit(solution)/shard_map/ppermute | solution.py:282
  56.5 18.8 %collective-permute-start.19 = (bf16[64,512]{1,0:T(8,128)(2,1)S(1)}, bf16[64,512]{1,0:T(8,128)(2,1)S(1)}, u32[]{:S(2)}, u32[]{:S(2)}) collective-permute-start(bf16[64,512]{1,0:T(8,128)(2,1)S(1)} %get-tuple-element.40), channel_id=1, source_target_pairs={{0,16},{8,24},{16,0},{24,8},{1,17},{9,25},{17,1},{25,9},{2,18},{10... | collective-permute-start | bytes 196616 | tf_op jit(solution)/shard_map/ppermute | solution.py:282
  75.3 6.2 %collective-permute-start.21 = (bf16[64,512]{1,0:T(8,128)(2,1)S(1)}, bf16[64,512]{1,0:T(8,128)(2,1)S(1)}, u32[]{:S(2)}, u32[]{:S(2)}) collective-permute-start(bf16[64,512]{1,0:T(8,128)(2,1)S(1)} %get-tuple-element.35.refs_3_), channel_id=1, source_target_pairs={{0,1},{1,0},{2,3},{3,2},{4,5},{5,4},{6,7},{7,6},{8,9},{9,8},{10,11... | collective-permute-start | bytes 196616 | tf_op jit(solution)/shard_map/ppermute | solution.py:290
  76.8 7.0 %collective-permute-start.22 = (bf16[64,512]{1,0:T(8,128)(2,1)S(1)}, bf16[64,512]{1,0:T(8,128)(2,1)S(1)}, u32[]{:S(2)}, u32[]{:S(2)}) collective-permute-start(bf16[64,512]{1,0:T(8,128)(2,1)S(1)} %get-tuple-element.35.refs_3_), channel_id=1, source_target_pairs={{0,7},{1,2},{2,1},{3,4},{4,3},{5,6},{6,5},{7,0},{8,15},{9,10},{10,... | collective-permute-start | bytes 196616 | tf_op jit(solution)/shard_map/ppermute | solution.py:290
  79.3 7.4 %collective-permute-start.20 = (bf16[64,512]{1,0:T(8,128)(2,1)S(1)}, bf16[64,512]{1,0:T(8,128)(2,1)S(1)}, u32[]{:S(2)}, u32[]{:S(2)}) collective-permute-start(bf16[64,512]{1,0:T(8,128)(2,1)S(1)} %get-tuple-element.39), channel_id=1, source_target_pairs={{0,16},{8,24},{16,0},{24,8},{1,17},{9,25},{17,1},{25,9},{2,18},{10... | collective-permute-start | bytes 196616 | tf_op jit(solution)/shard_map/ppermute | solution.py:282
  84.1 4.3 %collective-permute-start.23 = (bf16[64,512]{1,0:T(8,128)(2,1)S(1)}, bf16[64,512]{1,0:T(8,128)(2,1)S(1)}, u32[]{:S(2)}, u32[]{:S(2)}) collective-permute-start(bf16[64,512]{1,0:T(8,128)(2,1)S(1)} %get-tuple-element.28.refs_3_), channel_id=1, source_target_pairs={{0,1},{1,0},{2,3},{3,2},{4,5},{5,4},{6,7},{7,6},{8,9},{9,8},{10,11... | collective-permute-start | bytes 196616 | tf_op jit(solution)/shard_map/ppermute | solution.py:290
  84.2 7.1 %collective-permute-start.24 = (bf16[64,512]{1,0:T(8,128)(2,1)S(1)}, bf16[64,512]{1,0:T(8,128)(2,1)S(1)}, u32[]{:S(2)}, u32[]{:S(2)}) collective-permute-start(bf16[64,512]{1,0:T(8,128)(2,1)S(1)} %get-tuple-element.28.refs_3_), channel_id=1, source_target_pairs={{0,7},{1,2},{2,1},{3,4},{4,3},{5,6},{6,5},{7,0},{8,15},{9,10},{10,... | collective-permute-start | bytes 196616 | tf_op jit(solution)/shard_map/ppermute | solution.py:290
  91.6 4.3 %collective-permute-start.25 = (bf16[64,512]{1,0:T(8,128)(2,1)S(1)}, bf16[64,512]{1,0:T(8,128)(2,1)S(1)}, u32[]{:S(2)}, u32[]{:S(2)}) collective-permute-start(bf16[64,512]{1,0:T(8,128)(2,1)S(1)} %get-tuple-element.30.refs_3_), channel_id=1, source_target_pairs={{0,1},{1,0},{2,3},{3,2},{4,5},{5,4},{6,7},{7,6},{8,9},{9,8},{10,11... | collective-permute-start | bytes 196616 | tf_op jit(solution)/shard_map/ppermute | solution.py:290
  91.7 7.0 %collective-permute-start.26 = (bf16[64,512]{1,0:T(8,128)(2,1)S(1)}, bf16[64,512]{1,0:T(8,128)(2,1)S(1)}, u32[]{:S(2)}, u32[]{:S(2)}) collective-permute-start(bf16[64,512]{1,0:T(8,128)(2,1)S(1)} %get-tuple-element.30.refs_3_), channel_id=1, source_target_pairs={{0,7},{1,2},{2,1},{3,4},{4,3},{5,6},{6,5},{7,0},{8,15},{9,10},{10,... | collective-permute-start | bytes 196616 | tf_op jit(solution)/shard_map/ppermute | solution.py:290
  99.0 1.9 %collective-permute-start.27 = (f32[64,128]{1,0:T(8,128)S(1)}, f32[64,128]{1,0:T(8,128)S(1)}, u32[]{:S(2)}, u32[]{:S(2)}) collective-permute-start(f32[64,128]{1,0:T(8,128)S(1)} %get-tuple-element.32), channel_id=1, source_target_pairs={{0,8},{8,0},{16,24},{24,16},{1,9},{9,1},{17,25},{25,17},{2,10},{10... | collective-permute-start | bytes 98312 | tf_op jit(solution)/shard_map/ppermute | solution.py:282
  99.1 4.0 %collective-permute-start.28 = (f32[64,128]{1,0:T(8,128)S(1)}, f32[64,128]{1,0:T(8,128)S(1)}, u32[]{:S(2)}, u32[]{:S(2)}) collective-permute-start(f32[64,128]{1,0:T(8,128)S(1)} %get-tuple-element.33), channel_id=1, source_target_pairs={{0,16},{8,24},{16,0},{24,8},{1,17},{9,25},{17,1},{25,9},{2,18},{10... | collective-permute-start | bytes 98312 | tf_op jit(solution)/shard_map/ppermute | solution.py:282
  100.7 3.4 %collective-permute-start.29 = (f32[64,128]{1,0:T(8,128)S(1)}, f32[64,128]{1,0:T(8,128)S(1)}, u32[]{:S(2)}, u32[]{:S(2)}) collective-permute-start(f32[64,128]{1,0:T(8,128)S(1)} %get-tuple-element.34), channel_id=1, source_target_pairs={{0,24},{8,16},{16,8},{24,0},{1,25},{9,17},{17,9},{25,1},{2,26},{10... | collective-permute-start | bytes 98312 | tf_op jit(solution)/shard_map/ppermute | solution.py:282
  (6 other events, 56.7 us)

commit v6 on v5

--- a/solution.py
+++ b/solution.py
@@ -1,3 +1,5 @@
+import math
+
 import jax
 import jax.numpy as jnp
 from jax import lax
@@ -108,7 +110,7 @@
     cols = lax.axis_size("col")
     count = len(blocks)
     lags, depth, columns = blocks[0][3].shape
-    tall = -(-(depth + LANES - 1) // LANES) * LANES
+    tall = -(-(depth + LANES - math.gcd(depth, LANES)) // LANES) * LANES
     extra = ([] if seed is None else [seed]) + ([] if incident is None else [incident, chosen])
 
     def body(kernel_ref, *refs):
@@ -331,12 +333,16 @@
         moving = turns[0] | turns[1]
         for rank in range(2):
             blocks = [(step, side, i, x) for (side, i), x in turns[rank].items()]
-            field = (incident[0], chosen) if (step, rank) == (final - 1, 0) else (None, None)
-            total = multiply(kernels, blocks, total, *field, 0)
+            early = (step, rank) == (final - 1, 0)
+            field = (incident[0], chosen) if early else (None, None)
+            total = multiply(kernels, blocks, total, *field, row_count if early else 0)
+            if early:
+                early_sum, _ = over_rows(total[0], total[1:], jnp.float32)
+                total = None
     for i, ((_, part), x) in enumerate(reversed(turn(final, 0).items())):
         total = multiply(kernels, [(final, 1, part, x)], total, None, None, i * row_count)
-    summed, lost = over_rows(total[0], total[1:], jnp.bfloat16)
-    driven = -summed
+    late_sum, lost = over_rows(total[0], total[1:], jnp.bfloat16)
+    driven = -(late_sum + early_sum)
 
     density = driven
     rounded = density.astype(jnp.bfloat16)

time: 105 us -> 111 us (1.057)
  waiting for transfers between devices: 44.4 us -> 49.7 us
  starting transfers between devices: 38.4 us -> 40.9 us
  Pallas kernels: 14.1 us -> 12 us
    ppermute x10 -> x13, waiting for transfers between devices: 20.3 us -> 22.5 us  [across_rows(): return lax.ppermute(x, 'row', [(i, i ^ m) for i in range(row_count)])]
    ppermute x14, starting transfers between devices: 21.6 us -> 23.7 us  [swap_walk(): lax.ppermute(x, 'col', [(walk[p], walk[mate(p, side, col_count)]) for p i...]
    pallas_call x9, Pallas kernels: 8.57 us -> 6.49 us  [multiply(): pl.pallas_call(body, out_shape=out_shape, in_specs=in_specs, out_specs=[V...]
    ppermute x10 -> x13, starting transfers between devices: 7.73 us -> 9.49 us  [across_rows(): return lax.ppermute(x, 'row', [(i, i ^ m) for i in range(row_count)])]
    ppermute x14, waiting for transfers between devices: 14.6 us -> 16.2 us  [swap_walk(): lax.ppermute(x, 'col', [(walk[p], walk[mate(p, side, col_count)]) for p i...]
    ppermute x6, starting transfers between devices: 9.11 us -> 7.7 us  [swap_cols(): lax.ppermute(x, 'col', [(c, mate(c, side, col_count)) for c in range(col_...]
    ppermute x6, waiting for transfers between devices: 9.59 us -> 11 us  [swap_cols(): lax.ppermute(x, 'col', [(c, mate(c, side, col_count)) for c in range(col_...]
  transfers between devices with their start and end apart: 30 -> 33, of which waited for: 14 -> 17; matrix products, arithmetic and copies ran while one was open for 0% -> 0% of each run, Pallas kernels for 12% -> 10%
where the time goes in v6:
time: 111 us
  waiting for transfers between devices  49.7 us (45%)
  starting transfers between devices  40.9 us (37%)
  Pallas kernels  12 us (11%)
  local copies, waits for them, and re-layouts  7.34 us (7%)
    ppermute x14, starting transfers between devices, swap_walk(): lax.ppermute(x, 'col', [(walk[p], walk[mate(p, side, col_count)]) for p i...  23.7 us
    ppermute x13, waiting for transfers between devices, across_rows(): return lax.ppermute(x, 'row', [(i, i ^ m) for i in range(row_count)])  22.5 us
    ppermute x14, waiting for transfers between devices, swap_walk(): lax.ppermute(x, 'col', [(walk[p], walk[mate(p, side, col_count)]) for p i...  16.2 us
    ppermute x6, waiting for transfers between devices, swap_cols(): lax.ppermute(x, 'col', [(c, mate(c, side, col_count)) for c in range(col_...  11 us
    ppermute x13, starting transfers between devices, across_rows(): return lax.ppermute(x, 'row', [(i, i ^ m) for i in range(row_count)])  9.49 us
    ppermute x6, starting transfers between devices, swap_cols(): lax.ppermute(x, 'col', [(c, mate(c, side, col_count)) for c in range(col_...  7.7 us
    pallas_call x9, Pallas kernels, multiply(): pl.pallas_call(body, out_shape=out_shape, in_specs=in_specs, out_specs=[V...  6.49 us
    unnamed x16, local copies, waits for them, and re-layouts  6.2 us
  transfers between devices with their start and end apart: 33, of which 17 were waited for; matrix products, arithmetic and copies ran while one was open for 0% of the time, Pallas kernels for 10%

profile of v6, /device:TPU:0, one launch (start us, length us, event | category | flops | bytes accessed | tf_op | source)
XLA Modules:
  0.0 111.0 jit_solution(13013964338222687484)
XLA Ops:
  1.2 3.1 %collective-permute-start.7 = (bf16[3,192,256]{2,1,0:T(8,128)(2,1)S(1)}, bf16[3,192,256]{2,1,0:T(8,128)(2,1)S(1)}, u32[]{:S(2)}, u32[]{:S(2)}) collective-permute-start(bf16[3,192,256]{2,1,0:T(8,128)(2,1)S(1)} %get-tuple-element.43.refs_1_), channel_id=1, source_target_pairs={{0,2},{2,0},{4,6},{6,4},{7,5},{5,7},{3,1},{1,3},{8,10},{10,8},{12,... | collective-permute-start | bytes 884744 | tf_op jit(solution)/shard_map/ppermute | solution.py:289
  5.8 1.7 %collective-permute-start.11 = (bf16[3,192,256]{2,1,0:T(8,128)(2,1)S(1)}, bf16[3,192,256]{2,1,0:T(8,128)(2,1)S(1)}, u32[]{:S(2)}, u32[]{:S(2)}) collective-permute-start(bf16[3,192,256]{2,1,0:T(8,128)(2,1)S(1)} %get-tuple-element.44.refs_0_), channel_id=1, source_target_pairs={{0,2},{2,0},{4,6},{6,4},{7,5},{5,7},{3,1},{1,3},{8,10},{10,8},{12,... | collective-permute-start | bytes 884744 | tf_op jit(solution)/shard_map/ppermute | solution.py:289
  8.9 3.2 %collective-permute-done.7.refs_1_ = bf16[3,192,256]{2,1,0:T(8,128)(2,1)S(1)} collective-permute-done((bf16[3,192,256]{2,1,0:T(8,128)(2,1)S(1)}, bf16[3,192,256]{2,1,0:T(8,128)(2,1)S(1)}, u32[]{:S(2)}, u32[]{:S(2)}) %collective-permute-start.7) | collective-permute-done | bytes 294944 | tf_op jit(solution)/shard_map/ppermute | solution.py:289
  12.1 1.9 %collective-permute-start.8 = (bf16[3,192,256]{2,1,0:T(8,128)(2,1)S(1)}, bf16[3,192,256]{2,1,0:T(8,128)(2,1)S(1)}, u32[]{:S(2)}, u32[]{:S(2)}) collective-permute-start(bf16[3,192,256]{2,1,0:T(8,128)(2,1)S(1)} %collective-permute-done.7.refs_1_), channel_id=1, source_target_pairs={{0,1},{2,4},{4,2},{6,7},{7,6},{5,3},{3,5},{1,0},{8,9},{10,12},{12,... | collective-permute-start | bytes 884744 | tf_op jit(solution)/shard_map/ppermute | solution.py:289
  14.2 1.6 %collective-permute-start.4 = (bf16[3,192,256]{2,1,0:T(8,128)(2,1)S(1)}, bf16[3,192,256]{2,1,0:T(8,128)(2,1)S(1)}, u32[]{:S(2)}, u32[]{:S(2)}) collective-permute-start(bf16[3,192,256]{2,1,0:T(8,128)(2,1)S(1)} %collective-permute-done.3.refs_0_), channel_id=1, source_target_pairs={{0,2},{2,0},{4,6},{6,4},{7,5},{5,7},{3,1},{1,3},{8,10},{10,8},{12,... | collective-permute-start | bytes 884744 | tf_op jit(solution)/shard_map/ppermute | solution.py:289
  15.7 2.7 %collective-permute-done.11.refs_0_ = bf16[3,192,256]{2,1,0:T(8,128)(2,1)S(1)} collective-permute-done((bf16[3,192,256]{2,1,0:T(8,128)(2,1)S(1)}, bf16[3,192,256]{2,1,0:T(8,128)(2,1)S(1)}, u32[]{:S(2)}, u32[]{:S(2)}) %collective-permute-start.11) | collective-permute-done | bytes 294944 | tf_op jit(solution)/shard_map/ppermute | solution.py:289
  18.5 1.9 %collective-permute-start.12 = (bf16[3,192,256]{2,1,0:T(8,128)(2,1)S(1)}, bf16[3,192,256]{2,1,0:T(8,128)(2,1)S(1)}, u32[]{:S(2)}, u32[]{:S(2)}) collective-permute-start(bf16[3,192,256]{2,1,0:T(8,128)(2,1)S(1)} %collective-permute-done.11.refs_0_), channel_id=1, source_target_pairs={{0,1},{2,4},{4,2},{6,7},{7,6},{5,3},{3,5},{1,0},{8,9},{10,12},{12,... | collective-permute-start | bytes 884744 | tf_op jit(solution)/shard_map/ppermute | solution.py:289
  20.5 1.6 %collective-permute-start.15 = (bf16[3,192,256]{2,1,0:T(8,128)(2,1)S(1)}, bf16[3,192,256]{2,1,0:T(8,128)(2,1)S(1)}, u32[]{:S(2)}, u32[]{:S(2)}) collective-permute-start(bf16[3,192,256]{2,1,0:T(8,128)(2,1)S(1)} %collective-permute-done.14.refs_1_), channel_id=1, source_target_pairs={{0,2},{2,0},{4,6},{6,4},{7,5},{5,7},{3,1},{1,3},{8,10},{10,8},{12,... | collective-permute-start | bytes 884744 | tf_op jit(solution)/shard_map/ppermute | solution.py:289
  22.1 4.7 %collective-permute-done.8.refs_1_ = bf16[3,192,256]{2,1,0:T(8,128)(2,1)S(1)} collective-permute-done((bf16[3,192,256]{2,1,0:T(8,128)(2,1)S(1)}, bf16[3,192,256]{2,1,0:T(8,128)(2,1)S(1)}, u32[]{:S(2)}, u32[]{:S(2)}) %collective-permute-start.8) | collective-permute-done | bytes 294944 | tf_op jit(solution)/shard_map/ppermute | solution.py:289
  27.9 1.5 %collective-permute-start.5 = (bf16[3,192,256]{2,1,0:T(8,128)(2,1)S(1)}, bf16[3,192,256]{2,1,0:T(8,128)(2,1)S(1)}, u32[]{:S(2)}, u32[]{:S(2)}) collective-permute-start(bf16[3,192,256]{2,1,0:T(8,128)(2,1)S(1)} %collective-permute-done.4.refs_0_), channel_id=1, source_target_pairs={{0,1},{2,4},{4,2},{6,7},{7,6},{5,3},{3,5},{1,0},{8,9},{10,12},{12,... | collective-permute-start | bytes 884744 | tf_op jit(solution)/shard_map/ppermute | solution.py:289
  29.4 3.7 %collective-permute-done.12.refs_0_ = bf16[3,192,256]{2,1,0:T(8,128)(2,1)S(1)} collective-permute-done((bf16[3,192,256]{2,1,0:T(8,128)(2,1)S(1)}, bf16[3,192,256]{2,1,0:T(8,128)(2,1)S(1)}, u32[]{:S(2)}, u32[]{:S(2)}) %collective-permute-start.12) | collective-permute-done | bytes 294944 | tf_op jit(solution)/shard_map/ppermute | solution.py:289
  35.7 1.7 %collective-permute-done.9.refs_1_ = bf16[3,192,256]{2,1,0:T(8,128)(2,1)S(1)} collective-permute-done((bf16[3,192,256]{2,1,0:T(8,128)(2,1)S(1)}, bf16[3,192,256]{2,1,0:T(8,128)(2,1)S(1)}, u32[]{:S(2)}, u32[]{:S(2)}) %collective-permute-start.9) | collective-permute-done | bytes 294944 | tf_op jit(solution)/shard_map/ppermute | solution.py:289
  37.4 1.9 %collective-permute-start.10 = (bf16[3,192,256]{2,1,0:T(8,128)(2,1)S(1)}, bf16[3,192,256]{2,1,0:T(8,128)(2,1)S(1)}, u32[]{:S(2)}, u32[]{:S(2)}) collective-permute-start(bf16[3,192,256]{2,1,0:T(8,128)(2,1)S(1)} %collective-permute-done.9.refs_1_), channel_id=1, source_target_pairs={{0,1},{2,4},{4,2},{6,7},{7,6},{5,3},{3,5},{1,0},{8,9},{10,12},{12,... | collective-permute-start | bytes 884744 | tf_op jit(solution)/shard_map/ppermute | solution.py:289
  39.3 3.7 %copy-done = bf16[6,512,1536]{2,1,0:T(8,128)(2,1)S(1)} copy-done((bf16[6,512,1536]{2,1,0:T(8,128)(2,1)S(1)}, bf16[6,512,1536]{2,1,0:T(8,128)(2,1)}, u32[]{:S(2)}) %copy-start) | copy-done | bytes 9437208
  45.8 1.7 %collective-permute-start.6 = (bf16[3,192,256]{2,1,0:T(8,128)(2,1)S(1)}, bf16[3,192,256]{2,1,0:T(8,128)(2,1)S(1)}, u32[]{:S(2)}, u32[]{:S(2)}) collective-permute-start(bf16[3,192,256]{2,1,0:T(8,128)(2,1)S(1)} %collective-permute-done.5.refs_0_), channel_id=1, source_target_pairs={{0,2},{2,0},{4,6},{6,4},{7,5},{5,7},{3,1},{1,3},{8,10},{10,8},{12,... | collective-permute-start | bytes 884744 | tf_op jit(solution)/shard_map/ppermute | solution.py:289
  54.8 1.5 %collective-permute-start.1 = (bf16[128,1536]{1,0:T(8,128)(2,1)S(1)}, bf16[128,1536]{1,0:T(8,128)(2,1)S(1)}, u32[]{:S(2)}, u32[]{:S(2)}) collective-permute-start(bf16[128,1536]{1,0:T(8,128)(2,1)S(1)} %get-tuple-element.24.refs_0_), channel_id=1, source_target_pairs={{0,16},{8,24},{16,0},{24,8},{1,17},{9,25},{17,1},{25,9},{2,18},{10... | collective-permute-start | bytes 1179656 | tf_op jit(solution)/shard_map/ppermute | solution.py:284
  59.2 1.5 %collective-permute-start.22 = (f32[64,512]{1,0:T(8,128)S(1)}, f32[64,512]{1,0:T(8,128)S(1)}, u32[]{:S(2)}, u32[]{:S(2)}) collective-permute-start(f32[64,512]{1,0:T(8,128)S(1)} %bitcast_add_fusion), channel_id=1, source_target_pairs={{0,16},{8,24},{16,0},{24,8},{1,17},{9,25},{17,1},{25,9},{2,18},{10... | collective-permute-start | bytes 393224 | tf_op jit(solution)/shard_map/ppermute | solution.py:284
  60.9 16.3 %collective-permute-done.22 = f32[64,512]{1,0:T(8,128)S(1)} collective-permute-done((f32[64,512]{1,0:T(8,128)S(1)}, f32[64,512]{1,0:T(8,128)S(1)}, u32[]{:S(2)}, u32[]{:S(2)}) %collective-permute-start.22) | collective-permute-done | bytes 131104 | tf_op jit(solution)/shard_map/ppermute | solution.py:284
  77.2 1.5 %collective-permute-start.19 = (bf16[64,512]{1,0:T(8,128)(2,1)S(1)}, bf16[64,512]{1,0:T(8,128)(2,1)S(1)}, u32[]{:S(2)}, u32[]{:S(2)}) collective-permute-start(bf16[64,512]{1,0:T(8,128)(2,1)S(1)} %get-tuple-element.46), channel_id=1, source_target_pairs={{0,16},{8,24},{16,0},{24,8},{1,17},{9,25},{17,1},{25,9},{2,18},{10... | collective-permute-start | bytes 196616 | tf_op jit(solution)/shard_map/ppermute | solution.py:284
  78.7 2.7 %collective-permute-done.19 = bf16[64,512]{1,0:T(8,128)(2,1)S(1)} collective-permute-done((bf16[64,512]{1,0:T(8,128)(2,1)S(1)}, bf16[64,512]{1,0:T(8,128)(2,1)S(1)}, u32[]{:S(2)}, u32[]{:S(2)}) %collective-permute-start.19) | collective-permute-done | bytes 65568 | tf_op jit(solution)/shard_map/ppermute | solution.py:284
  81.5 1.5 %collective-permute-start.24 = (bf16[64,512]{1,0:T(8,128)(2,1)S(1)}, bf16[64,512]{1,0:T(8,128)(2,1)S(1)}, u32[]{:S(2)}, u32[]{:S(2)}) collective-permute-start(bf16[64,512]{1,0:T(8,128)(2,1)S(1)} %get-tuple-element.41.refs_3_), channel_id=1, source_target_pairs={{0,1},{1,0},{2,3},{3,2},{4,5},{5,4},{6,7},{7,6},{8,9},{9,8},{10,11... | collective-permute-start | bytes 196616 | tf_op jit(solution)/shard_map/ppermute | solution.py:292
  83.1 1.9 %collective-permute-start.25 = (bf16[64,512]{1,0:T(8,128)(2,1)S(1)}, bf16[64,512]{1,0:T(8,128)(2,1)S(1)}, u32[]{:S(2)}, u32[]{:S(2)}) collective-permute-start(bf16[64,512]{1,0:T(8,128)(2,1)S(1)} %get-tuple-element.41.refs_3_), channel_id=1, source_target_pairs={{0,7},{1,2},{2,1},{3,4},{4,3},{5,6},{6,5},{7,0},{8,15},{9,10},{10,... | collective-permute-start | bytes 196616 | tf_op jit(solution)/shard_map/ppermute | solution.py:292
  85.0 1.5 %collective-permute-start.23 = (bf16[64,512]{1,0:T(8,128)(2,1)S(1)}, bf16[64,512]{1,0:T(8,128)(2,1)S(1)}, u32[]{:S(2)}, u32[]{:S(2)}) collective-permute-start(bf16[64,512]{1,0:T(8,128)(2,1)S(1)} %get-tuple-element.45), channel_id=1, source_target_pairs={{0,16},{8,24},{16,0},{24,8},{1,17},{9,25},{17,1},{25,9},{2,18},{10... | collective-permute-start | bytes 196616 | tf_op jit(solution)/shard_map/ppermute | solution.py:284
  87.7 2.4 %collective-permute-done.25.side_ref = bf16[64,512]{1,0:T(8,128)(2,1)S(1)} collective-permute-done((bf16[64,512]{1,0:T(8,128)(2,1)S(1)}, bf16[64,512]{1,0:T(8,128)(2,1)S(1)}, u32[]{:S(2)}, u32[]{:S(2)}) %collective-permute-start.25) | collective-permute-done | bytes 65568 | tf_op jit(solution)/shard_map/ppermute | solution.py:292
  90.4 2.0 %collective-permute-start.27 = (bf16[64,512]{1,0:T(8,128)(2,1)S(1)}, bf16[64,512]{1,0:T(8,128)(2,1)S(1)}, u32[]{:S(2)}, u32[]{:S(2)}) collective-permute-start(bf16[64,512]{1,0:T(8,128)(2,1)S(1)} %get-tuple-element.34.refs_3_), channel_id=1, source_target_pairs={{0,7},{1,2},{2,1},{3,4},{4,3},{5,6},{6,5},{7,0},{8,15},{9,10},{10,... | collective-permute-start | bytes 196616 | tf_op jit(solution)/shard_map/ppermute | solution.py:292
  92.5 2.2 %collective-permute-done.26.refs_4_ = bf16[64,512]{1,0:T(8,128)(2,1)S(1)} collective-permute-done((bf16[64,512]{1,0:T(8,128)(2,1)S(1)}, bf16[64,512]{1,0:T(8,128)(2,1)S(1)}, u32[]{:S(2)}, u32[]{:S(2)}) %collective-permute-start.26) | collective-permute-done | bytes 65568 | tf_op jit(solution)/shard_map/ppermute | solution.py:292
  95.1 2.3 %collective-permute-done.27.side_ref = bf16[64,512]{1,0:T(8,128)(2,1)S(1)} collective-permute-done((bf16[64,512]{1,0:T(8,128)(2,1)S(1)}, bf16[64,512]{1,0:T(8,128)(2,1)S(1)}, u32[]{:S(2)}, u32[]{:S(2)}) %collective-permute-start.27) | collective-permute-done | bytes 65568 | tf_op jit(solution)/shard_map/ppermute | solution.py:292
  98.0 1.9 %collective-permute-start.29 = (bf16[64,512]{1,0:T(8,128)(2,1)S(1)}, bf16[64,512]{1,0:T(8,128)(2,1)S(1)}, u32[]{:S(2)}, u32[]{:S(2)}) collective-permute-start(bf16[64,512]{1,0:T(8,128)(2,1)S(1)} %get-tuple-element.36.refs_3_), channel_id=1, source_target_pairs={{0,7},{1,2},{2,1},{3,4},{4,3},{5,6},{6,5},{7,0},{8,15},{9,10},{10,... | collective-permute-start | bytes 196616 | tf_op jit(solution)/shard_map/ppermute | solution.py:292
  99.9 2.2 %collective-permute-done.28.refs_4_ = bf16[64,512]{1,0:T(8,128)(2,1)S(1)} collective-permute-done((bf16[64,512]{1,0:T(8,128)(2,1)S(1)}, bf16[64,512]{1,0:T(8,128)(2,1)S(1)}, u32[]{:S(2)}, u32[]{:S(2)}) %collective-permute-start.28) | collective-permute-done | bytes 65568 | tf_op jit(solution)/shard_map/ppermute | solution.py:292
  103.1 1.8 %collective-permute-done.29.side_ref = bf16[64,512]{1,0:T(8,128)(2,1)S(1)} collective-permute-done((bf16[64,512]{1,0:T(8,128)(2,1)S(1)}, bf16[64,512]{1,0:T(8,128)(2,1)S(1)}, u32[]{:S(2)}, u32[]{:S(2)}) %collective-permute-start.29) | collective-permute-done | bytes 65568 | tf_op jit(solution)/shard_map/ppermute | solution.py:292
  105.3 1.6 %collective-permute-start.31 = (f32[64,128]{1,0:T(8,128)S(1)}, f32[64,128]{1,0:T(8,128)S(1)}, u32[]{:S(2)}, u32[]{:S(2)}) collective-permute-start(f32[64,128]{1,0:T(8,128)S(1)} %get-tuple-element.39), channel_id=1, source_target_pairs={{0,16},{8,24},{16,0},{24,8},{1,17},{9,25},{17,1},{25,9},{2,18},{10... | collective-permute-start | bytes 98312 | tf_op jit(solution)/shard_map/ppermute | solution.py:284
  107.1 2.1 %collective-permute-done.31.refs_2_ = f32[64,128]{1,0:T(8,128)S(1)} collective-permute-done((f32[64,128]{1,0:T(8,128)S(1)}, f32[64,128]{1,0:T(8,128)S(1)}, u32[]{:S(2)}, u32[]{:S(2)}) %collective-permute-start.31) | collective-permute-done | bytes 32800 | tf_op jit(solution)/shard_map/ppermute | solution.py:284
  (74 shorter events, 26.1 us)
Async XLA Ops:
  1.2 11.0 %collective-permute-start.7 = (bf16[3,192,256]{2,1,0:T(8,128)(2,1)S(1)}, bf16[3,192,256]{2,1,0:T(8,128)(2,1)S(1)}, u32[]{:S(2)}, u32[]{:S(2)}) collective-permute-start(bf16[3,192,256]{2,1,0:T(8,128)(2,1)S(1)} %get-tuple-element.43.refs_1_), channel_id=1, source_target_pairs={{0,2},{2,0},{4,6},{6,4},{7,5},{5,7},{3,1},{1,3},{8,10},{10,8},{12,... | collective-permute-start | bytes 884744 | tf_op jit(solution)/shard_map/ppermute | solution.py:289
  4.3 9.9 %collective-permute-start.3 = (bf16[3,192,256]{2,1,0:T(8,128)(2,1)S(1)}, bf16[3,192,256]{2,1,0:T(8,128)(2,1)S(1)}, u32[]{:S(2)}, u32[]{:S(2)}) collective-permute-start(bf16[3,192,256]{2,1,0:T(8,128)(2,1)S(1)} %get-tuple-element.44.refs_0_), channel_id=1, source_target_pairs={{0,1},{2,4},{4,2},{6,7},{7,6},{5,3},{3,5},{1,0},{8,9},{10,12},{12,... | collective-permute-start | bytes 884744 | tf_op jit(solution)/shard_map/ppermute | solution.py:289
  5.8 12.7 %collective-permute-start.11 = (bf16[3,192,256]{2,1,0:T(8,128)(2,1)S(1)}, bf16[3,192,256]{2,1,0:T(8,128)(2,1)S(1)}, u32[]{:S(2)}, u32[]{:S(2)}) collective-permute-start(bf16[3,192,256]{2,1,0:T(8,128)(2,1)S(1)} %get-tuple-element.44.refs_0_), channel_id=1, source_target_pairs={{0,2},{2,0},{4,6},{6,4},{7,5},{5,7},{3,1},{1,3},{8,10},{10,8},{12,... | collective-permute-start | bytes 884744 | tf_op jit(solution)/shard_map/ppermute | solution.py:289
  7.4 13.0 %collective-permute-start.14 = (bf16[3,192,256]{2,1,0:T(8,128)(2,1)S(1)}, bf16[3,192,256]{2,1,0:T(8,128)(2,1)S(1)}, u32[]{:S(2)}, u32[]{:S(2)}) collective-permute-start(bf16[3,192,256]{2,1,0:T(8,128)(2,1)S(1)} %get-tuple-element.43.refs_1_), channel_id=1, source_target_pairs={{0,1},{2,4},{4,2},{6,7},{7,6},{5,3},{3,5},{1,0},{8,9},{10,12},{12,... | collective-permute-start | bytes 884744 | tf_op jit(solution)/shard_map/ppermute | solution.py:289
  12.1 14.7 %collective-permute-start.8 = (bf16[3,192,256]{2,1,0:T(8,128)(2,1)S(1)}, bf16[3,192,256]{2,1,0:T(8,128)(2,1)S(1)}, u32[]{:S(2)}, u32[]{:S(2)}) collective-permute-start(bf16[3,192,256]{2,1,0:T(8,128)(2,1)S(1)} %collective-permute-done.7.refs_1_), channel_id=1, source_target_pairs={{0,1},{2,4},{4,2},{6,7},{7,6},{5,3},{3,5},{1,0},{8,9},{10,12},{12,... | collective-permute-start | bytes 884744 | tf_op jit(solution)/shard_map/ppermute | solution.py:289
  14.2 13.8 %collective-permute-start.4 = (bf16[3,192,256]{2,1,0:T(8,128)(2,1)S(1)}, bf16[3,192,256]{2,1,0:T(8,128)(2,1)S(1)}, u32[]{:S(2)}, u32[]{:S(2)}) collective-permute-start(bf16[3,192,256]{2,1,0:T(8,128)(2,1)S(1)} %collective-permute-done.3.refs_0_), channel_id=1, source_target_pairs={{0,2},{2,0},{4,6},{6,4},{7,5},{5,7},{3,1},{1,3},{8,10},{10,8},{12,... | collective-permute-start | bytes 884744 | tf_op jit(solution)/shard_map/ppermute | solution.py:289
  18.5 14.7 %collective-permute-start.12 = (bf16[3,192,256]{2,1,0:T(8,128)(2,1)S(1)}, bf16[3,192,256]{2,1,0:T(8,128)(2,1)S(1)}, u32[]{:S(2)}, u32[]{:S(2)}) collective-permute-start(bf16[3,192,256]{2,1,0:T(8,128)(2,1)S(1)} %collective-permute-done.11.refs_0_), channel_id=1, source_target_pairs={{0,1},{2,4},{4,2},{6,7},{7,6},{5,3},{3,5},{1,0},{8,9},{10,12},{12,... | collective-permute-start | bytes 884744 | tf_op jit(solution)/shard_map/ppermute | solution.py:289
  20.5 13.8 %collective-permute-start.15 = (bf16[3,192,256]{2,1,0:T(8,128)(2,1)S(1)}, bf16[3,192,256]{2,1,0:T(8,128)(2,1)S(1)}, u32[]{:S(2)}, u32[]{:S(2)}) collective-permute-start(bf16[3,192,256]{2,1,0:T(8,128)(2,1)S(1)} %collective-permute-done.14.refs_1_), channel_id=1, source_target_pairs={{0,2},{2,0},{4,6},{6,4},{7,5},{5,7},{3,1},{1,3},{8,10},{10,8},{12,... | collective-permute-start | bytes 884744 | tf_op jit(solution)/shard_map/ppermute | solution.py:289
  26.8 10.6 %collective-permute-start.9 = (bf16[3,192,256]{2,1,0:T(8,128)(2,1)S(1)}, bf16[3,192,256]{2,1,0:T(8,128)(2,1)S(1)}, u32[]{:S(2)}, u32[]{:S(2)}) collective-permute-start(bf16[3,192,256]{2,1,0:T(8,128)(2,1)S(1)} %collective-permute-done.8.refs_1_), channel_id=1, source_target_pairs={{0,2},{2,0},{4,6},{6,4},{7,5},{5,7},{3,1},{1,3},{8,10},{10,8},{12,... | collective-permute-start | bytes 884744 | tf_op jit(solution)/shard_map/ppermute | solution.py:289
  27.9 17.8 %collective-permute-start.5 = (bf16[3,192,256]{2,1,0:T(8,128)(2,1)S(1)}, bf16[3,192,256]{2,1,0:T(8,128)(2,1)S(1)}, u32[]{:S(2)}, u32[]{:S(2)}) collective-permute-start(bf16[3,192,256]{2,1,0:T(8,128)(2,1)S(1)} %collective-permute-done.4.refs_0_), channel_id=1, source_target_pairs={{0,1},{2,4},{4,2},{6,7},{7,6},{5,3},{3,5},{1,0},{8,9},{10,12},{12,... | collective-permute-start | bytes 884744 | tf_op jit(solution)/shard_map/ppermute | solution.py:289
  33.1 21.2 %collective-permute-start.13 = (bf16[3,192,256]{2,1,0:T(8,128)(2,1)S(1)}, bf16[3,192,256]{2,1,0:T(8,128)(2,1)S(1)}, u32[]{:S(2)}, u32[]{:S(2)}) collective-permute-start(bf16[3,192,256]{2,1,0:T(8,128)(2,1)S(1)} %collective-permute-done.12.refs_0_), channel_id=1, source_target_pairs={{0,2},{2,0},{4,6},{6,4},{7,5},{5,7},{3,1},{1,3},{8,10},{10,8},{12,... | collective-permute-start | bytes 884744 | tf_op jit(solution)/shard_map/ppermute | solution.py:289
  34.2 20.6 %collective-permute-start.16 = (bf16[3,192,256]{2,1,0:T(8,128)(2,1)S(1)}, bf16[3,192,256]{2,1,0:T(8,128)(2,1)S(1)}, u32[]{:S(2)}, u32[]{:S(2)}) collective-permute-start(bf16[3,192,256]{2,1,0:T(8,128)(2,1)S(1)} %collective-permute-done.15.refs_1_), channel_id=1, source_target_pairs={{0,1},{2,4},{4,2},{6,7},{7,6},{5,3},{3,5},{1,0},{8,9},{10,12},{12,... | collective-permute-start | bytes 884744 | tf_op jit(solution)/shard_map/ppermute | solution.py:289
  37.4 19.6 %collective-permute-start.10 = (bf16[3,192,256]{2,1,0:T(8,128)(2,1)S(1)}, bf16[3,192,256]{2,1,0:T(8,128)(2,1)S(1)}, u32[]{:S(2)}, u32[]{:S(2)}) collective-permute-start(bf16[3,192,256]{2,1,0:T(8,128)(2,1)S(1)} %collective-permute-done.9.refs_1_), channel_id=1, source_target_pairs={{0,1},{2,4},{4,2},{6,7},{7,6},{5,3},{3,5},{1,0},{8,9},{10,12},{12,... | collective-permute-start | bytes 884744 | tf_op jit(solution)/shard_map/ppermute | solution.py:289
  45.8 11.8 %collective-permute-start.6 = (bf16[3,192,256]{2,1,0:T(8,128)(2,1)S(1)}, bf16[3,192,256]{2,1,0:T(8,128)(2,1)S(1)}, u32[]{:S(2)}, u32[]{:S(2)}) collective-permute-start(bf16[3,192,256]{2,1,0:T(8,128)(2,1)S(1)} %collective-permute-done.5.refs_0_), channel_id=1, source_target_pairs={{0,2},{2,0},{4,6},{6,4},{7,5},{5,7},{3,1},{1,3},{8,10},{10,8},{12,... | collective-permute-start | bytes 884744 | tf_op jit(solution)/shard_map/ppermute | solution.py:289
  54.3 4.5 %collective-permute-start.21 = (f32[64,512]{1,0:T(8,128)S(1)}, f32[64,512]{1,0:T(8,128)S(1)}, u32[]{:S(2)}, u32[]{:S(2)}) collective-permute-start(f32[64,512]{1,0:T(8,128)S(1)} %get-tuple-element.32), channel_id=1, source_target_pairs={{0,8},{8,0},{16,24},{24,16},{1,9},{9,1},{17,25},{25,17},{2,10},{10... | collective-permute-start | bytes 393224 | tf_op jit(solution)/shard_map/ppermute | solution.py:284
  54.4 30.6 %collective-permute-start = (bf16[128,1536]{1,0:T(8,128)(2,1)S(1)}, bf16[128,1536]{1,0:T(8,128)(2,1)S(1)}, u32[]{:S(2)}, u32[]{:S(2)}) collective-permute-start(bf16[128,1536]{1,0:T(8,128)(2,1)S(1)} %get-tuple-element.24.refs_0_), channel_id=1, source_target_pairs={{0,8},{8,0},{16,24},{24,16},{1,9},{9,1},{17,25},{25,17},{2,10},{10... | collective-permute-start | bytes 1179656 | tf_op jit(solution)/shard_map/ppermute | solution.py:284
  54.8 31.7 %collective-permute-start.1 = (bf16[128,1536]{1,0:T(8,128)(2,1)S(1)}, bf16[128,1536]{1,0:T(8,128)(2,1)S(1)}, u32[]{:S(2)}, u32[]{:S(2)}) collective-permute-start(bf16[128,1536]{1,0:T(8,128)(2,1)S(1)} %get-tuple-element.24.refs_0_), channel_id=1, source_target_pairs={{0,16},{8,24},{16,0},{24,8},{1,17},{9,25},{17,1},{25,9},{2,18},{10... | collective-permute-start | bytes 1179656 | tf_op jit(solution)/shard_map/ppermute | solution.py:284
  57.1 29.5 %collective-permute-start.2 = (bf16[128,1536]{1,0:T(8,128)(2,1)S(1)}, bf16[128,1536]{1,0:T(8,128)(2,1)S(1)}, u32[]{:S(2)}, u32[]{:S(2)}) collective-permute-start(bf16[128,1536]{1,0:T(8,128)(2,1)S(1)} %get-tuple-element.24.refs_0_), channel_id=1, source_target_pairs={{0,24},{8,16},{16,8},{24,0},{1,25},{9,17},{17,9},{25,1},{2,26},{10... | collective-permute-start | bytes 1179656 | tf_op jit(solution)/shard_map/ppermute | solution.py:284
  58.8 1.9 %collective-permute-start.18 = (f32[64,512]{1,0:T(8,128)S(1)}, f32[64,512]{1,0:T(8,128)S(1)}, u32[]{:S(2)}, u32[]{:S(2)}) collective-permute-start(f32[64,512]{1,0:T(8,128)S(1)} %get-tuple-element.29), channel_id=1, source_target_pairs={{0,8},{8,0},{16,24},{24,16},{1,9},{9,1},{17,25},{25,17},{2,10},{10... | collective-permute-start | bytes 393224 | tf_op jit(solution)/shard_map/ppermute | solution.py:284
  59.2 17.9 %collective-permute-start.22 = (f32[64,512]{1,0:T(8,128)S(1)}, f32[64,512]{1,0:T(8,128)S(1)}, u32[]{:S(2)}, u32[]{:S(2)}) collective-permute-start(f32[64,512]{1,0:T(8,128)S(1)} %bitcast_add_fusion), channel_id=1, source_target_pairs={{0,16},{8,24},{16,0},{24,8},{1,17},{9,25},{17,1},{25,9},{2,18},{10... | collective-permute-start | bytes 393224 | tf_op jit(solution)/shard_map/ppermute | solution.py:284
  60.8 17.9 %collective-permute-start.17 = (f32[64,512]{1,0:T(8,128)S(1)}, f32[64,512]{1,0:T(8,128)S(1)}, u32[]{:S(2)}, u32[]{:S(2)}) collective-permute-start(f32[64,512]{1,0:T(8,128)S(1)} %get-tuple-element.28), channel_id=1, source_target_pairs={{0,8},{8,0},{16,24},{24,16},{1,9},{9,1},{17,25},{25,17},{2,10},{10... | collective-permute-start | bytes 393224 | tf_op jit(solution)/shard_map/ppermute | solution.py:284
  77.2 4.3 %collective-permute-start.19 = (bf16[64,512]{1,0:T(8,128)(2,1)S(1)}, bf16[64,512]{1,0:T(8,128)(2,1)S(1)}, u32[]{:S(2)}, u32[]{:S(2)}) collective-permute-start(bf16[64,512]{1,0:T(8,128)(2,1)S(1)} %get-tuple-element.46), channel_id=1, source_target_pairs={{0,16},{8,24},{16,0},{24,8},{1,17},{9,25},{17,1},{25,9},{2,18},{10... | collective-permute-start | bytes 196616 | tf_op jit(solution)/shard_map/ppermute | solution.py:284
  81.5 5.7 %collective-permute-start.24 = (bf16[64,512]{1,0:T(8,128)(2,1)S(1)}, bf16[64,512]{1,0:T(8,128)(2,1)S(1)}, u32[]{:S(2)}, u32[]{:S(2)}) collective-permute-start(bf16[64,512]{1,0:T(8,128)(2,1)S(1)} %get-tuple-element.41.refs_3_), channel_id=1, source_target_pairs={{0,1},{1,0},{2,3},{3,2},{4,5},{5,4},{6,7},{7,6},{8,9},{9,8},{10,11... | collective-permute-start | bytes 196616 | tf_op jit(solution)/shard_map/ppermute | solution.py:292
  83.1 7.0 %collective-permute-start.25 = (bf16[64,512]{1,0:T(8,128)(2,1)S(1)}, bf16[64,512]{1,0:T(8,128)(2,1)S(1)}, u32[]{:S(2)}, u32[]{:S(2)}) collective-permute-start(bf16[64,512]{1,0:T(8,128)(2,1)S(1)} %get-tuple-element.41.refs_3_), channel_id=1, source_target_pairs={{0,7},{1,2},{2,1},{3,4},{4,3},{5,6},{6,5},{7,0},{8,15},{9,10},{10,... | collective-permute-start | bytes 196616 | tf_op jit(solution)/shard_map/ppermute | solution.py:292
  85.0 7.4 %collective-permute-start.23 = (bf16[64,512]{1,0:T(8,128)(2,1)S(1)}, bf16[64,512]{1,0:T(8,128)(2,1)S(1)}, u32[]{:S(2)}, u32[]{:S(2)}) collective-permute-start(bf16[64,512]{1,0:T(8,128)(2,1)S(1)} %get-tuple-element.45), channel_id=1, source_target_pairs={{0,16},{8,24},{16,0},{24,8},{1,17},{9,25},{17,1},{25,9},{2,18},{10... | collective-permute-start | bytes 196616 | tf_op jit(solution)/shard_map/ppermute | solution.py:284
  90.3 4.3 %collective-permute-start.26 = (bf16[64,512]{1,0:T(8,128)(2,1)S(1)}, bf16[64,512]{1,0:T(8,128)(2,1)S(1)}, u32[]{:S(2)}, u32[]{:S(2)}) collective-permute-start(bf16[64,512]{1,0:T(8,128)(2,1)S(1)} %get-tuple-element.34.refs_3_), channel_id=1, source_target_pairs={{0,1},{1,0},{2,3},{3,2},{4,5},{5,4},{6,7},{7,6},{8,9},{9,8},{10,11... | collective-permute-start | bytes 196616 | tf_op jit(solution)/shard_map/ppermute | solution.py:292
  90.4 7.0 %collective-permute-start.27 = (bf16[64,512]{1,0:T(8,128)(2,1)S(1)}, bf16[64,512]{1,0:T(8,128)(2,1)S(1)}, u32[]{:S(2)}, u32[]{:S(2)}) collective-permute-start(bf16[64,512]{1,0:T(8,128)(2,1)S(1)} %get-tuple-element.34.refs_3_), channel_id=1, source_target_pairs={{0,7},{1,2},{2,1},{3,4},{4,3},{5,6},{6,5},{7,0},{8,15},{9,10},{10,... | collective-permute-start | bytes 196616 | tf_op jit(solution)/shard_map/ppermute | solution.py:292
  97.7 4.3 %collective-permute-start.28 = (bf16[64,512]{1,0:T(8,128)(2,1)S(1)}, bf16[64,512]{1,0:T(8,128)(2,1)S(1)}, u32[]{:S(2)}, u32[]{:S(2)}) collective-permute-start(bf16[64,512]{1,0:T(8,128)(2,1)S(1)} %get-tuple-element.36.refs_3_), channel_id=1, source_target_pairs={{0,1},{1,0},{2,3},{3,2},{4,5},{5,4},{6,7},{7,6},{8,9},{9,8},{10,11... | collective-permute-start | bytes 196616 | tf_op jit(solution)/shard_map/ppermute | solution.py:292
  98.0 7.0 %collective-permute-start.29 = (bf16[64,512]{1,0:T(8,128)(2,1)S(1)}, bf16[64,512]{1,0:T(8,128)(2,1)S(1)}, u32[]{:S(2)}, u32[]{:S(2)}) collective-permute-start(bf16[64,512]{1,0:T(8,128)(2,1)S(1)} %get-tuple-element.36.refs_3_), channel_id=1, source_target_pairs={{0,7},{1,2},{2,1},{3,4},{4,3},{5,6},{6,5},{7,0},{8,15},{9,10},{10,... | collective-permute-start | bytes 196616 | tf_op jit(solution)/shard_map/ppermute | solution.py:292
  105.2 1.9 %collective-permute-start.30 = (f32[64,128]{1,0:T(8,128)S(1)}, f32[64,128]{1,0:T(8,128)S(1)}, u32[]{:S(2)}, u32[]{:S(2)}) collective-permute-start(f32[64,128]{1,0:T(8,128)S(1)} %get-tuple-element.38), channel_id=1, source_target_pairs={{0,8},{8,0},{16,24},{24,16},{1,9},{9,1},{17,25},{25,17},{2,10},{10... | collective-permute-start | bytes 98312 | tf_op jit(solution)/shard_map/ppermute | solution.py:284
  105.3 4.0 %collective-permute-start.31 = (f32[64,128]{1,0:T(8,128)S(1)}, f32[64,128]{1,0:T(8,128)S(1)}, u32[]{:S(2)}, u32[]{:S(2)}) collective-permute-start(f32[64,128]{1,0:T(8,128)S(1)} %get-tuple-element.39), channel_id=1, source_target_pairs={{0,16},{8,24},{16,0},{24,8},{1,17},{9,25},{17,1},{25,9},{2,18},{10... | collective-permute-start | bytes 98312 | tf_op jit(solution)/shard_map/ppermute | solution.py:284
  106.9 3.4 %collective-permute-start.32 = (f32[64,128]{1,0:T(8,128)S(1)}, f32[64,128]{1,0:T(8,128)S(1)}, u32[]{:S(2)}, u32[]{:S(2)}) collective-permute-start(f32[64,128]{1,0:T(8,128)S(1)} %get-tuple-element.40), channel_id=1, source_target_pairs={{0,24},{8,16},{16,8},{24,0},{1,25},{9,17},{17,9},{25,1},{2,26},{10... | collective-permute-start | bytes 98312 | tf_op jit(solution)/shard_map/ppermute | solution.py:284
  (9 other events, 150.7 us)

commit v7 on v6

--- a/solution.py
+++ b/solution.py
@@ -333,7 +333,7 @@
         moving = turns[0] | turns[1]
         for rank in range(2):
             blocks = [(step, side, i, x) for (side, i), x in turns[rank].items()]
-            early = (step, rank) == (final - 1, 0)
+            early = (step, rank) == (final - 1, 1)
             field = (incident[0], chosen) if early else (None, None)
             total = multiply(kernels, blocks, total, *field, row_count if early else 0)
             if early:
@@ -347,7 +347,8 @@
     density = driven
     rounded = density.astype(jnp.bfloat16)
     for step in range(SWEEPS):
-        far_side, near_side = swap_cols(rounded, 2), swap_cols(rounded, 1)
+        far_side = swap_cols(rounded, 2)
+        near_side = swap_cols(rounded, 1)
         last = step == SWEEPS - 1
         if step == 0:
             rest = sum(across_rows(x, m).astype(jnp.float32) for m, x in lost)

time: 111 us -> 110 us (level)
  waiting for transfers between devices: 49.7 us -> 47.2 us
  local copies, waits for them, and re-layouts: 7.34 us -> 9.57 us
    unnamed x16, local copies, waits for them, and re-layouts: 6.2 us -> 8.48 us
    ppermute x14, starting transfers between devices: 23.7 us -> 21.6 us  [swap_walk(): lax.ppermute(x, 'col', [(walk[p], walk[mate(p, side, col_count)]) for p i...]
    ppermute x14, waiting for transfers between devices: 16.2 us -> 14.6 us  [swap_walk(): lax.ppermute(x, 'col', [(walk[p], walk[mate(p, side, col_count)]) for p i...]
    ppermute x6, starting transfers between devices: 7.7 us -> 9.28 us  [swap_cols(): lax.ppermute(x, 'col', [(c, mate(c, side, col_count)) for c in range(col_...]
    ppermute x6, waiting for transfers between devices: 11 us -> 9.41 us  [swap_cols(): lax.ppermute(x, 'col', [(c, mate(c, side, col_count)) for c in range(col_...]
  transfers between devices with their start and end apart: 33 -> 33, of which waited for: 17 -> 16; matrix products, arithmetic and copies ran while one was open for 0% -> 0% of each run, Pallas kernels for 10% -> 10%
where the time goes in v7:
time: 110 us
  waiting for transfers between devices  47.2 us (43%)
  starting transfers between devices  40.3 us (37%)
  Pallas kernels  12 us (11%)
  local copies, waits for them, and re-layouts  9.57 us (9%)
    ppermute x13, waiting for transfers between devices, across_rows(): return lax.ppermute(x, 'row', [(i, i ^ m) for i in range(row_count)])  23.2 us
    ppermute x14, starting transfers between devices, swap_walk(): lax.ppermute(x, 'col', [(walk[p], walk[mate(p, side, col_count)]) for p i...  21.6 us
    ppermute x14, waiting for transfers between devices, swap_walk(): lax.ppermute(x, 'col', [(walk[p], walk[mate(p, side, col_count)]) for p i...  14.6 us
    ppermute x13, starting transfers between devices, across_rows(): return lax.ppermute(x, 'row', [(i, i ^ m) for i in range(row_count)])  9.43 us
    ppermute x6, waiting for transfers between devices, swap_cols(): lax.ppermute(x, 'col', [(c, mate(c, side, col_count)) for c in range(col_...  9.41 us
    ppermute x6, starting transfers between devices, swap_cols(): lax.ppermute(x, 'col', [(c, mate(c, side, col_count)) for c in range(col_...  9.28 us
    unnamed x16, local copies, waits for them, and re-layouts  8.48 us
    pallas_call x9, Pallas kernels, multiply(): pl.pallas_call(body, out_shape=out_shape, in_specs=in_specs, out_specs=[V...  6.49 us
  transfers between devices with their start and end apart: 33, of which 16 were waited for; matrix products, arithmetic and copies ran while one was open for 0% of the time, Pallas kernels for 10%

profile of v7, /device:TPU:0, one launch (start us, length us, event | category | flops | bytes accessed | tf_op | source)
XLA Modules:
  0.0 110.2 jit_solution(18166844559716144902)
XLA Ops:
  1.1 3.1 %collective-permute-start.7 = (bf16[3,192,256]{2,1,0:T(8,128)(2,1)S(1)}, bf16[3,192,256]{2,1,0:T(8,128)(2,1)S(1)}, u32[]{:S(2)}, u32[]{:S(2)}) collective-permute-start(bf16[3,192,256]{2,1,0:T(8,128)(2,1)S(1)} %get-tuple-element.43.refs_1_), channel_id=1, source_target_pairs={{0,2},{2,0},{4,6},{6,4},{7,5},{5,7},{3,1},{1,3},{8,10},{10,8},{12,... | collective-permute-start | bytes 884744 | tf_op jit(solution)/shard_map/ppermute | solution.py:289
  4.2 1.5 %collective-permute-start.3 = (bf16[3,192,256]{2,1,0:T(8,128)(2,1)S(1)}, bf16[3,192,256]{2,1,0:T(8,128)(2,1)S(1)}, u32[]{:S(2)}, u32[]{:S(2)}) collective-permute-start(bf16[3,192,256]{2,1,0:T(8,128)(2,1)S(1)} %get-tuple-element.44.refs_0_), channel_id=1, source_target_pairs={{0,1},{2,4},{4,2},{6,7},{7,6},{5,3},{3,5},{1,0},{8,9},{10,12},{12,... | collective-permute-start | bytes 884744 | tf_op jit(solution)/shard_map/ppermute | solution.py:289
  5.7 1.7 %collective-permute-start.14 = (bf16[3,192,256]{2,1,0:T(8,128)(2,1)S(1)}, bf16[3,192,256]{2,1,0:T(8,128)(2,1)S(1)}, u32[]{:S(2)}, u32[]{:S(2)}) collective-permute-start(bf16[3,192,256]{2,1,0:T(8,128)(2,1)S(1)} %get-tuple-element.44.refs_0_), channel_id=1, source_target_pairs={{0,2},{2,0},{4,6},{6,4},{7,5},{5,7},{3,1},{1,3},{8,10},{10,8},{12,... | collective-permute-start | bytes 884744 | tf_op jit(solution)/shard_map/ppermute | solution.py:289
  7.4 1.5 %collective-permute-start.17 = (bf16[3,192,256]{2,1,0:T(8,128)(2,1)S(1)}, bf16[3,192,256]{2,1,0:T(8,128)(2,1)S(1)}, u32[]{:S(2)}, u32[]{:S(2)}) collective-permute-start(bf16[3,192,256]{2,1,0:T(8,128)(2,1)S(1)} %get-tuple-element.43.refs_1_), channel_id=1, source_target_pairs={{0,1},{2,4},{4,2},{6,7},{7,6},{5,3},{3,5},{1,0},{8,9},{10,12},{12,... | collective-permute-start | bytes 884744 | tf_op jit(solution)/shard_map/ppermute | solution.py:289
  8.9 3.2 %collective-permute-done.7.refs_1_ = bf16[3,192,256]{2,1,0:T(8,128)(2,1)S(1)} collective-permute-done((bf16[3,192,256]{2,1,0:T(8,128)(2,1)S(1)}, bf16[3,192,256]{2,1,0:T(8,128)(2,1)S(1)}, u32[]{:S(2)}, u32[]{:S(2)}) %collective-permute-start.7) | collective-permute-done | bytes 294944 | tf_op jit(solution)/shard_map/ppermute | solution.py:289
  12.1 1.9 %collective-permute-start.8 = (bf16[3,192,256]{2,1,0:T(8,128)(2,1)S(1)}, bf16[3,192,256]{2,1,0:T(8,128)(2,1)S(1)}, u32[]{:S(2)}, u32[]{:S(2)}) collective-permute-start(bf16[3,192,256]{2,1,0:T(8,128)(2,1)S(1)} %collective-permute-done.7.refs_1_), channel_id=1, source_target_pairs={{0,1},{2,4},{4,2},{6,7},{7,6},{5,3},{3,5},{1,0},{8,9},{10,12},{12,... | collective-permute-start | bytes 884744 | tf_op jit(solution)/shard_map/ppermute | solution.py:289
  14.1 1.6 %collective-permute-start.4 = (bf16[3,192,256]{2,1,0:T(8,128)(2,1)S(1)}, bf16[3,192,256]{2,1,0:T(8,128)(2,1)S(1)}, u32[]{:S(2)}, u32[]{:S(2)}) collective-permute-start(bf16[3,192,256]{2,1,0:T(8,128)(2,1)S(1)} %collective-permute-done.3.refs_0_), channel_id=1, source_target_pairs={{0,2},{2,0},{4,6},{6,4},{7,5},{5,7},{3,1},{1,3},{8,10},{10,8},{12,... | collective-permute-start | bytes 884744 | tf_op jit(solution)/shard_map/ppermute | solution.py:289
  15.7 2.7 %collective-permute-done.14.refs_0_ = bf16[3,192,256]{2,1,0:T(8,128)(2,1)S(1)} collective-permute-done((bf16[3,192,256]{2,1,0:T(8,128)(2,1)S(1)}, bf16[3,192,256]{2,1,0:T(8,128)(2,1)S(1)}, u32[]{:S(2)}, u32[]{:S(2)}) %collective-permute-start.14) | collective-permute-done | bytes 294944 | tf_op jit(solution)/shard_map/ppermute | solution.py:289
  18.4 1.9 %collective-permute-start.15 = (bf16[3,192,256]{2,1,0:T(8,128)(2,1)S(1)}, bf16[3,192,256]{2,1,0:T(8,128)(2,1)S(1)}, u32[]{:S(2)}, u32[]{:S(2)}) collective-permute-start(bf16[3,192,256]{2,1,0:T(8,128)(2,1)S(1)} %collective-permute-done.14.refs_0_), channel_id=1, source_target_pairs={{0,1},{2,4},{4,2},{6,7},{7,6},{5,3},{3,5},{1,0},{8,9},{10,12},{12,... | collective-permute-start | bytes 884744 | tf_op jit(solution)/shard_map/ppermute | solution.py:289
  20.4 1.6 %collective-permute-start.18 = (bf16[3,192,256]{2,1,0:T(8,128)(2,1)S(1)}, bf16[3,192,256]{2,1,0:T(8,128)(2,1)S(1)}, u32[]{:S(2)}, u32[]{:S(2)}) collective-permute-start(bf16[3,192,256]{2,1,0:T(8,128)(2,1)S(1)} %collective-permute-done.17.refs_1_), channel_id=1, source_target_pairs={{0,2},{2,0},{4,6},{6,4},{7,5},{5,7},{3,1},{1,3},{8,10},{10,8},{12,... | collective-permute-start | bytes 884744 | tf_op jit(solution)/shard_map/ppermute | solution.py:289
  22.0 4.7 %collective-permute-done.8.refs_1_ = bf16[3,192,256]{2,1,0:T(8,128)(2,1)S(1)} collective-permute-done((bf16[3,192,256]{2,1,0:T(8,128)(2,1)S(1)}, bf16[3,192,256]{2,1,0:T(8,128)(2,1)S(1)}, u32[]{:S(2)}, u32[]{:S(2)}) %collective-permute-start.8) | collective-permute-done | bytes 294944 | tf_op jit(solution)/shard_map/ppermute | solution.py:289
  27.9 1.5 %collective-permute-start.5 = (bf16[3,192,256]{2,1,0:T(8,128)(2,1)S(1)}, bf16[3,192,256]{2,1,0:T(8,128)(2,1)S(1)}, u32[]{:S(2)}, u32[]{:S(2)}) collective-permute-start(bf16[3,192,256]{2,1,0:T(8,128)(2,1)S(1)} %collective-permute-done.4.refs_0_), channel_id=1, source_target_pairs={{0,1},{2,4},{4,2},{6,7},{7,6},{5,3},{3,5},{1,0},{8,9},{10,12},{12,... | collective-permute-start | bytes 884744 | tf_op jit(solution)/shard_map/ppermute | solution.py:289
  29.4 3.7 %collective-permute-done.15.refs_0_ = bf16[3,192,256]{2,1,0:T(8,128)(2,1)S(1)} collective-permute-done((bf16[3,192,256]{2,1,0:T(8,128)(2,1)S(1)}, bf16[3,192,256]{2,1,0:T(8,128)(2,1)S(1)}, u32[]{:S(2)}, u32[]{:S(2)}) %collective-permute-start.15) | collective-permute-done | bytes 294944 | tf_op jit(solution)/shard_map/ppermute | solution.py:289
  34.2 1.5 %collective-permute-start.19 = (bf16[3,192,256]{2,1,0:T(8,128)(2,1)S(1)}, bf16[3,192,256]{2,1,0:T(8,128)(2,1)S(1)}, u32[]{:S(2)}, u32[]{:S(2)}) collective-permute-start(bf16[3,192,256]{2,1,0:T(8,128)(2,1)S(1)} %collective-permute-done.18.refs_1_), channel_id=1, source_target_pairs={{0,1},{2,4},{4,2},{6,7},{7,6},{5,3},{3,5},{1,0},{8,9},{10,12},{12,... | collective-permute-start | bytes 884744 | tf_op jit(solution)/shard_map/ppermute | solution.py:289
  40.1 3.7 %copy-done = bf16[6,512,1536]{2,1,0:T(8,128)(2,1)S(1)} copy-done((bf16[6,512,1536]{2,1,0:T(8,128)(2,1)S(1)}, bf16[6,512,1536]{2,1,0:T(8,128)(2,1)}, u32[]{:S(2)}) %copy-start) | copy-done | bytes 9437208
  54.0 1.5 %collective-permute-start.1 = (bf16[128,1536]{1,0:T(8,128)(2,1)S(1)}, bf16[128,1536]{1,0:T(8,128)(2,1)S(1)}, u32[]{:S(2)}, u32[]{:S(2)}) collective-permute-start(bf16[128,1536]{1,0:T(8,128)(2,1)S(1)} %get-tuple-element.24.refs_0_), channel_id=1, source_target_pairs={{0,16},{8,24},{16,0},{24,8},{1,17},{9,25},{17,1},{25,9},{2,18},{10... | collective-permute-start | bytes 1179656 | tf_op jit(solution)/shard_map/ppermute | solution.py:284
  57.6 1.5 %collective-permute-start.22 = (f32[64,512]{1,0:T(8,128)S(1)}, f32[64,512]{1,0:T(8,128)S(1)}, u32[]{:S(2)}, u32[]{:S(2)}) collective-permute-start(f32[64,512]{1,0:T(8,128)S(1)} %bitcast_add_fusion), channel_id=1, source_target_pairs={{0,16},{8,24},{16,0},{24,8},{1,17},{9,25},{17,1},{25,9},{2,18},{10... | collective-permute-start | bytes 393224 | tf_op jit(solution)/shard_map/ppermute | solution.py:284
  59.3 17.1 %collective-permute-done.22 = f32[64,512]{1,0:T(8,128)S(1)} collective-permute-done((f32[64,512]{1,0:T(8,128)S(1)}, f32[64,512]{1,0:T(8,128)S(1)}, u32[]{:S(2)}, u32[]{:S(2)}) %collective-permute-start.22) | collective-permute-done | bytes 131104 | tf_op jit(solution)/shard_map/ppermute | solution.py:284
  76.3 1.5 %collective-permute-start.13 = (bf16[64,512]{1,0:T(8,128)(2,1)S(1)}, bf16[64,512]{1,0:T(8,128)(2,1)S(1)}, u32[]{:S(2)}, u32[]{:S(2)}) collective-permute-start(bf16[64,512]{1,0:T(8,128)(2,1)S(1)} %get-tuple-element.46), channel_id=1, source_target_pairs={{0,16},{8,24},{16,0},{24,8},{1,17},{9,25},{17,1},{25,9},{2,18},{10... | collective-permute-start | bytes 196616 | tf_op jit(solution)/shard_map/ppermute | solution.py:284
  77.8 2.7 %collective-permute-done.13 = bf16[64,512]{1,0:T(8,128)(2,1)S(1)} collective-permute-done((bf16[64,512]{1,0:T(8,128)(2,1)S(1)}, bf16[64,512]{1,0:T(8,128)(2,1)S(1)}, u32[]{:S(2)}, u32[]{:S(2)}) %collective-permute-start.13) | collective-permute-done | bytes 65568 | tf_op jit(solution)/shard_map/ppermute | solution.py:284
  80.7 1.6 %collective-permute-start.24 = (bf16[64,512]{1,0:T(8,128)(2,1)S(1)}, bf16[64,512]{1,0:T(8,128)(2,1)S(1)}, u32[]{:S(2)}, u32[]{:S(2)}) collective-permute-start(bf16[64,512]{1,0:T(8,128)(2,1)S(1)} %get-tuple-element.41.refs_3_), channel_id=1, source_target_pairs={{0,1},{1,0},{2,3},{3,2},{4,5},{5,4},{6,7},{7,6},{8,9},{9,8},{10,11... | collective-permute-start | bytes 196616 | tf_op jit(solution)/shard_map/ppermute | solution.py:292
  82.2 2.5 %collective-permute-start.25 = (bf16[64,512]{1,0:T(8,128)(2,1)S(1)}, bf16[64,512]{1,0:T(8,128)(2,1)S(1)}, u32[]{:S(2)}, u32[]{:S(2)}) collective-permute-start(bf16[64,512]{1,0:T(8,128)(2,1)S(1)} %get-tuple-element.41.refs_3_), channel_id=1, source_target_pairs={{0,7},{1,2},{2,1},{3,4},{4,3},{5,6},{6,5},{7,0},{8,15},{9,10},{10,... | collective-permute-start | bytes 196616 | tf_op jit(solution)/shard_map/ppermute | solution.py:292
  84.7 1.5 %collective-permute-start.23 = (bf16[64,512]{1,0:T(8,128)(2,1)S(1)}, bf16[64,512]{1,0:T(8,128)(2,1)S(1)}, u32[]{:S(2)}, u32[]{:S(2)}) collective-permute-start(bf16[64,512]{1,0:T(8,128)(2,1)S(1)} %get-tuple-element.45), channel_id=1, source_target_pairs={{0,16},{8,24},{16,0},{24,8},{1,17},{9,25},{17,1},{25,9},{2,18},{10... | collective-permute-start | bytes 196616 | tf_op jit(solution)/shard_map/ppermute | solution.py:284
  87.3 1.9 %collective-permute-done.25.side_ref = bf16[64,512]{1,0:T(8,128)(2,1)S(1)} collective-permute-done((bf16[64,512]{1,0:T(8,128)(2,1)S(1)}, bf16[64,512]{1,0:T(8,128)(2,1)S(1)}, u32[]{:S(2)}, u32[]{:S(2)}) %collective-permute-start.25) | collective-permute-done | bytes 65568 | tf_op jit(solution)/shard_map/ppermute | solution.py:292
  89.6 2.5 %collective-permute-start.27 = (bf16[64,512]{1,0:T(8,128)(2,1)S(1)}, bf16[64,512]{1,0:T(8,128)(2,1)S(1)}, u32[]{:S(2)}, u32[]{:S(2)}) collective-permute-start(bf16[64,512]{1,0:T(8,128)(2,1)S(1)} %get-tuple-element.34.refs_3_), channel_id=1, source_target_pairs={{0,7},{1,2},{2,1},{3,4},{4,3},{5,6},{6,5},{7,0},{8,15},{9,10},{10,... | collective-permute-start | bytes 196616 | tf_op jit(solution)/shard_map/ppermute | solution.py:292
  92.1 1.7 %collective-permute-done.26.refs_4_ = bf16[64,512]{1,0:T(8,128)(2,1)S(1)} collective-permute-done((bf16[64,512]{1,0:T(8,128)(2,1)S(1)}, bf16[64,512]{1,0:T(8,128)(2,1)S(1)}, u32[]{:S(2)}, u32[]{:S(2)}) %collective-permute-start.26) | collective-permute-done | bytes 65568 | tf_op jit(solution)/shard_map/ppermute | solution.py:292
  94.3 2.3 %collective-permute-done.27.side_ref = bf16[64,512]{1,0:T(8,128)(2,1)S(1)} collective-permute-done((bf16[64,512]{1,0:T(8,128)(2,1)S(1)}, bf16[64,512]{1,0:T(8,128)(2,1)S(1)}, u32[]{:S(2)}, u32[]{:S(2)}) %collective-permute-start.27) | collective-permute-done | bytes 65568 | tf_op jit(solution)/shard_map/ppermute | solution.py:292
  97.1 2.5 %collective-permute-start.29 = (bf16[64,512]{1,0:T(8,128)(2,1)S(1)}, bf16[64,512]{1,0:T(8,128)(2,1)S(1)}, u32[]{:S(2)}, u32[]{:S(2)}) collective-permute-start(bf16[64,512]{1,0:T(8,128)(2,1)S(1)} %get-tuple-element.36.refs_3_), channel_id=1, source_target_pairs={{0,7},{1,2},{2,1},{3,4},{4,3},{5,6},{6,5},{7,0},{8,15},{9,10},{10,... | collective-permute-start | bytes 196616 | tf_op jit(solution)/shard_map/ppermute | solution.py:292
  99.6 1.6 %collective-permute-done.28.refs_4_ = bf16[64,512]{1,0:T(8,128)(2,1)S(1)} collective-permute-done((bf16[64,512]{1,0:T(8,128)(2,1)S(1)}, bf16[64,512]{1,0:T(8,128)(2,1)S(1)}, u32[]{:S(2)}, u32[]{:S(2)}) %collective-permute-start.28) | collective-permute-done | bytes 65568 | tf_op jit(solution)/shard_map/ppermute | solution.py:292
  102.2 1.8 %collective-permute-done.29.side_ref = bf16[64,512]{1,0:T(8,128)(2,1)S(1)} collective-permute-done((bf16[64,512]{1,0:T(8,128)(2,1)S(1)}, bf16[64,512]{1,0:T(8,128)(2,1)S(1)}, u32[]{:S(2)}, u32[]{:S(2)}) %collective-permute-start.29) | collective-permute-done | bytes 65568 | tf_op jit(solution)/shard_map/ppermute | solution.py:292
  104.4 1.6 %collective-permute-start.31 = (f32[64,128]{1,0:T(8,128)S(1)}, f32[64,128]{1,0:T(8,128)S(1)}, u32[]{:S(2)}, u32[]{:S(2)}) collective-permute-start(f32[64,128]{1,0:T(8,128)S(1)} %get-tuple-element.39), channel_id=1, source_target_pairs={{0,16},{8,24},{16,0},{24,8},{1,17},{9,25},{17,1},{25,9},{2,18},{10... | collective-permute-start | bytes 98312 | tf_op jit(solution)/shard_map/ppermute | solution.py:284
  106.3 2.1 %collective-permute-done.31.refs_2_ = f32[64,128]{1,0:T(8,128)S(1)} collective-permute-done((f32[64,128]{1,0:T(8,128)S(1)}, f32[64,128]{1,0:T(8,128)S(1)}, u32[]{:S(2)}, u32[]{:S(2)}) %collective-permute-start.31) | collective-permute-done | bytes 32800 | tf_op jit(solution)/shard_map/ppermute | solution.py:284
  (74 shorter events, 25.4 us)
Async XLA Ops:
  1.1 11.0 %collective-permute-start.7 = (bf16[3,192,256]{2,1,0:T(8,128)(2,1)S(1)}, bf16[3,192,256]{2,1,0:T(8,128)(2,1)S(1)}, u32[]{:S(2)}, u32[]{:S(2)}) collective-permute-start(bf16[3,192,256]{2,1,0:T(8,128)(2,1)S(1)} %get-tuple-element.43.refs_1_), channel_id=1, source_target_pairs={{0,2},{2,0},{4,6},{6,4},{7,5},{5,7},{3,1},{1,3},{8,10},{10,8},{12,... | collective-permute-start | bytes 884744 | tf_op jit(solution)/shard_map/ppermute | solution.py:289
  4.2 9.9 %collective-permute-start.3 = (bf16[3,192,256]{2,1,0:T(8,128)(2,1)S(1)}, bf16[3,192,256]{2,1,0:T(8,128)(2,1)S(1)}, u32[]{:S(2)}, u32[]{:S(2)}) collective-permute-start(bf16[3,192,256]{2,1,0:T(8,128)(2,1)S(1)} %get-tuple-element.44.refs_0_), channel_id=1, source_target_pairs={{0,1},{2,4},{4,2},{6,7},{7,6},{5,3},{3,5},{1,0},{8,9},{10,12},{12,... | collective-permute-start | bytes 884744 | tf_op jit(solution)/shard_map/ppermute | solution.py:289
  5.7 12.7 %collective-permute-start.14 = (bf16[3,192,256]{2,1,0:T(8,128)(2,1)S(1)}, bf16[3,192,256]{2,1,0:T(8,128)(2,1)S(1)}, u32[]{:S(2)}, u32[]{:S(2)}) collective-permute-start(bf16[3,192,256]{2,1,0:T(8,128)(2,1)S(1)} %get-tuple-element.44.refs_0_), channel_id=1, source_target_pairs={{0,2},{2,0},{4,6},{6,4},{7,5},{5,7},{3,1},{1,3},{8,10},{10,8},{12,... | collective-permute-start | bytes 884744 | tf_op jit(solution)/shard_map/ppermute | solution.py:289
  7.4 13.0 %collective-permute-start.17 = (bf16[3,192,256]{2,1,0:T(8,128)(2,1)S(1)}, bf16[3,192,256]{2,1,0:T(8,128)(2,1)S(1)}, u32[]{:S(2)}, u32[]{:S(2)}) collective-permute-start(bf16[3,192,256]{2,1,0:T(8,128)(2,1)S(1)} %get-tuple-element.43.refs_1_), channel_id=1, source_target_pairs={{0,1},{2,4},{4,2},{6,7},{7,6},{5,3},{3,5},{1,0},{8,9},{10,12},{12,... | collective-permute-start | bytes 884744 | tf_op jit(solution)/shard_map/ppermute | solution.py:289
  12.1 14.7 %collective-permute-start.8 = (bf16[3,192,256]{2,1,0:T(8,128)(2,1)S(1)}, bf16[3,192,256]{2,1,0:T(8,128)(2,1)S(1)}, u32[]{:S(2)}, u32[]{:S(2)}) collective-permute-start(bf16[3,192,256]{2,1,0:T(8,128)(2,1)S(1)} %collective-permute-done.7.refs_1_), channel_id=1, source_target_pairs={{0,1},{2,4},{4,2},{6,7},{7,6},{5,3},{3,5},{1,0},{8,9},{10,12},{12,... | collective-permute-start | bytes 884744 | tf_op jit(solution)/shard_map/ppermute | solution.py:289
  14.1 13.8 %collective-permute-start.4 = (bf16[3,192,256]{2,1,0:T(8,128)(2,1)S(1)}, bf16[3,192,256]{2,1,0:T(8,128)(2,1)S(1)}, u32[]{:S(2)}, u32[]{:S(2)}) collective-permute-start(bf16[3,192,256]{2,1,0:T(8,128)(2,1)S(1)} %collective-permute-done.3.refs_0_), channel_id=1, source_target_pairs={{0,2},{2,0},{4,6},{6,4},{7,5},{5,7},{3,1},{1,3},{8,10},{10,8},{12,... | collective-permute-start | bytes 884744 | tf_op jit(solution)/shard_map/ppermute | solution.py:289
  18.4 14.7 %collective-permute-start.15 = (bf16[3,192,256]{2,1,0:T(8,128)(2,1)S(1)}, bf16[3,192,256]{2,1,0:T(8,128)(2,1)S(1)}, u32[]{:S(2)}, u32[]{:S(2)}) collective-permute-start(bf16[3,192,256]{2,1,0:T(8,128)(2,1)S(1)} %collective-permute-done.14.refs_0_), channel_id=1, source_target_pairs={{0,1},{2,4},{4,2},{6,7},{7,6},{5,3},{3,5},{1,0},{8,9},{10,12},{12,... | collective-permute-start | bytes 884744 | tf_op jit(solution)/shard_map/ppermute | solution.py:289
  20.4 13.8 %collective-permute-start.18 = (bf16[3,192,256]{2,1,0:T(8,128)(2,1)S(1)}, bf16[3,192,256]{2,1,0:T(8,128)(2,1)S(1)}, u32[]{:S(2)}, u32[]{:S(2)}) collective-permute-start(bf16[3,192,256]{2,1,0:T(8,128)(2,1)S(1)} %collective-permute-done.17.refs_1_), channel_id=1, source_target_pairs={{0,2},{2,0},{4,6},{6,4},{7,5},{5,7},{3,1},{1,3},{8,10},{10,8},{12,... | collective-permute-start | bytes 884744 | tf_op jit(solution)/shard_map/ppermute | solution.py:289
  26.7 17.7 %collective-permute-start.9 = (bf16[3,192,256]{2,1,0:T(8,128)(2,1)S(1)}, bf16[3,192,256]{2,1,0:T(8,128)(2,1)S(1)}, u32[]{:S(2)}, u32[]{:S(2)}) collective-permute-start(bf16[3,192,256]{2,1,0:T(8,128)(2,1)S(1)} %collective-permute-done.8.refs_1_), channel_id=1, source_target_pairs={{0,2},{2,0},{4,6},{6,4},{7,5},{5,7},{3,1},{1,3},{8,10},{10,8},{12,... | collective-permute-start | bytes 884744 | tf_op jit(solution)/shard_map/ppermute | solution.py:289
  27.9 17.8 %collective-permute-start.5 = (bf16[3,192,256]{2,1,0:T(8,128)(2,1)S(1)}, bf16[3,192,256]{2,1,0:T(8,128)(2,1)S(1)}, u32[]{:S(2)}, u32[]{:S(2)}) collective-permute-start(bf16[3,192,256]{2,1,0:T(8,128)(2,1)S(1)} %collective-permute-done.4.refs_0_), channel_id=1, source_target_pairs={{0,1},{2,4},{4,2},{6,7},{7,6},{5,3},{3,5},{1,0},{8,9},{10,12},{12,... | collective-permute-start | bytes 884744 | tf_op jit(solution)/shard_map/ppermute | solution.py:289
  33.0 16.4 %collective-permute-start.16 = (bf16[3,192,256]{2,1,0:T(8,128)(2,1)S(1)}, bf16[3,192,256]{2,1,0:T(8,128)(2,1)S(1)}, u32[]{:S(2)}, u32[]{:S(2)}) collective-permute-start(bf16[3,192,256]{2,1,0:T(8,128)(2,1)S(1)} %collective-permute-done.15.refs_0_), channel_id=1, source_target_pairs={{0,2},{2,0},{4,6},{6,4},{7,5},{5,7},{3,1},{1,3},{8,10},{10,8},{12,... | collective-permute-start | bytes 884744 | tf_op jit(solution)/shard_map/ppermute | solution.py:289
  34.2 15.3 %collective-permute-start.19 = (bf16[3,192,256]{2,1,0:T(8,128)(2,1)S(1)}, bf16[3,192,256]{2,1,0:T(8,128)(2,1)S(1)}, u32[]{:S(2)}, u32[]{:S(2)}) collective-permute-start(bf16[3,192,256]{2,1,0:T(8,128)(2,1)S(1)} %collective-permute-done.18.refs_1_), channel_id=1, source_target_pairs={{0,1},{2,4},{4,2},{6,7},{7,6},{5,3},{3,5},{1,0},{8,9},{10,12},{12,... | collective-permute-start | bytes 884744 | tf_op jit(solution)/shard_map/ppermute | solution.py:289
  44.4 11.1 %collective-permute-start.10 = (bf16[3,192,256]{2,1,0:T(8,128)(2,1)S(1)}, bf16[3,192,256]{2,1,0:T(8,128)(2,1)S(1)}, u32[]{:S(2)}, u32[]{:S(2)}) collective-permute-start(bf16[3,192,256]{2,1,0:T(8,128)(2,1)S(1)} %collective-permute-done.9.refs_1_), channel_id=1, source_target_pairs={{0,1},{2,4},{4,2},{6,7},{7,6},{5,3},{3,5},{1,0},{8,9},{10,12},{12,... | collective-permute-start | bytes 884744 | tf_op jit(solution)/shard_map/ppermute | solution.py:289
  45.7 10.2 %collective-permute-start.6 = (bf16[3,192,256]{2,1,0:T(8,128)(2,1)S(1)}, bf16[3,192,256]{2,1,0:T(8,128)(2,1)S(1)}, u32[]{:S(2)}, u32[]{:S(2)}) collective-permute-start(bf16[3,192,256]{2,1,0:T(8,128)(2,1)S(1)} %collective-permute-done.5.refs_0_), channel_id=1, source_target_pairs={{0,2},{2,0},{4,6},{6,4},{7,5},{5,7},{3,1},{1,3},{8,10},{10,8},{12,... | collective-permute-start | bytes 884744 | tf_op jit(solution)/shard_map/ppermute | solution.py:289
  53.4 3.8 %collective-permute-start.21 = (f32[64,512]{1,0:T(8,128)S(1)}, f32[64,512]{1,0:T(8,128)S(1)}, u32[]{:S(2)}, u32[]{:S(2)}) collective-permute-start(f32[64,512]{1,0:T(8,128)S(1)} %get-tuple-element.32), channel_id=1, source_target_pairs={{0,8},{8,0},{16,24},{24,16},{1,9},{9,1},{17,25},{25,17},{2,10},{10... | collective-permute-start | bytes 393224 | tf_op jit(solution)/shard_map/ppermute | solution.py:284
  53.5 31.2 %collective-permute-start = (bf16[128,1536]{1,0:T(8,128)(2,1)S(1)}, bf16[128,1536]{1,0:T(8,128)(2,1)S(1)}, u32[]{:S(2)}, u32[]{:S(2)}) collective-permute-start(bf16[128,1536]{1,0:T(8,128)(2,1)S(1)} %get-tuple-element.24.refs_0_), channel_id=1, source_target_pairs={{0,8},{8,0},{16,24},{24,16},{1,9},{9,1},{17,25},{25,17},{2,10},{10... | collective-permute-start | bytes 1179656 | tf_op jit(solution)/shard_map/ppermute | solution.py:284
  54.0 32.2 %collective-permute-start.1 = (bf16[128,1536]{1,0:T(8,128)(2,1)S(1)}, bf16[128,1536]{1,0:T(8,128)(2,1)S(1)}, u32[]{:S(2)}, u32[]{:S(2)}) collective-permute-start(bf16[128,1536]{1,0:T(8,128)(2,1)S(1)} %get-tuple-element.24.refs_0_), channel_id=1, source_target_pairs={{0,16},{8,24},{16,0},{24,8},{1,17},{9,25},{17,1},{25,9},{2,18},{10... | collective-permute-start | bytes 1179656 | tf_op jit(solution)/shard_map/ppermute | solution.py:284
  55.5 30.7 %collective-permute-start.2 = (bf16[128,1536]{1,0:T(8,128)(2,1)S(1)}, bf16[128,1536]{1,0:T(8,128)(2,1)S(1)}, u32[]{:S(2)}, u32[]{:S(2)}) collective-permute-start(bf16[128,1536]{1,0:T(8,128)(2,1)S(1)} %get-tuple-element.24.refs_0_), channel_id=1, source_target_pairs={{0,24},{8,16},{16,8},{24,0},{1,25},{9,17},{17,9},{25,1},{2,26},{10... | collective-permute-start | bytes 1179656 | tf_op jit(solution)/shard_map/ppermute | solution.py:284
  57.2 1.9 %collective-permute-start.12 = (f32[64,512]{1,0:T(8,128)S(1)}, f32[64,512]{1,0:T(8,128)S(1)}, u32[]{:S(2)}, u32[]{:S(2)}) collective-permute-start(f32[64,512]{1,0:T(8,128)S(1)} %get-tuple-element.29), channel_id=1, source_target_pairs={{0,8},{8,0},{16,24},{24,16},{1,9},{9,1},{17,25},{25,17},{2,10},{10... | collective-permute-start | bytes 393224 | tf_op jit(solution)/shard_map/ppermute | solution.py:284
  57.6 18.7 %collective-permute-start.22 = (f32[64,512]{1,0:T(8,128)S(1)}, f32[64,512]{1,0:T(8,128)S(1)}, u32[]{:S(2)}, u32[]{:S(2)}) collective-permute-start(f32[64,512]{1,0:T(8,128)S(1)} %bitcast_add_fusion), channel_id=1, source_target_pairs={{0,16},{8,24},{16,0},{24,8},{1,17},{9,25},{17,1},{25,9},{2,18},{10... | collective-permute-start | bytes 393224 | tf_op jit(solution)/shard_map/ppermute | solution.py:284
  59.1 18.7 %collective-permute-start.11 = (f32[64,512]{1,0:T(8,128)S(1)}, f32[64,512]{1,0:T(8,128)S(1)}, u32[]{:S(2)}, u32[]{:S(2)}) collective-permute-start(f32[64,512]{1,0:T(8,128)S(1)} %get-tuple-element.28), channel_id=1, source_target_pairs={{0,8},{8,0},{16,24},{24,16},{1,9},{9,1},{17,25},{25,17},{2,10},{10... | collective-permute-start | bytes 393224 | tf_op jit(solution)/shard_map/ppermute | solution.py:284
  76.3 4.3 %collective-permute-start.13 = (bf16[64,512]{1,0:T(8,128)(2,1)S(1)}, bf16[64,512]{1,0:T(8,128)(2,1)S(1)}, u32[]{:S(2)}, u32[]{:S(2)}) collective-permute-start(bf16[64,512]{1,0:T(8,128)(2,1)S(1)} %get-tuple-element.46), channel_id=1, source_target_pairs={{0,16},{8,24},{16,0},{24,8},{1,17},{9,25},{17,1},{25,9},{2,18},{10... | collective-permute-start | bytes 196616 | tf_op jit(solution)/shard_map/ppermute | solution.py:284
  80.7 6.2 %collective-permute-start.24 = (bf16[64,512]{1,0:T(8,128)(2,1)S(1)}, bf16[64,512]{1,0:T(8,128)(2,1)S(1)}, u32[]{:S(2)}, u32[]{:S(2)}) collective-permute-start(bf16[64,512]{1,0:T(8,128)(2,1)S(1)} %get-tuple-element.41.refs_3_), channel_id=1, source_target_pairs={{0,1},{1,0},{2,3},{3,2},{4,5},{5,4},{6,7},{7,6},{8,9},{9,8},{10,11... | collective-permute-start | bytes 196616 | tf_op jit(solution)/shard_map/ppermute | solution.py:292
  82.2 7.0 %collective-permute-start.25 = (bf16[64,512]{1,0:T(8,128)(2,1)S(1)}, bf16[64,512]{1,0:T(8,128)(2,1)S(1)}, u32[]{:S(2)}, u32[]{:S(2)}) collective-permute-start(bf16[64,512]{1,0:T(8,128)(2,1)S(1)} %get-tuple-element.41.refs_3_), channel_id=1, source_target_pairs={{0,7},{1,2},{2,1},{3,4},{4,3},{5,6},{6,5},{7,0},{8,15},{9,10},{10,... | collective-permute-start | bytes 196616 | tf_op jit(solution)/shard_map/ppermute | solution.py:292
  84.7 7.4 %collective-permute-start.23 = (bf16[64,512]{1,0:T(8,128)(2,1)S(1)}, bf16[64,512]{1,0:T(8,128)(2,1)S(1)}, u32[]{:S(2)}, u32[]{:S(2)}) collective-permute-start(bf16[64,512]{1,0:T(8,128)(2,1)S(1)} %get-tuple-element.45), channel_id=1, source_target_pairs={{0,16},{8,24},{16,0},{24,8},{1,17},{9,25},{17,1},{25,9},{2,18},{10... | collective-permute-start | bytes 196616 | tf_op jit(solution)/shard_map/ppermute | solution.py:284
  89.5 4.3 %collective-permute-start.26 = (bf16[64,512]{1,0:T(8,128)(2,1)S(1)}, bf16[64,512]{1,0:T(8,128)(2,1)S(1)}, u32[]{:S(2)}, u32[]{:S(2)}) collective-permute-start(bf16[64,512]{1,0:T(8,128)(2,1)S(1)} %get-tuple-element.34.refs_3_), channel_id=1, source_target_pairs={{0,1},{1,0},{2,3},{3,2},{4,5},{5,4},{6,7},{7,6},{8,9},{9,8},{10,11... | collective-permute-start | bytes 196616 | tf_op jit(solution)/shard_map/ppermute | solution.py:292
  89.6 7.0 %collective-permute-start.27 = (bf16[64,512]{1,0:T(8,128)(2,1)S(1)}, bf16[64,512]{1,0:T(8,128)(2,1)S(1)}, u32[]{:S(2)}, u32[]{:S(2)}) collective-permute-start(bf16[64,512]{1,0:T(8,128)(2,1)S(1)} %get-tuple-element.34.refs_3_), channel_id=1, source_target_pairs={{0,7},{1,2},{2,1},{3,4},{4,3},{5,6},{6,5},{7,0},{8,15},{9,10},{10,... | collective-permute-start | bytes 196616 | tf_op jit(solution)/shard_map/ppermute | solution.py:292
  96.9 4.3 %collective-permute-start.28 = (bf16[64,512]{1,0:T(8,128)(2,1)S(1)}, bf16[64,512]{1,0:T(8,128)(2,1)S(1)}, u32[]{:S(2)}, u32[]{:S(2)}) collective-permute-start(bf16[64,512]{1,0:T(8,128)(2,1)S(1)} %get-tuple-element.36.refs_3_), channel_id=1, source_target_pairs={{0,1},{1,0},{2,3},{3,2},{4,5},{5,4},{6,7},{7,6},{8,9},{9,8},{10,11... | collective-permute-start | bytes 196616 | tf_op jit(solution)/shard_map/ppermute | solution.py:292
  97.1 7.0 %collective-permute-start.29 = (bf16[64,512]{1,0:T(8,128)(2,1)S(1)}, bf16[64,512]{1,0:T(8,128)(2,1)S(1)}, u32[]{:S(2)}, u32[]{:S(2)}) collective-permute-start(bf16[64,512]{1,0:T(8,128)(2,1)S(1)} %get-tuple-element.36.refs_3_), channel_id=1, source_target_pairs={{0,7},{1,2},{2,1},{3,4},{4,3},{5,6},{6,5},{7,0},{8,15},{9,10},{10,... | collective-permute-start | bytes 196616 | tf_op jit(solution)/shard_map/ppermute | solution.py:292
  104.4 1.9 %collective-permute-start.30 = (f32[64,128]{1,0:T(8,128)S(1)}, f32[64,128]{1,0:T(8,128)S(1)}, u32[]{:S(2)}, u32[]{:S(2)}) collective-permute-start(f32[64,128]{1,0:T(8,128)S(1)} %get-tuple-element.38), channel_id=1, source_target_pairs={{0,8},{8,0},{16,24},{24,16},{1,9},{9,1},{17,25},{25,17},{2,10},{10... | collective-permute-start | bytes 98312 | tf_op jit(solution)/shard_map/ppermute | solution.py:284
  104.4 4.0 %collective-permute-start.31 = (f32[64,128]{1,0:T(8,128)S(1)}, f32[64,128]{1,0:T(8,128)S(1)}, u32[]{:S(2)}, u32[]{:S(2)}) collective-permute-start(f32[64,128]{1,0:T(8,128)S(1)} %get-tuple-element.39), channel_id=1, source_target_pairs={{0,16},{8,24},{16,0},{24,8},{1,17},{9,25},{17,1},{25,9},{2,18},{10... | collective-permute-start | bytes 98312 | tf_op jit(solution)/shard_map/ppermute | solution.py:284
  106.0 3.4 %collective-permute-start.32 = (f32[64,128]{1,0:T(8,128)S(1)}, f32[64,128]{1,0:T(8,128)S(1)}, u32[]{:S(2)}, u32[]{:S(2)}) collective-permute-start(f32[64,128]{1,0:T(8,128)S(1)} %get-tuple-element.40), channel_id=1, source_target_pairs={{0,24},{8,16},{16,8},{24,0},{1,25},{9,17},{17,9},{25,1},{2,26},{10... | collective-permute-start | bytes 98312 | tf_op jit(solution)/shard_map/ppermute | solution.py:284
  (9 other events, 20.0 us)

commit v8 on v7

--- a/solution.py
+++ b/solution.py
@@ -185,7 +185,8 @@
     width, rows = driven.shape
 
     def body(*refs):
-        dense_ref, driven_ref, density_ref, rounded_ref, side_ref, out_ref = refs[:5] + refs[-1 if last else 5 :][:1]
+        dense_ref, driven_ref, density_ref, rounded_ref = refs[:4]
+        out_ref = refs[-1]
 
         def term(ref, k):
             return lax.dot_general(
@@ -195,7 +196,9 @@
                 preferred_element_type=jnp.float32,
             )
 
-        near = term(rounded_ref, 1) + term(side_ref, 2)
+        near = term(rounded_ref, 1)
+        if near_side is not None:
+            near = near + term(refs[4], 2)
         old = density_ref[...]
         out_ref[...] = old + damping * (driven_ref[...] - old - near)
         if last:
@@ -206,25 +209,35 @@
                 refs[6][:, m * height : (m + 1) * height] = out_ref[:, pl.ds(at, height)]
 
     last = chosen is not None
+    sides = [] if near_side is None else [near_side]
     whole = (width, rows)
     return pl.pallas_call(
         body,
         out_shape=jax.ShapeDtypeStruct(whole, jnp.float32),
-        in_specs=[VMEM] * 5 + [SMEM] * last,
+        in_specs=[VMEM] * (4 + len(sides)) + [SMEM] * last,
         out_specs=VMEM,
         scratch_shapes=[pltpu.VMEM(whole, jnp.float32)] * last,
         compiler_params=params(8 if rows <= 512 else 24),
         cost_estimate=cost(4 * width * rows * rows, 4 * rows * rows + 16 * width * rows),
         name="steady",
-    )(dense, driven, density, rounded, near_side, *([chosen] if last else []))
-
-
-def sweep(dense, base, far_side, pieces):
+    )(dense, driven, density, rounded, *sides, *([chosen] if last else []))
+
+
+def sweep(dense, base, far_side, near_side, pieces):
     width, rows = base.shape
 
-    def body(dense_ref, base_ref, side_ref, *outs):
-        near = lax.dot_general(
-            side_ref[...], dense_ref[:, :rows], (((1,), (1,)), ((), ())), preferred_element_type=jnp.float32
+    sides = [(far_side, 0)] + ([] if near_side is None else [(near_side, 2)])
+
+    def body(dense_ref, base_ref, *refs):
+        side_refs, outs = refs[: len(sides)], refs[len(sides) :]
+        near = sum(
+            lax.dot_general(
+                ref[...],
+                dense_ref[:, k * rows : (k + 1) * rows],
+                (((1,), (1,)), ((), ())),
+                preferred_element_type=jnp.float32,
+            )
+            for ref, (_, k) in zip(side_refs, sides)
         )
         new = base_ref[...] - damping * near
         if pieces:
@@ -242,12 +255,12 @@
     return pl.pallas_call(
         body,
         out_shape=out_shape,
-        in_specs=[VMEM] * 3,
+        in_specs=[VMEM] * (2 + len(sides)),
         out_specs=[VMEM] * len(out_shape),
         compiler_params=params(8 if rows <= 512 else 24),
         cost_estimate=cost(2 * width * rows * rows, 2 * rows * rows + 12 * width * rows),
         name="sweep",
-    )(dense, base, far_side)
+    )(dense, base, *[side for side, _ in sides])
 
 
 def assemble(pieces):
@@ -333,7 +346,7 @@
         moving = turns[0] | turns[1]
         for rank in range(2):
             blocks = [(step, side, i, x) for (side, i), x in turns[rank].items()]
-            early = (step, rank) == (final - 1, 1)
+            early = (step, rank) == (final - 1, 0)
             field = (incident[0], chosen) if early else (None, None)
             total = multiply(kernels, blocks, total, *field, row_count if early else 0)
             if early:
@@ -354,8 +367,9 @@
             rest = sum(across_rows(x, m).astype(jnp.float32) for m, x in lost)
         if step == 1:
             driven, density = driven - rest, density - rest
-        base = steady(dense, driven, density, rounded, near_side, chosen if last else None)
-        result = sweep(dense_last if last else dense, base, far_side, row_count if last else 0)
+        early_side_only, late_side = (None, near_side) if step == 0 else (near_side, None)
+        base = steady(dense, driven, density, rounded, early_side_only, chosen if last else None)
+        result = sweep(dense_last if last else dense, base, far_side, late_side, row_count if last else 0)
         if step < SWEEPS - 1:
             density, rounded = result
 

time: 110 us -> 110 us (level)
  local copies, waits for them, and re-layouts: 9.57 us -> 7.34 us
  waiting for transfers between devices: 47.2 us -> 48.8 us
    unnamed x16, local copies, waits for them, and re-layouts: 8.48 us -> 6.2 us
    ppermute x14, starting transfers between devices: 21.6 us -> 23.7 us  [swap_walk(): lax.ppermute(x, 'col', [(walk[p], walk[mate(p, side, col_count)]) for p i...]
    ppermute x14, waiting for transfers between devices: 14.6 us -> 16.2 us  [swap_walk(): lax.ppermute(x, 'col', [(walk[p], walk[mate(p, side, col_count)]) for p i...]
    ppermute x6, starting transfers between devices: 9.28 us -> 7.7 us  [swap_cols(): lax.ppermute(x, 'col', [(c, mate(c, side, col_count)) for c in range(col_...]
  transfers between devices with their start and end apart: 33 -> 33, of which waited for: 16 -> 18; matrix products, arithmetic and copies ran while one was open for 0% -> 0% of each run, Pallas kernels for 10% -> 10%
where the time goes in v8:
time: 110 us
  waiting for transfers between devices  48.8 us (44%)
  starting transfers between devices  40.9 us (37%)
  Pallas kernels  12.1 us (11%)
  local copies, waits for them, and re-layouts  7.34 us (7%)
    ppermute x14, starting transfers between devices, swap_walk(): lax.ppermute(x, 'col', [(walk[p], walk[mate(p, side, col_count)]) for p i...  23.7 us
    ppermute x13, waiting for transfers between devices, across_rows(): return lax.ppermute(x, 'row', [(i, i ^ m) for i in range(row_count)])  22.4 us
    ppermute x14, waiting for transfers between devices, swap_walk(): lax.ppermute(x, 'col', [(walk[p], walk[mate(p, side, col_count)]) for p i...  16.2 us
    ppermute x6, waiting for transfers between devices, swap_cols(): lax.ppermute(x, 'col', [(c, mate(c, side, col_count)) for c in range(col_...  10.1 us
    ppermute x13, starting transfers between devices, across_rows(): return lax.ppermute(x, 'row', [(i, i ^ m) for i in range(row_count)])  9.49 us
    ppermute x6, starting transfers between devices, swap_cols(): lax.ppermute(x, 'col', [(c, mate(c, side, col_count)) for c in range(col_...  7.7 us
    pallas_call x9, Pallas kernels, multiply(): pl.pallas_call(body, out_shape=out_shape, in_specs=in_specs, out_specs=[V...  6.49 us
    unnamed x16, local copies, waits for them, and re-layouts  6.2 us
  transfers between devices with their start and end apart: 33, of which 18 were waited for; matrix products, arithmetic and copies ran while one was open for 0% of the time, Pallas kernels for 10%

profile of v8, /device:TPU:0, one launch (start us, length us, event | category | flops | bytes accessed | tf_op | source)
XLA Modules:
  0.0 110.1 jit_solution(4431422502835786335)
XLA Ops:
  1.2 3.1 %collective-permute-start.7 = (bf16[3,192,256]{2,1,0:T(8,128)(2,1)S(1)}, bf16[3,192,256]{2,1,0:T(8,128)(2,1)S(1)}, u32[]{:S(2)}, u32[]{:S(2)}) collective-permute-start(bf16[3,192,256]{2,1,0:T(8,128)(2,1)S(1)} %get-tuple-element.43.refs_1_), channel_id=1, source_target_pairs={{0,2},{2,0},{4,6},{6,4},{7,5},{5,7},{3,1},{1,3},{8,10},{10,8},{12,... | collective-permute-start | bytes 884744 | tf_op jit(solution)/shard_map/ppermute | solution.py:302
  5.8 1.7 %collective-permute-start.11 = (bf16[3,192,256]{2,1,0:T(8,128)(2,1)S(1)}, bf16[3,192,256]{2,1,0:T(8,128)(2,1)S(1)}, u32[]{:S(2)}, u32[]{:S(2)}) collective-permute-start(bf16[3,192,256]{2,1,0:T(8,128)(2,1)S(1)} %get-tuple-element.44.refs_0_), channel_id=1, source_target_pairs={{0,2},{2,0},{4,6},{6,4},{7,5},{5,7},{3,1},{1,3},{8,10},{10,8},{12,... | collective-permute-start | bytes 884744 | tf_op jit(solution)/shard_map/ppermute | solution.py:302
  8.9 3.2 %collective-permute-done.7.refs_1_ = bf16[3,192,256]{2,1,0:T(8,128)(2,1)S(1)} collective-permute-done((bf16[3,192,256]{2,1,0:T(8,128)(2,1)S(1)}, bf16[3,192,256]{2,1,0:T(8,128)(2,1)S(1)}, u32[]{:S(2)}, u32[]{:S(2)}) %collective-permute-start.7) | collective-permute-done | bytes 294944 | tf_op jit(solution)/shard_map/ppermute | solution.py:302
  12.1 1.9 %collective-permute-start.8 = (bf16[3,192,256]{2,1,0:T(8,128)(2,1)S(1)}, bf16[3,192,256]{2,1,0:T(8,128)(2,1)S(1)}, u32[]{:S(2)}, u32[]{:S(2)}) collective-permute-start(bf16[3,192,256]{2,1,0:T(8,128)(2,1)S(1)} %collective-permute-done.7.refs_1_), channel_id=1, source_target_pairs={{0,1},{2,4},{4,2},{6,7},{7,6},{5,3},{3,5},{1,0},{8,9},{10,12},{12,... | collective-permute-start | bytes 884744 | tf_op jit(solution)/shard_map/ppermute | solution.py:302
  14.2 1.6 %collective-permute-start.4 = (bf16[3,192,256]{2,1,0:T(8,128)(2,1)S(1)}, bf16[3,192,256]{2,1,0:T(8,128)(2,1)S(1)}, u32[]{:S(2)}, u32[]{:S(2)}) collective-permute-start(bf16[3,192,256]{2,1,0:T(8,128)(2,1)S(1)} %collective-permute-done.3.refs_0_), channel_id=1, source_target_pairs={{0,2},{2,0},{4,6},{6,4},{7,5},{5,7},{3,1},{1,3},{8,10},{10,8},{12,... | collective-permute-start | bytes 884744 | tf_op jit(solution)/shard_map/ppermute | solution.py:302
  15.7 2.7 %collective-permute-done.11.refs_0_ = bf16[3,192,256]{2,1,0:T(8,128)(2,1)S(1)} collective-permute-done((bf16[3,192,256]{2,1,0:T(8,128)(2,1)S(1)}, bf16[3,192,256]{2,1,0:T(8,128)(2,1)S(1)}, u32[]{:S(2)}, u32[]{:S(2)}) %collective-permute-start.11) | collective-permute-done | bytes 294944 | tf_op jit(solution)/shard_map/ppermute | solution.py:302
  18.5 1.9 %collective-permute-start.12 = (bf16[3,192,256]{2,1,0:T(8,128)(2,1)S(1)}, bf16[3,192,256]{2,1,0:T(8,128)(2,1)S(1)}, u32[]{:S(2)}, u32[]{:S(2)}) collective-permute-start(bf16[3,192,256]{2,1,0:T(8,128)(2,1)S(1)} %collective-permute-done.11.refs_0_), channel_id=1, source_target_pairs={{0,1},{2,4},{4,2},{6,7},{7,6},{5,3},{3,5},{1,0},{8,9},{10,12},{12,... | collective-permute-start | bytes 884744 | tf_op jit(solution)/shard_map/ppermute | solution.py:302
  20.5 1.6 %collective-permute-start.15 = (bf16[3,192,256]{2,1,0:T(8,128)(2,1)S(1)}, bf16[3,192,256]{2,1,0:T(8,128)(2,1)S(1)}, u32[]{:S(2)}, u32[]{:S(2)}) collective-permute-start(bf16[3,192,256]{2,1,0:T(8,128)(2,1)S(1)} %collective-permute-done.14.refs_1_), channel_id=1, source_target_pairs={{0,2},{2,0},{4,6},{6,4},{7,5},{5,7},{3,1},{1,3},{8,10},{10,8},{12,... | collective-permute-start | bytes 884744 | tf_op jit(solution)/shard_map/ppermute | solution.py:302
  22.1 4.7 %collective-permute-done.8.refs_1_ = bf16[3,192,256]{2,1,0:T(8,128)(2,1)S(1)} collective-permute-done((bf16[3,192,256]{2,1,0:T(8,128)(2,1)S(1)}, bf16[3,192,256]{2,1,0:T(8,128)(2,1)S(1)}, u32[]{:S(2)}, u32[]{:S(2)}) %collective-permute-start.8) | collective-permute-done | bytes 294944 | tf_op jit(solution)/shard_map/ppermute | solution.py:302
  27.9 1.5 %collective-permute-start.5 = (bf16[3,192,256]{2,1,0:T(8,128)(2,1)S(1)}, bf16[3,192,256]{2,1,0:T(8,128)(2,1)S(1)}, u32[]{:S(2)}, u32[]{:S(2)}) collective-permute-start(bf16[3,192,256]{2,1,0:T(8,128)(2,1)S(1)} %collective-permute-done.4.refs_0_), channel_id=1, source_target_pairs={{0,1},{2,4},{4,2},{6,7},{7,6},{5,3},{3,5},{1,0},{8,9},{10,12},{12,... | collective-permute-start | bytes 884744 | tf_op jit(solution)/shard_map/ppermute | solution.py:302
  29.4 3.7 %collective-permute-done.12.refs_0_ = bf16[3,192,256]{2,1,0:T(8,128)(2,1)S(1)} collective-permute-done((bf16[3,192,256]{2,1,0:T(8,128)(2,1)S(1)}, bf16[3,192,256]{2,1,0:T(8,128)(2,1)S(1)}, u32[]{:S(2)}, u32[]{:S(2)}) %collective-permute-start.12) | collective-permute-done | bytes 294944 | tf_op jit(solution)/shard_map/ppermute | solution.py:302
  34.2 1.5 %collective-permute-start.16 = (bf16[3,192,256]{2,1,0:T(8,128)(2,1)S(1)}, bf16[3,192,256]{2,1,0:T(8,128)(2,1)S(1)}, u32[]{:S(2)}, u32[]{:S(2)}) collective-permute-start(bf16[3,192,256]{2,1,0:T(8,128)(2,1)S(1)} %collective-permute-done.15.refs_1_), channel_id=1, source_target_pairs={{0,1},{2,4},{4,2},{6,7},{7,6},{5,3},{3,5},{1,0},{8,9},{10,12},{12,... | collective-permute-start | bytes 884744 | tf_op jit(solution)/shard_map/ppermute | solution.py:302
  35.7 1.7 %collective-permute-done.9.refs_1_ = bf16[3,192,256]{2,1,0:T(8,128)(2,1)S(1)} collective-permute-done((bf16[3,192,256]{2,1,0:T(8,128)(2,1)S(1)}, bf16[3,192,256]{2,1,0:T(8,128)(2,1)S(1)}, u32[]{:S(2)}, u32[]{:S(2)}) %collective-permute-start.9) | collective-permute-done | bytes 294944 | tf_op jit(solution)/shard_map/ppermute | solution.py:302
  37.4 1.9 %collective-permute-start.10 = (bf16[3,192,256]{2,1,0:T(8,128)(2,1)S(1)}, bf16[3,192,256]{2,1,0:T(8,128)(2,1)S(1)}, u32[]{:S(2)}, u32[]{:S(2)}) collective-permute-start(bf16[3,192,256]{2,1,0:T(8,128)(2,1)S(1)} %collective-permute-done.9.refs_1_), channel_id=1, source_target_pairs={{0,1},{2,4},{4,2},{6,7},{7,6},{5,3},{3,5},{1,0},{8,9},{10,12},{12,... | collective-permute-start | bytes 884744 | tf_op jit(solution)/shard_map/ppermute | solution.py:302
  39.3 3.7 %copy-done = bf16[6,512,1536]{2,1,0:T(8,128)(2,1)S(1)} copy-done((bf16[6,512,1536]{2,1,0:T(8,128)(2,1)S(1)}, bf16[6,512,1536]{2,1,0:T(8,128)(2,1)}, u32[]{:S(2)}) %copy-start) | copy-done | bytes 9437208
  45.8 1.7 %collective-permute-start.6 = (bf16[3,192,256]{2,1,0:T(8,128)(2,1)S(1)}, bf16[3,192,256]{2,1,0:T(8,128)(2,1)S(1)}, u32[]{:S(2)}, u32[]{:S(2)}) collective-permute-start(bf16[3,192,256]{2,1,0:T(8,128)(2,1)S(1)} %collective-permute-done.5.refs_0_), channel_id=1, source_target_pairs={{0,2},{2,0},{4,6},{6,4},{7,5},{5,7},{3,1},{1,3},{8,10},{10,8},{12,... | collective-permute-start | bytes 884744 | tf_op jit(solution)/shard_map/ppermute | solution.py:302
  54.8 1.5 %collective-permute-start.1 = (bf16[128,1536]{1,0:T(8,128)(2,1)S(1)}, bf16[128,1536]{1,0:T(8,128)(2,1)S(1)}, u32[]{:S(2)}, u32[]{:S(2)}) collective-permute-start(bf16[128,1536]{1,0:T(8,128)(2,1)S(1)} %get-tuple-element.24.refs_0_), channel_id=1, source_target_pairs={{0,16},{8,24},{16,0},{24,8},{1,17},{9,25},{17,1},{25,9},{2,18},{10... | collective-permute-start | bytes 1179656 | tf_op jit(solution)/shard_map/ppermute | solution.py:297
  59.2 1.5 %collective-permute-start.22 = (f32[64,512]{1,0:T(8,128)S(1)}, f32[64,512]{1,0:T(8,128)S(1)}, u32[]{:S(2)}, u32[]{:S(2)}) collective-permute-start(f32[64,512]{1,0:T(8,128)S(1)} %bitcast_add_fusion), channel_id=1, source_target_pairs={{0,16},{8,24},{16,0},{24,8},{1,17},{9,25},{17,1},{25,9},{2,18},{10... | collective-permute-start | bytes 393224 | tf_op jit(solution)/shard_map/ppermute | solution.py:297
  60.9 16.3 %collective-permute-done.22 = f32[64,512]{1,0:T(8,128)S(1)} collective-permute-done((f32[64,512]{1,0:T(8,128)S(1)}, f32[64,512]{1,0:T(8,128)S(1)}, u32[]{:S(2)}, u32[]{:S(2)}) %collective-permute-start.22) | collective-permute-done | bytes 131104 | tf_op jit(solution)/shard_map/ppermute | solution.py:297
  77.2 1.5 %collective-permute-start.19 = (bf16[64,512]{1,0:T(8,128)(2,1)S(1)}, bf16[64,512]{1,0:T(8,128)(2,1)S(1)}, u32[]{:S(2)}, u32[]{:S(2)}) collective-permute-start(bf16[64,512]{1,0:T(8,128)(2,1)S(1)} %get-tuple-element.46), channel_id=1, source_target_pairs={{0,16},{8,24},{16,0},{24,8},{1,17},{9,25},{17,1},{25,9},{2,18},{10... | collective-permute-start | bytes 196616 | tf_op jit(solution)/shard_map/ppermute | solution.py:297
  78.7 2.7 %collective-permute-done.19 = bf16[64,512]{1,0:T(8,128)(2,1)S(1)} collective-permute-done((bf16[64,512]{1,0:T(8,128)(2,1)S(1)}, bf16[64,512]{1,0:T(8,128)(2,1)S(1)}, u32[]{:S(2)}, u32[]{:S(2)}) %collective-permute-start.19) | collective-permute-done | bytes 65568 | tf_op jit(solution)/shard_map/ppermute | solution.py:297
  81.5 2.3 %collective-permute-start.24 = (bf16[64,512]{1,0:T(8,128)(2,1)S(1)}, bf16[64,512]{1,0:T(8,128)(2,1)S(1)}, u32[]{:S(2)}, u32[]{:S(2)}) collective-permute-start(bf16[64,512]{1,0:T(8,128)(2,1)S(1)} %get-tuple-element.41.refs_3_), channel_id=1, source_target_pairs={{0,7},{1,2},{2,1},{3,4},{4,3},{5,6},{6,5},{7,0},{8,15},{9,10},{10,... | collective-permute-start | bytes 196616 | tf_op jit(solution)/shard_map/ppermute | solution.py:305
  83.9 1.5 %collective-permute-start.23 = (bf16[64,512]{1,0:T(8,128)(2,1)S(1)}, bf16[64,512]{1,0:T(8,128)(2,1)S(1)}, u32[]{:S(2)}, u32[]{:S(2)}) collective-permute-start(bf16[64,512]{1,0:T(8,128)(2,1)S(1)} %get-tuple-element.45), channel_id=1, source_target_pairs={{0,16},{8,24},{16,0},{24,8},{1,17},{9,25},{17,1},{25,9},{2,18},{10... | collective-permute-start | bytes 196616 | tf_op jit(solution)/shard_map/ppermute | solution.py:297
  86.4 2.3 %collective-permute-done.24.refs_0_ = bf16[64,512]{1,0:T(8,128)(2,1)S(1)} collective-permute-done((bf16[64,512]{1,0:T(8,128)(2,1)S(1)}, bf16[64,512]{1,0:T(8,128)(2,1)S(1)}, u32[]{:S(2)}, u32[]{:S(2)}) %collective-permute-start.24) | collective-permute-done | bytes 65568 | tf_op jit(solution)/shard_map/ppermute | solution.py:305
  89.5 2.6 %collective-permute-start.27 = (bf16[64,512]{1,0:T(8,128)(2,1)S(1)}, bf16[64,512]{1,0:T(8,128)(2,1)S(1)}, u32[]{:S(2)}, u32[]{:S(2)}) collective-permute-start(bf16[64,512]{1,0:T(8,128)(2,1)S(1)} %get-tuple-element.34.refs_3_), channel_id=1, source_target_pairs={{0,7},{1,2},{2,1},{3,4},{4,3},{5,6},{6,5},{7,0},{8,15},{9,10},{10,... | collective-permute-start | bytes 196616 | tf_op jit(solution)/shard_map/ppermute | solution.py:305
  92.1 1.7 %collective-permute-done.26.refs_4_ = bf16[64,512]{1,0:T(8,128)(2,1)S(1)} collective-permute-done((bf16[64,512]{1,0:T(8,128)(2,1)S(1)}, bf16[64,512]{1,0:T(8,128)(2,1)S(1)}, u32[]{:S(2)}, u32[]{:S(2)}) %collective-permute-start.26) | collective-permute-done | bytes 65568 | tf_op jit(solution)/shard_map/ppermute | solution.py:305
  94.2 2.3 %collective-permute-done.27.refs_0_ = bf16[64,512]{1,0:T(8,128)(2,1)S(1)} collective-permute-done((bf16[64,512]{1,0:T(8,128)(2,1)S(1)}, bf16[64,512]{1,0:T(8,128)(2,1)S(1)}, u32[]{:S(2)}, u32[]{:S(2)}) %collective-permute-start.27) | collective-permute-done | bytes 65568 | tf_op jit(solution)/shard_map/ppermute | solution.py:305
  97.1 2.5 %collective-permute-start.29 = (bf16[64,512]{1,0:T(8,128)(2,1)S(1)}, bf16[64,512]{1,0:T(8,128)(2,1)S(1)}, u32[]{:S(2)}, u32[]{:S(2)}) collective-permute-start(bf16[64,512]{1,0:T(8,128)(2,1)S(1)} %get-tuple-element.36.refs_3_), channel_id=1, source_target_pairs={{0,7},{1,2},{2,1},{3,4},{4,3},{5,6},{6,5},{7,0},{8,15},{9,10},{10,... | collective-permute-start | bytes 196616 | tf_op jit(solution)/shard_map/ppermute | solution.py:305
  99.6 1.6 %collective-permute-done.28.refs_4_ = bf16[64,512]{1,0:T(8,128)(2,1)S(1)} collective-permute-done((bf16[64,512]{1,0:T(8,128)(2,1)S(1)}, bf16[64,512]{1,0:T(8,128)(2,1)S(1)}, u32[]{:S(2)}, u32[]{:S(2)}) %collective-permute-start.28) | collective-permute-done | bytes 65568 | tf_op jit(solution)/shard_map/ppermute | solution.py:305
  102.2 1.8 %collective-permute-done.29.refs_0_ = bf16[64,512]{1,0:T(8,128)(2,1)S(1)} collective-permute-done((bf16[64,512]{1,0:T(8,128)(2,1)S(1)}, bf16[64,512]{1,0:T(8,128)(2,1)S(1)}, u32[]{:S(2)}, u32[]{:S(2)}) %collective-permute-start.29) | collective-permute-done | bytes 65568 | tf_op jit(solution)/shard_map/ppermute | solution.py:305
  104.4 1.6 %collective-permute-start.31 = (f32[64,128]{1,0:T(8,128)S(1)}, f32[64,128]{1,0:T(8,128)S(1)}, u32[]{:S(2)}, u32[]{:S(2)}) collective-permute-start(f32[64,128]{1,0:T(8,128)S(1)} %get-tuple-element.39), channel_id=1, source_target_pairs={{0,16},{8,24},{16,0},{24,8},{1,17},{9,25},{17,1},{25,9},{2,18},{10... | collective-permute-start | bytes 98312 | tf_op jit(solution)/shard_map/ppermute | solution.py:297
  106.2 2.1 %collective-permute-done.31.refs_2_ = f32[64,128]{1,0:T(8,128)S(1)} collective-permute-done((f32[64,128]{1,0:T(8,128)S(1)}, f32[64,128]{1,0:T(8,128)S(1)}, u32[]{:S(2)}, u32[]{:S(2)}) %collective-permute-start.31) | collective-permute-done | bytes 32800 | tf_op jit(solution)/shard_map/ppermute | solution.py:297
  (74 shorter events, 25.0 us)
Async XLA Ops:
  1.2 11.0 %collective-permute-start.7 = (bf16[3,192,256]{2,1,0:T(8,128)(2,1)S(1)}, bf16[3,192,256]{2,1,0:T(8,128)(2,1)S(1)}, u32[]{:S(2)}, u32[]{:S(2)}) collective-permute-start(bf16[3,192,256]{2,1,0:T(8,128)(2,1)S(1)} %get-tuple-element.43.refs_1_), channel_id=1, source_target_pairs={{0,2},{2,0},{4,6},{6,4},{7,5},{5,7},{3,1},{1,3},{8,10},{10,8},{12,... | collective-permute-start | bytes 884744 | tf_op jit(solution)/shard_map/ppermute | solution.py:302
  4.3 9.9 %collective-permute-start.3 = (bf16[3,192,256]{2,1,0:T(8,128)(2,1)S(1)}, bf16[3,192,256]{2,1,0:T(8,128)(2,1)S(1)}, u32[]{:S(2)}, u32[]{:S(2)}) collective-permute-start(bf16[3,192,256]{2,1,0:T(8,128)(2,1)S(1)} %get-tuple-element.44.refs_0_), channel_id=1, source_target_pairs={{0,1},{2,4},{4,2},{6,7},{7,6},{5,3},{3,5},{1,0},{8,9},{10,12},{12,... | collective-permute-start | bytes 884744 | tf_op jit(solution)/shard_map/ppermute | solution.py:302
  5.8 12.7 %collective-permute-start.11 = (bf16[3,192,256]{2,1,0:T(8,128)(2,1)S(1)}, bf16[3,192,256]{2,1,0:T(8,128)(2,1)S(1)}, u32[]{:S(2)}, u32[]{:S(2)}) collective-permute-start(bf16[3,192,256]{2,1,0:T(8,128)(2,1)S(1)} %get-tuple-element.44.refs_0_), channel_id=1, source_target_pairs={{0,2},{2,0},{4,6},{6,4},{7,5},{5,7},{3,1},{1,3},{8,10},{10,8},{12,... | collective-permute-start | bytes 884744 | tf_op jit(solution)/shard_map/ppermute | solution.py:302
  7.4 13.0 %collective-permute-start.14 = (bf16[3,192,256]{2,1,0:T(8,128)(2,1)S(1)}, bf16[3,192,256]{2,1,0:T(8,128)(2,1)S(1)}, u32[]{:S(2)}, u32[]{:S(2)}) collective-permute-start(bf16[3,192,256]{2,1,0:T(8,128)(2,1)S(1)} %get-tuple-element.43.refs_1_), channel_id=1, source_target_pairs={{0,1},{2,4},{4,2},{6,7},{7,6},{5,3},{3,5},{1,0},{8,9},{10,12},{12,... | collective-permute-start | bytes 884744 | tf_op jit(solution)/shard_map/ppermute | solution.py:302
  12.1 14.7 %collective-permute-start.8 = (bf16[3,192,256]{2,1,0:T(8,128)(2,1)S(1)}, bf16[3,192,256]{2,1,0:T(8,128)(2,1)S(1)}, u32[]{:S(2)}, u32[]{:S(2)}) collective-permute-start(bf16[3,192,256]{2,1,0:T(8,128)(2,1)S(1)} %collective-permute-done.7.refs_1_), channel_id=1, source_target_pairs={{0,1},{2,4},{4,2},{6,7},{7,6},{5,3},{3,5},{1,0},{8,9},{10,12},{12,... | collective-permute-start | bytes 884744 | tf_op jit(solution)/shard_map/ppermute | solution.py:302
  14.2 13.8 %collective-permute-start.4 = (bf16[3,192,256]{2,1,0:T(8,128)(2,1)S(1)}, bf16[3,192,256]{2,1,0:T(8,128)(2,1)S(1)}, u32[]{:S(2)}, u32[]{:S(2)}) collective-permute-start(bf16[3,192,256]{2,1,0:T(8,128)(2,1)S(1)} %collective-permute-done.3.refs_0_), channel_id=1, source_target_pairs={{0,2},{2,0},{4,6},{6,4},{7,5},{5,7},{3,1},{1,3},{8,10},{10,8},{12,... | collective-permute-start | bytes 884744 | tf_op jit(solution)/shard_map/ppermute | solution.py:302
  18.5 14.7 %collective-permute-start.12 = (bf16[3,192,256]{2,1,0:T(8,128)(2,1)S(1)}, bf16[3,192,256]{2,1,0:T(8,128)(2,1)S(1)}, u32[]{:S(2)}, u32[]{:S(2)}) collective-permute-start(bf16[3,192,256]{2,1,0:T(8,128)(2,1)S(1)} %collective-permute-done.11.refs_0_), channel_id=1, source_target_pairs={{0,1},{2,4},{4,2},{6,7},{7,6},{5,3},{3,5},{1,0},{8,9},{10,12},{12,... | collective-permute-start | bytes 884744 | tf_op jit(solution)/shard_map/ppermute | solution.py:302
  20.5 13.8 %collective-permute-start.15 = (bf16[3,192,256]{2,1,0:T(8,128)(2,1)S(1)}, bf16[3,192,256]{2,1,0:T(8,128)(2,1)S(1)}, u32[]{:S(2)}, u32[]{:S(2)}) collective-permute-start(bf16[3,192,256]{2,1,0:T(8,128)(2,1)S(1)} %collective-permute-done.14.refs_1_), channel_id=1, source_target_pairs={{0,2},{2,0},{4,6},{6,4},{7,5},{5,7},{3,1},{1,3},{8,10},{10,8},{12,... | collective-permute-start | bytes 884744 | tf_op jit(solution)/shard_map/ppermute | solution.py:302
  26.8 10.6 %collective-permute-start.9 = (bf16[3,192,256]{2,1,0:T(8,128)(2,1)S(1)}, bf16[3,192,256]{2,1,0:T(8,128)(2,1)S(1)}, u32[]{:S(2)}, u32[]{:S(2)}) collective-permute-start(bf16[3,192,256]{2,1,0:T(8,128)(2,1)S(1)} %collective-permute-done.8.refs_1_), channel_id=1, source_target_pairs={{0,2},{2,0},{4,6},{6,4},{7,5},{5,7},{3,1},{1,3},{8,10},{10,8},{12,... | collective-permute-start | bytes 884744 | tf_op jit(solution)/shard_map/ppermute | solution.py:302
  27.9 17.8 %collective-permute-start.5 = (bf16[3,192,256]{2,1,0:T(8,128)(2,1)S(1)}, bf16[3,192,256]{2,1,0:T(8,128)(2,1)S(1)}, u32[]{:S(2)}, u32[]{:S(2)}) collective-permute-start(bf16[3,192,256]{2,1,0:T(8,128)(2,1)S(1)} %collective-permute-done.4.refs_0_), channel_id=1, source_target_pairs={{0,1},{2,4},{4,2},{6,7},{7,6},{5,3},{3,5},{1,0},{8,9},{10,12},{12,... | collective-permute-start | bytes 884744 | tf_op jit(solution)/shard_map/ppermute | solution.py:302
  33.1 21.2 %collective-permute-start.13 = (bf16[3,192,256]{2,1,0:T(8,128)(2,1)S(1)}, bf16[3,192,256]{2,1,0:T(8,128)(2,1)S(1)}, u32[]{:S(2)}, u32[]{:S(2)}) collective-permute-start(bf16[3,192,256]{2,1,0:T(8,128)(2,1)S(1)} %collective-permute-done.12.refs_0_), channel_id=1, source_target_pairs={{0,2},{2,0},{4,6},{6,4},{7,5},{5,7},{3,1},{1,3},{8,10},{10,8},{12,... | collective-permute-start | bytes 884744 | tf_op jit(solution)/shard_map/ppermute | solution.py:302
  34.2 20.6 %collective-permute-start.16 = (bf16[3,192,256]{2,1,0:T(8,128)(2,1)S(1)}, bf16[3,192,256]{2,1,0:T(8,128)(2,1)S(1)}, u32[]{:S(2)}, u32[]{:S(2)}) collective-permute-start(bf16[3,192,256]{2,1,0:T(8,128)(2,1)S(1)} %collective-permute-done.15.refs_1_), channel_id=1, source_target_pairs={{0,1},{2,4},{4,2},{6,7},{7,6},{5,3},{3,5},{1,0},{8,9},{10,12},{12,... | collective-permute-start | bytes 884744 | tf_op jit(solution)/shard_map/ppermute | solution.py:302
  37.4 19.6 %collective-permute-start.10 = (bf16[3,192,256]{2,1,0:T(8,128)(2,1)S(1)}, bf16[3,192,256]{2,1,0:T(8,128)(2,1)S(1)}, u32[]{:S(2)}, u32[]{:S(2)}) collective-permute-start(bf16[3,192,256]{2,1,0:T(8,128)(2,1)S(1)} %collective-permute-done.9.refs_1_), channel_id=1, source_target_pairs={{0,1},{2,4},{4,2},{6,7},{7,6},{5,3},{3,5},{1,0},{8,9},{10,12},{12,... | collective-permute-start | bytes 884744 | tf_op jit(solution)/shard_map/ppermute | solution.py:302
  45.8 11.8 %collective-permute-start.6 = (bf16[3,192,256]{2,1,0:T(8,128)(2,1)S(1)}, bf16[3,192,256]{2,1,0:T(8,128)(2,1)S(1)}, u32[]{:S(2)}, u32[]{:S(2)}) collective-permute-start(bf16[3,192,256]{2,1,0:T(8,128)(2,1)S(1)} %collective-permute-done.5.refs_0_), channel_id=1, source_target_pairs={{0,2},{2,0},{4,6},{6,4},{7,5},{5,7},{3,1},{1,3},{8,10},{10,8},{12,... | collective-permute-start | bytes 884744 | tf_op jit(solution)/shard_map/ppermute | solution.py:302
  54.3 4.5 %collective-permute-start.21 = (f32[64,512]{1,0:T(8,128)S(1)}, f32[64,512]{1,0:T(8,128)S(1)}, u32[]{:S(2)}, u32[]{:S(2)}) collective-permute-start(f32[64,512]{1,0:T(8,128)S(1)} %get-tuple-element.32), channel_id=1, source_target_pairs={{0,8},{8,0},{16,24},{24,16},{1,9},{9,1},{17,25},{25,17},{2,10},{10... | collective-permute-start | bytes 393224 | tf_op jit(solution)/shard_map/ppermute | solution.py:297
  54.4 29.5 %collective-permute-start = (bf16[128,1536]{1,0:T(8,128)(2,1)S(1)}, bf16[128,1536]{1,0:T(8,128)(2,1)S(1)}, u32[]{:S(2)}, u32[]{:S(2)}) collective-permute-start(bf16[128,1536]{1,0:T(8,128)(2,1)S(1)} %get-tuple-element.24.refs_0_), channel_id=1, source_target_pairs={{0,8},{8,0},{16,24},{24,16},{1,9},{9,1},{17,25},{25,17},{2,10},{10... | collective-permute-start | bytes 1179656 | tf_op jit(solution)/shard_map/ppermute | solution.py:297
  54.8 30.6 %collective-permute-start.1 = (bf16[128,1536]{1,0:T(8,128)(2,1)S(1)}, bf16[128,1536]{1,0:T(8,128)(2,1)S(1)}, u32[]{:S(2)}, u32[]{:S(2)}) collective-permute-start(bf16[128,1536]{1,0:T(8,128)(2,1)S(1)} %get-tuple-element.24.refs_0_), channel_id=1, source_target_pairs={{0,16},{8,24},{16,0},{24,8},{1,17},{9,25},{17,1},{25,9},{2,18},{10... | collective-permute-start | bytes 1179656 | tf_op jit(solution)/shard_map/ppermute | solution.py:297
  57.1 28.3 %collective-permute-start.2 = (bf16[128,1536]{1,0:T(8,128)(2,1)S(1)}, bf16[128,1536]{1,0:T(8,128)(2,1)S(1)}, u32[]{:S(2)}, u32[]{:S(2)}) collective-permute-start(bf16[128,1536]{1,0:T(8,128)(2,1)S(1)} %get-tuple-element.24.refs_0_), channel_id=1, source_target_pairs={{0,24},{8,16},{16,8},{24,0},{1,25},{9,17},{17,9},{25,1},{2,26},{10... | collective-permute-start | bytes 1179656 | tf_op jit(solution)/shard_map/ppermute | solution.py:297
  58.8 1.9 %collective-permute-start.18 = (f32[64,512]{1,0:T(8,128)S(1)}, f32[64,512]{1,0:T(8,128)S(1)}, u32[]{:S(2)}, u32[]{:S(2)}) collective-permute-start(f32[64,512]{1,0:T(8,128)S(1)} %get-tuple-element.29), channel_id=1, source_target_pairs={{0,8},{8,0},{16,24},{24,16},{1,9},{9,1},{17,25},{25,17},{2,10},{10... | collective-permute-start | bytes 393224 | tf_op jit(solution)/shard_map/ppermute | solution.py:297
  59.2 17.9 %collective-permute-start.22 = (f32[64,512]{1,0:T(8,128)S(1)}, f32[64,512]{1,0:T(8,128)S(1)}, u32[]{:S(2)}, u32[]{:S(2)}) collective-permute-start(f32[64,512]{1,0:T(8,128)S(1)} %bitcast_add_fusion), channel_id=1, source_target_pairs={{0,16},{8,24},{16,0},{24,8},{1,17},{9,25},{17,1},{25,9},{2,18},{10... | collective-permute-start | bytes 393224 | tf_op jit(solution)/shard_map/ppermute | solution.py:297
  60.8 17.9 %collective-permute-start.17 = (f32[64,512]{1,0:T(8,128)S(1)}, f32[64,512]{1,0:T(8,128)S(1)}, u32[]{:S(2)}, u32[]{:S(2)}) collective-permute-start(f32[64,512]{1,0:T(8,128)S(1)} %get-tuple-element.28), channel_id=1, source_target_pairs={{0,8},{8,0},{16,24},{24,16},{1,9},{9,1},{17,25},{25,17},{2,10},{10... | collective-permute-start | bytes 393224 | tf_op jit(solution)/shard_map/ppermute | solution.py:297
  77.2 4.3 %collective-permute-start.19 = (bf16[64,512]{1,0:T(8,128)(2,1)S(1)}, bf16[64,512]{1,0:T(8,128)(2,1)S(1)}, u32[]{:S(2)}, u32[]{:S(2)}) collective-permute-start(bf16[64,512]{1,0:T(8,128)(2,1)S(1)} %get-tuple-element.46), channel_id=1, source_target_pairs={{0,16},{8,24},{16,0},{24,8},{1,17},{9,25},{17,1},{25,9},{2,18},{10... | collective-permute-start | bytes 196616 | tf_op jit(solution)/shard_map/ppermute | solution.py:297
  81.5 7.1 %collective-permute-start.24 = (bf16[64,512]{1,0:T(8,128)(2,1)S(1)}, bf16[64,512]{1,0:T(8,128)(2,1)S(1)}, u32[]{:S(2)}, u32[]{:S(2)}) collective-permute-start(bf16[64,512]{1,0:T(8,128)(2,1)S(1)} %get-tuple-element.41.refs_3_), channel_id=1, source_target_pairs={{0,7},{1,2},{2,1},{3,4},{4,3},{5,6},{6,5},{7,0},{8,15},{9,10},{10,... | collective-permute-start | bytes 196616 | tf_op jit(solution)/shard_map/ppermute | solution.py:305
  83.9 5.2 %collective-permute-start.25 = (bf16[64,512]{1,0:T(8,128)(2,1)S(1)}, bf16[64,512]{1,0:T(8,128)(2,1)S(1)}, u32[]{:S(2)}, u32[]{:S(2)}) collective-permute-start(bf16[64,512]{1,0:T(8,128)(2,1)S(1)} %get-tuple-element.41.refs_3_), channel_id=1, source_target_pairs={{0,1},{1,0},{2,3},{3,2},{4,5},{5,4},{6,7},{7,6},{8,9},{9,8},{10,11... | collective-permute-start | bytes 196616 | tf_op jit(solution)/shard_map/ppermute | solution.py:305
  83.9 8.2 %collective-permute-start.23 = (bf16[64,512]{1,0:T(8,128)(2,1)S(1)}, bf16[64,512]{1,0:T(8,128)(2,1)S(1)}, u32[]{:S(2)}, u32[]{:S(2)}) collective-permute-start(bf16[64,512]{1,0:T(8,128)(2,1)S(1)} %get-tuple-element.45), channel_id=1, source_target_pairs={{0,16},{8,24},{16,0},{24,8},{1,17},{9,25},{17,1},{25,9},{2,18},{10... | collective-permute-start | bytes 196616 | tf_op jit(solution)/shard_map/ppermute | solution.py:297
  89.5 4.3 %collective-permute-start.26 = (bf16[64,512]{1,0:T(8,128)(2,1)S(1)}, bf16[64,512]{1,0:T(8,128)(2,1)S(1)}, u32[]{:S(2)}, u32[]{:S(2)}) collective-permute-start(bf16[64,512]{1,0:T(8,128)(2,1)S(1)} %get-tuple-element.34.refs_3_), channel_id=1, source_target_pairs={{0,1},{1,0},{2,3},{3,2},{4,5},{5,4},{6,7},{7,6},{8,9},{9,8},{10,11... | collective-permute-start | bytes 196616 | tf_op jit(solution)/shard_map/ppermute | solution.py:305
  89.5 7.0 %collective-permute-start.27 = (bf16[64,512]{1,0:T(8,128)(2,1)S(1)}, bf16[64,512]{1,0:T(8,128)(2,1)S(1)}, u32[]{:S(2)}, u32[]{:S(2)}) collective-permute-start(bf16[64,512]{1,0:T(8,128)(2,1)S(1)} %get-tuple-element.34.refs_3_), channel_id=1, source_target_pairs={{0,7},{1,2},{2,1},{3,4},{4,3},{5,6},{6,5},{7,0},{8,15},{9,10},{10,... | collective-permute-start | bytes 196616 | tf_op jit(solution)/shard_map/ppermute | solution.py:305
  96.9 4.3 %collective-permute-start.28 = (bf16[64,512]{1,0:T(8,128)(2,1)S(1)}, bf16[64,512]{1,0:T(8,128)(2,1)S(1)}, u32[]{:S(2)}, u32[]{:S(2)}) collective-permute-start(bf16[64,512]{1,0:T(8,128)(2,1)S(1)} %get-tuple-element.36.refs_3_), channel_id=1, source_target_pairs={{0,1},{1,0},{2,3},{3,2},{4,5},{5,4},{6,7},{7,6},{8,9},{9,8},{10,11... | collective-permute-start | bytes 196616 | tf_op jit(solution)/shard_map/ppermute | solution.py:305
  97.1 7.0 %collective-permute-start.29 = (bf16[64,512]{1,0:T(8,128)(2,1)S(1)}, bf16[64,512]{1,0:T(8,128)(2,1)S(1)}, u32[]{:S(2)}, u32[]{:S(2)}) collective-permute-start(bf16[64,512]{1,0:T(8,128)(2,1)S(1)} %get-tuple-element.36.refs_3_), channel_id=1, source_target_pairs={{0,7},{1,2},{2,1},{3,4},{4,3},{5,6},{6,5},{7,0},{8,15},{9,10},{10,... | collective-permute-start | bytes 196616 | tf_op jit(solution)/shard_map/ppermute | solution.py:305
  104.3 1.9 %collective-permute-start.30 = (f32[64,128]{1,0:T(8,128)S(1)}, f32[64,128]{1,0:T(8,128)S(1)}, u32[]{:S(2)}, u32[]{:S(2)}) collective-permute-start(f32[64,128]{1,0:T(8,128)S(1)} %get-tuple-element.38), channel_id=1, source_target_pairs={{0,8},{8,0},{16,24},{24,16},{1,9},{9,1},{17,25},{25,17},{2,10},{10... | collective-permute-start | bytes 98312 | tf_op jit(solution)/shard_map/ppermute | solution.py:297
  104.4 4.0 %collective-permute-start.31 = (f32[64,128]{1,0:T(8,128)S(1)}, f32[64,128]{1,0:T(8,128)S(1)}, u32[]{:S(2)}, u32[]{:S(2)}) collective-permute-start(f32[64,128]{1,0:T(8,128)S(1)} %get-tuple-element.39), channel_id=1, source_target_pairs={{0,16},{8,24},{16,0},{24,8},{1,17},{9,25},{17,1},{25,9},{2,18},{10... | collective-permute-start | bytes 98312 | tf_op jit(solution)/shard_map/ppermute | solution.py:297
  106.0 3.4 %collective-permute-start.32 = (f32[64,128]{1,0:T(8,128)S(1)}, f32[64,128]{1,0:T(8,128)S(1)}, u32[]{:S(2)}, u32[]{:S(2)}) collective-permute-start(f32[64,128]{1,0:T(8,128)S(1)} %get-tuple-element.40), channel_id=1, source_target_pairs={{0,24},{8,16},{16,8},{24,0},{1,25},{9,17},{17,9},{25,1},{2,26},{10... | collective-permute-start | bytes 98312 | tf_op jit(solution)/shard_map/ppermute | solution.py:297
  (9 other events, 150.7 us)

commit v9 on v8

--- a/solution.py
+++ b/solution.py
@@ -330,10 +330,10 @@
             got = []
             for t, x in enumerate(odd):
                 near = x
-                if bit > 1 and kind != x.dtype:
+                if kind != x.dtype:
                     near = lax.reduce_precision(x, jnp.finfo(kind).nexp, jnp.finfo(kind).nmant)
                     lost.append(((2 * t + 1) * bit, (x - near).astype(kind)))
-                got.append(across_rows(near.astype(kind if bit > 1 else x.dtype), bit).astype(x.dtype))
+                got.append(across_rows(near.astype(kind), bit).astype(x.dtype))
             summed = [x + y for x, y in zip(even, got)]
             if len(summed) == 1:
                 return summed[0], lost
@@ -346,7 +346,7 @@
         moving = turns[0] | turns[1]
         for rank in range(2):
             blocks = [(step, side, i, x) for (side, i), x in turns[rank].items()]
-            early = (step, rank) == (final - 1, 0)
+            early = (step, rank) == (final - 1, 1)
             field = (incident[0], chosen) if early else (None, None)
             total = multiply(kernels, blocks, total, *field, row_count if early else 0)
             if early:

time: 110 us -> 110 us (level)
  local copies, waits for them, and re-layouts: 7.34 us -> 9.55 us
  starting transfers between devices: 40.9 us -> 39.1 us
    ppermute x13 -> x15, waiting for transfers between devices: 22.4 us -> 18 us  [across_rows(): return lax.ppermute(x, 'row', [(i, i ^ m) for i in range(row_count)])]
    ppermute x14, waiting for transfers between devices: 16.2 us -> 20 us  [swap_walk(): lax.ppermute(x, 'col', [(walk[p], walk[mate(p, side, col_count)]) for p i...]
    ppermute x14, starting transfers between devices: 23.7 us -> 21 us  [swap_walk(): lax.ppermute(x, 'col', [(walk[p], walk[mate(p, side, col_count)]) for p i...]
    unnamed x16, local copies, waits for them, and re-layouts: 6.2 us -> 8.46 us
    ppermute x13 -> x15, starting transfers between devices: 9.49 us -> 9.75 us  [across_rows(): return lax.ppermute(x, 'row', [(i, i ^ m) for i in range(row_count)])]
  transfers between devices with their start and end apart: 33 -> 35, of which waited for: 18 -> 16; matrix products, arithmetic and copies ran while one was open for 0% -> 0% of each run, Pallas kernels for 10% -> 8%
where the time goes in v9:
time: 110 us
  waiting for transfers between devices  47.8 us (43%)
  starting transfers between devices  39.1 us (36%)
  Pallas kernels  12 us (11%)
  local copies, waits for them, and re-layouts  9.55 us (9%)
    ppermute x14, starting transfers between devices, swap_walk(): lax.ppermute(x, 'col', [(walk[p], walk[mate(p, side, col_count)]) for p i...  21 us
    ppermute x14, waiting for transfers between devices, swap_walk(): lax.ppermute(x, 'col', [(walk[p], walk[mate(p, side, col_count)]) for p i...  20 us
    ppermute x15, waiting for transfers between devices, across_rows(): return lax.ppermute(x, 'row', [(i, i ^ m) for i in range(row_count)])  18 us
    ppermute x6, waiting for transfers between devices, swap_cols(): lax.ppermute(x, 'col', [(c, mate(c, side, col_count)) for c in range(col_...  9.75 us
    ppermute x15, starting transfers between devices, across_rows(): return lax.ppermute(x, 'row', [(i, i ^ m) for i in range(row_count)])  9.75 us
    unnamed x16, local copies, waits for them, and re-layouts  8.46 us
    ppermute x6, starting transfers between devices, swap_cols(): lax.ppermute(x, 'col', [(c, mate(c, side, col_count)) for c in range(col_...  8.39 us
    pallas_call x9, Pallas kernels, multiply(): pl.pallas_call(body, out_shape=out_shape, in_specs=in_specs, out_specs=[V...  6.5 us
  transfers between devices with their start and end apart: 35, of which 16 were waited for; matrix products, arithmetic and copies ran while one was open for 0% of the time, Pallas kernels for 8%

profile of v9, /device:TPU:0, one launch (start us, length us, event | category | flops | bytes accessed | tf_op | source)
XLA Modules:
  0.0 109.6 jit_solution(190000410466402363)
XLA Ops:
  1.1 3.0 %collective-permute-start.3 = (bf16[3,192,256]{2,1,0:T(8,128)(2,1)S(1)}, bf16[3,192,256]{2,1,0:T(8,128)(2,1)S(1)}, u32[]{:S(2)}, u32[]{:S(2)}) collective-permute-start(bf16[3,192,256]{2,1,0:T(8,128)(2,1)S(1)} %get-tuple-element.44.refs_0_), channel_id=1, source_target_pairs={{0,1},{2,4},{4,2},{6,7},{7,6},{5,3},{3,5},{1,0},{8,9},{10,12},{12,... | collective-permute-start | bytes 884744 | tf_op jit(solution)/shard_map/ppermute | solution.py:302
  4.1 1.7 %collective-permute-start.7 = (bf16[3,192,256]{2,1,0:T(8,128)(2,1)S(1)}, bf16[3,192,256]{2,1,0:T(8,128)(2,1)S(1)}, u32[]{:S(2)}, u32[]{:S(2)}) collective-permute-start(bf16[3,192,256]{2,1,0:T(8,128)(2,1)S(1)} %get-tuple-element.43.refs_1_), channel_id=1, source_target_pairs={{0,2},{2,0},{4,6},{6,4},{7,5},{5,7},{3,1},{1,3},{8,10},{10,8},{12,... | collective-permute-start | bytes 884744 | tf_op jit(solution)/shard_map/ppermute | solution.py:302
  7.3 4.7 %collective-permute-done.3.refs_0_ = bf16[3,192,256]{2,1,0:T(8,128)(2,1)S(1)} collective-permute-done((bf16[3,192,256]{2,1,0:T(8,128)(2,1)S(1)}, bf16[3,192,256]{2,1,0:T(8,128)(2,1)S(1)}, u32[]{:S(2)}, u32[]{:S(2)}) %collective-permute-start.3) | collective-permute-done | bytes 294944 | tf_op jit(solution)/shard_map/ppermute | solution.py:302
  12.0 2.1 %collective-permute-start.4 = (bf16[3,192,256]{2,1,0:T(8,128)(2,1)S(1)}, bf16[3,192,256]{2,1,0:T(8,128)(2,1)S(1)}, u32[]{:S(2)}, u32[]{:S(2)}) collective-permute-start(bf16[3,192,256]{2,1,0:T(8,128)(2,1)S(1)} %collective-permute-done.3.refs_0_), channel_id=1, source_target_pairs={{0,2},{2,0},{4,6},{6,4},{7,5},{5,7},{3,1},{1,3},{8,10},{10,8},{12,... | collective-permute-start | bytes 884744 | tf_op jit(solution)/shard_map/ppermute | solution.py:302
  14.1 1.5 %collective-permute-start.8 = (bf16[3,192,256]{2,1,0:T(8,128)(2,1)S(1)}, bf16[3,192,256]{2,1,0:T(8,128)(2,1)S(1)}, u32[]{:S(2)}, u32[]{:S(2)}) collective-permute-start(bf16[3,192,256]{2,1,0:T(8,128)(2,1)S(1)} %collective-permute-done.7.refs_1_), channel_id=1, source_target_pairs={{0,1},{2,4},{4,2},{6,7},{7,6},{5,3},{3,5},{1,0},{8,9},{10,12},{12,... | collective-permute-start | bytes 884744 | tf_op jit(solution)/shard_map/ppermute | solution.py:302
  15.6 4.7 %collective-permute-done.14.refs_0_ = bf16[3,192,256]{2,1,0:T(8,128)(2,1)S(1)} collective-permute-done((bf16[3,192,256]{2,1,0:T(8,128)(2,1)S(1)}, bf16[3,192,256]{2,1,0:T(8,128)(2,1)S(1)}, u32[]{:S(2)}, u32[]{:S(2)}) %collective-permute-start.14) | collective-permute-done | bytes 294944 | tf_op jit(solution)/shard_map/ppermute | solution.py:302
  21.5 1.6 %collective-permute-start.18 = (bf16[3,192,256]{2,1,0:T(8,128)(2,1)S(1)}, bf16[3,192,256]{2,1,0:T(8,128)(2,1)S(1)}, u32[]{:S(2)}, u32[]{:S(2)}) collective-permute-start(bf16[3,192,256]{2,1,0:T(8,128)(2,1)S(1)} %collective-permute-done.17.refs_1_), channel_id=1, source_target_pairs={{0,2},{2,0},{4,6},{6,4},{7,5},{5,7},{3,1},{1,3},{8,10},{10,8},{12,... | collective-permute-start | bytes 884744 | tf_op jit(solution)/shard_map/ppermute | solution.py:302
  23.0 3.6 %collective-permute-done.4.refs_0_ = bf16[3,192,256]{2,1,0:T(8,128)(2,1)S(1)} collective-permute-done((bf16[3,192,256]{2,1,0:T(8,128)(2,1)S(1)}, bf16[3,192,256]{2,1,0:T(8,128)(2,1)S(1)}, u32[]{:S(2)}, u32[]{:S(2)}) %collective-permute-start.4) | collective-permute-done | bytes 294944 | tf_op jit(solution)/shard_map/ppermute | solution.py:302
  27.8 1.6 %collective-permute-start.9 = (bf16[3,192,256]{2,1,0:T(8,128)(2,1)S(1)}, bf16[3,192,256]{2,1,0:T(8,128)(2,1)S(1)}, u32[]{:S(2)}, u32[]{:S(2)}) collective-permute-start(bf16[3,192,256]{2,1,0:T(8,128)(2,1)S(1)} %collective-permute-done.8.refs_1_), channel_id=1, source_target_pairs={{0,2},{2,0},{4,6},{6,4},{7,5},{5,7},{3,1},{1,3},{8,10},{10,8},{12,... | collective-permute-start | bytes 884744 | tf_op jit(solution)/shard_map/ppermute | solution.py:302
  29.4 1.6 %collective-permute-done.15.refs_0_ = bf16[3,192,256]{2,1,0:T(8,128)(2,1)S(1)} collective-permute-done((bf16[3,192,256]{2,1,0:T(8,128)(2,1)S(1)}, bf16[3,192,256]{2,1,0:T(8,128)(2,1)S(1)}, u32[]{:S(2)}, u32[]{:S(2)}) %collective-permute-start.15) | collective-permute-done | bytes 294944 | tf_op jit(solution)/shard_map/ppermute | solution.py:302
  30.9 2.1 %collective-permute-start.16 = (bf16[3,192,256]{2,1,0:T(8,128)(2,1)S(1)}, bf16[3,192,256]{2,1,0:T(8,128)(2,1)S(1)}, u32[]{:S(2)}, u32[]{:S(2)}) collective-permute-start(bf16[3,192,256]{2,1,0:T(8,128)(2,1)S(1)} %collective-permute-done.15.refs_0_), channel_id=1, source_target_pairs={{0,2},{2,0},{4,6},{6,4},{7,5},{5,7},{3,1},{1,3},{8,10},{10,8},{12,... | collective-permute-start | bytes 884744 | tf_op jit(solution)/shard_map/ppermute | solution.py:302
  33.1 1.5 %collective-permute-start.19 = (bf16[3,192,256]{2,1,0:T(8,128)(2,1)S(1)}, bf16[3,192,256]{2,1,0:T(8,128)(2,1)S(1)}, u32[]{:S(2)}, u32[]{:S(2)}) collective-permute-start(bf16[3,192,256]{2,1,0:T(8,128)(2,1)S(1)} %collective-permute-done.18.refs_1_), channel_id=1, source_target_pairs={{0,1},{2,4},{4,2},{6,7},{7,6},{5,3},{3,5},{1,0},{8,9},{10,12},{12,... | collective-permute-start | bytes 884744 | tf_op jit(solution)/shard_map/ppermute | solution.py:302
  37.5 1.4 %prepare.1 = (s32[4]{0:T(128)S(1)}, bf16[128,1536]{1,0:T(8,128)(2,1)S(1)}) custom-call(s32[32]{0:T(128)S(1)} %copy-done.4, s32[2,12]{1,0:T(2,128)S(1)} %bitcast.29, s32[1]{0:T(128)S(6)} %copy.8.counts_ref, bf16[12,128,128]{2,1,0:T(8,128)(2,1)S(1)} %copy-done.1), custom_call_target="tpu_custom_call" | custom-call | bytes 786432 | tf_op jit(solution)/shard_map/prepare/pallas_call | solution.py:68
  38.9 3.7 %copy-done = bf16[6,512,1536]{2,1,0:T(8,128)(2,1)S(1)} copy-done((bf16[6,512,1536]{2,1,0:T(8,128)(2,1)S(1)}, bf16[6,512,1536]{2,1,0:T(8,128)(2,1)}, u32[]{:S(2)}) %copy-start) | copy-done | bytes 9437208
  47.5 1.3 %slice-done.1 = s8[4194304]{0:T(1024)(128)(4,1)S(1)} async-done(((s8[9437184]{0:T(1024)(128)(4,1)}), s8[4194304]{0:T(1024)(128)(4,1)S(1)}, s32[]{:S(2)}) %slice-start.1) | async-done | bytes 4194328
  49.2 1.5 %multiply.17 = (f32[2,64,512]{2,1,0:T(8,128)S(1)}, f32[64,512]{1,0:T(8,128)S(1)}, f32[64,512]{1,0:T(8,128)S(1)}) custom-call(bf16[6,512,1536]{2,1,0:T(8,128)(2,1)S(1)} %bitcast.27, bf16[3,192,256]{2,1,0:T(8,128)(2,1)S(1)} %collective-permute-done.16.refs_0_, bf16[3,192,256]{2,1,0:T(8,128)(2,1)S(1)} %collective-permute-done.19.refs_1_, ...), custom_call_target="tpu_custom_call" | custom-call | flops 402653184 | bytes 2359296 | tf_op jit(solution)/shard_map/multiply/pallas_call | solution.py:172
  51.4 1.6 %collective-permute-start.6 = (bf16[3,192,256]{2,1,0:T(8,128)(2,1)S(1)}, bf16[3,192,256]{2,1,0:T(8,128)(2,1)S(1)}, u32[]{:S(2)}, u32[]{:S(2)}) collective-permute-start(bf16[3,192,256]{2,1,0:T(8,128)(2,1)S(1)} %collective-permute-done.5.refs_0_), channel_id=1, source_target_pairs={{0,2},{2,0},{4,6},{6,4},{7,5},{5,7},{3,1},{1,3},{8,10},{10,8},{12,... | collective-permute-start | bytes 884744 | tf_op jit(solution)/shard_map/ppermute | solution.py:302
  53.0 1.5 %collective-permute-start.1 = (bf16[128,1536]{1,0:T(8,128)(2,1)S(1)}, bf16[128,1536]{1,0:T(8,128)(2,1)S(1)}, u32[]{:S(2)}, u32[]{:S(2)}) collective-permute-start(bf16[128,1536]{1,0:T(8,128)(2,1)S(1)} %get-tuple-element.24.refs_0_), channel_id=1, source_target_pairs={{0,16},{8,24},{16,0},{24,8},{1,17},{9,25},{17,1},{25,9},{2,18},{10... | collective-permute-start | bytes 1179656 | tf_op jit(solution)/shard_map/ppermute | solution.py:297
  54.8 5.4 %collective-permute-done.10.refs_0_ = bf16[3,192,256]{2,1,0:T(8,128)(2,1)S(1)} collective-permute-done((bf16[3,192,256]{2,1,0:T(8,128)(2,1)S(1)}, bf16[3,192,256]{2,1,0:T(8,128)(2,1)S(1)}, u32[]{:S(2)}, u32[]{:S(2)}) %collective-permute-start.10) | collective-permute-done | bytes 294944 | tf_op jit(solution)/shard_map/ppermute | solution.py:302
  62.7 1.5 %collective-permute-start.22 = (f32[64,512]{1,0:T(8,128)S(1)}, f32[64,512]{1,0:T(8,128)S(1)}, u32[]{:S(2)}, u32[]{:S(2)}) collective-permute-start(f32[64,512]{1,0:T(8,128)S(1)} %bitcast_add_fusion), channel_id=1, source_target_pairs={{0,16},{8,24},{16,0},{24,8},{1,17},{9,25},{17,1},{25,9},{2,18},{10... | collective-permute-start | bytes 393224 | tf_op jit(solution)/shard_map/ppermute | solution.py:297
  64.4 11.3 %collective-permute-done.22 = f32[64,512]{1,0:T(8,128)S(1)} collective-permute-done((f32[64,512]{1,0:T(8,128)S(1)}, f32[64,512]{1,0:T(8,128)S(1)}, u32[]{:S(2)}, u32[]{:S(2)}) %collective-permute-start.22) | collective-permute-done | bytes 131104 | tf_op jit(solution)/shard_map/ppermute | solution.py:297
  75.7 1.5 %collective-permute-start.13 = (bf16[64,512]{1,0:T(8,128)(2,1)S(1)}, bf16[64,512]{1,0:T(8,128)(2,1)S(1)}, u32[]{:S(2)}, u32[]{:S(2)}) collective-permute-start(bf16[64,512]{1,0:T(8,128)(2,1)S(1)} %get-tuple-element.46), channel_id=1, source_target_pairs={{0,16},{8,24},{16,0},{24,8},{1,17},{9,25},{17,1},{25,9},{2,18},{10... | collective-permute-start | bytes 196616 | tf_op jit(solution)/shard_map/ppermute | solution.py:297
  77.2 2.7 %collective-permute-done.13 = bf16[64,512]{1,0:T(8,128)(2,1)S(1)} collective-permute-done((bf16[64,512]{1,0:T(8,128)(2,1)S(1)}, bf16[64,512]{1,0:T(8,128)(2,1)S(1)}, u32[]{:S(2)}, u32[]{:S(2)}) %collective-permute-start.13) | collective-permute-done | bytes 65568 | tf_op jit(solution)/shard_map/ppermute | solution.py:297
  80.0 3.5 %collective-permute-start.26 = (bf16[64,512]{1,0:T(8,128)(2,1)S(1)}, bf16[64,512]{1,0:T(8,128)(2,1)S(1)}, u32[]{:S(2)}, u32[]{:S(2)}) collective-permute-start(bf16[64,512]{1,0:T(8,128)(2,1)S(1)} %get-tuple-element.41.refs_3_), channel_id=1, source_target_pairs={{0,7},{1,2},{2,1},{3,4},{4,3},{5,6},{6,5},{7,0},{8,15},{9,10},{10,... | collective-permute-start | bytes 196616 | tf_op jit(solution)/shard_map/ppermute | solution.py:305
  83.5 1.6 %collective-permute-start.24 = (bf16[64,512]{1,0:T(8,128)(2,1)S(1)}, bf16[64,512]{1,0:T(8,128)(2,1)S(1)}, u32[]{:S(2)}, u32[]{:S(2)}) collective-permute-start(bf16[64,512]{1,0:T(8,128)(2,1)S(1)} %get-tuple-element.51), channel_id=1, source_target_pairs={{0,24},{8,16},{16,8},{24,0},{1,25},{9,17},{17,9},{25,1},{2,26},{10... | collective-permute-start | bytes 196616 | tf_op jit(solution)/shard_map/ppermute | solution.py:297
  89.2 1.9 %collective-permute-start.29 = (bf16[64,512]{1,0:T(8,128)(2,1)S(1)}, bf16[64,512]{1,0:T(8,128)(2,1)S(1)}, u32[]{:S(2)}, u32[]{:S(2)}) collective-permute-start(bf16[64,512]{1,0:T(8,128)(2,1)S(1)} %get-tuple-element.34.refs_3_), channel_id=1, source_target_pairs={{0,7},{1,2},{2,1},{3,4},{4,3},{5,6},{6,5},{7,0},{8,15},{9,10},{10,... | collective-permute-start | bytes 196616 | tf_op jit(solution)/shard_map/ppermute | solution.py:305
  91.1 1.4 %collective-permute-done.28.refs_4_ = bf16[64,512]{1,0:T(8,128)(2,1)S(1)} collective-permute-done((bf16[64,512]{1,0:T(8,128)(2,1)S(1)}, bf16[64,512]{1,0:T(8,128)(2,1)S(1)}, u32[]{:S(2)}, u32[]{:S(2)}) %collective-permute-start.28) | collective-permute-done | bytes 65568 | tf_op jit(solution)/shard_map/ppermute | solution.py:305
  93.0 3.2 %collective-permute-done.29.refs_0_ = bf16[64,512]{1,0:T(8,128)(2,1)S(1)} collective-permute-done((bf16[64,512]{1,0:T(8,128)(2,1)S(1)}, bf16[64,512]{1,0:T(8,128)(2,1)S(1)}, u32[]{:S(2)}, u32[]{:S(2)}) %collective-permute-start.29) | collective-permute-done | bytes 65568 | tf_op jit(solution)/shard_map/ppermute | solution.py:305
  96.5 2.0 %collective-permute-start.31 = (bf16[64,512]{1,0:T(8,128)(2,1)S(1)}, bf16[64,512]{1,0:T(8,128)(2,1)S(1)}, u32[]{:S(2)}, u32[]{:S(2)}) collective-permute-start(bf16[64,512]{1,0:T(8,128)(2,1)S(1)} %get-tuple-element.36.refs_3_), channel_id=1, source_target_pairs={{0,7},{1,2},{2,1},{3,4},{4,3},{5,6},{6,5},{7,0},{8,15},{9,10},{10,... | collective-permute-start | bytes 196616 | tf_op jit(solution)/shard_map/ppermute | solution.py:305
  98.5 2.9 %collective-permute-done.30.refs_4_ = bf16[64,512]{1,0:T(8,128)(2,1)S(1)} collective-permute-done((bf16[64,512]{1,0:T(8,128)(2,1)S(1)}, bf16[64,512]{1,0:T(8,128)(2,1)S(1)}, u32[]{:S(2)}, u32[]{:S(2)}) %collective-permute-start.30) | collective-permute-done | bytes 65568 | tf_op jit(solution)/shard_map/ppermute | solution.py:305
  103.9 1.6 %collective-permute-start.33 = (f32[64,128]{1,0:T(8,128)S(1)}, f32[64,128]{1,0:T(8,128)S(1)}, u32[]{:S(2)}, u32[]{:S(2)}) collective-permute-start(f32[64,128]{1,0:T(8,128)S(1)} %get-tuple-element.39), channel_id=1, source_target_pairs={{0,16},{8,24},{16,0},{24,8},{1,17},{9,25},{17,1},{25,9},{2,18},{10... | collective-permute-start | bytes 98312 | tf_op jit(solution)/shard_map/ppermute | solution.py:297
  105.8 2.1 %collective-permute-done.33.refs_2_ = f32[64,128]{1,0:T(8,128)S(1)} collective-permute-done((f32[64,128]{1,0:T(8,128)S(1)}, f32[64,128]{1,0:T(8,128)S(1)}, u32[]{:S(2)}, u32[]{:S(2)}) %collective-permute-start.33) | collective-permute-done | bytes 32800 | tf_op jit(solution)/shard_map/ppermute | solution.py:297
  (80 shorter events, 25.4 us)
Async XLA Ops:
  1.1 10.9 %collective-permute-start.3 = (bf16[3,192,256]{2,1,0:T(8,128)(2,1)S(1)}, bf16[3,192,256]{2,1,0:T(8,128)(2,1)S(1)}, u32[]{:S(2)}, u32[]{:S(2)}) collective-permute-start(bf16[3,192,256]{2,1,0:T(8,128)(2,1)S(1)} %get-tuple-element.44.refs_0_), channel_id=1, source_target_pairs={{0,1},{2,4},{4,2},{6,7},{7,6},{5,3},{3,5},{1,0},{8,9},{10,12},{12,... | collective-permute-start | bytes 884744 | tf_op jit(solution)/shard_map/ppermute | solution.py:302
  4.1 10.0 %collective-permute-start.7 = (bf16[3,192,256]{2,1,0:T(8,128)(2,1)S(1)}, bf16[3,192,256]{2,1,0:T(8,128)(2,1)S(1)}, u32[]{:S(2)}, u32[]{:S(2)}) collective-permute-start(bf16[3,192,256]{2,1,0:T(8,128)(2,1)S(1)} %get-tuple-element.43.refs_1_), channel_id=1, source_target_pairs={{0,2},{2,0},{4,6},{6,4},{7,5},{5,7},{3,1},{1,3},{8,10},{10,8},{12,... | collective-permute-start | bytes 884744 | tf_op jit(solution)/shard_map/ppermute | solution.py:302
  5.8 14.5 %collective-permute-start.14 = (bf16[3,192,256]{2,1,0:T(8,128)(2,1)S(1)}, bf16[3,192,256]{2,1,0:T(8,128)(2,1)S(1)}, u32[]{:S(2)}, u32[]{:S(2)}) collective-permute-start(bf16[3,192,256]{2,1,0:T(8,128)(2,1)S(1)} %get-tuple-element.44.refs_0_), channel_id=1, source_target_pairs={{0,2},{2,0},{4,6},{6,4},{7,5},{5,7},{3,1},{1,3},{8,10},{10,8},{12,... | collective-permute-start | bytes 884744 | tf_op jit(solution)/shard_map/ppermute | solution.py:302
  6.2 15.3 %collective-permute-start.17 = (bf16[3,192,256]{2,1,0:T(8,128)(2,1)S(1)}, bf16[3,192,256]{2,1,0:T(8,128)(2,1)S(1)}, u32[]{:S(2)}, u32[]{:S(2)}) collective-permute-start(bf16[3,192,256]{2,1,0:T(8,128)(2,1)S(1)} %get-tuple-element.43.refs_1_), channel_id=1, source_target_pairs={{0,1},{2,4},{4,2},{6,7},{7,6},{5,3},{3,5},{1,0},{8,9},{10,12},{12,... | collective-permute-start | bytes 884744 | tf_op jit(solution)/shard_map/ppermute | solution.py:302
  12.0 14.7 %collective-permute-start.4 = (bf16[3,192,256]{2,1,0:T(8,128)(2,1)S(1)}, bf16[3,192,256]{2,1,0:T(8,128)(2,1)S(1)}, u32[]{:S(2)}, u32[]{:S(2)}) collective-permute-start(bf16[3,192,256]{2,1,0:T(8,128)(2,1)S(1)} %collective-permute-done.3.refs_0_), channel_id=1, source_target_pairs={{0,2},{2,0},{4,6},{6,4},{7,5},{5,7},{3,1},{1,3},{8,10},{10,8},{12,... | collective-permute-start | bytes 884744 | tf_op jit(solution)/shard_map/ppermute | solution.py:302
  14.1 13.7 %collective-permute-start.8 = (bf16[3,192,256]{2,1,0:T(8,128)(2,1)S(1)}, bf16[3,192,256]{2,1,0:T(8,128)(2,1)S(1)}, u32[]{:S(2)}, u32[]{:S(2)}) collective-permute-start(bf16[3,192,256]{2,1,0:T(8,128)(2,1)S(1)} %collective-permute-done.7.refs_1_), channel_id=1, source_target_pairs={{0,1},{2,4},{4,2},{6,7},{7,6},{5,3},{3,5},{1,0},{8,9},{10,12},{12,... | collective-permute-start | bytes 884744 | tf_op jit(solution)/shard_map/ppermute | solution.py:302
  20.3 10.6 %collective-permute-start.15 = (bf16[3,192,256]{2,1,0:T(8,128)(2,1)S(1)}, bf16[3,192,256]{2,1,0:T(8,128)(2,1)S(1)}, u32[]{:S(2)}, u32[]{:S(2)}) collective-permute-start(bf16[3,192,256]{2,1,0:T(8,128)(2,1)S(1)} %collective-permute-done.14.refs_0_), channel_id=1, source_target_pairs={{0,1},{2,4},{4,2},{6,7},{7,6},{5,3},{3,5},{1,0},{8,9},{10,12},{12,... | collective-permute-start | bytes 884744 | tf_op jit(solution)/shard_map/ppermute | solution.py:302
  21.5 11.6 %collective-permute-start.18 = (bf16[3,192,256]{2,1,0:T(8,128)(2,1)S(1)}, bf16[3,192,256]{2,1,0:T(8,128)(2,1)S(1)}, u32[]{:S(2)}, u32[]{:S(2)}) collective-permute-start(bf16[3,192,256]{2,1,0:T(8,128)(2,1)S(1)} %collective-permute-done.17.refs_1_), channel_id=1, source_target_pairs={{0,2},{2,0},{4,6},{6,4},{7,5},{5,7},{3,1},{1,3},{8,10},{10,8},{12,... | collective-permute-start | bytes 884744 | tf_op jit(solution)/shard_map/ppermute | solution.py:302
  26.6 19.4 %collective-permute-start.5 = (bf16[3,192,256]{2,1,0:T(8,128)(2,1)S(1)}, bf16[3,192,256]{2,1,0:T(8,128)(2,1)S(1)}, u32[]{:S(2)}, u32[]{:S(2)}) collective-permute-start(bf16[3,192,256]{2,1,0:T(8,128)(2,1)S(1)} %collective-permute-done.4.refs_0_), channel_id=1, source_target_pairs={{0,1},{2,4},{4,2},{6,7},{7,6},{5,3},{3,5},{1,0},{8,9},{10,12},{12,... | collective-permute-start | bytes 884744 | tf_op jit(solution)/shard_map/ppermute | solution.py:302
  27.8 18.3 %collective-permute-start.9 = (bf16[3,192,256]{2,1,0:T(8,128)(2,1)S(1)}, bf16[3,192,256]{2,1,0:T(8,128)(2,1)S(1)}, u32[]{:S(2)}, u32[]{:S(2)}) collective-permute-start(bf16[3,192,256]{2,1,0:T(8,128)(2,1)S(1)} %collective-permute-done.8.refs_1_), channel_id=1, source_target_pairs={{0,2},{2,0},{4,6},{6,4},{7,5},{5,7},{3,1},{1,3},{8,10},{10,8},{12,... | collective-permute-start | bytes 884744 | tf_op jit(solution)/shard_map/ppermute | solution.py:302
  30.9 15.8 %collective-permute-start.16 = (bf16[3,192,256]{2,1,0:T(8,128)(2,1)S(1)}, bf16[3,192,256]{2,1,0:T(8,128)(2,1)S(1)}, u32[]{:S(2)}, u32[]{:S(2)}) collective-permute-start(bf16[3,192,256]{2,1,0:T(8,128)(2,1)S(1)} %collective-permute-done.15.refs_0_), channel_id=1, source_target_pairs={{0,2},{2,0},{4,6},{6,4},{7,5},{5,7},{3,1},{1,3},{8,10},{10,8},{12,... | collective-permute-start | bytes 884744 | tf_op jit(solution)/shard_map/ppermute | solution.py:302
  33.1 13.7 %collective-permute-start.19 = (bf16[3,192,256]{2,1,0:T(8,128)(2,1)S(1)}, bf16[3,192,256]{2,1,0:T(8,128)(2,1)S(1)}, u32[]{:S(2)}, u32[]{:S(2)}) collective-permute-start(bf16[3,192,256]{2,1,0:T(8,128)(2,1)S(1)} %collective-permute-done.18.refs_1_), channel_id=1, source_target_pairs={{0,1},{2,4},{4,2},{6,7},{7,6},{5,3},{3,5},{1,0},{8,9},{10,12},{12,... | collective-permute-start | bytes 884744 | tf_op jit(solution)/shard_map/ppermute | solution.py:302
  50.7 3.8 %collective-permute-start.21 = (f32[64,512]{1,0:T(8,128)S(1)}, f32[64,512]{1,0:T(8,128)S(1)}, u32[]{:S(2)}, u32[]{:S(2)}) collective-permute-start(f32[64,512]{1,0:T(8,128)S(1)} %get-tuple-element.32), channel_id=1, source_target_pairs={{0,8},{8,0},{16,24},{24,16},{1,9},{9,1},{17,25},{25,17},{2,10},{10... | collective-permute-start | bytes 393224 | tf_op jit(solution)/shard_map/ppermute | solution.py:297
  50.8 9.4 %collective-permute-start.10 = (bf16[3,192,256]{2,1,0:T(8,128)(2,1)S(1)}, bf16[3,192,256]{2,1,0:T(8,128)(2,1)S(1)}, u32[]{:S(2)}, u32[]{:S(2)}) collective-permute-start(bf16[3,192,256]{2,1,0:T(8,128)(2,1)S(1)} %collective-permute-done.9.refs_1_), channel_id=1, source_target_pairs={{0,1},{2,4},{4,2},{6,7},{7,6},{5,3},{3,5},{1,0},{8,9},{10,12},{12,... | collective-permute-start | bytes 884744 | tf_op jit(solution)/shard_map/ppermute | solution.py:302
  51.4 9.3 %collective-permute-start.6 = (bf16[3,192,256]{2,1,0:T(8,128)(2,1)S(1)}, bf16[3,192,256]{2,1,0:T(8,128)(2,1)S(1)}, u32[]{:S(2)}, u32[]{:S(2)}) collective-permute-start(bf16[3,192,256]{2,1,0:T(8,128)(2,1)S(1)} %collective-permute-done.5.refs_0_), channel_id=1, source_target_pairs={{0,2},{2,0},{4,6},{6,4},{7,5},{5,7},{3,1},{1,3},{8,10},{10,8},{12,... | collective-permute-start | bytes 884744 | tf_op jit(solution)/shard_map/ppermute | solution.py:302
  53.0 30.6 %collective-permute-start = (bf16[128,1536]{1,0:T(8,128)(2,1)S(1)}, bf16[128,1536]{1,0:T(8,128)(2,1)S(1)}, u32[]{:S(2)}, u32[]{:S(2)}) collective-permute-start(bf16[128,1536]{1,0:T(8,128)(2,1)S(1)} %get-tuple-element.24.refs_0_), channel_id=1, source_target_pairs={{0,8},{8,0},{16,24},{24,16},{1,9},{9,1},{17,25},{25,17},{2,10},{10... | collective-permute-start | bytes 1179656 | tf_op jit(solution)/shard_map/ppermute | solution.py:297
  53.0 30.6 %collective-permute-start.1 = (bf16[128,1536]{1,0:T(8,128)(2,1)S(1)}, bf16[128,1536]{1,0:T(8,128)(2,1)S(1)}, u32[]{:S(2)}, u32[]{:S(2)}) collective-permute-start(bf16[128,1536]{1,0:T(8,128)(2,1)S(1)} %get-tuple-element.24.refs_0_), channel_id=1, source_target_pairs={{0,16},{8,24},{16,0},{24,8},{1,17},{9,25},{17,1},{25,9},{2,18},{10... | collective-permute-start | bytes 1179656 | tf_op jit(solution)/shard_map/ppermute | solution.py:297
  54.5 30.7 %collective-permute-start.2 = (bf16[128,1536]{1,0:T(8,128)(2,1)S(1)}, bf16[128,1536]{1,0:T(8,128)(2,1)S(1)}, u32[]{:S(2)}, u32[]{:S(2)}) collective-permute-start(bf16[128,1536]{1,0:T(8,128)(2,1)S(1)} %get-tuple-element.24.refs_0_), channel_id=1, source_target_pairs={{0,24},{8,16},{16,8},{24,0},{1,25},{9,17},{17,9},{25,1},{2,26},{10... | collective-permute-start | bytes 1179656 | tf_op jit(solution)/shard_map/ppermute | solution.py:297
  60.2 4.1 %collective-permute-start.20 = (f32[64,512]{1,0:T(8,128)S(1)}, f32[64,512]{1,0:T(8,128)S(1)}, u32[]{:S(2)}, u32[]{:S(2)}) collective-permute-start(f32[64,512]{1,0:T(8,128)S(1)} %get-tuple-element.31), channel_id=1, source_target_pairs={{0,8},{8,0},{16,24},{24,16},{1,9},{9,1},{17,25},{25,17},{2,10},{10... | collective-permute-start | bytes 393224 | tf_op jit(solution)/shard_map/ppermute | solution.py:297
  62.7 13.0 %collective-permute-start.22 = (f32[64,512]{1,0:T(8,128)S(1)}, f32[64,512]{1,0:T(8,128)S(1)}, u32[]{:S(2)}, u32[]{:S(2)}) collective-permute-start(f32[64,512]{1,0:T(8,128)S(1)} %bitcast_add_fusion), channel_id=1, source_target_pairs={{0,16},{8,24},{16,0},{24,8},{1,17},{9,25},{17,1},{25,9},{2,18},{10... | collective-permute-start | bytes 393224 | tf_op jit(solution)/shard_map/ppermute | solution.py:297
  64.3 13.0 %collective-permute-start.11 = (bf16[64,512]{1,0:T(8,128)(2,1)S(1)}, bf16[64,512]{1,0:T(8,128)(2,1)S(1)}, u32[]{:S(2)}, u32[]{:S(2)}) collective-permute-start(bf16[64,512]{1,0:T(8,128)(2,1)S(1)} %get-tuple-element.50), channel_id=1, source_target_pairs={{0,8},{8,0},{16,24},{24,16},{1,9},{9,1},{17,25},{25,17},{2,10},{10... | collective-permute-start | bytes 196616 | tf_op jit(solution)/shard_map/ppermute | solution.py:297
  75.7 4.3 %collective-permute-start.13 = (bf16[64,512]{1,0:T(8,128)(2,1)S(1)}, bf16[64,512]{1,0:T(8,128)(2,1)S(1)}, u32[]{:S(2)}, u32[]{:S(2)}) collective-permute-start(bf16[64,512]{1,0:T(8,128)(2,1)S(1)} %get-tuple-element.46), channel_id=1, source_target_pairs={{0,16},{8,24},{16,0},{24,8},{1,17},{9,25},{17,1},{25,9},{2,18},{10... | collective-permute-start | bytes 196616 | tf_op jit(solution)/shard_map/ppermute | solution.py:297
  80.0 7.0 %collective-permute-start.26 = (bf16[64,512]{1,0:T(8,128)(2,1)S(1)}, bf16[64,512]{1,0:T(8,128)(2,1)S(1)}, u32[]{:S(2)}, u32[]{:S(2)}) collective-permute-start(bf16[64,512]{1,0:T(8,128)(2,1)S(1)} %get-tuple-element.41.refs_3_), channel_id=1, source_target_pairs={{0,7},{1,2},{2,1},{3,4},{4,3},{5,6},{6,5},{7,0},{8,15},{9,10},{10,... | collective-permute-start | bytes 196616 | tf_op jit(solution)/shard_map/ppermute | solution.py:305
  83.5 4.3 %collective-permute-start.27 = (bf16[64,512]{1,0:T(8,128)(2,1)S(1)}, bf16[64,512]{1,0:T(8,128)(2,1)S(1)}, u32[]{:S(2)}, u32[]{:S(2)}) collective-permute-start(bf16[64,512]{1,0:T(8,128)(2,1)S(1)} %get-tuple-element.41.refs_3_), channel_id=1, source_target_pairs={{0,1},{1,0},{2,3},{3,2},{4,5},{5,4},{6,7},{7,6},{8,9},{9,8},{10,11... | collective-permute-start | bytes 196616 | tf_op jit(solution)/shard_map/ppermute | solution.py:305
  83.5 7.5 %collective-permute-start.23 = (bf16[64,512]{1,0:T(8,128)(2,1)S(1)}, bf16[64,512]{1,0:T(8,128)(2,1)S(1)}, u32[]{:S(2)}, u32[]{:S(2)}) collective-permute-start(bf16[64,512]{1,0:T(8,128)(2,1)S(1)} %get-tuple-element.49), channel_id=1, source_target_pairs={{0,8},{8,0},{16,24},{24,16},{1,9},{9,1},{17,25},{25,17},{2,10},{10... | collective-permute-start | bytes 196616 | tf_op jit(solution)/shard_map/ppermute | solution.py:297
  83.5 7.5 %collective-permute-start.24 = (bf16[64,512]{1,0:T(8,128)(2,1)S(1)}, bf16[64,512]{1,0:T(8,128)(2,1)S(1)}, u32[]{:S(2)}, u32[]{:S(2)}) collective-permute-start(bf16[64,512]{1,0:T(8,128)(2,1)S(1)} %get-tuple-element.51), channel_id=1, source_target_pairs={{0,24},{8,16},{16,8},{24,0},{1,25},{9,17},{17,9},{25,1},{2,26},{10... | collective-permute-start | bytes 196616 | tf_op jit(solution)/shard_map/ppermute | solution.py:297
  85.2 5.9 %collective-permute-start.25 = (bf16[64,512]{1,0:T(8,128)(2,1)S(1)}, bf16[64,512]{1,0:T(8,128)(2,1)S(1)}, u32[]{:S(2)}, u32[]{:S(2)}) collective-permute-start(bf16[64,512]{1,0:T(8,128)(2,1)S(1)} %get-tuple-element.45), channel_id=1, source_target_pairs={{0,16},{8,24},{16,0},{24,8},{1,17},{9,25},{17,1},{25,9},{2,18},{10... | collective-permute-start | bytes 196616 | tf_op jit(solution)/shard_map/ppermute | solution.py:297
  88.2 4.3 %collective-permute-start.28 = (bf16[64,512]{1,0:T(8,128)(2,1)S(1)}, bf16[64,512]{1,0:T(8,128)(2,1)S(1)}, u32[]{:S(2)}, u32[]{:S(2)}) collective-permute-start(bf16[64,512]{1,0:T(8,128)(2,1)S(1)} %get-tuple-element.34.refs_3_), channel_id=1, source_target_pairs={{0,1},{1,0},{2,3},{3,2},{4,5},{5,4},{6,7},{7,6},{8,9},{9,8},{10,11... | collective-permute-start | bytes 196616 | tf_op jit(solution)/shard_map/ppermute | solution.py:305
  89.2 7.0 %collective-permute-start.29 = (bf16[64,512]{1,0:T(8,128)(2,1)S(1)}, bf16[64,512]{1,0:T(8,128)(2,1)S(1)}, u32[]{:S(2)}, u32[]{:S(2)}) collective-permute-start(bf16[64,512]{1,0:T(8,128)(2,1)S(1)} %get-tuple-element.34.refs_3_), channel_id=1, source_target_pairs={{0,7},{1,2},{2,1},{3,4},{4,3},{5,6},{6,5},{7,0},{8,15},{9,10},{10,... | collective-permute-start | bytes 196616 | tf_op jit(solution)/shard_map/ppermute | solution.py:305
  96.5 5.0 %collective-permute-start.30 = (bf16[64,512]{1,0:T(8,128)(2,1)S(1)}, bf16[64,512]{1,0:T(8,128)(2,1)S(1)}, u32[]{:S(2)}, u32[]{:S(2)}) collective-permute-start(bf16[64,512]{1,0:T(8,128)(2,1)S(1)} %get-tuple-element.36.refs_3_), channel_id=1, source_target_pairs={{0,1},{1,0},{2,3},{3,2},{4,5},{5,4},{6,7},{7,6},{8,9},{9,8},{10,11... | collective-permute-start | bytes 196616 | tf_op jit(solution)/shard_map/ppermute | solution.py:305
  96.5 7.0 %collective-permute-start.31 = (bf16[64,512]{1,0:T(8,128)(2,1)S(1)}, bf16[64,512]{1,0:T(8,128)(2,1)S(1)}, u32[]{:S(2)}, u32[]{:S(2)}) collective-permute-start(bf16[64,512]{1,0:T(8,128)(2,1)S(1)} %get-tuple-element.36.refs_3_), channel_id=1, source_target_pairs={{0,7},{1,2},{2,1},{3,4},{4,3},{5,6},{6,5},{7,0},{8,15},{9,10},{10,... | collective-permute-start | bytes 196616 | tf_op jit(solution)/shard_map/ppermute | solution.py:305
  103.9 4.0 %collective-permute-start.33 = (f32[64,128]{1,0:T(8,128)S(1)}, f32[64,128]{1,0:T(8,128)S(1)}, u32[]{:S(2)}, u32[]{:S(2)}) collective-permute-start(f32[64,128]{1,0:T(8,128)S(1)} %get-tuple-element.39), channel_id=1, source_target_pairs={{0,16},{8,24},{16,0},{24,8},{1,17},{9,25},{17,1},{25,9},{2,18},{10... | collective-permute-start | bytes 98312 | tf_op jit(solution)/shard_map/ppermute | solution.py:297
  (11 other events, 25.1 us)
